TPU v7x, 256 devices: a whole 4x4x8 slice. The times are simulated.
256 devices in a mesh: sec: 2 (over z_hi), tile: 32 (over x, z_lo, core), tp: 4 (over y).
Axes of the slice: x: 4, y: 4, z: 8 (z_hi: 2, z_lo: 4; z = z_hi * 4 + z_lo), core: 2. Of those that a mesh axis runs over, the one named last changes fastest.
Arguments:
- global_state: bfloat16 [32768, 1024], P(('sec', 'tile')), may hold values from -60 to 60
- band_codes: int32 [64], P(('sec', 'tile')), may hold values from 0 to 999999
- norm_gain: bfloat16 [1024], replicated, may hold values from 0.5 to 1.5
- w_query: bfloat16 [1024, 1024], P(None, 'tp'), may hold values from -32 to 32
- w_key: bfloat16 [1024, 1024], P(None, 'tp'), may hold values from -1 to 1
- w_value: bfloat16 [1024, 1024], P(None, 'tp'), may hold values from -0.1875 to 0.1875
- w_out: bfloat16 [1024, 1024], P('tp'), may hold values from -2.390625 to 2.390625
- reg_state: bfloat16 [2048, 16, 512], P(('sec', 'tile', 'tp')), may hold values from -6 to 6
- src_band: int32 [2048, 16, 1], P(('sec', 'tile', 'tp')), may hold values from 0 to 63; in each aligned block of 128 rows (0 to 127, 128 to 255, ..., all dimensions but the last counted through in order) at most 4 rows name the same one
- src_tok: int32 [2048, 16], P(('sec', 'tile', 'tp')), may hold values from 0 to 127
- w_bound: bfloat16 [1024, 512], replicated, may hold values from -0.1875 to 0.1875
- conv_w: bfloat16 [9, 512, 512], replicated, may hold values from -0.09375 to 0.09375
Outputs:
- global_out: bfloat16 [3, 32768, 1024], P(None, ('sec', 'tile', 'tp'))
- regional_out: bfloat16 [3, 2048, 16, 512], P(None, ('sec', 'tile', 'tp'))
Inputs may be any that keep to these rules, and one draw needn't show every extreme that they name: `src_band`: among the cells of one device (aligned blocks of 128 cells in the order column, then row), no band is named by more than 4 cells.
All inputs are finite; a program needn't handle non-finite values.
Results may differ from a plain program's by a relative error of at most 0.02.
Values may be sent and summed in bfloat16 or wider, within the bound.
No kernel may reach another device: no remote copies, remote signals or barrier semaphores. Data moves between devices by JAX's collectives and lax.ppermute only.
A program may use at most 128 MiB of HBM per device.

v0:
```python
import functools

import jax
import jax.numpy as jnp
from jax import lax
from jax.experimental import pallas as pl
from jax.experimental.pallas import tpu as pltpu
from jax.sharding import PartitionSpec as P

HD = 64
SIGNS = (0.0, 1.0, -1.0)
BANDS = ("sec", "tile")
CELLS = ("sec", "tile", "tp")
LOG2E = 1.4426950408889634
VMEM_LIMIT = 56 * 1024 * 1024

mix_band = 73856093
mix_token = 19349663
mix_feature = 83492791
mix_again = 668265261


def iota(shape, dim):
    return lax.broadcasted_iota(jnp.int32, shape, dim)


def dot(a, b):
    return jnp.dot(a, b, preferred_element_type=jnp.float32)


def dot_t(a, b):
    return lax.dot_general(a, b, (((1,), (1,)), ((), ())), preferred_element_type=jnp.float32)


def wiggle(code, first_token, rows, features):
    by_row = code * mix_band + (first_token + iota((rows, 1), 0)) * mix_token
    mixed = by_row + iota((1, features), 1) * mix_feature
    mixed = lax.bitwise_xor(mixed, lax.shift_right_arithmetic(mixed, jnp.full_like(mixed, 15)))
    mixed = mixed * mix_again
    mixed = lax.bitwise_xor(mixed, lax.shift_right_arithmetic(mixed, jnp.full_like(mixed, 13)))
    level = lax.bitwise_and(mixed, 1023).astype(jnp.float32)
    return (level - 511.5) * (0.5 / 295.6)


def project_kernel(band_ref, *refs, halo):
    if halo:
        step = pl.program_id(0)
        before_ref, after_ref, gain_ref, *refs = refs
        rows = before_ref.shape[0] - 16
        came = jnp.where(step == 0, before_ref[...], after_ref[...]).astype(jnp.float32)
        x = came[:rows]
        first = (1 - step) * rows
        digits = came[rows : rows + 1, 0:128]
        lane = iota((1, 128), 1)
        place = jnp.where(lane == 0, 65536.0, jnp.where(lane == 1, 256.0, 1.0))
        code = jnp.sum(jnp.where(lane < 3, digits * place, 0.0), -1, keepdims=True)
        code = code.astype(jnp.int32)
    else:
        x_ref, gain_ref, *refs = refs
        rows = x_ref.shape[0]
        x = x_ref[...].astype(jnp.float32)
        first = pl.program_id(0) * rows
        code = jnp.full((1, 1), band_ref[2], jnp.int32)
    weights, outs = refs[: len(refs) // 2], refs[len(refs) // 2 :]
    features = x.shape[1]
    p = wiggle(code, first, rows, features)
    gain = gain_ref[...].astype(jnp.float32)
    x_scaled = (x * gain).astype(jnp.bfloat16)
    p_scaled = (p * gain).astype(jnp.bfloat16)
    inv = []
    for sign in SIGNS:
        state = x if sign == 0.0 else (x + p if sign > 0 else x - p)
        inv.append(lax.rsqrt(jnp.sum(state * state, -1, keepdims=True) / features + 1e-06))
    for index, (w_ref, out_ref) in enumerate(zip(weights, outs)):
        scale = HD**-0.5 * LOG2E if (index == 0 and not halo) else 1.0
        base = dot(x_scaled, w_ref[...])
        diff = dot(p_scaled, w_ref[...])
        for s, sign in enumerate(SIGNS):
            out_ref[s] = ((base + sign * diff) * (inv[s] * scale)).astype(jnp.bfloat16)


def project(band, arrays, gain, weights, halo):
    features = gain.shape[1]
    cols = weights[0].shape[1]
    whole = lambda i, b: (0, 0)
    if halo:
        tokens = 2 * (arrays[0].shape[0] - 16)
        specs = [pl.BlockSpec(a.shape, whole) for a in arrays]
    else:
        tokens = arrays[0].shape[0]
        specs = [pl.BlockSpec((tokens // 2, features), lambda i, b: (i, 0))]
    rows = tokens // 2
    return pl.pallas_call(
        functools.partial(project_kernel, halo=halo),
        out_shape=[jax.ShapeDtypeStruct((3, tokens, cols), jnp.bfloat16) for _ in weights],
        grid_spec=pltpu.PrefetchScalarGridSpec(
            num_scalar_prefetch=1,
            grid=(2,),
            in_specs=specs
            + [pl.BlockSpec(gain.shape, whole)]
            + [pl.BlockSpec(w.shape, whole) for w in weights],
            out_specs=[pl.BlockSpec((3, rows, cols), lambda i, b: (0, i, 0)) for _ in weights],
        ),
        compiler_params=pltpu.CompilerParams(vmem_limit_bytes=VMEM_LIMIT),
        name="project_halo" if halo else "project_own",
    )(band, *arrays, gain, *weights)


def attend_kernel(band_ref, q_ref, k_ref, v_ref, k_halo_ref, v_halo_ref, out_ref, *, bands):
    tokens, cols = q_ref.shape[1:]
    half = tokens // 2
    left = band_ref[0] > 0
    right = band_ref[0] < bands - 1
    head_of = iota((1, cols), 1) // HD
    k = k_ref[0]
    v = v_ref[0]
    row = iota((tokens, 1), 0)
    there = jnp.where(row < half, left.astype(jnp.int32), right.astype(jnp.int32)) > 0
    k_halo = jnp.where(there, k_halo_ref[0], k)
    v_halo = v_halo_ref[0]
    one = there.astype(jnp.bfloat16)
    v_halo = v_halo * one
    result = [None] * 4
    block = half
    for part in range(tokens // block):
        q = q_ref[0, part * block : (part + 1) * block, :]
        gathered = jnp.zeros((block, cols), jnp.float32)
        for head in range(cols // HD):
            mine = head_of == head
            q_head = jnp.where(mine, q, jnp.zeros_like(q))
            own = dot_t(q_head, k)
            far = dot_t(q_head, k_halo)
            top = jnp.maximum(
                jnp.max(own, -1, keepdims=True), jnp.max(far, -1, keepdims=True)
            )
            own = jnp.exp2(own - top).astype(jnp.bfloat16)
            far = jnp.exp2(far - top).astype(jnp.bfloat16)
            v_own = jnp.where(mine, v, jnp.ones_like(v))
            v_far = jnp.where(mine, v_halo, jnp.broadcast_to(one, v.shape))
            acc = dot(own, v_own) + dot(far, v_far)
            total = pltpu.roll(acc, cols // 2, 1)
            gathered = jnp.where(mine, acc / total, gathered)
        gathered = gathered.astype(jnp.bfloat16)
        quarter = out_ref.shape[2]
        for piece in range(block // quarter):
            out_ref[part * (block // quarter) + piece, 0] = gathered[
                piece * quarter : (piece + 1) * quarter
            ]


def attend(band, q, k, v, k_halo, v_halo, ranks, bands):
    forwards, tokens, cols = q.shape
    spec = pl.BlockSpec((1, tokens, cols), lambda i, b: (i, 0, 0))
    quarter = tokens // ranks
    return pl.pallas_call(
        functools.partial(attend_kernel, bands=bands),
        out_shape=jax.ShapeDtypeStruct((ranks, forwards, quarter, cols), jnp.bfloat16),
        grid_spec=pltpu.PrefetchScalarGridSpec(
            num_scalar_prefetch=1,
            grid=(forwards,),
            in_specs=[spec] * 5,
            out_specs=pl.BlockSpec((ranks, 1, quarter, cols), lambda i, b: (0, i, 0, 0)),
        ),
        compiler_params=pltpu.CompilerParams(vmem_limit_bytes=VMEM_LIMIT),
        name="attend",
    )(band, q, k, v, k_halo, v_halo)


def ask_kernel(row_ref, col_ref, ask_ref, take_ref):
    bands = ask_ref.shape[0]
    cells = row_ref.shape[1]
    named = row_ref[...]
    band_row = lax.shift_right_arithmetic(named, jnp.full_like(named, 7))
    token = lax.bitwise_and(named, 127).astype(jnp.float32)
    match = (band_row == iota((bands, cells), 0)).astype(jnp.float32)
    before = (iota((cells, cells), 0) < iota((cells, cells), 1)).astype(jnp.float32)
    slot = dot(match.astype(jnp.bfloat16), before.astype(jnp.bfloat16))
    lanes = iota((bands, cells), 1)
    asked = jnp.zeros((bands, cells), jnp.float32)
    for s in range(4):
        hit = jnp.where(slot == s, match, 0.0)
        token_s = jnp.sum(hit * (token + 1.0), -1, keepdims=True) - 1.0
        asked = jnp.where(lanes == s, token_s, asked)
    ask_ref[...] = asked[:, :4].astype(jnp.int32)

    named = col_ref[...]
    band_col = lax.shift_right_arithmetic(named, jnp.full_like(named, 7))
    earlier = (band_col == band_row) & (iota((cells, cells), 1) < iota((cells, cells), 0))
    slot_col = jnp.sum(earlier.astype(jnp.float32), -1, keepdims=True).astype(jnp.int32)
    target = band_col * 16 + slot_col * 4
    rows = take_ref.shape[1]
    for part in range(4):
        take_ref[part * cells : (part + 1) * cells, :] = (
            (iota((cells, rows), 1) == target + part).astype(jnp.float32).astype(jnp.bfloat16)
        )


def ask(row, col, bands):
    cells = row.shape[1]
    return pl.pallas_call(
        ask_kernel,
        out_shape=[
            jax.ShapeDtypeStruct((bands, 4), jnp.int32),
            jax.ShapeDtypeStruct((4 * cells, bands * 16), jnp.bfloat16),
        ],
        compiler_params=pltpu.CompilerParams(vmem_limit_bytes=VMEM_LIMIT),
        name="ask",
    )(row, col)


def pick_rows(asked, rows, cells):
    bands = asked.shape[0]
    spread = (iota((rows, bands), 0) // 16 == iota((rows, bands), 1)).astype(jnp.float32)
    per_row = dot(spread.astype(jnp.bfloat16), asked.astype(jnp.float32).astype(jnp.bfloat16))
    r = iota((rows, 1), 0)
    mine = iota((rows, 4), 1) == (r // 4) % 4
    token_r = jnp.sum(jnp.where(mine, per_row, 0.0), -1, keepdims=True).astype(jnp.int32)
    target = jnp.where(token_r >= 0, (r % 4) * cells + token_r, -1)
    return (iota((rows, 4 * cells), 1) == target).astype(jnp.float32).astype(jnp.bfloat16)


def combine_kernel(where_ref, att_ref, w_out_ref, x_ref, w_bound_ref, asked_ref, out_ref, send_ref):
    ranks, _, cols = att_ref.shape
    quarter, features = x_ref.shape
    code = jnp.full((1, 1), where_ref[2], jnp.int32)
    x = x_ref[...].astype(jnp.float32)
    p = wiggle(code, where_ref[1] * quarter, quarter, features)
    rows = []
    for s, sign in enumerate(SIGNS):
        part = x + sign * p
        for g in range(ranks):
            part = part + dot(
                att_ref[g, s * quarter : (s + 1) * quarter, :],
                w_out_ref[g * cols : (g + 1) * cols, :],
            )
        part = part.astype(jnp.bfloat16)
        out_ref[s] = part
        rows.append(dot(part, w_bound_ref[...]).astype(jnp.bfloat16))
    parts = rows[0].shape[1] // 128
    table = jnp.concatenate(
        [
            jnp.concatenate([f[:, c * 128 : (c + 1) * 128] for f in rows], 1)
            for c in range(parts)
        ],
        0,
    )
    pick = pick_rows(asked_ref[...], send_ref.shape[0] * 16, quarter)
    picked = dot(pick, table).astype(jnp.bfloat16)
    send_ref[...] = picked.reshape(send_ref.shape)


def combine(where, att, w_out, x, w_bound, asked):
    ranks = att.shape[0]
    quarter = x.shape[0] // ranks
    features = x.shape[1]
    shapes = [(3, quarter, features), (asked.shape[0], 16, 384)]
    whole2 = lambda i, b: (0, 0)
    whole3 = lambda i, b: (0, 0, 0)
    return pl.pallas_call(
        combine_kernel,
        out_shape=[jax.ShapeDtypeStruct(s, jnp.bfloat16) for s in shapes],
        grid_spec=pltpu.PrefetchScalarGridSpec(
            num_scalar_prefetch=1,
            grid=(1,),
            in_specs=[
                pl.BlockSpec(att.shape, whole3),
                pl.BlockSpec(w_out.shape, whole2),
                pl.BlockSpec((quarter, features), lambda i, b: (b[1], 0)),
                pl.BlockSpec(w_bound.shape, whole2),
                pl.BlockSpec(asked.shape, whole2),
            ],
            out_specs=[pl.BlockSpec(s, whole3) for s in shapes],
        ),
        compiler_params=pltpu.CompilerParams(vmem_limit_bytes=VMEM_LIMIT),
        name="combine",
    )(where, att, w_out, x, w_bound, asked)


def inputs_kernel(arrived_ref, take_ref, reg_ref, out_ref, first_ref, last_ref):
    cols, rows, channels = reg_ref.shape
    cells = cols * rows
    table = arrived_ref[...].reshape(take_ref.shape[1], 384)
    taken = dot(take_ref[...], table)
    for part in range(channels // 128):
        lanes = slice(part * 128, (part + 1) * 128)
        reg = reg_ref[:, :, lanes].astype(jnp.float32)
        for s in range(3):
            forced = taken[part * cells : (part + 1) * cells, s * 128 : (s + 1) * 128]
            made = (reg + forced.reshape(cols, rows, 128)).astype(jnp.bfloat16)
            out_ref[:, s * rows : (s + 1) * rows, lanes] = made
            first_ref[s * rows : (s + 1) * rows, lanes] = made[0]
            last_ref[s * rows : (s + 1) * rows, lanes] = made[cols - 1]


def make_inputs(arrived, take, reg):
    cols, rows, channels = reg.shape
    shapes = [(cols, 3 * rows, channels), (3 * rows, channels), (3 * rows, channels)]
    return pl.pallas_call(
        inputs_kernel,
        out_shape=[jax.ShapeDtypeStruct(s, jnp.bfloat16) for s in shapes],
        compiler_params=pltpu.CompilerParams(vmem_limit_bytes=VMEM_LIMIT),
        name="inputs",
    )(arrived, take, reg)


def conv_kernel(x_ref, before_ref, after_ref, w_ref, out_ref):
    cols, slab, channels = x_ref.shape
    rows = slab // 3
    x = x_ref[...].reshape(cols * slab, channels)
    padded = jnp.concatenate([before_ref[...], x, after_ref[...]], 0)
    wide = padded.astype(jnp.float32)
    total = padded.shape[0]
    row = iota((total, 1), 0) % rows
    shifted = [
        jnp.where(row > 0, pltpu.roll(wide, 1, 0), 0.0).astype(jnp.bfloat16),
        padded,
        jnp.where(row < rows - 1, pltpu.roll(wide, total - 1, 0), 0.0).astype(jnp.bfloat16),
    ]
    conv = None
    for a in range(3):
        for b in range(3):
            piece = dot(shifted[b][a * slab : a * slab + cols * slab], w_ref[3 * a + b])
            conv = piece if conv is None else conv + piece
    result = x.astype(jnp.float32) + conv / (1.0 + jnp.exp(-conv))
    result = result.astype(jnp.bfloat16).reshape(cols, slab, channels)
    for s in range(3):
        out_ref[s] = result[:, s * rows : (s + 1) * rows, :]


def convolve(x, before, after, conv_w):
    cols, slab, channels = x.shape
    return pl.pallas_call(
        conv_kernel,
        out_shape=jax.ShapeDtypeStruct((3, cols, slab // 3, channels), jnp.bfloat16),
        compiler_params=pltpu.CompilerParams(vmem_limit_bytes=VMEM_LIMIT),
        name="convolve",
    )(x, before, after, conv_w)


def neighbours(last, first, axis):
    count = lax.axis_size(axis)
    up = [(i, i + 1) for i in range(count - 1)]
    down = [(j, i) for i, j in up]
    return lax.ppermute(last, axis, up), lax.ppermute(first, axis, down)


def per_device(
    global_state,
    band_codes,
    norm_gain,
    w_query,
    w_key,
    w_value,
    w_out,
    reg_state,
    src_band,
    src_tok,
    w_bound,
    conv_w,
):
    ranks = lax.axis_size("tp")
    bands = lax.axis_size(BANDS)
    rank = lax.axis_index("tp")
    band = lax.axis_index(BANDS)
    tokens = global_state.shape[0]
    half = tokens // 2
    cells = src_tok.size
    gain = norm_gain[None, :]

    named = src_band.reshape(cells) * 128 + src_tok.reshape(cells)
    asked, take = ask(named[None, :], named[:, None], bands)
    w_out_all = lax.all_gather(w_out, "tp", axis=0, tiled=True)
    code = band_codes[0]
    digits = jnp.stack([code // 65536, (code // 256) % 256, code % 256]).astype(jnp.bfloat16)
    digits = jnp.pad(digits[None], ((0, 15), (0, global_state.shape[1] - 3)))
    before, after = neighbours(
        jnp.concatenate([global_state[half:], digits]),
        jnp.concatenate([global_state[:half], digits]),
        BANDS,
    )
    asked = lax.all_to_all(asked[:, None, :], BANDS, 0, 0, tiled=True)[:, 0, :]

    where = jnp.stack([band, rank, code])
    q, k, v = project(where, [global_state], gain, [w_query, w_key, w_value], False)
    k_halo, v_halo = project(where, [before, after], gain, [w_key, w_value], True)
    attended = attend(where, q, k, v, k_halo, v_halo, ranks, bands)
    attended = lax.all_to_all(
        attended.reshape(ranks, -1, attended.shape[-1]), "tp", 0, 0, tiled=True
    )
    global_out, send = combine(where, attended, w_out_all, global_state, w_bound, asked)
    arrived = lax.all_to_all(send, BANDS, 0, 0, tiled=True)
    inputs, first, last = make_inputs(arrived, take, reg_state)
    before, after = neighbours(last, first, CELLS)
    return global_out, convolve(inputs, before, after, conv_w)


def solution(mesh):
    placed = (
        P(("sec", "tile"), None),
        P(("sec", "tile")),
        P(),
        P(None, "tp"),
        P(None, "tp"),
        P(None, "tp"),
        P("tp", None),
        P(("sec", "tile", "tp"), None, None),
        P(("sec", "tile", "tp"), None, None),
        P(("sec", "tile", "tp"), None),
        P(),
        P(),
    )
    return jax.shard_map(
        per_device,
        mesh=mesh,
        in_specs=placed,
        out_specs=(
            P(None, ("sec", "tile", "tp"), None),
            P(None, ("sec", "tile", "tp"), None, None),
        ),
        check_vma=False,
    )
```

profile of v0, /device:TPU:4, one launch (start us, length us, event | category | flops | bytes accessed | tf_op | source)
XLA Modules:
  0.0 146.2 jit_solution(11084142652848012819)
XLA Ops:
  7.2 0.0 all-gather.2.cloned.1.call-start
  7.2 0.7 all-gather.2.cloned.1.call-update
  8.6 0.1 fusion.8
  8.7 1.3 fusion.10
  10.0 0.1 pad_maximum_fusion
  10.1 1.9 %collective-permute-start = (bf16[272,1024]{1,0:T(8,128)(2,1)S(1)}, bf16[272,1024]{1,0:T(8,128)(2,1)S(1)}, u32[]{:S(2)}, u32[]{:S(2)}) collective-permute-start(bf16[272,1024]{1,0:T(8,128)(2,1)S(1)} %get-tuple-element.29), channel_id=1, source_target_pairs={{0,4},{4,8},{8,12},{12,16},{16,20},{20,24},{24,28},{28,32},{32,36}... | collective-permute-start | bytes 1671176 | tf_op jit(solution)/shard_map/ppermute | solution.py:344
  12.0 6.3 %collective-permute-start.1 = (bf16[272,1024]{1,0:T(8,128)(2,1)S(1)}, bf16[272,1024]{1,0:T(8,128)(2,1)S(1)}, u32[]{:S(2)}, u32[]{:S(2)}) collective-permute-start(bf16[272,1024]{1,0:T(8,128)(2,1)S(1)} %get-tuple-element.28), channel_id=1, source_target_pairs={{4,0},{8,4},{12,8},{16,12},{20,16},{24,20},{28,24},{32,28},{36,32}... | collective-permute-start | bytes 1671176 | tf_op jit(solution)/shard_map/ppermute | solution.py:344
  18.4 0.1 reshape.107
  18.5 0.1 reshape.106
  18.6 0.1 mul.33
  18.7 0.7 copy.19.col_ref
  19.4 0.1 mul.32
  19.5 0.5 add.36.row_ref
  20.0 2.2 %ask.1 = (s32[64,4]{1,0:T(8,128)}, bf16[512,1024]{1,0:T(8,128)(2,1)}) custom-call(s32[1,128]{1,0:T(1,128)} %add.36.row_ref, s32[128,1]{1,0:T(8,128)} %copy.19.col_ref), custom_call_target="tpu_custom_call" | custom-call | tf_op jit(solution)/shard_map/ask/pallas_call | solution.py:200
  22.3 12.0 %all-to-all-start.1 = ((s32[64,1,4]{2,1,0:T(1,128)}), s32[64,1,4]{2,1,0:T(1,128)S(1)}, u32[]{:S(2)}, u32[]{:S(2)}) async-start(s32[64,1,4]{2,1,0:T(1,128)} %bitcast.18), calls=%async_computation.1 | async-start | bytes 65536 | tf_op jit(solution)/shard_map/all_to_all | solution.py:381
  34.3 0.6 pad_add_fusion.band_ref.where_ref
  34.9 0.6 broadcast_in_dim.4.refs_1_.refs_2_
  35.5 6.2 %project_own.1 = (bf16[3,512,256]{2,1,0:T(8,128)(2,1)}, bf16[3,512,256]{2,1,0:T(8,128)(2,1)}, bf16[3,512,256]{2,1,0:T(8,128)(2,1)}) custom-call(s32[3]{0:T(128)} %pad_add_fusion.band_ref.where_ref, bf16[512,1024]{1,0:T(8,128)(2,1)} %x_ref.1, bf16[1,1024]{1,0:T(2,128)(2,1)} %broadcast_in_dim.4.refs_1_.refs_2_, bf16[1024,256]{1,0:T(8,128)(2,1)} %refs_2_.1, ...), custom_call_target="tpu_custom_call" | custom-call | tf_op jit(solution)/shard_map/project_own/pallas_call | solution.py:93
  41.7 0.8 copy-done
  42.5 0.8 copy-done.1
  43.3 5.9 %project_halo.1 = (bf16[3,512,256]{2,1,0:T(8,128)(2,1)}, bf16[3,512,256]{2,1,0:T(8,128)(2,1)}) custom-call(s32[3]{0:T(128)} %pad_add_fusion.band_ref.where_ref, bf16[272,1024]{1,0:T(8,128)(2,1)} %copy-done, bf16[272,1024]{1,0:T(8,128)(2,1)} %copy-done.1, bf16[1,1024]{1,0:T(2,128)(2,1)} %broadcast_in_dim.4.refs_1_.refs_2_, bf16[1024,256]{1,0:T(8,128)(2,1)} %refs_3_.3, ...), custom_call_target="tpu_custom_call" | custom-call | tf_op jit(solution)/shard_map/project_halo/pallas_call | solution.py:93
  49.2 11.6 %attend.1 = bf16[4,3,128,256]{3,2,1,0:T(8,128)(2,1)} custom-call(s32[3]{0:T(128)} %pad_add_fusion.band_ref.where_ref, bf16[3,512,256]{2,1,0:T(8,128)(2,1)} %get-tuple-element.14.q_ref, bf16[3,512,256]{2,1,0:T(8,128)(2,1)} %get-tuple-element.15.k_ref, bf16[3,512,256]{2,1,0:T(8,128)(2,1)} %get-tuple-element.16.v_ref, ...), custom_call_target="tpu_custom_call" | custom-call | tf_op jit(solution)/shard_map/attend/pallas_call | solution.py:155
  60.8 17.2 %all_to_all.15.att_ref = bf16[4,384,256]{2,1,0:T(8,128)(2,1)} all-to-all(bf16[4,384,256]{2,1,0:T(8,128)(2,1)} %bitcast.16), channel_id=1, replica_groups=mesh['sec'=2,'tile'=32,'tp'=4] {'tp'}, dimensions={0} | all-to-all | bytes 1572864 | tf_op jit(solution)/shard_map/all_to_all | solution.py:387
  78.0 6.3 %combine.1 = (bf16[3,128,1024]{2,1,0:T(8,128)(2,1)}, bf16[64,16,384]{2,1,0:T(8,128)(2,1)}) custom-call(s32[3]{0:T(128)} %pad_add_fusion.band_ref.where_ref, bf16[4,384,256]{2,1,0:T(8,128)(2,1)} %all_to_all.15.att_ref, bf16[1024,1024]{1,0:T(8,128)(2,1)} %all-gather.2.cloned.1.call-done.w_out_ref, bf16[512,1024]{1,0:T(8,128)(2,1)} %x_ref.1, ...), custom_call_target="tpu_custom_call" | custom-call | tf_op jit(solution)/shard_map/combine/pallas_call | solution.py:259
  84.3 33.7 %all_to_all.16.arrived_ref = bf16[64,16,384]{2,1,0:T(8,128)(2,1)} all-to-all(bf16[64,16,384]{2,1,0:T(8,128)(2,1)} %get-tuple-element.21), channel_id=1, replica_groups=mesh['sec'=2,'tile'=32,'tp'=4] {'sec','tile'}, dimensions={0} | all-to-all | bytes 1572864 | tf_op jit(solution)/shard_map/all_to_all | solution.py:391
  118.0 2.9 %inputs.1 = (bf16[8,48,512]{2,1,0:T(8,128)(2,1)}, bf16[48,512]{1,0:T(8,128)(2,1)}, bf16[48,512]{1,0:T(8,128)(2,1)}) custom-call(bf16[64,16,384]{2,1,0:T(8,128)(2,1)} %all_to_all.16.arrived_ref, bf16[512,1024]{1,0:T(8,128)(2,1)} %get-tuple-element.22.take_ref, bf16[8,16,512]{2,1,0:T(8,128)(2,1)} %reg_ref.1), custom_call_target="tpu_custom_call" | custom-call | tf_op jit(solution)/shard_map/inputs/pallas_call | solution.py:298
  120.9 2.5 %collective-permute-start.2 = (bf16[48,512]{1,0:T(8,128)(2,1)}, bf16[48,512]{1,0:T(8,128)(2,1)S(1)}, u32[]{:S(2)}, u32[]{:S(2)}) collective-permute-start(bf16[48,512]{1,0:T(8,128)(2,1)} %get-tuple-element.24), channel_id=1, source_target_pairs={{0,1},{1,2},{2,3},{3,4},{4,5},{5,6},{6,7},{7,8},{8,9},{9,10},{10,1... | collective-permute-start | bytes 147464 | tf_op jit(solution)/shard_map/ppermute | solution.py:344
  123.4 7.9 %collective-permute-start.3 = (bf16[48,512]{1,0:T(8,128)(2,1)}, bf16[48,512]{1,0:T(8,128)(2,1)S(1)}, u32[]{:S(2)}, u32[]{:S(2)}) collective-permute-start(bf16[48,512]{1,0:T(8,128)(2,1)} %get-tuple-element.25), channel_id=1, source_target_pairs={{1,0},{2,1},{3,2},{4,3},{5,4},{6,5},{7,6},{8,7},{9,8},{10,9},{11,1... | collective-permute-start | bytes 147464 | tf_op jit(solution)/shard_map/ppermute | solution.py:344
  131.3 0.0 collective-permute-done.2.before_ref
  131.3 2.0 %collective-permute-done.3.after_ref = bf16[48,512]{1,0:T(8,128)(2,1)S(1)} collective-permute-done((bf16[48,512]{1,0:T(8,128)(2,1)}, bf16[48,512]{1,0:T(8,128)(2,1)S(1)}, u32[]{:S(2)}, u32[]{:S(2)}) %collective-permute-start.3) | collective-permute-done | bytes 49184 | tf_op jit(solution)/shard_map/ppermute | solution.py:344
  133.3 0.6 copy-done.4
  133.9 5.4 %convolve.1 = bf16[3,8,16,512]{3,2,1,0:T(8,128)(2,1)} custom-call(bf16[8,48,512]{2,1,0:T(8,128)(2,1)} %get-tuple-element.23.x_ref, bf16[48,512]{1,0:T(8,128)(2,1)} %copy-done.3, bf16[48,512]{1,0:T(8,128)(2,1)} %copy-done.4, bf16[9,512,512]{2,1,0:T(8,128)(2,1)} %w_ref.1), custom_call_target="tpu_custom_call" | custom-call | tf_op jit(solution)/shard_map/convolve/pallas_call | solution.py:332
  (19 shorter events, 0.1 us)
Async XLA Ops:
  7.2 70.8 %all-gather.2.cloned.1.call-start = ((), (), s32[]{:S(2)}) async-start(), calls=%async_computation.3 | async-start | bytes 2621440 | tf_op jit(solution)/shard_map/all_gather | solution.py:372
  10.0 8.4 %copy-start.5 = (s32[8,16]{1,0:T(8,128)S(1)}, s32[8,16]{1,0:T(8,128)}, u32[]{:S(2)}) copy-start(s32[8,16]{1,0:T(8,128)} %param.21) | copy-start | bytes 1540
  10.0 8.6 %copy-start.6 = (s32[8,16,1]{1,2,0:T(1,128)S(1)}, s32[8,16,1]{1,2,0:T(1,128)}, u32[]{:S(2)}) copy-start(s32[8,16,1]{1,2,0:T(1,128)} %param.20) | copy-start | bytes 1540
  10.0 24.9 %copy-start.7 = (bf16[1024]{0:T(1024)(128)(2,1)S(1)}, bf16[1024]{0:T(1024)(128)(2,1)}, u32[]{:S(2)}) copy-start(bf16[1024]{0:T(1024)(128)(2,1)} %param.14) | copy-start | bytes 6148
  10.1 31.6 %collective-permute-start = (bf16[272,1024]{1,0:T(8,128)(2,1)S(1)}, bf16[272,1024]{1,0:T(8,128)(2,1)S(1)}, u32[]{:S(2)}, u32[]{:S(2)}) collective-permute-start(bf16[272,1024]{1,0:T(8,128)(2,1)S(1)} %get-tuple-element.29), channel_id=1, source_target_pairs={{0,4},{4,8},{8,12},{12,16},{16,20},{20,24},{24,28},{28,32},{32,36}... | collective-permute-start | bytes 1671176 | tf_op jit(solution)/shard_map/ppermute | solution.py:344
  12.0 29.6 %collective-permute-start.1 = (bf16[272,1024]{1,0:T(8,128)(2,1)S(1)}, bf16[272,1024]{1,0:T(8,128)(2,1)S(1)}, u32[]{:S(2)}, u32[]{:S(2)}) collective-permute-start(bf16[272,1024]{1,0:T(8,128)(2,1)S(1)} %get-tuple-element.28), channel_id=1, source_target_pairs={{4,0},{8,4},{12,8},{16,12},{20,16},{24,20},{28,24},{32,28},{36,32}... | collective-permute-start | bytes 1671176 | tf_op jit(solution)/shard_map/ppermute | solution.py:344
  22.3 38.5 %all-to-all-start.1 = ((s32[64,1,4]{2,1,0:T(1,128)}), s32[64,1,4]{2,1,0:T(1,128)S(1)}, u32[]{:S(2)}, u32[]{:S(2)}) async-start(s32[64,1,4]{2,1,0:T(1,128)} %bitcast.18), calls=%async_computation.1 | async-start | bytes 65536 | tf_op jit(solution)/shard_map/all_to_all | solution.py:381
  41.7 0.8 copy-start
  42.5 0.8 copy-start.1
  60.8 17.2 %copy-start.2 = (s32[64,1,4]{2,1,0:T(1,128)}, s32[64,1,4]{2,1,0:T(1,128)S(1)}, u32[]{:S(2)}) copy-start(s32[64,1,4]{2,1,0:T(1,128)S(1)} %all-to-all-done.1) | copy-start | bytes 3076
  120.9 10.4 %collective-permute-start.2 = (bf16[48,512]{1,0:T(8,128)(2,1)}, bf16[48,512]{1,0:T(8,128)(2,1)S(1)}, u32[]{:S(2)}, u32[]{:S(2)}) collective-permute-start(bf16[48,512]{1,0:T(8,128)(2,1)} %get-tuple-element.24), channel_id=1, source_target_pairs={{0,1},{1,2},{2,3},{3,4},{4,5},{5,6},{6,7},{7,8},{8,9},{9,10},{10,1... | collective-permute-start | bytes 147464 | tf_op jit(solution)/shard_map/ppermute | solution.py:344
  123.4 9.9 %collective-permute-start.3 = (bf16[48,512]{1,0:T(8,128)(2,1)}, bf16[48,512]{1,0:T(8,128)(2,1)S(1)}, u32[]{:S(2)}, u32[]{:S(2)}) collective-permute-start(bf16[48,512]{1,0:T(8,128)(2,1)} %get-tuple-element.25), channel_id=1, source_target_pairs={{1,0},{2,1},{3,2},{4,3},{5,4},{6,5},{7,6},{8,7},{9,8},{10,9},{11,1... | collective-permute-start | bytes 147464 | tf_op jit(solution)/shard_map/ppermute | solution.py:344
  131.3 2.0 %copy-start.3 = (bf16[48,512]{1,0:T(8,128)(2,1)}, bf16[48,512]{1,0:T(8,128)(2,1)S(1)}, u32[]{:S(2)}) copy-start(bf16[48,512]{1,0:T(8,128)(2,1)S(1)} %collective-permute-done.2.before_ref) | copy-start | bytes 147460
  133.3 0.6 copy-start.4
Sparse Core Ops, SparseCore 0:
  9.8 36.3 all-gather.1
where the time goes:
time: 147 us; the launch traced here: 146 us
  blocking collectives  50.9 us (35%)
  Pallas kernels  40.5 us (28%)
  starting transfers between devices  30.6 us (21%)
  between operations  14.9 us (10%)
  local copies, waits for them, and re-layouts  5.17 us (4%)
  waiting for transfers between devices  2.73 us (2%)
    all_to_all x1, blocking collectives, per_device(): arrived = lax.all_to_all(send, BANDS, 0, 0, tiled=True)  33.7 us
    ppermute x4, starting transfers between devices, neighbours(): return (lax.ppermute(last, axis, up), lax.ppermute(first, axis, down))  18.6 us
    all_to_all x1, blocking collectives, per_device(): lax.all_to_all(attended.reshape(ranks, -1, attended.shape[-1]), 'tp', 0,...  17.2 us
    pallas_call x2, Pallas kernels, project(): pl.pallas_call(functools.partial(project_kernel, halo=halo), out_shape=[j...  12.1 us
    all_to_all x1, starting transfers between devices, per_device(): asked = lax.all_to_all(asked[:, None, :], BANDS, 0, 0, tiled=True)[:, 0, :]  12 us
    pallas_call x1, Pallas kernels, attend(): pl.pallas_call(functools.partial(attend_kernel, bands=bands), out_shape=j...  11.6 us
    pallas_call x1, Pallas kernels, combine(): pl.pallas_call(combine_kernel, out_shape=[jax.ShapeDtypeStruct(s, jnp.bfl...  6.31 us
    pallas_call x1, Pallas kernels, convolve(): pl.pallas_call(conv_kernel, out_shape=jax.ShapeDtypeStruct((3, cols, slab...  5.39 us
  transfers between devices with their start and end apart: 6, of which 1 were waited for; matrix products, arithmetic and copies ran while one was open for 3% of the time, Pallas kernels for 18%

commit v1 on v0

v1 whole, which is shorter than its diff:
```python
import functools

import jax
import jax.numpy as jnp
from jax import lax
from jax.experimental import pallas as pl
from jax.experimental.pallas import tpu as pltpu
from jax.sharding import PartitionSpec as P

HD = 64
SIGNS = (0.0, 1.0, -1.0)
BANDS = ("sec", "tile")
CELLS = ("sec", "tile", "tp")
LOG2E = 1.4426950408889634
MIB = 1024 * 1024
ON_CHIP = pl.BlockSpec(memory_space=pltpu.VMEM)
SCALARS = pl.BlockSpec(memory_space=pltpu.SMEM)

mix_band = 73856093
mix_token = 19349663
mix_feature = 83492791
mix_again = 668265261


def iota(shape, dim):
    return lax.broadcasted_iota(jnp.int32, shape, dim)


def dot(a, b):
    return jnp.dot(a, b, preferred_element_type=jnp.float32)


def dot_t(a, b):
    return lax.dot_general(a, b, (((1,), (1,)), ((), ())), preferred_element_type=jnp.float32)


def wiggle(code, first_token, rows, features):
    by_row = code * mix_band + (first_token + iota((rows, 1), 0)) * mix_token
    mixed = by_row + iota((1, features), 1) * mix_feature
    mixed = lax.bitwise_xor(mixed, lax.shift_right_arithmetic(mixed, jnp.full_like(mixed, 15)))
    mixed = mixed * mix_again
    mixed = lax.bitwise_xor(mixed, lax.shift_right_arithmetic(mixed, jnp.full_like(mixed, 13)))
    level = lax.bitwise_and(mixed, 1023).astype(jnp.float32)
    return (level - 511.5) * (0.5 / 295.6)


def project_kernel(code_ref, *refs, halo):
    step = pl.program_id(0)
    both_ref, inv_ref = refs[-2:]
    if halo:
        before_ref, after_ref, gain_ref, *refs = refs[:-2]
        rows = before_ref.shape[0] - 16
        first = (1 - step) * rows
        digits = jnp.where(
            step == 0, before_ref[rows : rows + 16, 0:128], after_ref[rows : rows + 16, 0:128]
        ).astype(jnp.float32)[0:1]
        lane = iota((1, 128), 1)
        place = jnp.where(lane == 0, 65536.0, jnp.where(lane == 1, 256.0, 1.0))
        code = jnp.sum(jnp.where(lane < 3, digits * place, 0.0), -1, keepdims=True)
        code = code.astype(jnp.int32)
    else:
        x_ref, gain_ref, *refs = refs[:-2]
        rows = x_ref.shape[0]
        first = step * rows
        code = jnp.full((1, 1), code_ref[0], jnp.int32)
    weights, outs = refs[: len(refs) // 2], refs[len(refs) // 2 :]
    features = gain_ref.shape[1]
    gain = gain_ref[...].astype(jnp.float32)
    chunk, block = 16, 128
    for at in range(0, rows, block):
        for r in range(at, at + block, chunk):
            if halo:
                x = jnp.where(step == 0, before_ref[r : r + chunk], after_ref[r : r + chunk])
            else:
                x = x_ref[r : r + chunk]
            x = x.astype(jnp.float32)
            p = wiggle(code, first + r, chunk, features)
            place = 2 * at + (r - at)
            both_ref[place : place + chunk] = (x * gain).astype(jnp.bfloat16)
            both_ref[place + block : place + block + chunk] = (p * gain).astype(jnp.bfloat16)
            for s, sign in enumerate(SIGNS):
                state = x if sign == 0.0 else (x + p if sign > 0 else x - p)
                mean = jnp.sum(state * state, -1, keepdims=True) * (1.0 / features)
                inv_ref[s, r : r + chunk] = lax.rsqrt(mean + 1e-06)
        here = slice(at, at + block)
        for index, (w_ref, out_ref) in enumerate(zip(weights, outs)):
            scale = HD**-0.5 * LOG2E if (index == 0 and not halo) else 1.0
            made = dot(both_ref[2 * at : 2 * at + 2 * block], w_ref[...])
            base, diff = made[:block], made[block:]
            for s, sign in enumerate(SIGNS):
                full = base if sign == 0.0 else (base + diff if sign > 0 else base - diff)
                out_ref[s, here] = (full * (inv_ref[s, here] * scale)).astype(jnp.bfloat16)


def project(code, arrays, gain, weights, halo):
    features = gain.shape[1]
    cols = weights[0].shape[1]
    whole = lambda i: (0, 0)
    if halo:
        tokens = 2 * (arrays[0].shape[0] - 16)
        specs = [ON_CHIP for a in arrays]
    else:
        tokens = arrays[0].shape[0]
        specs = [pl.BlockSpec((tokens // 2, features), lambda i: (i, 0))]
    rows = tokens // 2
    return pl.pallas_call(
        functools.partial(project_kernel, halo=halo),
        out_shape=[jax.ShapeDtypeStruct((3, tokens, cols), jnp.bfloat16) for _ in weights],
        grid=(2,),
        in_specs=[SCALARS]
        + specs
        + [pl.BlockSpec(gain.shape, whole)]
        + [pl.BlockSpec(w.shape, whole) for w in weights],
        out_specs=[pl.BlockSpec((3, rows, cols), lambda i: (0, i, 0)) for _ in weights],
        scratch_shapes=[
            pltpu.VMEM((2 * rows, features), jnp.bfloat16),
            pltpu.VMEM((3, rows, 1), jnp.float32),
        ],
        compiler_params=pltpu.CompilerParams(vmem_limit_bytes=20 * MIB),
        name="project_halo" if halo else "project_own",
    )(code, *arrays, gain, *weights)


def attend_kernel(q_ref, k_ref, v_ref, k_halo_ref, v_halo_ref, out_ref, *, bands):
    tokens, cols = q_ref.shape[1:]
    half = tokens // 2
    band = lax.axis_index(BANDS)
    left = band > 0
    right = band < bands - 1
    head_of = iota((1, cols), 1) // HD
    k = k_ref[0]
    v = v_ref[0]
    row = iota((tokens, 1), 0)
    there = jnp.where(row < half, left.astype(jnp.int32), right.astype(jnp.int32)) > 0
    k_halo = jnp.where(there, k_halo_ref[0], k)
    v_halo = v_halo_ref[0]
    one = there.astype(jnp.bfloat16)
    v_halo = v_halo * one
    result = [None] * 4
    block = half
    for part in range(tokens // block):
        q = q_ref[0, part * block : (part + 1) * block, :]
        gathered = jnp.zeros((block, cols), jnp.float32)
        for head in range(cols // HD):
            mine = head_of == head
            q_head = jnp.where(mine, q, jnp.zeros_like(q))
            own = dot_t(q_head, k)
            far = dot_t(q_head, k_halo)
            top = jnp.maximum(
                jnp.max(own, -1, keepdims=True), jnp.max(far, -1, keepdims=True)
            )
            own = jnp.exp2(own - top).astype(jnp.bfloat16)
            far = jnp.exp2(far - top).astype(jnp.bfloat16)
            v_own = jnp.where(mine, v, jnp.ones_like(v))
            v_far = jnp.where(mine, v_halo, jnp.broadcast_to(one, v.shape))
            acc = dot(own, v_own) + dot(far, v_far)
            total = pltpu.roll(acc, cols // 2, 1)
            gathered = jnp.where(mine, acc / total, gathered)
        gathered = gathered.astype(jnp.bfloat16)
        quarter = out_ref.shape[2]
        for piece in range(block // quarter):
            out_ref[part * (block // quarter) + piece, 0] = gathered[
                piece * quarter : (piece + 1) * quarter
            ]


def attend(q, k, v, k_halo, v_halo, ranks, bands):
    forwards, tokens, cols = q.shape
    spec = pl.BlockSpec((1, tokens, cols), lambda i: (i, 0, 0))
    quarter = tokens // ranks
    return pl.pallas_call(
        functools.partial(attend_kernel, bands=bands),
        out_shape=jax.ShapeDtypeStruct((ranks, forwards, quarter, cols), jnp.bfloat16),
        grid=(forwards,),
        in_specs=[spec] * 5,
        out_specs=pl.BlockSpec((ranks, 1, quarter, cols), lambda i: (0, i, 0, 0)),
        compiler_params=pltpu.CompilerParams(vmem_limit_bytes=24 * MIB),
        name="attend",
    )(q, k, v, k_halo, v_halo)


def cells_row(x):
    cols, rows = x.shape
    cells = cols * rows
    spread = (iota((rows, cells), 1) % rows == iota((rows, cells), 0)).astype(jnp.float32)
    wide = dot(x.astype(jnp.float32).astype(jnp.bfloat16), spread.astype(jnp.bfloat16))
    mine = iota((cols, cells), 1) // rows == iota((cols, cells), 0)
    return jnp.sum(jnp.where(mine, wide, 0.0), 0, keepdims=True)


def ask_kernel(band_ref, tok_ref, ask_ref):
    bands = ask_ref.shape[0]
    named = cells_row(band_ref[...])
    token = cells_row(tok_ref[...])
    cells = named.shape[1]
    match = (named.astype(jnp.int32) == iota((bands, cells), 0)).astype(jnp.float32)
    before = (iota((cells, cells), 0) < iota((cells, cells), 1)).astype(jnp.float32)
    slot = dot(match.astype(jnp.bfloat16), before.astype(jnp.bfloat16))
    lanes = iota((bands, cells), 1)
    asked = jnp.zeros((bands, cells), jnp.float32)
    for s in range(4):
        hit = jnp.where(slot == s, match, 0.0)
        token_s = jnp.sum(hit * (token + 1.0), -1, keepdims=True) - 1.0
        asked = jnp.where(lanes == s, token_s, asked)
    ask_ref[...] = asked[:, :4].astype(jnp.int32)


def ask(band, tok, bands):
    return pl.pallas_call(
        ask_kernel,
        out_shape=jax.ShapeDtypeStruct((bands, 4), jnp.int32),
        in_specs=[ON_CHIP] * 2,
        out_specs=ON_CHIP,
        compiler_params=pltpu.CompilerParams(vmem_limit_bytes=4 * MIB),
        name="ask",
    )(band, tok)


def take_kernel(band_ref, take_ref):
    band_row = cells_row(band_ref[...])
    cells = band_row.shape[1]
    rows = take_ref.shape[1]
    r, c = iota((cells, cells), 0), iota((cells, cells), 1)
    band_col = jnp.sum(jnp.where(r == c, band_row, 0.0), -1, keepdims=True)
    earlier = (band_col == band_row) & (c < r)
    slot = jnp.sum(jnp.where(earlier, 1.0, 0.0), -1, keepdims=True)
    target = (band_col * 16.0 + slot * 4.0).astype(jnp.int32)
    for part in range(4):
        take_ref[part * cells : (part + 1) * cells, :] = (
            (iota((cells, rows), 1) == target + part).astype(jnp.float32).astype(jnp.bfloat16)
        )


def make_take(band, bands):
    return pl.pallas_call(
        take_kernel,
        out_shape=jax.ShapeDtypeStruct((4 * band.size, bands * 16), jnp.bfloat16),
        in_specs=[ON_CHIP],
        out_specs=ON_CHIP,
        compiler_params=pltpu.CompilerParams(vmem_limit_bytes=8 * MIB),
        name="take",
    )(band)


def prepare_kernel(code_ref, asked_ref, pick_ref, p_ref):
    rows, wide = pick_ref.shape
    bands = asked_ref.shape[0]
    cells = wide // 4
    spread = (iota((rows, bands), 0) // 16 == iota((rows, bands), 1)).astype(jnp.float32)
    asked = asked_ref[...].astype(jnp.float32)
    per_row = dot(spread.astype(jnp.bfloat16), asked.astype(jnp.bfloat16))
    r = iota((rows, 1), 0)
    mine = iota((rows, 4), 1) == (r // 4) % 4
    token_r = jnp.sum(jnp.where(mine, per_row, 0.0), -1, keepdims=True).astype(jnp.int32)
    target = jnp.where(token_r >= 0, (r % 4) * cells + token_r, -1)
    pick_ref[...] = (iota((rows, wide), 1) == target).astype(jnp.float32).astype(jnp.bfloat16)
    quarter, features = p_ref.shape
    code = jnp.full((1, 1), code_ref[0], jnp.int32)
    p_ref[...] = wiggle(code, lax.axis_index("tp") * quarter, quarter, features)


def prepare(code, asked, quarter, features):
    return pl.pallas_call(
        prepare_kernel,
        out_shape=[
            jax.ShapeDtypeStruct((asked.shape[0] * 16, 4 * quarter), jnp.bfloat16),
            jax.ShapeDtypeStruct((quarter, features), jnp.float32),
        ],
        in_specs=[SCALARS, ON_CHIP],
        out_specs=[ON_CHIP] * 2,
        compiler_params=pltpu.CompilerParams(vmem_limit_bytes=12 * MIB),
        name="prepare",
    )(code, asked)


def combine_kernel(att_ref, w0_ref, w1_ref, w2_ref, w3_ref, x_ref, p_ref, w_bound_ref, pick_ref, out_ref, send_ref):
    ranks, _, cols = att_ref.shape
    quarter = p_ref.shape[0]
    rank = lax.axis_index("tp")
    x = x_ref[pl.ds(pl.multiple_of(rank * quarter, quarter), quarter), :].astype(jnp.float32)
    p = p_ref[...]
    total = None
    for d, w_ref in enumerate((w0_ref, w1_ref, w2_ref, w3_ref)):
        piece = dot(att_ref[lax.rem(rank + ranks - d, ranks)], w_ref[...])
        total = piece if total is None else total + piece
    made = []
    for s, sign in enumerate(SIGNS):
        part = x if sign == 0.0 else (x + p if sign > 0 else x - p)
        part = (part + total[s * quarter : (s + 1) * quarter]).astype(jnp.bfloat16)
        out_ref[s] = part
        made.append(part)
    forced = dot(jnp.concatenate(made, 0), w_bound_ref[...]).astype(jnp.bfloat16)
    rows = [forced[s * quarter : (s + 1) * quarter] for s in range(3)]
    parts = forced.shape[1] // 128
    table = jnp.concatenate(
        [
            jnp.concatenate([f[:, c * 128 : (c + 1) * 128] for f in rows], 1)
            for c in range(parts)
        ],
        0,
    )
    picked = dot(pick_ref[...], table).astype(jnp.bfloat16)
    send_ref[...] = picked.reshape(send_ref.shape)


def combine(att, w_outs, x, p, w_bound, pick):
    shapes = [(3, *p.shape), (pick.shape[0] // 16, 16, 384)]
    operands = [att, *w_outs, x, p, w_bound, pick]
    return pl.pallas_call(
        combine_kernel,
        out_shape=[jax.ShapeDtypeStruct(s, jnp.bfloat16) for s in shapes],
        in_specs=[ON_CHIP] * len(operands),
        out_specs=[ON_CHIP] * 2,
        compiler_params=pltpu.CompilerParams(vmem_limit_bytes=24 * MIB),
        name="combine",
    )(*operands)


def inputs_kernel(arrived_ref, take_ref, reg_ref, out_ref, first_ref, last_ref):
    cols, rows, channels = reg_ref.shape
    cells = cols * rows
    table = arrived_ref[...].reshape(take_ref.shape[1], 384)
    taken = dot(take_ref[...], table)
    for part in range(channels // 128):
        lanes = slice(part * 128, (part + 1) * 128)
        reg = reg_ref[:, :, lanes].astype(jnp.float32)
        for s in range(3):
            forced = taken[part * cells : (part + 1) * cells, s * 128 : (s + 1) * 128]
            made = (reg + forced.reshape(cols, rows, 128)).astype(jnp.bfloat16)
            out_ref[:, s * rows : (s + 1) * rows, lanes] = made
            first_ref[s * rows : (s + 1) * rows, lanes] = made[0]
            last_ref[s * rows : (s + 1) * rows, lanes] = made[cols - 1]


def make_inputs(arrived, take, reg):
    cols, rows, channels = reg.shape
    shapes = [(cols, 3 * rows, channels), (3 * rows, channels), (3 * rows, channels)]
    return pl.pallas_call(
        inputs_kernel,
        out_shape=[jax.ShapeDtypeStruct(s, jnp.bfloat16) for s in shapes],
        in_specs=[ON_CHIP] * 3,
        out_specs=[ON_CHIP] * 3,
        compiler_params=pltpu.CompilerParams(vmem_limit_bytes=12 * MIB),
        name="inputs",
    )(arrived, take, reg)


def conv_kernel(x_ref, before_ref, after_ref, w_ref, out_ref):
    cols, slab, channels = x_ref.shape
    rows = slab // 3
    x = x_ref[...].reshape(cols * slab, channels)
    padded = jnp.concatenate([before_ref[...], x, after_ref[...]], 0)
    wide = padded.astype(jnp.float32)
    total = padded.shape[0]
    row = iota((total, 1), 0) % rows
    shifted = [
        jnp.where(row > 0, pltpu.roll(wide, 1, 0), 0.0).astype(jnp.bfloat16),
        padded,
        jnp.where(row < rows - 1, pltpu.roll(wide, total - 1, 0), 0.0).astype(jnp.bfloat16),
    ]
    conv = None
    for a in range(3):
        for b in range(3):
            piece = dot(shifted[b][a * slab : a * slab + cols * slab], w_ref[3 * a + b])
            conv = piece if conv is None else conv + piece
    result = x.astype(jnp.float32) + conv / (1.0 + jnp.exp(-conv))
    result = result.astype(jnp.bfloat16).reshape(cols, slab, channels)
    for s in range(3):
        out_ref[s] = result[:, s * rows : (s + 1) * rows, :]


def convolve(x, before, after, conv_w):
    cols, slab, channels = x.shape
    return pl.pallas_call(
        conv_kernel,
        out_shape=jax.ShapeDtypeStruct((3, cols, slab // 3, channels), jnp.bfloat16),
        in_specs=[ON_CHIP] * 4,
        out_specs=ON_CHIP,
        compiler_params=pltpu.CompilerParams(vmem_limit_bytes=20 * MIB),
        name="convolve",
    )(x, before, after, conv_w)


def neighbours(last, first, axis):
    count = lax.axis_size(axis)
    up = [(i, i + 1) for i in range(count - 1)]
    down = [(j, i) for i, j in up]
    return lax.ppermute(last, axis, up), lax.ppermute(first, axis, down)


def per_device(
    global_state,
    band_codes,
    norm_gain,
    w_query,
    w_key,
    w_value,
    w_out,
    reg_state,
    src_band,
    src_tok,
    w_bound,
    conv_w,
):
    ranks = lax.axis_size("tp")
    bands = lax.axis_size(BANDS)
    tokens, features = global_state.shape
    half = tokens // 2
    gain = norm_gain[None, :]
    cell_band = src_band.reshape(src_tok.shape)

    code = band_codes[0]
    digits = jnp.stack([code // 65536, (code // 256) % 256, code % 256]).astype(jnp.bfloat16)
    digits = jnp.pad(digits[None], ((0, 15), (0, features - 3)))
    before, after = neighbours(
        jnp.concatenate([global_state[half:], digits]),
        jnp.concatenate([global_state[:half], digits]),
        BANDS,
    )
    asked = ask(cell_band, src_tok, bands)
    asked = lax.all_to_all(asked[:, None, :], BANDS, 0, 0, tiled=True)[:, 0, :]
    w_outs = [w_out] + [
        lax.ppermute(w_out, "tp", [(i, (i + d) % ranks) for i in range(ranks)])
        for d in range(1, ranks)
    ]

    q, k, v = project(band_codes, [global_state], gain, [w_query, w_key, w_value], False)
    k_halo, v_halo = project(band_codes, [before, after], gain, [w_key, w_value], True)
    attended = attend(q, k, v, k_halo, v_halo, ranks, bands)
    asked, attended = lax.optimization_barrier((asked, attended))
    pick, p = prepare(band_codes, asked, tokens // ranks, features)
    attended = lax.all_to_all(
        attended.reshape(ranks, -1, attended.shape[-1]), "tp", 0, 0, tiled=True
    )
    global_out, send = combine(attended, w_outs, global_state, p, w_bound, pick)
    cell_band, send = lax.optimization_barrier((cell_band, send))
    take = make_take(cell_band, bands)
    arrived = lax.all_to_all(send, BANDS, 0, 0, tiled=True)
    inputs, first, last = make_inputs(arrived, take, reg_state)
    before, after = neighbours(last, first, CELLS)
    return global_out, convolve(inputs, before, after, conv_w)


def solution(mesh):
    placed = (
        P(("sec", "tile"), None),
        P(("sec", "tile")),
        P(),
        P(None, "tp"),
        P(None, "tp"),
        P(None, "tp"),
        P("tp", None),
        P(("sec", "tile", "tp"), None, None),
        P(("sec", "tile", "tp"), None, None),
        P(("sec", "tile", "tp"), None),
        P(),
        P(),
    )
    return jax.shard_map(
        per_device,
        mesh=mesh,
        in_specs=placed,
        out_specs=(
            P(None, ("sec", "tile", "tp"), None),
            P(None, ("sec", "tile", "tp"), None, None),
        ),
        check_vma=False,
    )
```

time: 147 us -> 145 us (0.986)
  blocking collectives: 50.9 us -> 0 us
  waiting for transfers between devices: 2.73 us -> 50.1 us
  starting transfers between devices: 30.6 us -> 52.1 us
  Pallas kernels: 40.5 us -> 23.8 us
  between operations: 14.9 us -> 1.6 us
  local copies, waits for them, and re-layouts: 5.17 us -> 15.1 us
    all_to_all x2 -> x0, blocking collectives: 50.9 us -> none  [the longest x1 33.7 us: per_device(): arrived = lax.all_to_all(send, BANDS, 0, 0, tiled=True)]
    ppermute x0 -> x3, waiting for transfers between devices: none -> 25.6 us  [per_device(): lax.ppermute(w_out, 'tp', [(i, (i + d) % ranks) for i in range(ranks)])]
    all_to_all x0 -> x2, waiting for transfers between devices: none -> 22.7 us  [the longest x1 22.7 us: per_device(): arrived = lax.all_to_all(send, BANDS, 0, 0, tiled=True)]
    all_to_all x0 -> x2, starting transfers between devices: none -> 15.3 us  [the longest x1 10.7 us: per_device(): arrived = lax.all_to_all(send, BANDS, 0, 0, tiled=True)]
    unnamed x16 -> x44, local copies, waits for them, and re-layouts: 2.24 us -> 13.9 us
    ppermute x0 -> x3, starting transfers between devices: none -> 6.16 us  [per_device(): lax.ppermute(w_out, 'tp', [(i, (i + d) % ranks) for i in range(ranks)])]
    pallas_call x2, Pallas kernels: 12.1 us -> 6.31 us  [project(): pl.pallas_call(functools.partial(project_kernel, halo=halo), out_shape=[j...]
    pallas_call x1, Pallas kernels: 6.31 us -> 2.07 us  [combine(): pl.pallas_call(combine_kernel, out_shape=[jax.ShapeDtypeStruct(s, jnp.bfl...]
  transfers between devices with their start and end apart: 6 -> 10, of which waited for: 1 -> 4; matrix products, arithmetic and copies ran while one was open for 3% -> 0% of each run, Pallas kernels for 18% -> 13%
where the time goes in v1:
time: 145 us; the launch traced here: 144 us
  starting transfers between devices  52.1 us (36%)
  waiting for transfers between devices  50.1 us (35%)
  Pallas kernels  23.8 us (16%)
  local copies, waits for them, and re-layouts  15.1 us (10%)
  between operations  1.6 us (1%)
    ppermute x3, waiting for transfers between devices, per_device(): lax.ppermute(w_out, 'tp', [(i, (i + d) % ranks) for i in range(ranks)])  25.6 us
    all_to_all x1, waiting for transfers between devices, per_device(): arrived = lax.all_to_all(send, BANDS, 0, 0, tiled=True)  22.7 us
    ppermute x4, starting transfers between devices, neighbours(): return (lax.ppermute(last, axis, up), lax.ppermute(first, axis, down))  18.6 us
    unnamed x44, local copies, waits for them, and re-layouts  13.9 us
    all_to_all x1, starting transfers between devices, per_device(): asked = lax.all_to_all(asked[:, None, :], BANDS, 0, 0, tiled=True)[:, 0, :]  12 us
    all_to_all x1, starting transfers between devices, per_device(): arrived = lax.all_to_all(send, BANDS, 0, 0, tiled=True)  10.7 us
    pallas_call x1, Pallas kernels, attend(): pl.pallas_call(functools.partial(attend_kernel, bands=bands), out_shape=j...  9.64 us
    pallas_call x2, Pallas kernels, project(): pl.pallas_call(functools.partial(project_kernel, halo=halo), out_shape=[j...  6.31 us
  transfers between devices with their start and end apart: 10, of which 4 were waited for; matrix products, arithmetic and copies ran while one was open for 0% of the time, Pallas kernels for 13%

profile of v1, /device:TPU:4, one launch (start us, length us, event | category | flops | bytes accessed | tf_op | source)
XLA Modules:
  0.0 143.8 jit_solution(16235875728576516763)
XLA Ops:
  1.3 1.3 fusion.9
  2.8 1.1 pad_maximum_fusion
  3.8 1.9 %collective-permute-start = (bf16[272,1024]{1,0:T(8,128)(2,1)}, bf16[272,1024]{1,0:T(8,128)(2,1)S(1)}, u32[]{:S(2)}, u32[]{:S(2)}) collective-permute-start(bf16[272,1024]{1,0:T(8,128)(2,1)} %get-tuple-element.37), channel_id=1, source_target_pairs={{0,4},{4,8},{8,12},{12,16},{16,20},{20,24},{24,28},{28,32},{32,36}... | collective-permute-start | bytes 1671176 | tf_op jit(solution)/shard_map/ppermute | solution.py:388
  5.7 6.3 %collective-permute-start.1 = (bf16[272,1024]{1,0:T(8,128)(2,1)}, bf16[272,1024]{1,0:T(8,128)(2,1)S(1)}, u32[]{:S(2)}, u32[]{:S(2)}) collective-permute-start(bf16[272,1024]{1,0:T(8,128)(2,1)} %get-tuple-element.36), channel_id=1, source_target_pairs={{4,0},{8,4},{12,8},{16,12},{20,16},{24,20},{28,24},{32,28},{36,32}... | collective-permute-start | bytes 1671176 | tf_op jit(solution)/shard_map/ppermute | solution.py:388
  12.1 1.0 ask.1
  13.1 12.0 %all-to-all-start = ((s32[64,1,4]{2,1,0:T(1,128)}), s32[64,1,4]{2,1,0:T(1,128)S(1)}, u32[]{:S(2)}, u32[]{:S(2)}) async-start(s32[64,1,4]{2,1,0:T(1,128)} %bitcast.2), calls=%async_computation | async-start | bytes 65536 | tf_op jit(solution)/shard_map/all_to_all | solution.py:421
  25.1 1.0 copy-done.17
  26.2 3.4 %project_own.1 = (bf16[3,512,256]{2,1,0:T(8,128)(2,1)S(1)}, bf16[3,512,256]{2,1,0:T(8,128)(2,1)S(1)}, bf16[3,512,256]{2,1,0:T(8,128)(2,1)S(1)}) custom-call(s32[1]{0:T(128)} %copy.15.code_ref, bf16[512,1024]{1,0:T(8,128)(2,1)S(1)} %copy-done, bf16[1,1024]{1,0:T(2,128)(2,1)S(1)} %broadcast_in_dim.8.refs_1_.refs_2_, bf16[1024,256]{1,0:T(8,128)(2,1)S(1)} %copy-done.17, ...), custom_call_target="tpu_custom_call" | custom-call | tf_op jit(solution)/shard_map/project_own/pallas_call | solution.py:106
  29.6 2.9 %project_halo.1 = (bf16[3,512,256]{2,1,0:T(8,128)(2,1)S(1)}, bf16[3,512,256]{2,1,0:T(8,128)(2,1)S(1)}) custom-call(s32[1]{0:T(128)} %copy.15.code_ref, bf16[272,1024]{1,0:T(8,128)(2,1)S(1)} %collective-permute-done.refs_0_, bf16[272,1024]{1,0:T(8,128)(2,1)S(1)} %collective-permute-done.1.refs_1_, bf16[1,1024]{1,0:T(2,128)(2,1)S(1)} %broadcast_in_dim.8.refs_1_.refs_2_, ...), custom_call_target="tpu_custom_call" | custom-call | tf_op jit(solution)/shard_map/project_halo/pallas_call | solution.py:106
  32.5 9.6 %attend.1 = bf16[4,3,128,256]{3,2,1,0:T(8,128)(2,1)} custom-call(bf16[3,512,256]{2,1,0:T(8,128)(2,1)S(1)} %get-tuple-element.18.q_ref, bf16[3,512,256]{2,1,0:T(8,128)(2,1)S(1)} %get-tuple-element.19.k_ref, bf16[3,512,256]{2,1,0:T(8,128)(2,1)S(1)} %get-tuple-element.20.v_ref, bf16[3,512,256]{2,1,0:T(8,128)(2,1)S(1)} %get-tuple-element.21.k_halo_ref, ...), custom_call_target="tpu_custom_call" | custom-call | tf_op jit(solution)/shard_map/attend/pallas_call | solution.py:171
  42.2 4.6 %all-to-all-start.1 = ((bf16[4,384,256]{2,1,0:T(8,128)(2,1)}), bf16[4,384,256]{2,1,0:T(8,128)(2,1)S(1)}, u32[]{:S(2)}, u32[]{:S(2)}) async-start(bf16[4,384,256]{2,1,0:T(8,128)(2,1)} %bitcast.8), calls=%async_computation.1 | async-start | bytes 1572864 | tf_op jit(solution)/shard_map/all_to_all | solution.py:432
  46.8 2.0 %collective-permute-start.2 = (bf16[256,1024]{1,0:T(8,128)(2,1)S(1)}, bf16[256,1024]{1,0:T(8,128)(2,1)S(1)}, u32[]{:S(2)}, u32[]{:S(2)}) collective-permute-start(bf16[256,1024]{1,0:T(8,128)(2,1)S(1)} %copy-done.8), channel_id=1, source_target_pairs={{0,1},{1,2},{2,3},{3,0},{4,5},{5,6},{6,7},{7,4},{8,9},{9,10},{10,1... | collective-permute-start | bytes 1572872 | tf_op jit(solution)/shard_map/ppermute | solution.py:423
  48.8 2.7 %collective-permute-start.3 = (bf16[256,1024]{1,0:T(8,128)(2,1)S(1)}, bf16[256,1024]{1,0:T(8,128)(2,1)S(1)}, u32[]{:S(2)}, u32[]{:S(2)}) collective-permute-start(bf16[256,1024]{1,0:T(8,128)(2,1)S(1)} %copy-done.8), channel_id=1, source_target_pairs={{0,2},{1,3},{2,0},{3,1},{4,6},{5,7},{6,4},{7,5},{8,10},{9,11},{10,... | collective-permute-start | bytes 1572872 | tf_op jit(solution)/shard_map/ppermute | solution.py:423
  51.5 1.5 %collective-permute-start.4 = (bf16[256,1024]{1,0:T(8,128)(2,1)S(1)}, bf16[256,1024]{1,0:T(8,128)(2,1)S(1)}, u32[]{:S(2)}, u32[]{:S(2)}) collective-permute-start(bf16[256,1024]{1,0:T(8,128)(2,1)S(1)} %copy-done.8), channel_id=1, source_target_pairs={{0,3},{1,0},{2,1},{3,2},{4,7},{5,4},{6,5},{7,6},{8,11},{9,8},{10,9... | collective-permute-start | bytes 1572872 | tf_op jit(solution)/shard_map/ppermute | solution.py:423
  53.7 1.0 copy-done.5
  55.5 15.6 %collective-permute-done.2.w1_ref = bf16[256,1024]{1,0:T(8,128)(2,1)S(1)} collective-permute-done((bf16[256,1024]{1,0:T(8,128)(2,1)S(1)}, bf16[256,1024]{1,0:T(8,128)(2,1)S(1)}, u32[]{:S(2)}, u32[]{:S(2)}) %collective-permute-start.2) | collective-permute-done | bytes 524320 | tf_op jit(solution)/shard_map/ppermute | solution.py:423
  71.1 0.8 copy-done.9
  71.9 10.0 %collective-permute-done.3.w2_ref = bf16[256,1024]{1,0:T(8,128)(2,1)S(1)} collective-permute-done((bf16[256,1024]{1,0:T(8,128)(2,1)S(1)}, bf16[256,1024]{1,0:T(8,128)(2,1)S(1)}, u32[]{:S(2)}, u32[]{:S(2)}) %collective-permute-start.3) | collective-permute-done | bytes 524320 | tf_op jit(solution)/shard_map/ppermute | solution.py:423
  83.5 1.2 copy-done.6
  84.7 1.0 copy-done.10
  85.8 1.0 copy-done.12
  86.8 1.0 copy-done.14
  87.8 1.0 copy-done.16
  88.9 2.1 %combine.1 = (bf16[3,128,1024]{2,1,0:T(8,128)(2,1)}, bf16[64,16,384]{2,1,0:T(8,128)(2,1)S(1)}) custom-call(bf16[4,384,256]{2,1,0:T(8,128)(2,1)S(1)} %all-to-all-done.1.att_ref, bf16[256,1024]{1,0:T(8,128)(2,1)S(1)} %copy-done.8, bf16[256,1024]{1,0:T(8,128)(2,1)S(1)} %copy-done.10, bf16[256,1024]{1,0:T(8,128)(2,1)S(1)} %copy-done.12, ...), custom_call_target="tpu_custom_call" | custom-call | tf_op jit(solution)/shard_map/combine/pallas_call | solution.py:309
  91.0 0.9 copy-done.7
  91.8 10.7 %all-to-all-start.2 = ((bf16[64,16,384]{2,1,0:T(8,128)(2,1)}), bf16[64,16,384]{2,1,0:T(8,128)(2,1)S(1)}, u32[]{:S(2)}, u32[]{:S(2)}) async-start(bf16[64,16,384]{2,1,0:T(8,128)(2,1)} %copy-done.7), calls=%async_computation.2 | async-start | bytes 1572864 | tf_op jit(solution)/shard_map/all_to_all | solution.py:438
  103.0 22.7 %all-to-all-done.2.arrived_ref = bf16[64,16,384]{2,1,0:T(8,128)(2,1)S(1)} async-done(((bf16[64,16,384]{2,1,0:T(8,128)(2,1)}), bf16[64,16,384]{2,1,0:T(8,128)(2,1)S(1)}, u32[]{:S(2)}, u32[]{:S(2)}) %all-to-all-start.2) | async-done | bytes 786464 | tf_op jit(solution)/shard_map/all_to_all | solution.py:438
  126.5 1.9 %collective-permute-start.5 = (bf16[48,512]{1,0:T(8,128)(2,1)S(1)}, bf16[48,512]{1,0:T(8,128)(2,1)S(1)}, u32[]{:S(2)}, u32[]{:S(2)}) collective-permute-start(bf16[48,512]{1,0:T(8,128)(2,1)S(1)} %get-tuple-element.32), channel_id=1, source_target_pairs={{0,1},{1,2},{2,3},{3,4},{4,5},{5,6},{6,7},{7,8},{8,9},{9,10},{10,1... | collective-permute-start | bytes 147464 | tf_op jit(solution)/shard_map/ppermute | solution.py:388
  128.4 8.4 %collective-permute-start.6 = (bf16[48,512]{1,0:T(8,128)(2,1)S(1)}, bf16[48,512]{1,0:T(8,128)(2,1)S(1)}, u32[]{:S(2)}, u32[]{:S(2)}) collective-permute-start(bf16[48,512]{1,0:T(8,128)(2,1)S(1)} %get-tuple-element.33), channel_id=1, source_target_pairs={{1,0},{2,1},{3,2},{4,3},{5,4},{6,5},{7,6},{8,7},{9,8},{10,9},{11,1... | collective-permute-start | bytes 147464 | tf_op jit(solution)/shard_map/ppermute | solution.py:388
  136.9 1.7 %collective-permute-done.6.after_ref = bf16[48,512]{1,0:T(8,128)(2,1)S(1)} collective-permute-done((bf16[48,512]{1,0:T(8,128)(2,1)S(1)}, bf16[48,512]{1,0:T(8,128)(2,1)S(1)}, u32[]{:S(2)}, u32[]{:S(2)}) %collective-permute-start.6) | collective-permute-done | bytes 49184 | tf_op jit(solution)/shard_map/ppermute | solution.py:388
  138.6 2.3 %copy-done.1 = bf16[9,512,512]{2,1,0:T(8,128)(2,1)S(1)} copy-done((bf16[9,512,512]{2,1,0:T(8,128)(2,1)S(1)}, bf16[9,512,512]{2,1,0:T(8,128)(2,1)}, u32[]{:S(2)}) %copy-start.1) | copy-done | bytes 4718616
  140.9 2.9 %convolve.1 = bf16[3,8,16,512]{3,2,1,0:T(8,128)(2,1)} custom-call(bf16[8,48,512]{2,1,0:T(8,128)(2,1)S(1)} %get-tuple-element.31.x_ref, bf16[48,512]{1,0:T(8,128)(2,1)S(1)} %collective-permute-done.5.before_ref, bf16[48,512]{1,0:T(8,128)(2,1)S(1)} %collective-permute-done.6.after_ref, bf16[9,512,512]{2,1,0:T(8,128)(2,1)S(1)} %copy-done.1), custom_call_target="tpu_custom_call" | custom-call | tf_op jit(solution)/shard_map/convolve/pallas_call | solution.py:374
  (45 shorter events, 4.5 us)
Async XLA Ops:
  2.6 9.5 %copy-start.19 = (s32[8,16,1]{1,2,0:T(1,128)S(1)}, s32[8,16,1]{1,2,0:T(1,128)}, u32[]{:S(2)}) copy-start(s32[8,16,1]{1,2,0:T(1,128)} %param.20) | copy-start | bytes 1540
  2.6 9.5 %copy-start.20 = (s32[8,16]{1,0:T(8,128)S(1)}, s32[8,16]{1,0:T(8,128)}, u32[]{:S(2)}) copy-start(s32[8,16]{1,0:T(8,128)} %tok_ref.1) | copy-start | bytes 1540
  2.7 22.3 %copy-start.21 = (bf16[1024]{0:T(1024)(128)(2,1)S(1)}, bf16[1024]{0:T(1024)(128)(2,1)}, u32[]{:S(2)}) copy-start(bf16[1024]{0:T(1024)(128)(2,1)} %param.14) | copy-start | bytes 6148
  2.7 22.4 %copy-start = (bf16[512,1024]{1,0:T(8,128)(2,1)S(1)}, bf16[512,1024]{1,0:T(8,128)(2,1)}, u32[]{:S(2)}) copy-start(bf16[512,1024]{1,0:T(8,128)(2,1)} %x_ref.1) | copy-start | bytes 3145732
  2.7 22.4 %copy-start.2 = (bf16[1024,256]{1,0:T(8,128)(2,1)S(1)}, bf16[1024,256]{1,0:T(8,128)(2,1)}, u32[]{:S(2)}) copy-start(bf16[1024,256]{1,0:T(8,128)(2,1)} %refs_3_.3) | copy-start | bytes 1572868
  2.7 22.4 %copy-start.3 = (bf16[1024,256]{1,0:T(8,128)(2,1)S(1)}, bf16[1024,256]{1,0:T(8,128)(2,1)}, u32[]{:S(2)}) copy-start(bf16[1024,256]{1,0:T(8,128)(2,1)} %refs_4_.3) | copy-start | bytes 1572868
  3.8 25.8 %collective-permute-start = (bf16[272,1024]{1,0:T(8,128)(2,1)}, bf16[272,1024]{1,0:T(8,128)(2,1)S(1)}, u32[]{:S(2)}, u32[]{:S(2)}) collective-permute-start(bf16[272,1024]{1,0:T(8,128)(2,1)} %get-tuple-element.37), channel_id=1, source_target_pairs={{0,4},{4,8},{8,12},{12,16},{16,20},{20,24},{24,28},{28,32},{32,36}... | collective-permute-start | bytes 1671176 | tf_op jit(solution)/shard_map/ppermute | solution.py:388
  5.7 23.9 %collective-permute-start.1 = (bf16[272,1024]{1,0:T(8,128)(2,1)}, bf16[272,1024]{1,0:T(8,128)(2,1)S(1)}, u32[]{:S(2)}, u32[]{:S(2)}) collective-permute-start(bf16[272,1024]{1,0:T(8,128)(2,1)} %get-tuple-element.36), channel_id=1, source_target_pairs={{4,0},{8,4},{12,8},{16,12},{20,16},{24,20},{28,24},{32,28},{36,32}... | collective-permute-start | bytes 1671176 | tf_op jit(solution)/shard_map/ppermute | solution.py:388
  13.1 29.1 %all-to-all-start = ((s32[64,1,4]{2,1,0:T(1,128)}), s32[64,1,4]{2,1,0:T(1,128)S(1)}, u32[]{:S(2)}, u32[]{:S(2)}) async-start(s32[64,1,4]{2,1,0:T(1,128)} %bitcast.2), calls=%async_computation | async-start | bytes 65536 | tf_op jit(solution)/shard_map/all_to_all | solution.py:421
  25.1 1.0 copy-start.17
  42.2 4.6 %copy-start.8 = (bf16[256,1024]{1,0:T(8,128)(2,1)S(1)}, bf16[256,1024]{1,0:T(8,128)(2,1)}, u32[]{:S(2)}) copy-start(bf16[256,1024]{1,0:T(8,128)(2,1)} %w0_ref.1) | copy-start | bytes 1572868
  42.2 41.3 %copy-start.4 = (bf16[1024,512]{1,0:T(8,128)(2,1)S(1)}, bf16[1024,512]{1,0:T(8,128)(2,1)}, u32[]{:S(2)}) copy-start(bf16[1024,512]{1,0:T(8,128)(2,1)} %w_bound_ref.1) | copy-start | bytes 3145732
  42.2 41.3 %all-to-all-start.1 = ((bf16[4,384,256]{2,1,0:T(8,128)(2,1)}), bf16[4,384,256]{2,1,0:T(8,128)(2,1)S(1)}, u32[]{:S(2)}, u32[]{:S(2)}) async-start(bf16[4,384,256]{2,1,0:T(8,128)(2,1)} %bitcast.8), calls=%async_computation.1 | async-start | bytes 1572864 | tf_op jit(solution)/shard_map/all_to_all | solution.py:432
  46.8 24.3 %collective-permute-start.2 = (bf16[256,1024]{1,0:T(8,128)(2,1)S(1)}, bf16[256,1024]{1,0:T(8,128)(2,1)S(1)}, u32[]{:S(2)}, u32[]{:S(2)}) collective-permute-start(bf16[256,1024]{1,0:T(8,128)(2,1)S(1)} %copy-done.8), channel_id=1, source_target_pairs={{0,1},{1,2},{2,3},{3,0},{4,5},{5,6},{6,7},{7,4},{8,9},{9,10},{10,1... | collective-permute-start | bytes 1572872 | tf_op jit(solution)/shard_map/ppermute | solution.py:423
  48.8 33.1 %collective-permute-start.3 = (bf16[256,1024]{1,0:T(8,128)(2,1)S(1)}, bf16[256,1024]{1,0:T(8,128)(2,1)S(1)}, u32[]{:S(2)}, u32[]{:S(2)}) collective-permute-start(bf16[256,1024]{1,0:T(8,128)(2,1)S(1)} %copy-done.8), channel_id=1, source_target_pairs={{0,2},{1,3},{2,0},{3,1},{4,6},{5,7},{6,4},{7,5},{8,10},{9,11},{10,... | collective-permute-start | bytes 1572872 | tf_op jit(solution)/shard_map/ppermute | solution.py:423
  51.5 31.2 %collective-permute-start.4 = (bf16[256,1024]{1,0:T(8,128)(2,1)S(1)}, bf16[256,1024]{1,0:T(8,128)(2,1)S(1)}, u32[]{:S(2)}, u32[]{:S(2)}) collective-permute-start(bf16[256,1024]{1,0:T(8,128)(2,1)S(1)} %copy-done.8), channel_id=1, source_target_pairs={{0,3},{1,0},{2,1},{3,2},{4,7},{5,4},{6,5},{7,6},{8,11},{9,8},{10,9... | collective-permute-start | bytes 1572872 | tf_op jit(solution)/shard_map/ppermute | solution.py:423
  53.7 1.0 copy-start.5
  54.7 0.8 copy-start.15
  71.1 0.8 copy-start.9
  81.9 0.8 copy-start.11
  82.7 0.8 copy-start.13
  83.5 1.2 copy-start.6
  84.7 1.0 copy-start.10
  85.8 1.0 copy-start.12
  86.8 1.0 copy-start.14
  87.8 1.0 copy-start.16
  91.0 0.9 copy-start.7
  91.8 33.9 %copy-start.18 = (bf16[8,16,512]{2,1,0:T(8,128)(2,1)S(1)}, bf16[8,16,512]{2,1,0:T(8,128)(2,1)}, u32[]{:S(2)}) copy-start(bf16[8,16,512]{2,1,0:T(8,128)(2,1)} %reg_ref.1) | copy-start | bytes 393220
  91.8 33.9 %all-to-all-start.2 = ((bf16[64,16,384]{2,1,0:T(8,128)(2,1)}), bf16[64,16,384]{2,1,0:T(8,128)(2,1)S(1)}, u32[]{:S(2)}, u32[]{:S(2)}) async-start(bf16[64,16,384]{2,1,0:T(8,128)(2,1)} %copy-done.7), calls=%async_computation.2 | async-start | bytes 1572864 | tf_op jit(solution)/shard_map/all_to_all | solution.py:438
  126.5 10.4 %collective-permute-start.5 = (bf16[48,512]{1,0:T(8,128)(2,1)S(1)}, bf16[48,512]{1,0:T(8,128)(2,1)S(1)}, u32[]{:S(2)}, u32[]{:S(2)}) collective-permute-start(bf16[48,512]{1,0:T(8,128)(2,1)S(1)} %get-tuple-element.32), channel_id=1, source_target_pairs={{0,1},{1,2},{2,3},{3,4},{4,5},{5,6},{6,7},{7,8},{8,9},{9,10},{10,1... | collective-permute-start | bytes 147464 | tf_op jit(solution)/shard_map/ppermute | solution.py:388
  128.4 10.2 %collective-permute-start.6 = (bf16[48,512]{1,0:T(8,128)(2,1)S(1)}, bf16[48,512]{1,0:T(8,128)(2,1)S(1)}, u32[]{:S(2)}, u32[]{:S(2)}) collective-permute-start(bf16[48,512]{1,0:T(8,128)(2,1)S(1)} %get-tuple-element.33), channel_id=1, source_target_pairs={{1,0},{2,1},{3,2},{4,3},{5,4},{6,5},{7,6},{8,7},{9,8},{10,9},{11,1... | collective-permute-start | bytes 147464 | tf_op jit(solution)/shard_map/ppermute | solution.py:388
  138.6 2.3 %copy-start.1 = (bf16[9,512,512]{2,1,0:T(8,128)(2,1)S(1)}, bf16[9,512,512]{2,1,0:T(8,128)(2,1)}, u32[]{:S(2)}) copy-start(bf16[9,512,512]{2,1,0:T(8,128)(2,1)} %w_ref.1) | copy-start | bytes 14155780

commit v2 on v1

--- a/solution.py
+++ b/solution.py
@@ -26,6 +26,10 @@
     return lax.broadcasted_iota(jnp.int32, shape, dim)
 
 
+def in_hbm(x):
+    return pltpu.with_memory_space_constraint(x, pltpu.HBM)
+
+
 def dot(a, b):
     return jnp.dot(a, b, preferred_element_type=jnp.float32)
 
@@ -42,6 +46,39 @@
     mixed = lax.bitwise_xor(mixed, lax.shift_right_arithmetic(mixed, jnp.full_like(mixed, 13)))
     level = lax.bitwise_and(mixed, 1023).astype(jnp.float32)
     return (level - 511.5) * (0.5 / 295.6)
+
+
+def edges_kernel(code_ref, x_ref, last_ref, first_ref, sems):
+    half = x_ref.shape[0] // 2
+    copies = [
+        pltpu.make_async_copy(x_ref.at[pl.ds(half, half)], last_ref.at[pl.ds(0, half)], sems.at[0]),
+        pltpu.make_async_copy(x_ref.at[pl.ds(0, half)], first_ref.at[pl.ds(0, half)], sems.at[1]),
+    ]
+    for copy in copies:
+        copy.start()
+    code = jnp.full((16, x_ref.shape[1]), code_ref[0], jnp.int32)
+    lane = iota(code.shape, 1)
+    shift = jnp.where(lane == 0, 16, jnp.where(lane == 1, 8, 0))
+    digit = lax.bitwise_and(lax.shift_right_arithmetic(code, shift), 255)
+    digit = digit.astype(jnp.float32).astype(jnp.bfloat16)
+    last_ref[half:] = digit
+    first_ref[half:] = digit
+    for copy in copies:
+        copy.wait()
+
+
+def make_edges(code, x):
+    tokens, features = x.shape
+    shape = jax.ShapeDtypeStruct((tokens // 2 + 16, features), jnp.bfloat16)
+    return pl.pallas_call(
+        edges_kernel,
+        out_shape=[shape, shape],
+        in_specs=[SCALARS, pl.BlockSpec(memory_space=pltpu.HBM)],
+        out_specs=[ON_CHIP] * 2,
+        scratch_shapes=[pltpu.SemaphoreType.DMA((2,))],
+        compiler_params=pltpu.CompilerParams(vmem_limit_bytes=4 * MIB),
+        name="edges",
+    )(code, x)
 
 
 def project_kernel(code_ref, *refs, halo):
@@ -116,12 +153,13 @@
             pltpu.VMEM((2 * rows, features), jnp.bfloat16),
             pltpu.VMEM((3, rows, 1), jnp.float32),
         ],
-        compiler_params=pltpu.CompilerParams(vmem_limit_bytes=20 * MIB),
+        compiler_params=pltpu.CompilerParams(vmem_limit_bytes=12 * MIB),
         name="project_halo" if halo else "project_own",
     )(code, *arrays, gain, *weights)
 
 
-def attend_kernel(q_ref, k_ref, v_ref, k_halo_ref, v_halo_ref, out_ref, *, bands):
+def attend_kernel(q_ref, k_ref, v_ref, k_halo_ref, v_halo_ref, *refs, bands):
+    *out_refs, held_ref = refs
     tokens, cols = q_ref.shape[1:]
     half = tokens // 2
     band = lax.axis_index(BANDS)
@@ -136,7 +174,6 @@
     v_halo = v_halo_ref[0]
     one = there.astype(jnp.bfloat16)
     v_halo = v_halo * one
-    result = [None] * 4
     block = half
     for part in range(tokens // block):
         q = q_ref[0, part * block : (part + 1) * block, :]
@@ -156,12 +193,13 @@
             acc = dot(own, v_own) + dot(far, v_far)
             total = pltpu.roll(acc, cols // 2, 1)
             gathered = jnp.where(mine, acc / total, gathered)
-        gathered = gathered.astype(jnp.bfloat16)
-        quarter = out_ref.shape[2]
-        for piece in range(block // quarter):
-            out_ref[part * (block // quarter) + piece, 0] = gathered[
-                piece * quarter : (piece + 1) * quarter
-            ]
+        held_ref[part * block : (part + 1) * block] = gathered.astype(jnp.bfloat16)
+    ranks = len(out_refs)
+    quarter = tokens // ranks
+    rank = lax.axis_index("tp")
+    for distance, out_ref in enumerate(out_refs):
+        first = pl.multiple_of(lax.rem(rank + distance, ranks) * quarter, quarter)
+        out_ref[...] = held_ref[pl.ds(first, quarter), :]
 
 
 def attend(q, k, v, k_halo, v_halo, ranks, bands):
@@ -170,11 +208,12 @@
     quarter = tokens // ranks
     return pl.pallas_call(
         functools.partial(attend_kernel, bands=bands),
-        out_shape=jax.ShapeDtypeStruct((ranks, forwards, quarter, cols), jnp.bfloat16),
+        out_shape=[jax.ShapeDtypeStruct((forwards * quarter, cols), jnp.bfloat16)] * ranks,
         grid=(forwards,),
         in_specs=[spec] * 5,
-        out_specs=pl.BlockSpec((ranks, 1, quarter, cols), lambda i: (0, i, 0, 0)),
-        compiler_params=pltpu.CompilerParams(vmem_limit_bytes=24 * MIB),
+        out_specs=[pl.BlockSpec((quarter, cols), lambda i: (i, 0))] * ranks,
+        scratch_shapes=[pltpu.VMEM((tokens, cols), jnp.bfloat16)],
+        compiler_params=pltpu.CompilerParams(vmem_limit_bytes=14 * MIB),
         name="attend",
     )(q, k, v, k_halo, v_halo)
 
@@ -237,52 +276,35 @@
         out_shape=jax.ShapeDtypeStruct((4 * band.size, bands * 16), jnp.bfloat16),
         in_specs=[ON_CHIP],
         out_specs=ON_CHIP,
-        compiler_params=pltpu.CompilerParams(vmem_limit_bytes=8 * MIB),
+        compiler_params=pltpu.CompilerParams(vmem_limit_bytes=4 * MIB),
         name="take",
     )(band)
 
 
-def prepare_kernel(code_ref, asked_ref, pick_ref, p_ref):
-    rows, wide = pick_ref.shape
-    bands = asked_ref.shape[0]
-    cells = wide // 4
+def pick_rows(asked, rows, cells):
+    bands = asked.shape[0]
     spread = (iota((rows, bands), 0) // 16 == iota((rows, bands), 1)).astype(jnp.float32)
-    asked = asked_ref[...].astype(jnp.float32)
-    per_row = dot(spread.astype(jnp.bfloat16), asked.astype(jnp.bfloat16))
+    per_row = dot(spread.astype(jnp.bfloat16), asked.astype(jnp.float32).astype(jnp.bfloat16))
     r = iota((rows, 1), 0)
     mine = iota((rows, 4), 1) == (r // 4) % 4
     token_r = jnp.sum(jnp.where(mine, per_row, 0.0), -1, keepdims=True).astype(jnp.int32)
     target = jnp.where(token_r >= 0, (r % 4) * cells + token_r, -1)
-    pick_ref[...] = (iota((rows, wide), 1) == target).astype(jnp.float32).astype(jnp.bfloat16)
-    quarter, features = p_ref.shape
-    code = jnp.full((1, 1), code_ref[0], jnp.int32)
-    p_ref[...] = wiggle(code, lax.axis_index("tp") * quarter, quarter, features)
-
-
-def prepare(code, asked, quarter, features):
-    return pl.pallas_call(
-        prepare_kernel,
-        out_shape=[
-            jax.ShapeDtypeStruct((asked.shape[0] * 16, 4 * quarter), jnp.bfloat16),
-            jax.ShapeDtypeStruct((quarter, features), jnp.float32),
-        ],
-        in_specs=[SCALARS, ON_CHIP],
-        out_specs=[ON_CHIP] * 2,
-        compiler_params=pltpu.CompilerParams(vmem_limit_bytes=12 * MIB),
-        name="prepare",
-    )(code, asked)
-
-
-def combine_kernel(att_ref, w0_ref, w1_ref, w2_ref, w3_ref, x_ref, p_ref, w_bound_ref, pick_ref, out_ref, send_ref):
-    ranks, _, cols = att_ref.shape
-    quarter = p_ref.shape[0]
+    return (iota((rows, 4 * cells), 1) == target).astype(jnp.float32).astype(jnp.bfloat16)
+
+
+def combine_kernel(code_ref, att0_ref, att1_ref, att2_ref, att3_ref, w0_ref, w1_ref, w3_ref, top_ref, low_ref, x_ref, w_bound_ref, asked_ref, out_ref, send_ref):
+    cols = att0_ref.shape[1]
+    features = x_ref.shape[1]
+    quarter = out_ref.shape[1]
     rank = lax.axis_index("tp")
     x = x_ref[pl.ds(pl.multiple_of(rank * quarter, quarter), quarter), :].astype(jnp.float32)
-    p = p_ref[...]
-    total = None
-    for d, w_ref in enumerate((w0_ref, w1_ref, w2_ref, w3_ref)):
-        piece = dot(att_ref[lax.rem(rank + ranks - d, ranks)], w_ref[...])
-        total = piece if total is None else total + piece
+    code = jnp.full((1, 1), code_ref[0], jnp.int32)
+    p = wiggle(code, rank * quarter, quarter, features)
+    pick = pick_rows(asked_ref[...], send_ref.shape[0] * 16, quarter)
+    total = dot(att0_ref[...], w0_ref[...]) + dot(att1_ref[...], w1_ref[...])
+    total = total + dot(att3_ref[...], w3_ref[...])
+    total = total + dot(att2_ref[:, : cols // 2], top_ref[...])
+    total = total + dot(att2_ref[:, cols // 2 :], low_ref[...])
     made = []
     for s, sign in enumerate(SIGNS):
         part = x if sign == 0.0 else (x + p if sign > 0 else x - p)
@@ -299,21 +321,22 @@
         ],
         0,
     )
-    picked = dot(pick_ref[...], table).astype(jnp.bfloat16)
+    picked = dot(pick, table).astype(jnp.bfloat16)
     send_ref[...] = picked.reshape(send_ref.shape)
 
 
-def combine(att, w_outs, x, p, w_bound, pick):
-    shapes = [(3, *p.shape), (pick.shape[0] // 16, 16, 384)]
-    operands = [att, *w_outs, x, p, w_bound, pick]
+def combine(code, att, w_outs, x, w_bound, asked):
+    shapes = [(3, att[0].shape[0] // 3, x.shape[1]), (asked.shape[0], 16, 384)]
+    operands = [*att, *w_outs, x, w_bound, asked]
+    whole = lambda: (0, 0, 0)
     return pl.pallas_call(
         combine_kernel,
         out_shape=[jax.ShapeDtypeStruct(s, jnp.bfloat16) for s in shapes],
-        in_specs=[ON_CHIP] * len(operands),
-        out_specs=[ON_CHIP] * 2,
-        compiler_params=pltpu.CompilerParams(vmem_limit_bytes=24 * MIB),
+        in_specs=[SCALARS] + [ON_CHIP] * len(operands),
+        out_specs=[pl.BlockSpec(s, whole) for s in shapes],
+        compiler_params=pltpu.CompilerParams(vmem_limit_bytes=16 * MIB),
         name="combine",
-    )(*operands)
+    )(code, *operands)
 
 
 def inputs_kernel(arrived_ref, take_ref, reg_ref, out_ref, first_ref, last_ref):
@@ -340,43 +363,64 @@
         out_shape=[jax.ShapeDtypeStruct(s, jnp.bfloat16) for s in shapes],
         in_specs=[ON_CHIP] * 3,
         out_specs=[ON_CHIP] * 3,
-        compiler_params=pltpu.CompilerParams(vmem_limit_bytes=12 * MIB),
+        compiler_params=pltpu.CompilerParams(vmem_limit_bytes=5 * MIB),
         name="inputs",
     )(arrived, take, reg)
 
 
-def conv_kernel(x_ref, before_ref, after_ref, w_ref, out_ref):
+def conv_kernel(x_ref, before_ref, after_ref, w_ref, out_ref, low_ref, mid_ref, high_ref, sum_ref):
+    step = pl.program_id(0)
     cols, slab, channels = x_ref.shape
+    cells = cols * slab
     rows = slab // 3
-    x = x_ref[...].reshape(cols * slab, channels)
-    padded = jnp.concatenate([before_ref[...], x, after_ref[...]], 0)
-    wide = padded.astype(jnp.float32)
-    total = padded.shape[0]
-    row = iota((total, 1), 0) % rows
-    shifted = [
-        jnp.where(row > 0, pltpu.roll(wide, 1, 0), 0.0).astype(jnp.bfloat16),
-        padded,
-        jnp.where(row < rows - 1, pltpu.roll(wide, total - 1, 0), 0.0).astype(jnp.bfloat16),
-    ]
-    conv = None
-    for a in range(3):
-        for b in range(3):
-            piece = dot(shifted[b][a * slab : a * slab + cols * slab], w_ref[3 * a + b])
-            conv = piece if conv is None else conv + piece
-    result = x.astype(jnp.float32) + conv / (1.0 + jnp.exp(-conv))
-    result = result.astype(jnp.bfloat16).reshape(cols, slab, channels)
-    for s in range(3):
-        out_ref[s] = result[:, s * rows : (s + 1) * rows, :]
+
+    @pl.when(step == 0)
+    def _():
+        x = x_ref[...].reshape(cells, channels)
+        padded = jnp.concatenate([before_ref[...], x, after_ref[...]], 0)
+        wide = padded.astype(jnp.float32)
+        total = padded.shape[0]
+        row = iota((total, 1), 0) % rows
+        low_ref[...] = jnp.where(row > 0, pltpu.roll(wide, 1, 0), 0.0).astype(jnp.bfloat16)
+        mid_ref[...] = padded
+        high_ref[...] = jnp.where(
+            row < rows - 1, pltpu.roll(wide, total - 1, 0), 0.0
+        ).astype(jnp.bfloat16)
+
+    here = pl.ds(pl.multiple_of(step * slab, slab), cells)
+    part = dot(low_ref[here], w_ref[0]) + dot(mid_ref[here], w_ref[1]) + dot(high_ref[here], w_ref[2])
+
+    @pl.when(step == 0)
+    def _():
+        sum_ref[...] = part
+
+    @pl.when(step == 1)
+    def _():
+        sum_ref[...] += part
+
+    @pl.when(step == 2)
+    def _():
+        conv = sum_ref[...] + part
+        x = x_ref[...].reshape(cells, channels).astype(jnp.float32)
+        result = (x + conv / (1.0 + jnp.exp(-conv))).astype(jnp.bfloat16)
+        result = result.reshape(cols, slab, channels)
+        for s in range(3):
+            out_ref[s] = result[:, s * rows : (s + 1) * rows, :]
 
 
 def convolve(x, before, after, conv_w):
     cols, slab, channels = x.shape
+    shape = (3, cols, slab // 3, channels)
+    padded = ((cols + 2) * slab, channels)
     return pl.pallas_call(
         conv_kernel,
-        out_shape=jax.ShapeDtypeStruct((3, cols, slab // 3, channels), jnp.bfloat16),
-        in_specs=[ON_CHIP] * 4,
-        out_specs=ON_CHIP,
-        compiler_params=pltpu.CompilerParams(vmem_limit_bytes=20 * MIB),
+        out_shape=jax.ShapeDtypeStruct(shape, jnp.bfloat16),
+        grid=(3,),
+        in_specs=[ON_CHIP] * 3 + [pl.BlockSpec((3, channels, channels), lambda i: (i, 0, 0))],
+        out_specs=pl.BlockSpec(shape, lambda i: (0, 0, 0, 0)),
+        scratch_shapes=[pltpu.VMEM(padded, jnp.bfloat16)] * 3
+        + [pltpu.VMEM((cols * slab, channels), jnp.float32)],
+        compiler_params=pltpu.CompilerParams(vmem_limit_bytes=16 * MIB),
         name="convolve",
     )(x, before, after, conv_w)
 
@@ -408,37 +452,36 @@
     half = tokens // 2
     gain = norm_gain[None, :]
     cell_band = src_band.reshape(src_tok.shape)
-
-    code = band_codes[0]
-    digits = jnp.stack([code // 65536, (code // 256) % 256, code % 256]).astype(jnp.bfloat16)
-    digits = jnp.pad(digits[None], ((0, 15), (0, features - 3)))
-    before, after = neighbours(
-        jnp.concatenate([global_state[half:], digits]),
-        jnp.concatenate([global_state[:half], digits]),
-        BANDS,
-    )
+    w_query, w_key, w_value = (in_hbm(w) for w in (w_query, w_key, w_value))
+
+    up = [(i, (i + 1) % ranks) for i in range(ranks)]
+    down = [(j, i) for i, j in up]
+    before, after = neighbours(*make_edges(band_codes, in_hbm(global_state)), BANDS)
+    w1, w3 = lax.ppermute(w_out, "tp", up), lax.ppermute(w_out, "tp", down)
     asked = ask(cell_band, src_tok, bands)
-    asked = lax.all_to_all(asked[:, None, :], BANDS, 0, 0, tiled=True)[:, 0, :]
-    w_outs = [w_out] + [
-        lax.ppermute(w_out, "tp", [(i, (i + d) % ranks) for i in range(ranks)])
+
+    q, k, v = project(band_codes, [in_hbm(global_state)], gain, [w_query, w_key, w_value], False)
+    q, before, after = lax.optimization_barrier((q, before, after))
+    k_halo, v_halo = project(band_codes, [before, after], gain, [w_key, w_value], True)
+    k_halo, w1, w3 = lax.optimization_barrier((k_halo, w1, w3))
+    middle = w_out.shape[0] // 2
+    top, low = lax.ppermute(w1[:middle], "tp", up), lax.ppermute(w3[middle:], "tp", down)
+    attended = attend(q, k, v, k_halo, v_halo, ranks, bands)
+    attended, asked, top, low = lax.optimization_barrier((attended, asked, top, low))
+    attended = [attended[0]] + [
+        lax.ppermute(attended[d], "tp", [(i, (i + d) % ranks) for i in range(ranks)])
         for d in range(1, ranks)
     ]
-
-    q, k, v = project(band_codes, [global_state], gain, [w_query, w_key, w_value], False)
-    k_halo, v_halo = project(band_codes, [before, after], gain, [w_key, w_value], True)
-    attended = attend(q, k, v, k_halo, v_halo, ranks, bands)
-    asked, attended = lax.optimization_barrier((asked, attended))
-    pick, p = prepare(band_codes, asked, tokens // ranks, features)
-    attended = lax.all_to_all(
-        attended.reshape(ranks, -1, attended.shape[-1]), "tp", 0, 0, tiled=True
+    asked = lax.all_to_all(asked[:, None, :], BANDS, 0, 0, tiled=True)[:, 0, :]
+    global_out, send = combine(
+        band_codes, attended, [w_out, w1, w3, top, low], global_state, w_bound, asked
     )
-    global_out, send = combine(attended, w_outs, global_state, p, w_bound, pick)
     cell_band, send = lax.optimization_barrier((cell_band, send))
     take = make_take(cell_band, bands)
     arrived = lax.all_to_all(send, BANDS, 0, 0, tiled=True)
     inputs, first, last = make_inputs(arrived, take, reg_state)
     before, after = neighbours(last, first, CELLS)
-    return global_out, convolve(inputs, before, after, conv_w)
+    return global_out, convolve(inputs, before, after, in_hbm(conv_w))
 
 
 def solution(mesh):

time: 145 us -> 116 us (0.80)
  blocking collectives: 0 us -> 20.6 us
  starting transfers between devices: 52.1 us -> 31.5 us
  waiting for transfers between devices: 50.1 us -> 29.8 us
  local copies, waits for them, and re-layouts: 15.1 us -> 0.75 us
  Pallas kernels: 23.8 us -> 30.5 us
    ppermute x3 -> x7, waiting for transfers between devices: 25.6 us -> 0.02 us  [the longest x3 0.01 us: per_device(): lax.ppermute(attended[d], 'tp', [(i, (i + d) % ranks) for i in range(rank...]
    all_to_all x0 -> x1, blocking collectives: none -> 20.6 us  [per_device(): asked = lax.all_to_all(asked[:, None, :], BANDS, 0, 0, tiled=True)[:, 0, :]]
    all_to_all x2 -> x0, starting transfers between devices: 16.6 us -> none  [the longest x1 12 us: per_device(): asked = lax.all_to_all(asked[:, None, :], BANDS, 0, 0, tiled=True)[:, 0, :]]
    unnamed x44 -> x12, local copies, waits for them, and re-layouts: 13.9 us -> 0.03 us
    ppermute x4, waiting for transfers between devices: 1.73 us -> 7.07 us  [neighbours(): return (lax.ppermute(last, axis, up), lax.ppermute(first, axis, down))]
    ppermute x3 -> x7, starting transfers between devices: 6.16 us -> 10.8 us  [the longest x3 4.14 us: per_device(): lax.ppermute(attended[d], 'tp', [(i, (i + d) % ranks) for i in range(rank...]
    ppermute x4, starting transfers between devices: 18.6 us -> 14.1 us  [neighbours(): return (lax.ppermute(last, axis, up), lax.ppermute(first, axis, down))]
    all_to_all x1, starting transfers between devices: 10.7 us -> 6.6 us  [per_device(): arrived = lax.all_to_all(send, BANDS, 0, 0, tiled=True)]
  transfers between devices with their start and end apart: 10 -> 12, of which waited for: 4 -> 3; matrix products, arithmetic and copies ran while one was open for 0% -> 1% of each run, Pallas kernels for 13% -> 17%
where the time goes in v2:
time: 116 us; the launch traced here: 115 us
  starting transfers between devices  31.5 us (27%)
  Pallas kernels  30.5 us (26%)
  waiting for transfers between devices  29.8 us (26%)
  blocking collectives  20.6 us (18%)
  between operations  1.52 us (1%)
    all_to_all x1, waiting for transfers between devices, per_device(): arrived = lax.all_to_all(send, BANDS, 0, 0, tiled=True)  22.8 us
    all_to_all x1, blocking collectives, per_device(): asked = lax.all_to_all(asked[:, None, :], BANDS, 0, 0, tiled=True)[:, 0, :]  20.6 us
    ppermute x4, starting transfers between devices, neighbours(): return (lax.ppermute(last, axis, up), lax.ppermute(first, axis, down))  14.1 us
    pallas_call x2, Pallas kernels, project(): pl.pallas_call(functools.partial(project_kernel, halo=halo), out_shape=[j...  9.21 us
    pallas_call x1, Pallas kernels, attend(): pl.pallas_call(functools.partial(attend_kernel, bands=bands), out_shape=[...  9.14 us
    ppermute x4, waiting for transfers between devices, neighbours(): return (lax.ppermute(last, axis, up), lax.ppermute(first, axis, down))  7.07 us
    all_to_all x1, starting transfers between devices, per_device(): arrived = lax.all_to_all(send, BANDS, 0, 0, tiled=True)  6.6 us
    pallas_call x1, Pallas kernels, convolve(): pl.pallas_call(conv_kernel, out_shape=jax.ShapeDtypeStruct(shape, jnp.bfl...  5.72 us
  transfers between devices with their start and end apart: 12, of which 3 were waited for; matrix products, arithmetic and copies ran while one was open for 1% of the time, Pallas kernels for 17%

profile of v2, /device:TPU:4, one launch (start us, length us, event | category | flops | bytes accessed | tf_op | source)
XLA Modules:
  0.0 114.8 jit_solution(14893512533322828487)
XLA Ops:
  1.3 1.2 %edges.1 = (bf16[272,1024]{1,0:T(8,128)(2,1)S(1)}, bf16[272,1024]{1,0:T(8,128)(2,1)S(1)}) custom-call(s32[1]{0:T(128)S(6)} %copy.15.code_ref, bf16[512,1024]{1,0:T(8,128)(2,1)} %x_ref.3), custom_call_target="tpu_custom_call" | custom-call | tf_op jit(solution)/shard_map/edges/pallas_call | solution.py:73
  2.5 1.9 %collective-permute-start = (bf16[272,1024]{1,0:T(8,128)(2,1)S(1)}, bf16[272,1024]{1,0:T(8,128)(2,1)S(1)}, u32[]{:S(2)}, u32[]{:S(2)}) collective-permute-start(bf16[272,1024]{1,0:T(8,128)(2,1)S(1)} %get-tuple-element.34), channel_id=1, source_target_pairs={{0,4},{4,8},{8,12},{12,16},{16,20},{20,24},{24,28},{28,32},{32,36}... | collective-permute-start | bytes 1671176 | tf_op jit(solution)/shard_map/ppermute | solution.py:432
  4.5 6.3 %collective-permute-start.1 = (bf16[272,1024]{1,0:T(8,128)(2,1)S(1)}, bf16[272,1024]{1,0:T(8,128)(2,1)S(1)}, u32[]{:S(2)}, u32[]{:S(2)}) collective-permute-start(bf16[272,1024]{1,0:T(8,128)(2,1)S(1)} %get-tuple-element.35), channel_id=1, source_target_pairs={{4,0},{8,4},{12,8},{16,12},{20,16},{24,20},{28,24},{32,28},{36,32}... | collective-permute-start | bytes 1671176 | tf_op jit(solution)/shard_map/ppermute | solution.py:432
  10.8 1.7 %collective-permute-start.2 = (bf16[256,1024]{1,0:T(8,128)(2,1)}, bf16[256,1024]{1,0:T(8,128)(2,1)S(1)}, u32[]{:S(2)}, u32[]{:S(2)}) collective-permute-start(bf16[256,1024]{1,0:T(8,128)(2,1)} %w0_ref.1), channel_id=1, source_target_pairs={{0,1},{1,2},{2,3},{3,0},{4,5},{5,6},{6,7},{7,4},{8,9},{9,10},{10,1... | collective-permute-start | bytes 1572872 | tf_op jit(solution)/shard_map/ppermute | solution.py:460
  12.5 1.7 %collective-permute-start.3 = (bf16[256,1024]{1,0:T(8,128)(2,1)}, bf16[256,1024]{1,0:T(8,128)(2,1)S(1)}, u32[]{:S(2)}, u32[]{:S(2)}) collective-permute-start(bf16[256,1024]{1,0:T(8,128)(2,1)} %w0_ref.1), channel_id=1, source_target_pairs={{1,0},{2,1},{3,2},{0,3},{5,4},{6,5},{7,6},{4,7},{9,8},{10,9},{11,1... | collective-permute-start | bytes 1572872 | tf_op jit(solution)/shard_map/ppermute | solution.py:460
  14.1 0.7 broadcast_in_dim.6.refs_1_.refs_2_
  14.8 5.1 %project_own.1 = (bf16[3,512,256]{2,1,0:T(8,128)(2,1)S(1)}, bf16[3,512,256]{2,1,0:T(8,128)(2,1)S(1)}, bf16[3,512,256]{2,1,0:T(8,128)(2,1)S(1)}) custom-call(s32[1]{0:T(128)S(6)} %copy.15.code_ref, bf16[512,1024]{1,0:T(8,128)(2,1)} %x_ref.3, bf16[1,1024]{1,0:T(2,128)(2,1)S(1)} %broadcast_in_dim.6.refs_1_.refs_2_, bf16[1024,256]{1,0:T(8,128)(2,1)} %refs_2_.1, ...), custom_call_target="tpu_custom_call" | custom-call | tf_op jit(solution)/shard_map/project_own/pallas_call | solution.py:143
  20.0 0.0 collective-permute-done.refs_0_
  20.0 0.0 collective-permute-done.1.refs_1_
  20.0 4.1 %project_halo.1 = (bf16[3,512,256]{2,1,0:T(8,128)(2,1)S(1)}, bf16[3,512,256]{2,1,0:T(8,128)(2,1)S(1)}) custom-call(s32[1]{0:T(128)S(6)} %copy.15.code_ref, bf16[272,1024]{1,0:T(8,128)(2,1)S(1)} %collective-permute-done.refs_0_, bf16[272,1024]{1,0:T(8,128)(2,1)S(1)} %collective-permute-done.1.refs_1_, bf16[1,1024]{1,0:T(2,128)(2,1)S(1)} %broadcast_in_dim.6.refs_1_.refs_2_, ...), custom_call_target="tpu_custom_call" | custom-call | tf_op jit(solution)/shard_map/project_halo/pallas_call | solution.py:143
  24.1 0.0 collective-permute-done.2.w1_ref
  24.1 0.0 collective-permute-done.3.w3_ref
  24.1 1.4 %collective-permute-start.4 = (bf16[128,1024]{1,0:T(8,128)(2,1)S(1)}, bf16[128,1024]{1,0:T(8,128)(2,1)S(1)}, u32[]{:S(2)}, u32[]{:S(2)}) collective-permute-start(bf16[128,1024]{1,0:T(8,128)(2,1)S(1)} %slice.6), channel_id=1, source_target_pairs={{0,1},{1,2},{2,3},{3,0},{4,5},{5,6},{6,7},{7,4},{8,9},{9,10},{10,1... | collective-permute-start | bytes 786440 | tf_op jit(solution)/shard_map/ppermute | solution.py:468
  25.5 2.0 %collective-permute-start.5 = (bf16[128,1024]{1,0:T(8,128)(2,1)S(1)}, bf16[128,1024]{1,0:T(8,128)(2,1)S(1)}, u32[]{:S(2)}, u32[]{:S(2)}) collective-permute-start(bf16[128,1024]{1,0:T(8,128)(2,1)S(1)} %slice.7), channel_id=1, source_target_pairs={{1,0},{2,1},{3,2},{0,3},{5,4},{6,5},{7,6},{4,7},{9,8},{10,9},{11,1... | collective-permute-start | bytes 786440 | tf_op jit(solution)/shard_map/ppermute | solution.py:468
  27.5 0.4 ask.1
  27.9 9.1 %attend.1 = (bf16[384,256]{1,0:T(8,128)(2,1)S(1)}, bf16[384,256]{1,0:T(8,128)(2,1)S(1)}, bf16[384,256]{1,0:T(8,128)(2,1)S(1)}, bf16[384,256]{1,0:T(8,128)(2,1)S(1)}) custom-call(bf16[3,512,256]{2,1,0:T(8,128)(2,1)S(1)} %get-tuple-element.36.q_ref, bf16[3,512,256]{2,1,0:T(8,128)(2,1)S(1)} %get-tuple-element.37.k_ref, ...), custom_call_target="tpu_custom_call" | custom-call | tf_op jit(solution)/shard_map/attend/pallas_call | solution.py:209
  37.1 0.0 copy-start.3
  37.1 0.0 collective-permute-done.5.low_ref
  37.1 0.2 collective-permute-start.6
  37.3 2.9 %collective-permute-start.7 = (bf16[384,256]{1,0:T(8,128)(2,1)S(1)}, bf16[384,256]{1,0:T(8,128)(2,1)S(1)}, u32[]{:S(2)}, u32[]{:S(2)}) collective-permute-start(bf16[384,256]{1,0:T(8,128)(2,1)S(1)} %get-tuple-element.52), channel_id=1, source_target_pairs={{0,2},{1,3},{2,0},{3,1},{4,6},{5,7},{6,4},{7,5},{8,10},{9,11},{10,... | collective-permute-start | bytes 589832 | tf_op jit(solution)/shard_map/ppermute | solution.py:472
  40.2 1.0 collective-permute-start.8
  41.2 20.6 %all_to_all.10 = s32[64,1,4]{2,1,0:T(1,128)S(1)} all-to-all(s32[64,1,4]{2,1,0:T(1,128)S(1)} %bitcast.5), channel_id=1, replica_groups=mesh['sec'=2,'tile'=32,'tp'=4] {'sec','tile'}, dimensions={0} | all-to-all | bytes 2048 | tf_op jit(solution)/shard_map/all_to_all | solution.py:475
  61.9 3.7 %combine.1 = (bf16[3,128,1024]{2,1,0:T(8,128)(2,1)}, bf16[64,16,384]{2,1,0:T(8,128)(2,1)}) custom-call(s32[1]{0:T(128)S(6)} %copy.15.code_ref, bf16[384,256]{1,0:T(8,128)(2,1)S(1)} %get-tuple-element.50.att0_ref, bf16[384,256]{1,0:T(8,128)(2,1)S(1)} %collective-permute-done.6.att1_ref, bf16[384,256]{1,0:T(8,128)(2,1)S(1)} %collective-permute-done.7.att2_ref, ...), custom_call_target="tpu_custom_call" | custom-call | tf_op jit(solution)/shard_map/combine/pallas_call | solution.py:332
  65.6 6.6 %all-to-all-start.1 = ((bf16[64,16,384]{2,1,0:T(8,128)(2,1)}), bf16[64,16,384]{2,1,0:T(8,128)(2,1)S(1)}, u32[]{:S(2)}, u32[]{:S(2)}) async-start(bf16[64,16,384]{2,1,0:T(8,128)(2,1)} %get-tuple-element.59), calls=%async_computation.1 | async-start | bytes 1572864 | tf_op jit(solution)/shard_map/all_to_all | solution.py:481
  72.2 0.5 take.1.take_ref
  72.7 22.8 %all-to-all-done.1.arrived_ref = bf16[64,16,384]{2,1,0:T(8,128)(2,1)S(1)} async-done(((bf16[64,16,384]{2,1,0:T(8,128)(2,1)}), bf16[64,16,384]{2,1,0:T(8,128)(2,1)S(1)}, u32[]{:S(2)}, u32[]{:S(2)}) %all-to-all-start.1) | async-done | bytes 786464 | tf_op jit(solution)/shard_map/all_to_all | solution.py:481
  95.5 0.7 inputs.1
  96.2 2.7 %collective-permute-start.10 = (bf16[48,512]{1,0:T(8,128)(2,1)S(1)}, bf16[48,512]{1,0:T(8,128)(2,1)S(1)}, u32[]{:S(2)}, u32[]{:S(2)}) collective-permute-start(bf16[48,512]{1,0:T(8,128)(2,1)S(1)} %get-tuple-element.63), channel_id=1, source_target_pairs={{1,0},{2,1},{3,2},{4,3},{5,4},{6,5},{7,6},{8,7},{9,8},{10,9},{11,1... | collective-permute-start | bytes 147464 | tf_op jit(solution)/shard_map/ppermute | solution.py:432
  98.9 3.1 %collective-permute-start.9 = (bf16[48,512]{1,0:T(8,128)(2,1)S(1)}, bf16[48,512]{1,0:T(8,128)(2,1)S(1)}, u32[]{:S(2)}, u32[]{:S(2)}) collective-permute-start(bf16[48,512]{1,0:T(8,128)(2,1)S(1)} %get-tuple-element.62), channel_id=1, source_target_pairs={{0,1},{1,2},{2,3},{3,4},{4,5},{5,6},{6,7},{7,8},{8,9},{9,10},{10,1... | collective-permute-start | bytes 147464 | tf_op jit(solution)/shard_map/ppermute | solution.py:432
  102.0 0.1 collective-permute-done.10.after_ref
  102.2 6.9 %collective-permute-done.9.before_ref = bf16[48,512]{1,0:T(8,128)(2,1)S(1)} collective-permute-done((bf16[48,512]{1,0:T(8,128)(2,1)S(1)}, bf16[48,512]{1,0:T(8,128)(2,1)S(1)}, u32[]{:S(2)}, u32[]{:S(2)}) %collective-permute-start.9) | collective-permute-done | bytes 49184 | tf_op jit(solution)/shard_map/ppermute | solution.py:432
  109.1 5.7 %convolve.1 = bf16[3,8,16,512]{3,2,1,0:T(8,128)(2,1)} custom-call(bf16[8,48,512]{2,1,0:T(8,128)(2,1)S(1)} %get-tuple-element.61.x_ref, bf16[48,512]{1,0:T(8,128)(2,1)S(1)} %collective-permute-done.9.before_ref, bf16[48,512]{1,0:T(8,128)(2,1)S(1)} %collective-permute-done.10.after_ref, bf16[9,512,512]{2,1,0:T(8,128)(2,1)} %w_ref.1), custom_call_target="tpu_custom_call" | custom-call | tf_op jit(solution)/shard_map/convolve/pallas_call | solution.py:415
  (17 shorter events, 0.1 us)
Async XLA Ops:
  0.6 26.9 %copy-start.4 = (s32[8,16,1]{1,2,0:T(1,128)S(1)}, s32[8,16,1]{1,2,0:T(1,128)}, u32[]{:S(2)}) copy-start(s32[8,16,1]{1,2,0:T(1,128)} %param.20) | copy-start | bytes 1540
  0.6 26.9 %copy-start.5 = (s32[8,16]{1,0:T(8,128)S(1)}, s32[8,16]{1,0:T(8,128)}, u32[]{:S(2)}) copy-start(s32[8,16]{1,0:T(8,128)} %tok_ref.1) | copy-start | bytes 1540
  2.5 17.4 %collective-permute-start = (bf16[272,1024]{1,0:T(8,128)(2,1)S(1)}, bf16[272,1024]{1,0:T(8,128)(2,1)S(1)}, u32[]{:S(2)}, u32[]{:S(2)}) collective-permute-start(bf16[272,1024]{1,0:T(8,128)(2,1)S(1)} %get-tuple-element.34), channel_id=1, source_target_pairs={{0,4},{4,8},{8,12},{12,16},{16,20},{20,24},{24,28},{28,32},{32,36}... | collective-permute-start | bytes 1671176 | tf_op jit(solution)/shard_map/ppermute | solution.py:432
  4.5 15.5 %collective-permute-start.1 = (bf16[272,1024]{1,0:T(8,128)(2,1)S(1)}, bf16[272,1024]{1,0:T(8,128)(2,1)S(1)}, u32[]{:S(2)}, u32[]{:S(2)}) collective-permute-start(bf16[272,1024]{1,0:T(8,128)(2,1)S(1)} %get-tuple-element.35), channel_id=1, source_target_pairs={{4,0},{8,4},{12,8},{16,12},{20,16},{24,20},{28,24},{32,28},{36,32}... | collective-permute-start | bytes 1671176 | tf_op jit(solution)/shard_map/ppermute | solution.py:432
  10.8 13.3 %collective-permute-start.2 = (bf16[256,1024]{1,0:T(8,128)(2,1)}, bf16[256,1024]{1,0:T(8,128)(2,1)S(1)}, u32[]{:S(2)}, u32[]{:S(2)}) collective-permute-start(bf16[256,1024]{1,0:T(8,128)(2,1)} %w0_ref.1), channel_id=1, source_target_pairs={{0,1},{1,2},{2,3},{3,0},{4,5},{5,6},{6,7},{7,4},{8,9},{9,10},{10,1... | collective-permute-start | bytes 1572872 | tf_op jit(solution)/shard_map/ppermute | solution.py:460
  12.5 11.6 %collective-permute-start.3 = (bf16[256,1024]{1,0:T(8,128)(2,1)}, bf16[256,1024]{1,0:T(8,128)(2,1)S(1)}, u32[]{:S(2)}, u32[]{:S(2)}) collective-permute-start(bf16[256,1024]{1,0:T(8,128)(2,1)} %w0_ref.1), channel_id=1, source_target_pairs={{1,0},{2,1},{3,2},{0,3},{5,4},{6,5},{7,6},{4,7},{9,8},{10,9},{11,1... | collective-permute-start | bytes 1572872 | tf_op jit(solution)/shard_map/ppermute | solution.py:460
  14.8 47.1 %copy-start = (bf16[512,1024]{1,0:T(8,128)(2,1)S(1)}, bf16[512,1024]{1,0:T(8,128)(2,1)}, u32[]{:S(2)}) copy-start(bf16[512,1024]{1,0:T(8,128)(2,1)} %x_ref.3) | copy-start | bytes 3145732
  14.8 47.1 %copy-start.1 = (bf16[1024,512]{1,0:T(8,128)(2,1)S(1)}, bf16[1024,512]{1,0:T(8,128)(2,1)}, u32[]{:S(2)}) copy-start(bf16[1024,512]{1,0:T(8,128)(2,1)} %w_bound_ref.1) | copy-start | bytes 3145732
  14.8 47.1 %copy-start.2 = (bf16[256,1024]{1,0:T(8,128)(2,1)S(1)}, bf16[256,1024]{1,0:T(8,128)(2,1)}, u32[]{:S(2)}) copy-start(bf16[256,1024]{1,0:T(8,128)(2,1)} %w0_ref.1) | copy-start | bytes 1572868
  24.1 12.9 %collective-permute-start.4 = (bf16[128,1024]{1,0:T(8,128)(2,1)S(1)}, bf16[128,1024]{1,0:T(8,128)(2,1)S(1)}, u32[]{:S(2)}, u32[]{:S(2)}) collective-permute-start(bf16[128,1024]{1,0:T(8,128)(2,1)S(1)} %slice.6), channel_id=1, source_target_pairs={{0,1},{1,2},{2,3},{3,0},{4,5},{5,6},{6,7},{7,4},{8,9},{9,10},{10,1... | collective-permute-start | bytes 786440 | tf_op jit(solution)/shard_map/ppermute | solution.py:468
  25.5 11.5 %collective-permute-start.5 = (bf16[128,1024]{1,0:T(8,128)(2,1)S(1)}, bf16[128,1024]{1,0:T(8,128)(2,1)S(1)}, u32[]{:S(2)}, u32[]{:S(2)}) collective-permute-start(bf16[128,1024]{1,0:T(8,128)(2,1)S(1)} %slice.7), channel_id=1, source_target_pairs={{1,0},{2,1},{3,2},{0,3},{5,4},{6,5},{7,6},{4,7},{9,8},{10,9},{11,1... | collective-permute-start | bytes 786440 | tf_op jit(solution)/shard_map/ppermute | solution.py:468
  37.1 58.4 %copy-start.3 = (bf16[8,16,512]{2,1,0:T(8,128)(2,1)S(1)}, bf16[8,16,512]{2,1,0:T(8,128)(2,1)}, u32[]{:S(2)}) copy-start(bf16[8,16,512]{2,1,0:T(8,128)(2,1)} %reg_ref.1) | copy-start | bytes 393220
  37.1 24.8 %collective-permute-start.6 = (bf16[384,256]{1,0:T(8,128)(2,1)S(1)}, bf16[384,256]{1,0:T(8,128)(2,1)S(1)}, u32[]{:S(2)}, u32[]{:S(2)}) collective-permute-start(bf16[384,256]{1,0:T(8,128)(2,1)S(1)} %get-tuple-element.51), channel_id=1, source_target_pairs={{0,1},{1,2},{2,3},{3,0},{4,5},{5,6},{6,7},{7,4},{8,9},{9,10},{10,1... | collective-permute-start | bytes 589832 | tf_op jit(solution)/shard_map/ppermute | solution.py:472
  37.3 24.6 %collective-permute-start.7 = (bf16[384,256]{1,0:T(8,128)(2,1)S(1)}, bf16[384,256]{1,0:T(8,128)(2,1)S(1)}, u32[]{:S(2)}, u32[]{:S(2)}) collective-permute-start(bf16[384,256]{1,0:T(8,128)(2,1)S(1)} %get-tuple-element.52), channel_id=1, source_target_pairs={{0,2},{1,3},{2,0},{3,1},{4,6},{5,7},{6,4},{7,5},{8,10},{9,11},{10,... | collective-permute-start | bytes 589832 | tf_op jit(solution)/shard_map/ppermute | solution.py:472
  40.2 21.7 %collective-permute-start.8 = (bf16[384,256]{1,0:T(8,128)(2,1)S(1)}, bf16[384,256]{1,0:T(8,128)(2,1)S(1)}, u32[]{:S(2)}, u32[]{:S(2)}) collective-permute-start(bf16[384,256]{1,0:T(8,128)(2,1)S(1)} %get-tuple-element.53), channel_id=1, source_target_pairs={{0,3},{1,0},{2,1},{3,2},{4,7},{5,4},{6,5},{7,6},{8,11},{9,8},{10,9... | collective-permute-start | bytes 589832 | tf_op jit(solution)/shard_map/ppermute | solution.py:472
  65.6 29.8 %all-to-all-start.1 = ((bf16[64,16,384]{2,1,0:T(8,128)(2,1)}), bf16[64,16,384]{2,1,0:T(8,128)(2,1)S(1)}, u32[]{:S(2)}, u32[]{:S(2)}) async-start(bf16[64,16,384]{2,1,0:T(8,128)(2,1)} %get-tuple-element.59), calls=%async_computation.1 | async-start | bytes 1572864 | tf_op jit(solution)/shard_map/all_to_all | solution.py:481
  96.2 6.0 %collective-permute-start.10 = (bf16[48,512]{1,0:T(8,128)(2,1)S(1)}, bf16[48,512]{1,0:T(8,128)(2,1)S(1)}, u32[]{:S(2)}, u32[]{:S(2)}) collective-permute-start(bf16[48,512]{1,0:T(8,128)(2,1)S(1)} %get-tuple-element.63), channel_id=1, source_target_pairs={{1,0},{2,1},{3,2},{4,3},{5,4},{6,5},{7,6},{8,7},{9,8},{10,9},{11,1... | collective-permute-start | bytes 147464 | tf_op jit(solution)/shard_map/ppermute | solution.py:432
  98.9 10.2 %collective-permute-start.9 = (bf16[48,512]{1,0:T(8,128)(2,1)S(1)}, bf16[48,512]{1,0:T(8,128)(2,1)S(1)}, u32[]{:S(2)}, u32[]{:S(2)}) collective-permute-start(bf16[48,512]{1,0:T(8,128)(2,1)S(1)} %get-tuple-element.62), channel_id=1, source_target_pairs={{0,1},{1,2},{2,3},{3,4},{4,5},{5,6},{6,7},{7,8},{8,9},{9,10},{10,1... | collective-permute-start | bytes 147464 | tf_op jit(solution)/shard_map/ppermute | solution.py:432

commit v3 on v2

--- a/solution.py
+++ b/solution.py
@@ -5,12 +5,15 @@
 from jax import lax
 from jax.experimental import pallas as pl
 from jax.experimental.pallas import tpu as pltpu
+from jax.sharding import Mesh
 from jax.sharding import PartitionSpec as P
 
 HD = 64
 SIGNS = (0.0, 1.0, -1.0)
-BANDS = ("sec", "tile")
-CELLS = ("sec", "tile", "tp")
+BANDS = ("sec", "x", "z", "core")
+CELLS = BANDS + ("tp",)
+ALONG = ("sec", "z")
+ACROSS = ("x", "core")
 LOG2E = 1.4426950408889634
 MIB = 1024 * 1024
 ON_CHIP = pl.BlockSpec(memory_space=pltpu.VMEM)
@@ -83,9 +86,9 @@
 
 def project_kernel(code_ref, *refs, halo):
     step = pl.program_id(0)
-    both_ref, inv_ref = refs[-2:]
+    both_ref, inv_ref, held_ref, sems = refs[-4:]
     if halo:
-        before_ref, after_ref, gain_ref, *refs = refs[:-2]
+        before_ref, after_ref, gain_ref, *refs = refs[:-4]
         rows = before_ref.shape[0] - 16
         first = (1 - step) * rows
         digits = jnp.where(
@@ -96,13 +99,22 @@
         code = jnp.sum(jnp.where(lane < 3, digits * place, 0.0), -1, keepdims=True)
         code = code.astype(jnp.int32)
     else:
-        x_ref, gain_ref, *refs = refs[:-2]
+        x_ref, gain_ref, *refs = refs[:-4]
         rows = x_ref.shape[0]
         first = step * rows
         code = jnp.full((1, 1), code_ref[0], jnp.int32)
     weights, outs = refs[: len(refs) // 2], refs[len(refs) // 2 :]
-    features = gain_ref.shape[1]
-    gain = gain_ref[...].astype(jnp.float32)
+    copies = [
+        pltpu.make_async_copy(w_ref, held_ref.at[i], sems.at[i]) for i, w_ref in enumerate(weights)
+    ]
+
+    @pl.when(step == 0)
+    def _():
+        for copy in copies:
+            copy.start()
+
+    features = both_ref.shape[1]
+    gain = gain_ref[...].astype(jnp.float32).reshape(1, features)
     chunk, block = 16, 128
     for at in range(0, rows, block):
         for r in range(at, at + block, chunk):
@@ -119,10 +131,17 @@
                 state = x if sign == 0.0 else (x + p if sign > 0 else x - p)
                 mean = jnp.sum(state * state, -1, keepdims=True) * (1.0 / features)
                 inv_ref[s, r : r + chunk] = lax.rsqrt(mean + 1e-06)
+        if at == 0:
+
+            @pl.when(step == 0)
+            def _():
+                for copy in copies:
+                    copy.wait()
+
         here = slice(at, at + block)
-        for index, (w_ref, out_ref) in enumerate(zip(weights, outs)):
+        for index, out_ref in enumerate(outs):
             scale = HD**-0.5 * LOG2E if (index == 0 and not halo) else 1.0
-            made = dot(both_ref[2 * at : 2 * at + 2 * block], w_ref[...])
+            made = dot(both_ref[2 * at : 2 * at + 2 * block], held_ref[index])
             base, diff = made[:block], made[block:]
             for s, sign in enumerate(SIGNS):
                 full = base if sign == 0.0 else (base + diff if sign > 0 else base - diff)
@@ -130,9 +149,8 @@
 
 
 def project(code, arrays, gain, weights, halo):
-    features = gain.shape[1]
+    features = gain.shape[0]
     cols = weights[0].shape[1]
-    whole = lambda i: (0, 0)
     if halo:
         tokens = 2 * (arrays[0].shape[0] - 16)
         specs = [ON_CHIP for a in arrays]
@@ -146,12 +164,14 @@
         grid=(2,),
         in_specs=[SCALARS]
         + specs
-        + [pl.BlockSpec(gain.shape, whole)]
-        + [pl.BlockSpec(w.shape, whole) for w in weights],
+        + [pl.BlockSpec(gain.shape, lambda i: (0,))]
+        + [pl.BlockSpec(memory_space=pltpu.HBM) for w in weights],
         out_specs=[pl.BlockSpec((3, rows, cols), lambda i: (0, i, 0)) for _ in weights],
         scratch_shapes=[
             pltpu.VMEM((2 * rows, features), jnp.bfloat16),
             pltpu.VMEM((3, rows, 1), jnp.float32),
+            pltpu.VMEM((len(weights), features, cols), jnp.bfloat16),
+            pltpu.SemaphoreType.DMA((len(weights),)),
         ],
         compiler_params=pltpu.CompilerParams(vmem_limit_bytes=12 * MIB),
         name="project_halo" if halo else "project_own",
@@ -227,8 +247,11 @@
     return jnp.sum(jnp.where(mine, wide, 0.0), 0, keepdims=True)
 
 
-def ask_kernel(band_ref, tok_ref, ask_ref):
-    bands = ask_ref.shape[0]
+def place_of(band):
+    return (band // 32) * 4 + (band // 2) % 4, ((band // 8) % 4) * 2 + band % 2
+
+
+def ask_kernel(band_ref, tok_ref, ask_ref, *, bands):
     named = cells_row(band_ref[...])
     token = cells_row(tok_ref[...])
     cells = named.shape[1]
@@ -241,13 +264,22 @@
         hit = jnp.where(slot == s, match, 0.0)
         token_s = jnp.sum(hit * (token + 1.0), -1, keepdims=True) - 1.0
         asked = jnp.where(lanes == s, token_s, asked)
-    ask_ref[...] = asked[:, :4].astype(jnp.int32)
+    along, wide = ask_ref.shape
+    lane = iota((4, wide), 1)
+    four = (lane % 4 == iota((4, wide), 0)).astype(jnp.float32).astype(jnp.bfloat16)
+    spread = dot(asked[:, :4].astype(jnp.bfloat16), four)
+    _, xc = place_of(iota((bands, 1), 0))
+    spread = jnp.where(iota((bands, wide), 1) // 4 == xc, spread, 0.0)
+    z, _ = place_of(iota((1, bands), 1))
+    rows = (iota((along, bands), 0) == z).astype(jnp.float32).astype(jnp.bfloat16)
+    ask_ref[...] = dot(rows, spread.astype(jnp.bfloat16)).astype(jnp.int32)
 
 
 def ask(band, tok, bands):
-    return pl.pallas_call(
-        ask_kernel,
-        out_shape=jax.ShapeDtypeStruct((bands, 4), jnp.int32),
+    along, across = lax.axis_size(ALONG), lax.axis_size(ACROSS)
+    return pl.pallas_call(
+        functools.partial(ask_kernel, bands=bands),
+        out_shape=jax.ShapeDtypeStruct((along, across * 4), jnp.int32),
         in_specs=[ON_CHIP] * 2,
         out_specs=ON_CHIP,
         compiler_params=pltpu.CompilerParams(vmem_limit_bytes=4 * MIB),
@@ -255,7 +287,15 @@
     )(band, tok)
 
 
-def take_kernel(band_ref, take_ref):
+def take_kernel(band_ref, conv_hbm_ref, take_ref, outer_ref, sems):
+    copies = [
+        pltpu.make_async_copy(
+            conv_hbm_ref.at[pl.ds(6 * i, 3)], outer_ref.at[pl.ds(3 * i, 3)], sems.at[i]
+        )
+        for i in range(2)
+    ]
+    for copy in copies:
+        copy.start()
     band_row = cells_row(band_ref[...])
     cells = band_row.shape[1]
     rows = take_ref.shape[1]
@@ -268,25 +308,59 @@
         take_ref[part * cells : (part + 1) * cells, :] = (
             (iota((cells, rows), 1) == target + part).astype(jnp.float32).astype(jnp.bfloat16)
         )
-
-
-def make_take(band, bands):
+    for copy in copies:
+        copy.wait()
+
+
+def make_take(band, bands, conv_w):
     return pl.pallas_call(
         take_kernel,
-        out_shape=jax.ShapeDtypeStruct((4 * band.size, bands * 16), jnp.bfloat16),
+        out_shape=[
+            jax.ShapeDtypeStruct((4 * band.size, bands * 16), jnp.bfloat16),
+            jax.ShapeDtypeStruct((6, *conv_w.shape[1:]), conv_w.dtype),
+        ],
+        in_specs=[ON_CHIP, pl.BlockSpec(memory_space=pltpu.HBM)],
+        out_specs=[ON_CHIP] * 2,
+        scratch_shapes=[pltpu.SemaphoreType.DMA((2,))],
+        compiler_params=pltpu.CompilerParams(vmem_limit_bytes=4 * MIB),
+        name="take",
+    )(band, conv_w)
+
+
+def turn_kernel(x_ref, out_ref):
+    count, wide = x_ref.shape
+    others, width = out_ref.shape
+    x = x_ref[...].astype(jnp.float32).astype(jnp.bfloat16)
+    lane = iota((wide, width), 1)
+    row = iota((wide, width), 0)
+    for other in range(others):
+        choose = (row == other * 4 + lane % 4).astype(jnp.float32).astype(jnp.bfloat16)
+        spread = dot(x, choose)
+        mine = iota((count, width), 1) // 4 == iota((count, width), 0)
+        out_ref[other : other + 1] = jnp.sum(
+            jnp.where(mine, spread, 0.0), 0, keepdims=True
+        ).astype(jnp.int32)
+
+
+def turn(x):
+    count, wide = x.shape
+    return pl.pallas_call(
+        turn_kernel,
+        out_shape=jax.ShapeDtypeStruct((wide // 4, 4 * count), jnp.int32),
         in_specs=[ON_CHIP],
         out_specs=ON_CHIP,
-        compiler_params=pltpu.CompilerParams(vmem_limit_bytes=4 * MIB),
-        name="take",
-    )(band)
+        compiler_params=pltpu.CompilerParams(vmem_limit_bytes=2 * MIB),
+        name="turn",
+    )(x)
 
 
 def pick_rows(asked, rows, cells):
-    bands = asked.shape[0]
-    spread = (iota((rows, bands), 0) // 16 == iota((rows, bands), 1)).astype(jnp.float32)
-    per_row = dot(spread.astype(jnp.bfloat16), asked.astype(jnp.float32).astype(jnp.bfloat16))
+    across, wide = asked.shape
     r = iota((rows, 1), 0)
-    mine = iota((rows, 4), 1) == (r // 4) % 4
+    z, xc = place_of(r // 16)
+    spread = (iota((rows, across), 1) == xc).astype(jnp.float32).astype(jnp.bfloat16)
+    per_row = dot(spread, asked.astype(jnp.float32).astype(jnp.bfloat16))
+    mine = iota((rows, wide), 1) == z * 4 + (r // 4) % 4
     token_r = jnp.sum(jnp.where(mine, per_row, 0.0), -1, keepdims=True).astype(jnp.int32)
     target = jnp.where(token_r >= 0, (r % 4) * cells + token_r, -1)
     return (iota((rows, 4 * cells), 1) == target).astype(jnp.float32).astype(jnp.bfloat16)
@@ -325,8 +399,8 @@
     send_ref[...] = picked.reshape(send_ref.shape)
 
 
-def combine(code, att, w_outs, x, w_bound, asked):
-    shapes = [(3, att[0].shape[0] // 3, x.shape[1]), (asked.shape[0], 16, 384)]
+def combine(code, att, w_outs, x, w_bound, asked, bands):
+    shapes = [(3, att[0].shape[0] // 3, x.shape[1]), (bands, 16, 384)]
     operands = [*att, *w_outs, x, w_bound, asked]
     whole = lambda: (0, 0, 0)
     return pl.pallas_call(
@@ -368,61 +442,86 @@
     )(arrived, take, reg)
 
 
-def conv_kernel(x_ref, before_ref, after_ref, w_ref, out_ref, low_ref, mid_ref, high_ref, sum_ref):
-    step = pl.program_id(0)
+def row_shifts(x, rows):
+    wide = x.astype(jnp.float32)
+    total = x.shape[0]
+    row = iota((total, 1), 0) % rows
+    low = jnp.where(row > 0, pltpu.roll(wide, 1, 0), 0.0).astype(jnp.bfloat16)
+    high = jnp.where(row < rows - 1, pltpu.roll(wide, total - 1, 0), 0.0).astype(jnp.bfloat16)
+    return low, x, high
+
+
+def inner_kernel(x_ref, outer_ref, conv_hbm_ref, sum_ref, held_ref, sem):
+    copy = pltpu.make_async_copy(conv_hbm_ref.at[pl.ds(3, 3)], held_ref, sem)
+    copy.start()
     cols, slab, channels = x_ref.shape
     cells = cols * slab
+    shifts = row_shifts(x_ref[...].reshape(cells, channels), slab // 3)
+    before = after = None
+    for b, x in enumerate(shifts):
+        one = dot(x[: cells - slab], outer_ref[b])
+        two = dot(x[slab:], outer_ref[3 + b])
+        before = one if before is None else before + one
+        after = two if after is None else after + two
+    copy.wait()
+    middle = None
+    for b, x in enumerate(shifts):
+        one = dot(x, held_ref[b])
+        middle = one if middle is None else middle + one
+    sum_ref[:slab] = middle[:slab] + after[:slab]
+    sum_ref[slab : cells - slab] = middle[slab : cells - slab] + before[: cells - 2 * slab] + after[slab:]
+    sum_ref[cells - slab :] = middle[cells - slab :] + before[cells - 2 * slab :]
+
+
+def convolve_inner(x, outer, conv_w):
+    cols, slab, channels = x.shape
+    return pl.pallas_call(
+        inner_kernel,
+        out_shape=jax.ShapeDtypeStruct((cols * slab, channels), jnp.float32),
+        in_specs=[ON_CHIP] * 2 + [pl.BlockSpec(memory_space=pltpu.HBM)],
+        out_specs=ON_CHIP,
+        scratch_shapes=[
+            pltpu.VMEM((3, channels, channels), jnp.bfloat16),
+            pltpu.SemaphoreType.DMA(()),
+        ],
+        compiler_params=pltpu.CompilerParams(vmem_limit_bytes=16 * MIB),
+        name="convolve_inner",
+    )(x, outer, conv_w)
+
+
+def finish_kernel(x_ref, before_ref, after_ref, outer_ref, sum_ref, out_ref):
+    cols, slab, channels = x_ref.shape
     rows = slab // 3
-
-    @pl.when(step == 0)
-    def _():
-        x = x_ref[...].reshape(cells, channels)
-        padded = jnp.concatenate([before_ref[...], x, after_ref[...]], 0)
-        wide = padded.astype(jnp.float32)
-        total = padded.shape[0]
-        row = iota((total, 1), 0) % rows
-        low_ref[...] = jnp.where(row > 0, pltpu.roll(wide, 1, 0), 0.0).astype(jnp.bfloat16)
-        mid_ref[...] = padded
-        high_ref[...] = jnp.where(
-            row < rows - 1, pltpu.roll(wide, total - 1, 0), 0.0
-        ).astype(jnp.bfloat16)
-
-    here = pl.ds(pl.multiple_of(step * slab, slab), cells)
-    part = dot(low_ref[here], w_ref[0]) + dot(mid_ref[here], w_ref[1]) + dot(high_ref[here], w_ref[2])
-
-    @pl.when(step == 0)
-    def _():
-        sum_ref[...] = part
-
-    @pl.when(step == 1)
-    def _():
-        sum_ref[...] += part
-
-    @pl.when(step == 2)
-    def _():
-        conv = sum_ref[...] + part
-        x = x_ref[...].reshape(cells, channels).astype(jnp.float32)
-        result = (x + conv / (1.0 + jnp.exp(-conv))).astype(jnp.bfloat16)
-        result = result.reshape(cols, slab, channels)
+    sides = []
+    for side, ref in enumerate((before_ref, after_ref)):
+        total = None
+        for b, x in enumerate(row_shifts(ref[...], rows)):
+            one = dot(x, outer_ref[3 * side + b])
+            total = one if total is None else total + one
+        sides.append(total)
+    for col in range(cols):
+        conv = sum_ref[col * slab : (col + 1) * slab]
+        if col == 0:
+            conv = conv + sides[0]
+        if col == cols - 1:
+            conv = conv + sides[1]
+        result = x_ref[col].astype(jnp.float32) + conv / (1.0 + jnp.exp(-conv))
+        result = result.astype(jnp.bfloat16)
         for s in range(3):
-            out_ref[s] = result[:, s * rows : (s + 1) * rows, :]
-
-
-def convolve(x, before, after, conv_w):
+            out_ref[s, col] = result[s * rows : (s + 1) * rows]
+
+
+def convolve_finish(x, before, after, outer, total):
     cols, slab, channels = x.shape
     shape = (3, cols, slab // 3, channels)
-    padded = ((cols + 2) * slab, channels)
-    return pl.pallas_call(
-        conv_kernel,
+    return pl.pallas_call(
+        finish_kernel,
         out_shape=jax.ShapeDtypeStruct(shape, jnp.bfloat16),
-        grid=(3,),
-        in_specs=[ON_CHIP] * 3 + [pl.BlockSpec((3, channels, channels), lambda i: (i, 0, 0))],
-        out_specs=pl.BlockSpec(shape, lambda i: (0, 0, 0, 0)),
-        scratch_shapes=[pltpu.VMEM(padded, jnp.bfloat16)] * 3
-        + [pltpu.VMEM((cols * slab, channels), jnp.float32)],
-        compiler_params=pltpu.CompilerParams(vmem_limit_bytes=16 * MIB),
-        name="convolve",
-    )(x, before, after, conv_w)
+        in_specs=[ON_CHIP] * 5,
+        out_specs=pl.BlockSpec(shape, lambda: (0, 0, 0, 0)),
+        compiler_params=pltpu.CompilerParams(vmem_limit_bytes=8 * MIB),
+        name="convolve_finish",
+    )(x, before, after, outer, total)
 
 
 def neighbours(last, first, axis):
@@ -450,7 +549,7 @@
     bands = lax.axis_size(BANDS)
     tokens, features = global_state.shape
     half = tokens // 2
-    gain = norm_gain[None, :]
+    gain = norm_gain
     cell_band = src_band.reshape(src_tok.shape)
     w_query, w_key, w_value = (in_hbm(w) for w in (w_query, w_key, w_value))
 
@@ -461,51 +560,54 @@
     asked = ask(cell_band, src_tok, bands)
 
     q, k, v = project(band_codes, [in_hbm(global_state)], gain, [w_query, w_key, w_value], False)
+    q, w1, w3 = lax.optimization_barrier((q, w1, w3))
+    middle = w_out.shape[0] // 2
+    top, low = lax.ppermute(w1[:middle], "tp", up), lax.ppermute(w3[middle:], "tp", down)
     q, before, after = lax.optimization_barrier((q, before, after))
     k_halo, v_halo = project(band_codes, [before, after], gain, [w_key, w_value], True)
-    k_halo, w1, w3 = lax.optimization_barrier((k_halo, w1, w3))
-    middle = w_out.shape[0] // 2
-    top, low = lax.ppermute(w1[:middle], "tp", up), lax.ppermute(w3[middle:], "tp", down)
     attended = attend(q, k, v, k_halo, v_halo, ranks, bands)
     attended, asked, top, low = lax.optimization_barrier((attended, asked, top, low))
     attended = [attended[0]] + [
         lax.ppermute(attended[d], "tp", [(i, (i + d) % ranks) for i in range(ranks)])
         for d in range(1, ranks)
     ]
-    asked = lax.all_to_all(asked[:, None, :], BANDS, 0, 0, tiled=True)[:, 0, :]
+    asked = lax.all_to_all(asked[:, None, :], ALONG, 0, 0, tiled=True)[:, 0, :]
+    asked = lax.all_to_all(turn(asked)[:, None, :], ACROSS, 0, 0, tiled=True)[:, 0, :]
     global_out, send = combine(
-        band_codes, attended, [w_out, w1, w3, top, low], global_state, w_bound, asked
+        band_codes, attended, [w_out, w1, w3, top, low], global_state, w_bound, asked, bands
     )
     cell_band, send = lax.optimization_barrier((cell_band, send))
-    take = make_take(cell_band, bands)
+    conv_w = in_hbm(conv_w)
+    take, outer = make_take(cell_band, bands, conv_w)
     arrived = lax.all_to_all(send, BANDS, 0, 0, tiled=True)
     inputs, first, last = make_inputs(arrived, take, reg_state)
     before, after = neighbours(last, first, CELLS)
-    return global_out, convolve(inputs, before, after, in_hbm(conv_w))
+    total = convolve_inner(inputs, outer, conv_w)
+    return global_out, convolve_finish(inputs, before, after, outer, total)
 
 
 def solution(mesh):
+    parts = Mesh(
+        mesh.devices.reshape(mesh.shape["sec"], 4, 4, 2, mesh.shape["tp"]), CELLS
+    )
     placed = (
-        P(("sec", "tile"), None),
-        P(("sec", "tile")),
+        P(BANDS, None),
+        P(BANDS),
         P(),
         P(None, "tp"),
         P(None, "tp"),
         P(None, "tp"),
         P("tp", None),
-        P(("sec", "tile", "tp"), None, None),
-        P(("sec", "tile", "tp"), None, None),
-        P(("sec", "tile", "tp"), None),
+        P(CELLS, None, None),
+        P(CELLS, None, None),
+        P(CELLS, None),
         P(),
         P(),
     )
     return jax.shard_map(
         per_device,
-        mesh=mesh,
+        mesh=parts,
         in_specs=placed,
-        out_specs=(
-            P(None, ("sec", "tile", "tp"), None),
-            P(None, ("sec", "tile", "tp"), None, None),
-        ),
+        out_specs=(P(None, CELLS, None), P(None, CELLS, None, None)),
         check_vma=False,
     )

time: 116 us -> 118 us (1.017)
  waiting for transfers between devices: 29.8 us -> 20.3 us
  starting transfers between devices: 31.5 us -> 36.3 us
  blocking collectives: 20.6 us -> 23.6 us
  local copies, waits for them, and re-layouts: 0.75 us -> 2.98 us
  Pallas kernels: 30.5 us -> 32.3 us
    ppermute x4, waiting for transfers between devices: 7.07 us -> 0.01 us  [neighbours(): return (lax.ppermute(last, axis, up), lax.ppermute(first, axis, down))]
    ppermute x4, starting transfers between devices: 14.1 us -> 18.8 us  [neighbours(): return (lax.ppermute(last, axis, up), lax.ppermute(first, axis, down))]
    all_to_all x1 -> x2, blocking collectives: 20.6 us -> 23.6 us  [the longest x1 16.1 us: per_device(): asked = lax.all_to_all(asked[:, None, :], ALONG, 0, 0, tiled=True)[:, 0, :]]
    unnamed x12 -> x18, local copies, waits for them, and re-layouts: 0.03 us -> 2.94 us
    all_to_all x1, waiting for transfers between devices: 22.8 us -> 20.3 us  [per_device(): arrived = lax.all_to_all(send, BANDS, 0, 0, tiled=True)]
    pallas_call x3 -> x5, Pallas kernels: 6.54 us -> 6.4 us  [the longest x1 2.2 us: convolve_inner(): pl.pallas_call(inner_kernel, out_shape=jax.ShapeDtypeStruct((cols * slab,...]
  transfers between devices with their start and end apart: 12 -> 12, of which waited for: 3 -> 1; matrix products, arithmetic and copies ran while one was open for 1% -> 0% of each run, Pallas kernels for 17% -> 21%
where the time goes in v3:
time: 118 us; the launch traced here: 117 us
  starting transfers between devices  36.3 us (31%)
  Pallas kernels  32.3 us (27%)
  blocking collectives  23.6 us (20%)
  waiting for transfers between devices  20.3 us (17%)
  local copies, waits for them, and re-layouts  2.98 us (3%)
  between operations  1.55 us (1%)
    all_to_all x1, waiting for transfers between devices, per_device(): arrived = lax.all_to_all(send, BANDS, 0, 0, tiled=True)  20.3 us
    ppermute x4, starting transfers between devices, neighbours(): return (lax.ppermute(last, axis, up), lax.ppermute(first, axis, down))  18.8 us
    all_to_all x1, blocking collectives, per_device(): asked = lax.all_to_all(asked[:, None, :], ALONG, 0, 0, tiled=True)[:, 0, :]  16.1 us
    pallas_call x2, Pallas kernels, project(): pl.pallas_call(functools.partial(project_kernel, halo=halo), out_shape=[j...  9.72 us
    pallas_call x1, Pallas kernels, attend(): pl.pallas_call(functools.partial(attend_kernel, bands=bands), out_shape=[...  9.14 us
    all_to_all x1, blocking collectives, per_device(): lax.all_to_all(turn(asked)[:, None, :], ACROSS, 0, 0, tiled=True)[:, 0, :]  7.5 us
    all_to_all x1, starting transfers between devices, per_device(): arrived = lax.all_to_all(send, BANDS, 0, 0, tiled=True)  7.31 us
    pallas_call x1, Pallas kernels, combine(): pl.pallas_call(combine_kernel, out_shape=[jax.ShapeDtypeStruct(s, jnp.bfl...  3.92 us
  transfers between devices with their start and end apart: 12, of which 1 were waited for; matrix products, arithmetic and copies ran while one was open for 0% of the time, Pallas kernels for 21%

profile of v3, /device:TPU:4, one launch (start us, length us, event | category | flops | bytes accessed | tf_op | source)
XLA Modules:
  0.0 116.9 jit_solution(10585623763309005082)
XLA Ops:
  0.7 1.7 %collective-permute-start = (bf16[256,1024]{1,0:T(8,128)(2,1)}, bf16[256,1024]{1,0:T(8,128)(2,1)S(1)}, u32[]{:S(2)}, u32[]{:S(2)}) collective-permute-start(bf16[256,1024]{1,0:T(8,128)(2,1)} %w0_ref.1), channel_id=1, source_target_pairs={{0,1},{1,2},{2,3},{3,0},{4,5},{5,6},{6,7},{7,4},{8,9},{9,10},{10,1... | collective-permute-start | bytes 1572872 | tf_op jit(solution)/shard_map/ppermute | solution.py:559
  2.3 1.7 %collective-permute-start.1 = (bf16[256,1024]{1,0:T(8,128)(2,1)}, bf16[256,1024]{1,0:T(8,128)(2,1)S(1)}, u32[]{:S(2)}, u32[]{:S(2)}) collective-permute-start(bf16[256,1024]{1,0:T(8,128)(2,1)} %w0_ref.1), channel_id=1, source_target_pairs={{1,0},{2,1},{3,2},{0,3},{5,4},{6,5},{7,6},{4,7},{9,8},{10,9},{11,1... | collective-permute-start | bytes 1572872 | tf_op jit(solution)/shard_map/ppermute | solution.py:559
  4.6 1.2 %edges.1 = (bf16[272,1024]{1,0:T(8,128)(2,1)S(1)}, bf16[272,1024]{1,0:T(8,128)(2,1)S(1)}) custom-call(s32[1]{0:T(128)S(6)} %copy.16.code_ref, bf16[512,1024]{1,0:T(8,128)(2,1)} %x_ref.3), custom_call_target="tpu_custom_call" | custom-call | tf_op jit(solution)/shard_map/edges/pallas_call | solution.py:76
  5.8 1.9 %collective-permute-start.2 = (bf16[272,1024]{1,0:T(8,128)(2,1)S(1)}, bf16[272,1024]{1,0:T(8,128)(2,1)S(1)}, u32[]{:S(2)}, u32[]{:S(2)}) collective-permute-start(bf16[272,1024]{1,0:T(8,128)(2,1)S(1)} %get-tuple-element.37), channel_id=1, source_target_pairs={{0,4},{4,8},{8,12},{12,16},{16,20},{20,24},{24,28},{28,32},{32,36}... | collective-permute-start | bytes 1671176 | tf_op jit(solution)/shard_map/ppermute | solution.py:531
  7.8 0.0 copy-start
  7.8 0.0 copy-start.3
  7.8 0.0 copy-start.4
  7.8 6.5 %collective-permute-start.3 = (bf16[272,1024]{1,0:T(8,128)(2,1)S(1)}, bf16[272,1024]{1,0:T(8,128)(2,1)S(1)}, u32[]{:S(2)}, u32[]{:S(2)}) collective-permute-start(bf16[272,1024]{1,0:T(8,128)(2,1)S(1)} %get-tuple-element.38), channel_id=1, source_target_pairs={{4,0},{8,4},{12,8},{16,12},{20,16},{24,20},{28,24},{32,28},{36,32}... | collective-permute-start | bytes 1671176 | tf_op jit(solution)/shard_map/ppermute | solution.py:531
  14.3 0.7 copy-done.7
  15.0 5.7 %project_own.1 = (bf16[3,512,256]{2,1,0:T(8,128)(2,1)S(1)}, bf16[3,512,256]{2,1,0:T(8,128)(2,1)S(1)}, bf16[3,512,256]{2,1,0:T(8,128)(2,1)S(1)}) custom-call(s32[1]{0:T(128)S(6)} %copy.16.code_ref, bf16[512,1024]{1,0:T(8,128)(2,1)} %x_ref.3, bf16[1024]{0:T(1024)(128)(2,1)S(1)} %copy-done.7, bf16[1024,256]{1,0:T(8,128)(2,1)} %refs_2_.2, ...), custom_call_target="tpu_custom_call" | custom-call | tf_op jit(solution)/shard_map/project_own/pallas_call | solution.py:161
  20.7 0.4 collective-permute-start.4
  21.2 2.9 %collective-permute-start.5 = (bf16[128,1024]{1,0:T(8,128)(2,1)S(1)}, bf16[128,1024]{1,0:T(8,128)(2,1)S(1)}, u32[]{:S(2)}, u32[]{:S(2)}) collective-permute-start(bf16[128,1024]{1,0:T(8,128)(2,1)S(1)} %slice.7), channel_id=1, source_target_pairs={{1,0},{2,1},{3,2},{0,3},{5,4},{6,5},{7,6},{4,7},{9,8},{10,9},{11,1... | collective-permute-start | bytes 786440 | tf_op jit(solution)/shard_map/ppermute | solution.py:565
  24.2 0.6 ask.1
  24.7 4.0 %project_halo.1 = (bf16[3,512,256]{2,1,0:T(8,128)(2,1)S(1)}, bf16[3,512,256]{2,1,0:T(8,128)(2,1)S(1)}) custom-call(s32[1]{0:T(128)S(6)} %copy.16.code_ref, bf16[272,1024]{1,0:T(8,128)(2,1)S(1)} %collective-permute-done.2.refs_0_, bf16[272,1024]{1,0:T(8,128)(2,1)S(1)} %collective-permute-done.3.refs_1_, bf16[1024]{0:T(1024)(128)(2,1)S(1)} %copy-done.7, ...), custom_call_target="tpu_custom_call" | custom-call | tf_op jit(solution)/shard_map/project_halo/pallas_call | solution.py:161
  28.8 9.1 %attend.1 = (bf16[384,256]{1,0:T(8,128)(2,1)S(1)}, bf16[384,256]{1,0:T(8,128)(2,1)S(1)}, bf16[384,256]{1,0:T(8,128)(2,1)S(1)}, bf16[384,256]{1,0:T(8,128)(2,1)S(1)}) custom-call(bf16[3,512,256]{2,1,0:T(8,128)(2,1)S(1)} %get-tuple-element.39.q_ref, bf16[3,512,256]{2,1,0:T(8,128)(2,1)S(1)} %get-tuple-element.40.k_ref, ...), custom_call_target="tpu_custom_call" | custom-call | tf_op jit(solution)/shard_map/attend/pallas_call | solution.py:229
  37.9 0.1 collective-permute-start.6
  38.0 2.1 %collective-permute-start.7 = (bf16[384,256]{1,0:T(8,128)(2,1)S(1)}, bf16[384,256]{1,0:T(8,128)(2,1)S(1)}, u32[]{:S(2)}, u32[]{:S(2)}) collective-permute-start(bf16[384,256]{1,0:T(8,128)(2,1)S(1)} %get-tuple-element.54), channel_id=1, source_target_pairs={{0,2},{1,3},{2,0},{3,1},{4,6},{5,7},{6,4},{7,5},{8,10},{9,11},{10,... | collective-permute-start | bytes 589832 | tf_op jit(solution)/shard_map/ppermute | solution.py:571
  40.1 1.3 %collective-permute-start.8 = (bf16[384,256]{1,0:T(8,128)(2,1)S(1)}, bf16[384,256]{1,0:T(8,128)(2,1)S(1)}, u32[]{:S(2)}, u32[]{:S(2)}) collective-permute-start(bf16[384,256]{1,0:T(8,128)(2,1)S(1)} %get-tuple-element.55), channel_id=1, source_target_pairs={{0,3},{1,0},{2,1},{3,2},{4,7},{5,4},{6,5},{7,6},{8,11},{9,8},{10,9... | collective-permute-start | bytes 589832 | tf_op jit(solution)/shard_map/ppermute | solution.py:571
  41.4 16.1 %all_to_all.15 = s32[8,1,32]{2,1,0:T(1,128)S(1)} all-to-all(s32[8,1,32]{2,1,0:T(1,128)S(1)} %bitcast.9), channel_id=1, replica_groups=mesh['sec'=2,'x'=4,'z'=4,'core'=2,'tp'=4] {'sec','z'}, dimensions={0} | all-to-all | bytes 2048 | tf_op jit(solution)/shard_map/all_to_all | solution.py:574
  57.5 0.1 turn.1
  57.7 7.5 %all_to_all.16 = s32[8,1,32]{2,1,0:T(1,128)S(1)} all-to-all(s32[8,1,32]{2,1,0:T(1,128)S(1)} %bitcast.11), channel_id=1, replica_groups=mesh['sec'=2,'x'=4,'z'=4,'core'=2,'tp'=4] {'x','core'}, dimensions={0} | all-to-all | bytes 2048 | tf_op jit(solution)/shard_map/all_to_all | solution.py:575
  65.3 3.9 %combine.1 = (bf16[3,128,1024]{2,1,0:T(8,128)(2,1)}, bf16[64,16,384]{2,1,0:T(8,128)(2,1)}) custom-call(s32[1]{0:T(128)S(6)} %copy.16.code_ref, bf16[384,256]{1,0:T(8,128)(2,1)S(1)} %get-tuple-element.52.att0_ref, bf16[384,256]{1,0:T(8,128)(2,1)S(1)} %collective-permute-done.6.att1_ref, bf16[384,256]{1,0:T(8,128)(2,1)S(1)} %collective-permute-done.7.att2_ref, ...), custom_call_target="tpu_custom_call" | custom-call | tf_op jit(solution)/shard_map/combine/pallas_call | solution.py:406
  69.2 7.3 %all-to-all-start.2 = ((bf16[64,16,384]{2,1,0:T(8,128)(2,1)}), bf16[64,16,384]{2,1,0:T(8,128)(2,1)}, u32[]{:S(2)}, u32[]{:S(2)}) async-start(bf16[64,16,384]{2,1,0:T(8,128)(2,1)} %get-tuple-element.61), calls=%async_computation.2 | async-start | bytes 1572864 | tf_op jit(solution)/shard_map/all_to_all | solution.py:582
  76.5 1.9 %take.1 = (bf16[512,1024]{1,0:T(8,128)(2,1)S(1)}, bf16[6,512,512]{2,1,0:T(8,128)(2,1)S(1)}) custom-call(s32[8,16]{1,0:T(8,128)S(1)} %bitcast.13, bf16[9,512,512]{2,1,0:T(8,128)(2,1)} %conv_hbm_ref.3), custom_call_target="tpu_custom_call" | custom-call | tf_op jit(solution)/shard_map/take/pallas_call | solution.py:316
  78.4 1.0 copy-done.1
  79.4 20.3 %all-to-all-done.2.arrived_ref = bf16[64,16,384]{2,1,0:T(8,128)(2,1)} async-done(((bf16[64,16,384]{2,1,0:T(8,128)(2,1)}), bf16[64,16,384]{2,1,0:T(8,128)(2,1)}, u32[]{:S(2)}, u32[]{:S(2)}) %all-to-all-start.2) | async-done | bytes 786464 | tf_op jit(solution)/shard_map/all_to_all | solution.py:582
  99.7 1.2 %copy-done.2 = bf16[512,1024]{1,0:T(8,128)(2,1)S(1)} copy-done((bf16[512,1024]{1,0:T(8,128)(2,1)S(1)}, bf16[512,1024]{1,0:T(8,128)(2,1)}, u32[]{:S(2)}) %copy-start.2) | copy-done | bytes 1048600
  100.9 1.8 %inputs.1 = (bf16[8,48,512]{2,1,0:T(8,128)(2,1)S(1)}, bf16[48,512]{1,0:T(8,128)(2,1)S(1)}, bf16[48,512]{1,0:T(8,128)(2,1)S(1)}) custom-call(bf16[64,16,384]{2,1,0:T(8,128)(2,1)} %all-to-all-done.2.arrived_ref, bf16[512,1024]{1,0:T(8,128)(2,1)S(1)} %copy-done.2, bf16[8,16,512]{2,1,0:T(8,128)(2,1)S(1)} %copy-done.5), custom_call_target="tpu_custom_call" | custom-call | tf_op jit(solution)/shard_map/inputs/pallas_call | solution.py:435
  102.8 2.6 %collective-permute-start.9 = (bf16[48,512]{1,0:T(8,128)(2,1)S(1)}, bf16[48,512]{1,0:T(8,128)(2,1)S(1)}, u32[]{:S(2)}, u32[]{:S(2)}) collective-permute-start(bf16[48,512]{1,0:T(8,128)(2,1)S(1)} %get-tuple-element.65), channel_id=1, source_target_pairs={{0,1},{1,2},{2,3},{3,4},{4,5},{5,6},{6,7},{7,8},{8,9},{9,10},{10,1... | collective-permute-start | bytes 147464 | tf_op jit(solution)/shard_map/ppermute | solution.py:531
  105.4 7.8 %collective-permute-start.10 = (bf16[48,512]{1,0:T(8,128)(2,1)S(1)}, bf16[48,512]{1,0:T(8,128)(2,1)S(1)}, u32[]{:S(2)}, u32[]{:S(2)}) collective-permute-start(bf16[48,512]{1,0:T(8,128)(2,1)S(1)} %get-tuple-element.66), channel_id=1, source_target_pairs={{1,0},{2,1},{3,2},{4,3},{5,4},{6,5},{7,6},{8,7},{9,8},{10,9},{11,1... | collective-permute-start | bytes 147464 | tf_op jit(solution)/shard_map/ppermute | solution.py:531
  113.1 2.2 %convolve_inner.1.sum_ref = f32[384,512]{1,0:T(8,128)S(1)} custom-call(bf16[8,48,512]{2,1,0:T(8,128)(2,1)S(1)} %get-tuple-element.64.x_ref, bf16[6,512,512]{2,1,0:T(8,128)(2,1)S(1)} %get-tuple-element.67.outer_ref, bf16[9,512,512]{2,1,0:T(8,128)(2,1)} %conv_hbm_ref.3), custom_call_target="tpu_custom_call" | custom-call | tf_op jit(solution)/shard_map/convolve_inner/pallas_call | solution.py:478
  115.4 1.6 %convolve_finish.1 = bf16[3,8,16,512]{3,2,1,0:T(8,128)(2,1)} custom-call(bf16[8,48,512]{2,1,0:T(8,128)(2,1)S(1)} %get-tuple-element.64.x_ref, bf16[48,512]{1,0:T(8,128)(2,1)S(1)} %collective-permute-done.9.before_ref, bf16[48,512]{1,0:T(8,128)(2,1)S(1)} %collective-permute-done.10.after_ref, bf16[6,512,512]{2,1,0:T(8,128)(2,1)S(1)} %get-tuple-element.67.outer_ref, ...), custom_call_target="tpu_custom_call" | custom-call | tf_op jit(solution)/shard_map/convolve_finish/pallas_call | solution.py:517
  (25 shorter events, 0.1 us)
Async XLA Ops:
  0.6 23.5 %copy-start.6 = (s32[8,16,1]{1,2,0:T(1,128)S(1)}, s32[8,16,1]{1,2,0:T(1,128)}, u32[]{:S(2)}) copy-start(s32[8,16,1]{1,2,0:T(1,128)} %param.20) | copy-start | bytes 1540
  0.6 23.5 %copy-start.8 = (s32[8,16]{1,0:T(8,128)S(1)}, s32[8,16]{1,0:T(8,128)}, u32[]{:S(2)}) copy-start(s32[8,16]{1,0:T(8,128)} %tok_ref.1) | copy-start | bytes 1540
  0.7 20.0 %collective-permute-start = (bf16[256,1024]{1,0:T(8,128)(2,1)}, bf16[256,1024]{1,0:T(8,128)(2,1)S(1)}, u32[]{:S(2)}, u32[]{:S(2)}) collective-permute-start(bf16[256,1024]{1,0:T(8,128)(2,1)} %w0_ref.1), channel_id=1, source_target_pairs={{0,1},{1,2},{2,3},{3,0},{4,5},{5,6},{6,7},{7,4},{8,9},{9,10},{10,1... | collective-permute-start | bytes 1572872 | tf_op jit(solution)/shard_map/ppermute | solution.py:559
  2.3 18.4 %collective-permute-start.1 = (bf16[256,1024]{1,0:T(8,128)(2,1)}, bf16[256,1024]{1,0:T(8,128)(2,1)S(1)}, u32[]{:S(2)}, u32[]{:S(2)}) collective-permute-start(bf16[256,1024]{1,0:T(8,128)(2,1)} %w0_ref.1), channel_id=1, source_target_pairs={{1,0},{2,1},{3,2},{0,3},{5,4},{6,5},{7,6},{4,7},{9,8},{10,9},{11,1... | collective-permute-start | bytes 1572872 | tf_op jit(solution)/shard_map/ppermute | solution.py:559
  5.8 18.9 %collective-permute-start.2 = (bf16[272,1024]{1,0:T(8,128)(2,1)S(1)}, bf16[272,1024]{1,0:T(8,128)(2,1)S(1)}, u32[]{:S(2)}, u32[]{:S(2)}) collective-permute-start(bf16[272,1024]{1,0:T(8,128)(2,1)S(1)} %get-tuple-element.37), channel_id=1, source_target_pairs={{0,4},{4,8},{8,12},{12,16},{16,20},{20,24},{24,28},{28,32},{32,36}... | collective-permute-start | bytes 1671176 | tf_op jit(solution)/shard_map/ppermute | solution.py:531
  7.8 57.4 %copy-start = (bf16[512,1024]{1,0:T(8,128)(2,1)S(1)}, bf16[512,1024]{1,0:T(8,128)(2,1)}, u32[]{:S(2)}) copy-start(bf16[512,1024]{1,0:T(8,128)(2,1)} %x_ref.3) | copy-start | bytes 3145732
  7.8 57.4 %copy-start.3 = (bf16[1024,512]{1,0:T(8,128)(2,1)S(1)}, bf16[1024,512]{1,0:T(8,128)(2,1)}, u32[]{:S(2)}) copy-start(bf16[1024,512]{1,0:T(8,128)(2,1)} %w_bound_ref.1) | copy-start | bytes 3145732
  7.8 57.4 %copy-start.4 = (bf16[256,1024]{1,0:T(8,128)(2,1)S(1)}, bf16[256,1024]{1,0:T(8,128)(2,1)}, u32[]{:S(2)}) copy-start(bf16[256,1024]{1,0:T(8,128)(2,1)} %w0_ref.1) | copy-start | bytes 1572868
  7.8 16.9 %collective-permute-start.3 = (bf16[272,1024]{1,0:T(8,128)(2,1)S(1)}, bf16[272,1024]{1,0:T(8,128)(2,1)S(1)}, u32[]{:S(2)}, u32[]{:S(2)}) collective-permute-start(bf16[272,1024]{1,0:T(8,128)(2,1)S(1)} %get-tuple-element.38), channel_id=1, source_target_pairs={{4,0},{8,4},{12,8},{16,12},{20,16},{24,20},{28,24},{32,28},{36,32}... | collective-permute-start | bytes 1671176 | tf_op jit(solution)/shard_map/ppermute | solution.py:531
  14.3 0.7 copy-start.7
  20.7 17.2 %collective-permute-start.4 = (bf16[128,1024]{1,0:T(8,128)(2,1)S(1)}, bf16[128,1024]{1,0:T(8,128)(2,1)S(1)}, u32[]{:S(2)}, u32[]{:S(2)}) collective-permute-start(bf16[128,1024]{1,0:T(8,128)(2,1)S(1)} %slice.6), channel_id=1, source_target_pairs={{0,1},{1,2},{2,3},{3,0},{4,5},{5,6},{6,7},{7,4},{8,9},{9,10},{10,1... | collective-permute-start | bytes 786440 | tf_op jit(solution)/shard_map/ppermute | solution.py:565
  21.2 16.7 %collective-permute-start.5 = (bf16[128,1024]{1,0:T(8,128)(2,1)S(1)}, bf16[128,1024]{1,0:T(8,128)(2,1)S(1)}, u32[]{:S(2)}, u32[]{:S(2)}) collective-permute-start(bf16[128,1024]{1,0:T(8,128)(2,1)S(1)} %slice.7), channel_id=1, source_target_pairs={{1,0},{2,1},{3,2},{0,3},{5,4},{6,5},{7,6},{4,7},{9,8},{10,9},{11,1... | collective-permute-start | bytes 786440 | tf_op jit(solution)/shard_map/ppermute | solution.py:565
  37.9 27.3 %collective-permute-start.6 = (bf16[384,256]{1,0:T(8,128)(2,1)S(1)}, bf16[384,256]{1,0:T(8,128)(2,1)S(1)}, u32[]{:S(2)}, u32[]{:S(2)}) collective-permute-start(bf16[384,256]{1,0:T(8,128)(2,1)S(1)} %get-tuple-element.53), channel_id=1, source_target_pairs={{0,1},{1,2},{2,3},{3,0},{4,5},{5,6},{6,7},{7,4},{8,9},{9,10},{10,1... | collective-permute-start | bytes 589832 | tf_op jit(solution)/shard_map/ppermute | solution.py:571
  38.0 27.2 %collective-permute-start.7 = (bf16[384,256]{1,0:T(8,128)(2,1)S(1)}, bf16[384,256]{1,0:T(8,128)(2,1)S(1)}, u32[]{:S(2)}, u32[]{:S(2)}) collective-permute-start(bf16[384,256]{1,0:T(8,128)(2,1)S(1)} %get-tuple-element.54), channel_id=1, source_target_pairs={{0,2},{1,3},{2,0},{3,1},{4,6},{5,7},{6,4},{7,5},{8,10},{9,11},{10,... | collective-permute-start | bytes 589832 | tf_op jit(solution)/shard_map/ppermute | solution.py:571
  40.1 25.1 %collective-permute-start.8 = (bf16[384,256]{1,0:T(8,128)(2,1)S(1)}, bf16[384,256]{1,0:T(8,128)(2,1)S(1)}, u32[]{:S(2)}, u32[]{:S(2)}) collective-permute-start(bf16[384,256]{1,0:T(8,128)(2,1)S(1)} %get-tuple-element.55), channel_id=1, source_target_pairs={{0,3},{1,0},{2,1},{3,2},{4,7},{5,4},{6,5},{7,6},{8,11},{9,8},{10,9... | collective-permute-start | bytes 589832 | tf_op jit(solution)/shard_map/ppermute | solution.py:571
  65.2 34.4 %copy-start.5 = (bf16[8,16,512]{2,1,0:T(8,128)(2,1)S(1)}, bf16[8,16,512]{2,1,0:T(8,128)(2,1)}, u32[]{:S(2)}) copy-start(bf16[8,16,512]{2,1,0:T(8,128)(2,1)} %reg_ref.1) | copy-start | bytes 393220
  69.2 30.5 %all-to-all-start.2 = ((bf16[64,16,384]{2,1,0:T(8,128)(2,1)}), bf16[64,16,384]{2,1,0:T(8,128)(2,1)}, u32[]{:S(2)}, u32[]{:S(2)}) async-start(bf16[64,16,384]{2,1,0:T(8,128)(2,1)} %get-tuple-element.61), calls=%async_computation.2 | async-start | bytes 1572864 | tf_op jit(solution)/shard_map/all_to_all | solution.py:582
  78.4 1.0 copy-start.1
  99.7 1.2 %copy-start.2 = (bf16[512,1024]{1,0:T(8,128)(2,1)S(1)}, bf16[512,1024]{1,0:T(8,128)(2,1)}, u32[]{:S(2)}) copy-start(bf16[512,1024]{1,0:T(8,128)(2,1)} %copy-done.1) | copy-start | bytes 3145732
  102.8 12.6 %collective-permute-start.9 = (bf16[48,512]{1,0:T(8,128)(2,1)S(1)}, bf16[48,512]{1,0:T(8,128)(2,1)S(1)}, u32[]{:S(2)}, u32[]{:S(2)}) collective-permute-start(bf16[48,512]{1,0:T(8,128)(2,1)S(1)} %get-tuple-element.65), channel_id=1, source_target_pairs={{0,1},{1,2},{2,3},{3,4},{4,5},{5,6},{6,7},{7,8},{8,9},{9,10},{10,1... | collective-permute-start | bytes 147464 | tf_op jit(solution)/shard_map/ppermute | solution.py:531
  105.4 10.0 %collective-permute-start.10 = (bf16[48,512]{1,0:T(8,128)(2,1)S(1)}, bf16[48,512]{1,0:T(8,128)(2,1)S(1)}, u32[]{:S(2)}, u32[]{:S(2)}) collective-permute-start(bf16[48,512]{1,0:T(8,128)(2,1)S(1)} %get-tuple-element.66), channel_id=1, source_target_pairs={{1,0},{2,1},{3,2},{4,3},{5,4},{6,5},{7,6},{8,7},{9,8},{10,9},{11,1... | collective-permute-start | bytes 147464 | tf_op jit(solution)/shard_map/ppermute | solution.py:531

commit v4 on v3

--- a/solution.py
+++ b/solution.py
@@ -5,15 +5,12 @@
 from jax import lax
 from jax.experimental import pallas as pl
 from jax.experimental.pallas import tpu as pltpu
-from jax.sharding import Mesh
 from jax.sharding import PartitionSpec as P
 
 HD = 64
 SIGNS = (0.0, 1.0, -1.0)
-BANDS = ("sec", "x", "z", "core")
-CELLS = BANDS + ("tp",)
-ALONG = ("sec", "z")
-ACROSS = ("x", "core")
+BANDS = ("sec", "tile")
+CELLS = ("sec", "tile", "tp")
 LOG2E = 1.4426950408889634
 MIB = 1024 * 1024
 ON_CHIP = pl.BlockSpec(memory_space=pltpu.VMEM)
@@ -51,12 +48,17 @@
     return (level - 511.5) * (0.5 / 295.6)
 
 
-def edges_kernel(code_ref, x_ref, last_ref, first_ref, sems):
+def edges_kernel(code_ref, x_ref, *refs):
+    *refs, sems = refs
+    count = (len(refs) - 2) // 2
+    weights, (last_ref, first_ref, *held) = refs[:count], refs[count:]
     half = x_ref.shape[0] // 2
-    copies = [
-        pltpu.make_async_copy(x_ref.at[pl.ds(half, half)], last_ref.at[pl.ds(0, half)], sems.at[0]),
-        pltpu.make_async_copy(x_ref.at[pl.ds(0, half)], first_ref.at[pl.ds(0, half)], sems.at[1]),
+    pairs = [
+        (x_ref.at[pl.ds(half, half)], last_ref.at[pl.ds(0, half)]),
+        (x_ref.at[pl.ds(0, half)], first_ref.at[pl.ds(0, half)]),
+        *zip(weights, held),
     ]
+    copies = [pltpu.make_async_copy(a, b, sems.at[i]) for i, (a, b) in enumerate(pairs)]
     for copy in copies:
         copy.start()
     code = jnp.full((16, x_ref.shape[1]), code_ref[0], jnp.int32)
@@ -70,25 +72,25 @@
         copy.wait()
 
 
-def make_edges(code, x):
+def make_edges(code, x, weights):
     tokens, features = x.shape
-    shape = jax.ShapeDtypeStruct((tokens // 2 + 16, features), jnp.bfloat16)
+    shapes = [(tokens // 2 + 16, features)] * 2 + [w.shape for w in weights]
     return pl.pallas_call(
         edges_kernel,
-        out_shape=[shape, shape],
-        in_specs=[SCALARS, pl.BlockSpec(memory_space=pltpu.HBM)],
-        out_specs=[ON_CHIP] * 2,
-        scratch_shapes=[pltpu.SemaphoreType.DMA((2,))],
-        compiler_params=pltpu.CompilerParams(vmem_limit_bytes=4 * MIB),
+        out_shape=[jax.ShapeDtypeStruct(s, jnp.bfloat16) for s in shapes],
+        in_specs=[SCALARS] + [pl.BlockSpec(memory_space=pltpu.HBM)] * (1 + len(weights)),
+        out_specs=[ON_CHIP] * len(shapes),
+        scratch_shapes=[pltpu.SemaphoreType.DMA((2 + len(weights),))],
+        compiler_params=pltpu.CompilerParams(vmem_limit_bytes=2 * MIB),
         name="edges",
-    )(code, x)
+    )(code, x, *weights)
 
 
 def project_kernel(code_ref, *refs, halo):
     step = pl.program_id(0)
-    both_ref, inv_ref, held_ref, sems = refs[-4:]
+    both_ref, inv_ref = refs[-2:]
     if halo:
-        before_ref, after_ref, gain_ref, *refs = refs[:-4]
+        before_ref, after_ref, gain_ref, *refs = refs[:-2]
         rows = before_ref.shape[0] - 16
         first = (1 - step) * rows
         digits = jnp.where(
@@ -99,20 +101,11 @@
         code = jnp.sum(jnp.where(lane < 3, digits * place, 0.0), -1, keepdims=True)
         code = code.astype(jnp.int32)
     else:
-        x_ref, gain_ref, *refs = refs[:-4]
+        x_ref, gain_ref, *refs = refs[:-2]
         rows = x_ref.shape[0]
         first = step * rows
         code = jnp.full((1, 1), code_ref[0], jnp.int32)
     weights, outs = refs[: len(refs) // 2], refs[len(refs) // 2 :]
-    copies = [
-        pltpu.make_async_copy(w_ref, held_ref.at[i], sems.at[i]) for i, w_ref in enumerate(weights)
-    ]
-
-    @pl.when(step == 0)
-    def _():
-        for copy in copies:
-            copy.start()
-
     features = both_ref.shape[1]
     gain = gain_ref[...].astype(jnp.float32).reshape(1, features)
     chunk, block = 16, 128
@@ -131,17 +124,10 @@
                 state = x if sign == 0.0 else (x + p if sign > 0 else x - p)
                 mean = jnp.sum(state * state, -1, keepdims=True) * (1.0 / features)
                 inv_ref[s, r : r + chunk] = lax.rsqrt(mean + 1e-06)
-        if at == 0:
-
-            @pl.when(step == 0)
-            def _():
-                for copy in copies:
-                    copy.wait()
-
         here = slice(at, at + block)
-        for index, out_ref in enumerate(outs):
+        for index, (w_ref, out_ref) in enumerate(zip(weights, outs)):
             scale = HD**-0.5 * LOG2E if (index == 0 and not halo) else 1.0
-            made = dot(both_ref[2 * at : 2 * at + 2 * block], held_ref[index])
+            made = dot(both_ref[2 * at : 2 * at + 2 * block], w_ref[...])
             base, diff = made[:block], made[block:]
             for s, sign in enumerate(SIGNS):
                 full = base if sign == 0.0 else (base + diff if sign > 0 else base - diff)
@@ -165,13 +151,11 @@
         in_specs=[SCALARS]
         + specs
         + [pl.BlockSpec(gain.shape, lambda i: (0,))]
-        + [pl.BlockSpec(memory_space=pltpu.HBM) for w in weights],
+        + [ON_CHIP for w in weights],
         out_specs=[pl.BlockSpec((3, rows, cols), lambda i: (0, i, 0)) for _ in weights],
         scratch_shapes=[
             pltpu.VMEM((2 * rows, features), jnp.bfloat16),
             pltpu.VMEM((3, rows, 1), jnp.float32),
-            pltpu.VMEM((len(weights), features, cols), jnp.bfloat16),
-            pltpu.SemaphoreType.DMA((len(weights),)),
         ],
         compiler_params=pltpu.CompilerParams(vmem_limit_bytes=12 * MIB),
         name="project_halo" if halo else "project_own",
@@ -247,11 +231,8 @@
     return jnp.sum(jnp.where(mine, wide, 0.0), 0, keepdims=True)
 
 
-def place_of(band):
-    return (band // 32) * 4 + (band // 2) % 4, ((band // 8) % 4) * 2 + band % 2
-
-
-def ask_kernel(band_ref, tok_ref, ask_ref, *, bands):
+def ask_kernel(band_ref, tok_ref, ask_ref):
+    bands = ask_ref.shape[0]
     named = cells_row(band_ref[...])
     token = cells_row(tok_ref[...])
     cells = named.shape[1]
@@ -264,22 +245,13 @@
         hit = jnp.where(slot == s, match, 0.0)
         token_s = jnp.sum(hit * (token + 1.0), -1, keepdims=True) - 1.0
         asked = jnp.where(lanes == s, token_s, asked)
-    along, wide = ask_ref.shape
-    lane = iota((4, wide), 1)
-    four = (lane % 4 == iota((4, wide), 0)).astype(jnp.float32).astype(jnp.bfloat16)
-    spread = dot(asked[:, :4].astype(jnp.bfloat16), four)
-    _, xc = place_of(iota((bands, 1), 0))
-    spread = jnp.where(iota((bands, wide), 1) // 4 == xc, spread, 0.0)
-    z, _ = place_of(iota((1, bands), 1))
-    rows = (iota((along, bands), 0) == z).astype(jnp.float32).astype(jnp.bfloat16)
-    ask_ref[...] = dot(rows, spread.astype(jnp.bfloat16)).astype(jnp.int32)
+    ask_ref[...] = asked[:, :4].astype(jnp.int32)
 
 
 def ask(band, tok, bands):
-    along, across = lax.axis_size(ALONG), lax.axis_size(ACROSS)
-    return pl.pallas_call(
-        functools.partial(ask_kernel, bands=bands),
-        out_shape=jax.ShapeDtypeStruct((along, across * 4), jnp.int32),
+    return pl.pallas_call(
+        ask_kernel,
+        out_shape=jax.ShapeDtypeStruct((bands, 4), jnp.int32),
         in_specs=[ON_CHIP] * 2,
         out_specs=ON_CHIP,
         compiler_params=pltpu.CompilerParams(vmem_limit_bytes=4 * MIB),
@@ -287,7 +259,7 @@
     )(band, tok)
 
 
-def take_kernel(band_ref, conv_hbm_ref, take_ref, outer_ref, sems):
+def fetch_kernel(conv_hbm_ref, outer_ref, sems):
     copies = [
         pltpu.make_async_copy(
             conv_hbm_ref.at[pl.ds(6 * i, 3)], outer_ref.at[pl.ds(3 * i, 3)], sems.at[i]
@@ -296,71 +268,28 @@
     ]
     for copy in copies:
         copy.start()
-    band_row = cells_row(band_ref[...])
-    cells = band_row.shape[1]
-    rows = take_ref.shape[1]
-    r, c = iota((cells, cells), 0), iota((cells, cells), 1)
-    band_col = jnp.sum(jnp.where(r == c, band_row, 0.0), -1, keepdims=True)
-    earlier = (band_col == band_row) & (c < r)
-    slot = jnp.sum(jnp.where(earlier, 1.0, 0.0), -1, keepdims=True)
-    target = (band_col * 16.0 + slot * 4.0).astype(jnp.int32)
-    for part in range(4):
-        take_ref[part * cells : (part + 1) * cells, :] = (
-            (iota((cells, rows), 1) == target + part).astype(jnp.float32).astype(jnp.bfloat16)
-        )
     for copy in copies:
         copy.wait()
 
 
-def make_take(band, bands, conv_w):
-    return pl.pallas_call(
-        take_kernel,
-        out_shape=[
-            jax.ShapeDtypeStruct((4 * band.size, bands * 16), jnp.bfloat16),
-            jax.ShapeDtypeStruct((6, *conv_w.shape[1:]), conv_w.dtype),
-        ],
-        in_specs=[ON_CHIP, pl.BlockSpec(memory_space=pltpu.HBM)],
-        out_specs=[ON_CHIP] * 2,
+def fetch_outer(conv_w):
+    return pl.pallas_call(
+        fetch_kernel,
+        out_shape=jax.ShapeDtypeStruct((6, *conv_w.shape[1:]), conv_w.dtype),
+        in_specs=[pl.BlockSpec(memory_space=pltpu.HBM)],
+        out_specs=ON_CHIP,
         scratch_shapes=[pltpu.SemaphoreType.DMA((2,))],
-        compiler_params=pltpu.CompilerParams(vmem_limit_bytes=4 * MIB),
-        name="take",
-    )(band, conv_w)
-
-
-def turn_kernel(x_ref, out_ref):
-    count, wide = x_ref.shape
-    others, width = out_ref.shape
-    x = x_ref[...].astype(jnp.float32).astype(jnp.bfloat16)
-    lane = iota((wide, width), 1)
-    row = iota((wide, width), 0)
-    for other in range(others):
-        choose = (row == other * 4 + lane % 4).astype(jnp.float32).astype(jnp.bfloat16)
-        spread = dot(x, choose)
-        mine = iota((count, width), 1) // 4 == iota((count, width), 0)
-        out_ref[other : other + 1] = jnp.sum(
-            jnp.where(mine, spread, 0.0), 0, keepdims=True
-        ).astype(jnp.int32)
-
-
-def turn(x):
-    count, wide = x.shape
-    return pl.pallas_call(
-        turn_kernel,
-        out_shape=jax.ShapeDtypeStruct((wide // 4, 4 * count), jnp.int32),
-        in_specs=[ON_CHIP],
-        out_specs=ON_CHIP,
         compiler_params=pltpu.CompilerParams(vmem_limit_bytes=2 * MIB),
-        name="turn",
-    )(x)
+        name="fetch",
+    )(conv_w)
 
 
 def pick_rows(asked, rows, cells):
-    across, wide = asked.shape
+    bands = asked.shape[0]
+    spread = (iota((rows, bands), 0) // 16 == iota((rows, bands), 1)).astype(jnp.float32)
+    per_row = dot(spread.astype(jnp.bfloat16), asked.astype(jnp.float32).astype(jnp.bfloat16))
     r = iota((rows, 1), 0)
-    z, xc = place_of(r // 16)
-    spread = (iota((rows, across), 1) == xc).astype(jnp.float32).astype(jnp.bfloat16)
-    per_row = dot(spread, asked.astype(jnp.float32).astype(jnp.bfloat16))
-    mine = iota((rows, wide), 1) == z * 4 + (r // 4) % 4
+    mine = iota((rows, 4), 1) == (r // 4) % 4
     token_r = jnp.sum(jnp.where(mine, per_row, 0.0), -1, keepdims=True).astype(jnp.int32)
     target = jnp.where(token_r >= 0, (r % 4) * cells + token_r, -1)
     return (iota((rows, 4 * cells), 1) == target).astype(jnp.float32).astype(jnp.bfloat16)
@@ -399,8 +328,8 @@
     send_ref[...] = picked.reshape(send_ref.shape)
 
 
-def combine(code, att, w_outs, x, w_bound, asked, bands):
-    shapes = [(3, att[0].shape[0] // 3, x.shape[1]), (bands, 16, 384)]
+def combine(code, att, w_outs, x, w_bound, asked):
+    shapes = [(3, att[0].shape[0] // 3, x.shape[1]), (asked.shape[0], 16, 384)]
     operands = [*att, *w_outs, x, w_bound, asked]
     whole = lambda: (0, 0, 0)
     return pl.pallas_call(
@@ -413,23 +342,32 @@
     )(code, *operands)
 
 
-def inputs_kernel(arrived_ref, take_ref, reg_ref, out_ref, first_ref, last_ref):
+def inputs_kernel(arrived_ref, band_ref, reg_ref, out_ref, first_ref, last_ref):
     cols, rows, channels = reg_ref.shape
     cells = cols * rows
-    table = arrived_ref[...].reshape(take_ref.shape[1], 384)
-    taken = dot(take_ref[...], table)
+    slots = arrived_ref.shape[0] * arrived_ref.shape[1]
+    table = arrived_ref[...].reshape(slots, 384)
+    band_row = cells_row(band_ref[...])
+    r, c = iota((cells, cells), 0), iota((cells, cells), 1)
+    band_col = jnp.sum(jnp.where(r == c, band_row, 0.0), -1, keepdims=True)
+    earlier = (band_col == band_row) & (c < r)
+    slot = jnp.sum(jnp.where(earlier, 1.0, 0.0), -1, keepdims=True)
+    target = (band_col * 16.0 + slot * 4.0).astype(jnp.int32)
+    lane = iota((cells, slots), 1) - target
     for part in range(channels // 128):
+        take = jnp.where(lane == part, 1.0, 0.0).astype(jnp.bfloat16)
+        taken = dot(take, table)
         lanes = slice(part * 128, (part + 1) * 128)
         reg = reg_ref[:, :, lanes].astype(jnp.float32)
         for s in range(3):
-            forced = taken[part * cells : (part + 1) * cells, s * 128 : (s + 1) * 128]
+            forced = taken[:, s * 128 : (s + 1) * 128]
             made = (reg + forced.reshape(cols, rows, 128)).astype(jnp.bfloat16)
             out_ref[:, s * rows : (s + 1) * rows, lanes] = made
             first_ref[s * rows : (s + 1) * rows, lanes] = made[0]
             last_ref[s * rows : (s + 1) * rows, lanes] = made[cols - 1]
 
 
-def make_inputs(arrived, take, reg):
+def make_inputs(arrived, band, reg):
     cols, rows, channels = reg.shape
     shapes = [(cols, 3 * rows, channels), (3 * rows, channels), (3 * rows, channels)]
     return pl.pallas_call(
@@ -437,9 +375,9 @@
         out_shape=[jax.ShapeDtypeStruct(s, jnp.bfloat16) for s in shapes],
         in_specs=[ON_CHIP] * 3,
         out_specs=[ON_CHIP] * 3,
-        compiler_params=pltpu.CompilerParams(vmem_limit_bytes=5 * MIB),
+        compiler_params=pltpu.CompilerParams(vmem_limit_bytes=6 * MIB),
         name="inputs",
-    )(arrived, take, reg)
+    )(arrived, band, reg)
 
 
 def row_shifts(x, rows):
@@ -551,63 +489,65 @@
     half = tokens // 2
     gain = norm_gain
     cell_band = src_band.reshape(src_tok.shape)
-    w_query, w_key, w_value = (in_hbm(w) for w in (w_query, w_key, w_value))
 
     up = [(i, (i + 1) % ranks) for i in range(ranks)]
     down = [(j, i) for i, j in up]
-    before, after = neighbours(*make_edges(band_codes, in_hbm(global_state)), BANDS)
+    last, first, *weights = make_edges(
+        band_codes, in_hbm(global_state), [in_hbm(w) for w in (w_query, w_key, w_value)]
+    )
+    before, after = neighbours(last, first, BANDS)
+    q, k, v = project(band_codes, [in_hbm(global_state)], gain, weights, False)
+    q, w_out = lax.optimization_barrier((q, w_out))
     w1, w3 = lax.ppermute(w_out, "tp", up), lax.ppermute(w_out, "tp", down)
     asked = ask(cell_band, src_tok, bands)
-
-    q, k, v = project(band_codes, [in_hbm(global_state)], gain, [w_query, w_key, w_value], False)
-    q, w1, w3 = lax.optimization_barrier((q, w1, w3))
+    q, before, after = lax.optimization_barrier((q, before, after))
+    k_halo, v_halo = project(band_codes, [before, after], gain, weights[1:], True)
+    k_halo, w1, w3 = lax.optimization_barrier((k_halo, w1, w3))
     middle = w_out.shape[0] // 2
     top, low = lax.ppermute(w1[:middle], "tp", up), lax.ppermute(w3[middle:], "tp", down)
-    q, before, after = lax.optimization_barrier((q, before, after))
-    k_halo, v_halo = project(band_codes, [before, after], gain, [w_key, w_value], True)
     attended = attend(q, k, v, k_halo, v_halo, ranks, bands)
     attended, asked, top, low = lax.optimization_barrier((attended, asked, top, low))
     attended = [attended[0]] + [
         lax.ppermute(attended[d], "tp", [(i, (i + d) % ranks) for i in range(ranks)])
         for d in range(1, ranks)
     ]
-    asked = lax.all_to_all(asked[:, None, :], ALONG, 0, 0, tiled=True)[:, 0, :]
-    asked = lax.all_to_all(turn(asked)[:, None, :], ACROSS, 0, 0, tiled=True)[:, 0, :]
+    asked = lax.all_to_all(asked[:, None, :], BANDS, 0, 0, tiled=True)[:, 0, :]
     global_out, send = combine(
-        band_codes, attended, [w_out, w1, w3, top, low], global_state, w_bound, asked, bands
+        band_codes, attended, [w_out, w1, w3, top, low], global_state, w_bound, asked
     )
-    cell_band, send = lax.optimization_barrier((cell_band, send))
+    conv_w, send = lax.optimization_barrier((conv_w, send))
     conv_w = in_hbm(conv_w)
-    take, outer = make_take(cell_band, bands, conv_w)
+    outer = fetch_outer(conv_w)
     arrived = lax.all_to_all(send, BANDS, 0, 0, tiled=True)
-    inputs, first, last = make_inputs(arrived, take, reg_state)
+    outer, arrived = lax.optimization_barrier((outer, arrived))
+    inputs, first, last = make_inputs(arrived, cell_band, reg_state)
     before, after = neighbours(last, first, CELLS)
     total = convolve_inner(inputs, outer, conv_w)
     return global_out, convolve_finish(inputs, before, after, outer, total)
 
 
 def solution(mesh):
-    parts = Mesh(
-        mesh.devices.reshape(mesh.shape["sec"], 4, 4, 2, mesh.shape["tp"]), CELLS
-    )
     placed = (
-        P(BANDS, None),
-        P(BANDS),
+        P(("sec", "tile"), None),
+        P(("sec", "tile")),
         P(),
         P(None, "tp"),
         P(None, "tp"),
         P(None, "tp"),
         P("tp", None),
-        P(CELLS, None, None),
-        P(CELLS, None, None),
-        P(CELLS, None),
+        P(("sec", "tile", "tp"), None, None),
+        P(("sec", "tile", "tp"), None, None),
+        P(("sec", "tile", "tp"), None),
         P(),
         P(),
     )
     return jax.shard_map(
         per_device,
-        mesh=parts,
+        mesh=mesh,
         in_specs=placed,
-        out_specs=(P(None, CELLS, None), P(None, CELLS, None, None)),
+        out_specs=(
+            P(None, ("sec", "tile", "tp"), None),
+            P(None, ("sec", "tile", "tp"), None, None),
+        ),
         check_vma=False,
     )

time: 118 us -> 117 us (level)
  waiting for transfers between devices: 20.3 us -> 27.8 us
  blocking collectives: 23.6 us -> 18.8 us
  local copies, waits for them, and re-layouts: 2.98 us -> 0.74 us
  Pallas kernels: 32.3 us -> 30.3 us
    ppermute x2, waiting for transfers between devices: 0.01 us -> 6.54 us  [per_device(): w1, w3 = (lax.ppermute(w_out, 'tp', up), lax.ppermute(w_out, 'tp', down))]
    all_to_all x2 -> x1, blocking collectives: 23.6 us -> 18.8 us  [per_device(): asked = lax.all_to_all(asked[:, None, :], BANDS, 0, 0, tiled=True)[:, 0, :]]
    unnamed x18 -> x14, local copies, waits for them, and re-layouts: 2.94 us -> 0.7 us
    pallas_call x2, Pallas kernels: 9.72 us -> 7.61 us  [project(): pl.pallas_call(functools.partial(project_kernel, halo=halo), out_shape=[j...]
    ppermute x1, starting transfers between devices: 0.44 us -> 1.65 us  [per_device(): lax.ppermute(w1[:middle], 'tp', up)]
    ppermute x1, starting transfers between devices: 2.95 us -> 1.74 us  [per_device(): lax.ppermute(w3[middle:], 'tp', down)]
    pallas_call x4 -> x3, Pallas kernels: 3.85 us -> 3.98 us  [the longest x1 1.9 us: fetch_outer(): pl.pallas_call(fetch_kernel, out_shape=jax.ShapeDtypeStruct((6, *conv_w.s...]
  transfers between devices with their start and end apart: 12 -> 12, of which waited for: 1 -> 2; matrix products, arithmetic and copies ran while one was open for 0% -> 0% of each run, Pallas kernels for 21% -> 18%
where the time goes in v4:
time: 117 us; the launch traced here: 116 us
  starting transfers between devices  37.2 us (32%)
  Pallas kernels  30.3 us (26%)
  waiting for transfers between devices  27.8 us (24%)
  blocking collectives  18.8 us (16%)
  between operations  1.54 us (1%)
    all_to_all x1, waiting for transfers between devices, per_device(): arrived = lax.all_to_all(send, BANDS, 0, 0, tiled=True)  21.3 us
    all_to_all x1, blocking collectives, per_device(): asked = lax.all_to_all(asked[:, None, :], BANDS, 0, 0, tiled=True)[:, 0, :]  18.8 us
    ppermute x4, starting transfers between devices, neighbours(): return (lax.ppermute(last, axis, up), lax.ppermute(first, axis, down))  18.6 us
    pallas_call x1, Pallas kernels, attend(): pl.pallas_call(functools.partial(attend_kernel, bands=bands), out_shape=[...  9.01 us
    pallas_call x2, Pallas kernels, project(): pl.pallas_call(functools.partial(project_kernel, halo=halo), out_shape=[j...  7.61 us
    all_to_all x1, starting transfers between devices, per_device(): arrived = lax.all_to_all(send, BANDS, 0, 0, tiled=True)  7.5 us
    ppermute x2, waiting for transfers between devices, per_device(): w1, w3 = (lax.ppermute(w_out, 'tp', up), lax.ppermute(w_out, 'tp', down))  6.54 us
    ppermute x3, starting transfers between devices, per_device(): lax.ppermute(attended[d], 'tp', [(i, (i + d) % ranks) for i in range(rank...  4.4 us
  transfers between devices with their start and end apart: 12, of which 2 were waited for; matrix products, arithmetic and copies ran while one was open for 0% of the time, Pallas kernels for 18%

profile of v4, /device:TPU:4, one launch (start us, length us, event | category | flops | bytes accessed | tf_op | source)
XLA Modules:
  0.0 116.3 jit_solution(8322102846377027615)
XLA Ops:
  1.4 1.7 %edges.1 = (bf16[272,1024]{1,0:T(8,128)(2,1)S(1)}, bf16[272,1024]{1,0:T(8,128)(2,1)S(1)}, bf16[1024,256]{1,0:T(8,128)(2,1)S(1)}, bf16[1024,256]{1,0:T(8,128)(2,1)S(1)}, bf16[1024,256]{1,0:T(8,128)(2,1)S(1)}) custom-call(s32[1]{0:T(128)S(6)} %copy.15.code_ref, bf16[512,1024]{1,0:T(8,128)(2,1)} %x_ref.3, bf16[1024,256]{1,0:T(8,128)(2,1)} %refs_0_.2, ...), custom_call_target="tpu_custom_call" | custom-call | tf_op jit(solution)/shard_map/edges/pallas_call | solution.py:78
  3.1 1.9 %collective-permute-start = (bf16[272,1024]{1,0:T(8,128)(2,1)S(1)}, bf16[272,1024]{1,0:T(8,128)(2,1)S(1)}, u32[]{:S(2)}, u32[]{:S(2)}) collective-permute-start(bf16[272,1024]{1,0:T(8,128)(2,1)S(1)} %get-tuple-element.45), channel_id=1, source_target_pairs={{0,4},{4,8},{8,12},{12,16},{16,20},{20,24},{24,28},{28,32},{32,36}... | collective-permute-start | bytes 1671176 | tf_op jit(solution)/shard_map/ppermute | solution.py:469
  5.0 6.3 %collective-permute-start.1 = (bf16[272,1024]{1,0:T(8,128)(2,1)S(1)}, bf16[272,1024]{1,0:T(8,128)(2,1)S(1)}, u32[]{:S(2)}, u32[]{:S(2)}) collective-permute-start(bf16[272,1024]{1,0:T(8,128)(2,1)S(1)} %get-tuple-element.46), channel_id=1, source_target_pairs={{4,0},{8,4},{12,8},{16,12},{20,16},{24,20},{28,24},{32,28},{36,32}... | collective-permute-start | bytes 1671176 | tf_op jit(solution)/shard_map/ppermute | solution.py:469
  11.4 0.0 copy-start.5
  11.4 0.7 copy-done.5
  12.1 4.7 %project_own.1 = (bf16[3,512,256]{2,1,0:T(8,128)(2,1)S(1)}, bf16[3,512,256]{2,1,0:T(8,128)(2,1)S(1)}, bf16[3,512,256]{2,1,0:T(8,128)(2,1)S(1)}) custom-call(s32[1]{0:T(128)S(6)} %copy.15.code_ref, bf16[512,1024]{1,0:T(8,128)(2,1)} %x_ref.3, bf16[1024]{0:T(1024)(128)(2,1)S(1)} %copy-done.5, bf16[1024,256]{1,0:T(8,128)(2,1)S(1)} %get-tuple-element.40.refs_2_, ...), custom_call_target="tpu_custom_call" | custom-call | tf_op jit(solution)/shard_map/project_own/pallas_call | solution.py:147
  16.7 1.7 %collective-permute-start.2 = (bf16[256,1024]{1,0:T(8,128)(2,1)S(1)}, bf16[256,1024]{1,0:T(8,128)(2,1)S(1)}, u32[]{:S(2)}, u32[]{:S(2)}) collective-permute-start(bf16[256,1024]{1,0:T(8,128)(2,1)S(1)} %copy-done.2), channel_id=1, source_target_pairs={{0,1},{1,2},{2,3},{3,0},{4,5},{5,6},{6,7},{7,4},{8,9},{9,10},{10,1... | collective-permute-start | bytes 1572872 | tf_op jit(solution)/shard_map/ppermute | solution.py:501
  18.4 1.7 %collective-permute-start.3 = (bf16[256,1024]{1,0:T(8,128)(2,1)S(1)}, bf16[256,1024]{1,0:T(8,128)(2,1)S(1)}, u32[]{:S(2)}, u32[]{:S(2)}) collective-permute-start(bf16[256,1024]{1,0:T(8,128)(2,1)S(1)} %copy-done.2), channel_id=1, source_target_pairs={{1,0},{2,1},{3,2},{0,3},{5,4},{6,5},{7,6},{4,7},{9,8},{10,9},{11,1... | collective-permute-start | bytes 1572872 | tf_op jit(solution)/shard_map/ppermute | solution.py:501
  20.1 0.0 collective-permute-done.refs_0_
  20.1 0.0 collective-permute-done.1.refs_1_
  20.1 2.9 %project_halo.1 = (bf16[3,512,256]{2,1,0:T(8,128)(2,1)S(1)}, bf16[3,512,256]{2,1,0:T(8,128)(2,1)S(1)}) custom-call(s32[1]{0:T(128)S(6)} %copy.15.code_ref, bf16[272,1024]{1,0:T(8,128)(2,1)S(1)} %collective-permute-done.refs_0_, bf16[272,1024]{1,0:T(8,128)(2,1)S(1)} %collective-permute-done.1.refs_1_, bf16[1024]{0:T(1024)(128)(2,1)S(1)} %copy-done.5, ...), custom_call_target="tpu_custom_call" | custom-call | tf_op jit(solution)/shard_map/project_halo/pallas_call | solution.py:147
  23.0 6.5 %collective-permute-done.2.w1_ref = bf16[256,1024]{1,0:T(8,128)(2,1)S(1)} collective-permute-done((bf16[256,1024]{1,0:T(8,128)(2,1)S(1)}, bf16[256,1024]{1,0:T(8,128)(2,1)S(1)}, u32[]{:S(2)}, u32[]{:S(2)}) %collective-permute-start.2) | collective-permute-done | bytes 524320 | tf_op jit(solution)/shard_map/ppermute | solution.py:501
  29.5 0.0 collective-permute-done.3.w3_ref
  29.6 1.7 %collective-permute-start.4 = (bf16[128,1024]{1,0:T(8,128)(2,1)S(1)}, bf16[128,1024]{1,0:T(8,128)(2,1)S(1)}, u32[]{:S(2)}, u32[]{:S(2)}) collective-permute-start(bf16[128,1024]{1,0:T(8,128)(2,1)S(1)} %slice.6), channel_id=1, source_target_pairs={{0,1},{1,2},{2,3},{3,0},{4,5},{5,6},{6,7},{7,4},{8,9},{9,10},{10,1... | collective-permute-start | bytes 786440 | tf_op jit(solution)/shard_map/ppermute | solution.py:507
  31.3 1.7 %collective-permute-start.5 = (bf16[128,1024]{1,0:T(8,128)(2,1)S(1)}, bf16[128,1024]{1,0:T(8,128)(2,1)S(1)}, u32[]{:S(2)}, u32[]{:S(2)}) collective-permute-start(bf16[128,1024]{1,0:T(8,128)(2,1)S(1)} %slice.7), channel_id=1, source_target_pairs={{1,0},{2,1},{3,2},{0,3},{5,4},{6,5},{7,6},{4,7},{9,8},{10,9},{11,1... | collective-permute-start | bytes 786440 | tf_op jit(solution)/shard_map/ppermute | solution.py:507
  33.0 0.4 ask.1
  33.4 9.0 %attend.1 = (bf16[384,256]{1,0:T(8,128)(2,1)S(1)}, bf16[384,256]{1,0:T(8,128)(2,1)S(1)}, bf16[384,256]{1,0:T(8,128)(2,1)S(1)}, bf16[384,256]{1,0:T(8,128)(2,1)S(1)}) custom-call(bf16[3,512,256]{2,1,0:T(8,128)(2,1)S(1)} %get-tuple-element.47.q_ref, bf16[3,512,256]{2,1,0:T(8,128)(2,1)S(1)} %get-tuple-element.48.k_ref, ...), custom_call_target="tpu_custom_call" | custom-call | tf_op jit(solution)/shard_map/attend/pallas_call | solution.py:213
  42.4 0.0 collective-permute-done.4.top_ref
  42.4 0.0 collective-permute-done.5.low_ref
  42.4 0.4 collective-permute-start.6
  42.8 2.9 %collective-permute-start.7 = (bf16[384,256]{1,0:T(8,128)(2,1)S(1)}, bf16[384,256]{1,0:T(8,128)(2,1)S(1)}, u32[]{:S(2)}, u32[]{:S(2)}) collective-permute-start(bf16[384,256]{1,0:T(8,128)(2,1)S(1)} %get-tuple-element.64), channel_id=1, source_target_pairs={{0,2},{1,3},{2,0},{3,1},{4,6},{5,7},{6,4},{7,5},{8,10},{9,11},{10,... | collective-permute-start | bytes 589832 | tf_op jit(solution)/shard_map/ppermute | solution.py:511
  45.8 1.0 collective-permute-start.8
  46.8 18.8 %all_to_all.10 = s32[64,1,4]{2,1,0:T(1,128)S(1)} all-to-all(s32[64,1,4]{2,1,0:T(1,128)S(1)} %bitcast.5), channel_id=1, replica_groups=mesh['sec'=2,'tile'=32,'tp'=4] {'sec','tile'}, dimensions={0} | all-to-all | bytes 2048 | tf_op jit(solution)/shard_map/all_to_all | solution.py:514
  65.6 3.8 %combine.1 = (bf16[3,128,1024]{2,1,0:T(8,128)(2,1)}, bf16[64,16,384]{2,1,0:T(8,128)(2,1)}) custom-call(s32[1]{0:T(128)S(6)} %copy.15.code_ref, bf16[384,256]{1,0:T(8,128)(2,1)S(1)} %get-tuple-element.62.att0_ref, bf16[384,256]{1,0:T(8,128)(2,1)S(1)} %collective-permute-done.6.att1_ref, bf16[384,256]{1,0:T(8,128)(2,1)S(1)} %collective-permute-done.7.att2_ref, ...), custom_call_target="tpu_custom_call" | custom-call | tf_op jit(solution)/shard_map/combine/pallas_call | solution.py:335
  69.4 7.5 %all-to-all-start.1 = ((bf16[64,16,384]{2,1,0:T(8,128)(2,1)}), bf16[64,16,384]{2,1,0:T(8,128)(2,1)}, u32[]{:S(2)}, u32[]{:S(2)}) async-start(bf16[64,16,384]{2,1,0:T(8,128)(2,1)} %get-tuple-element.72), calls=%async_computation.1 | async-start | bytes 1572864 | tf_op jit(solution)/shard_map/all_to_all | solution.py:521
  76.9 1.9 %fetch.1.outer_ref = bf16[6,512,512]{2,1,0:T(8,128)(2,1)S(1)} custom-call(bf16[9,512,512]{2,1,0:T(8,128)(2,1)} %conv_hbm_ref.1), custom_call_target="tpu_custom_call" | custom-call | tf_op jit(solution)/shard_map/fetch/pallas_call | solution.py:276
  78.8 21.3 %all-to-all-done.1.arrived_ref = bf16[64,16,384]{2,1,0:T(8,128)(2,1)} async-done(((bf16[64,16,384]{2,1,0:T(8,128)(2,1)}), bf16[64,16,384]{2,1,0:T(8,128)(2,1)}, u32[]{:S(2)}, u32[]{:S(2)}) %all-to-all-start.1) | async-done | bytes 786464 | tf_op jit(solution)/shard_map/all_to_all | solution.py:521
  100.0 2.1 %inputs.1 = (bf16[8,48,512]{2,1,0:T(8,128)(2,1)S(1)}, bf16[48,512]{1,0:T(8,128)(2,1)S(1)}, bf16[48,512]{1,0:T(8,128)(2,1)S(1)}) custom-call(bf16[64,16,384]{2,1,0:T(8,128)(2,1)} %all-to-all-done.1.arrived_ref, s32[8,16]{1,0:T(8,128)S(1)} %bitcast.8, bf16[8,16,512]{2,1,0:T(8,128)(2,1)S(1)} %copy-done.3), custom_call_target="tpu_custom_call" | custom-call | tf_op jit(solution)/shard_map/inputs/pallas_call | solution.py:373
  102.2 2.9 %collective-permute-start.9 = (bf16[48,512]{1,0:T(8,128)(2,1)S(1)}, bf16[48,512]{1,0:T(8,128)(2,1)S(1)}, u32[]{:S(2)}, u32[]{:S(2)}) collective-permute-start(bf16[48,512]{1,0:T(8,128)(2,1)S(1)} %get-tuple-element.75), channel_id=1, source_target_pairs={{0,1},{1,2},{2,3},{3,4},{4,5},{5,6},{6,7},{7,8},{8,9},{9,10},{10,1... | collective-permute-start | bytes 147464 | tf_op jit(solution)/shard_map/ppermute | solution.py:469
  105.1 7.5 %collective-permute-start.10 = (bf16[48,512]{1,0:T(8,128)(2,1)S(1)}, bf16[48,512]{1,0:T(8,128)(2,1)S(1)}, u32[]{:S(2)}, u32[]{:S(2)}) collective-permute-start(bf16[48,512]{1,0:T(8,128)(2,1)S(1)} %get-tuple-element.76), channel_id=1, source_target_pairs={{1,0},{2,1},{3,2},{4,3},{5,4},{6,5},{7,6},{8,7},{9,8},{10,9},{11,1... | collective-permute-start | bytes 147464 | tf_op jit(solution)/shard_map/ppermute | solution.py:469
  112.5 2.2 %convolve_inner.1.sum_ref = f32[384,512]{1,0:T(8,128)S(1)} custom-call(bf16[8,48,512]{2,1,0:T(8,128)(2,1)S(1)} %get-tuple-element.74.x_ref, bf16[6,512,512]{2,1,0:T(8,128)(2,1)S(1)} %fetch.1.outer_ref, bf16[9,512,512]{2,1,0:T(8,128)(2,1)} %conv_hbm_ref.1), custom_call_target="tpu_custom_call" | custom-call | tf_op jit(solution)/shard_map/convolve_inner/pallas_call | solution.py:416
  114.8 1.6 %convolve_finish.1 = bf16[3,8,16,512]{3,2,1,0:T(8,128)(2,1)} custom-call(bf16[8,48,512]{2,1,0:T(8,128)(2,1)S(1)} %get-tuple-element.74.x_ref, bf16[48,512]{1,0:T(8,128)(2,1)S(1)} %collective-permute-done.9.before_ref, bf16[48,512]{1,0:T(8,128)(2,1)S(1)} %collective-permute-done.10.after_ref, bf16[6,512,512]{2,1,0:T(8,128)(2,1)S(1)} %fetch.1.outer_ref, ...), custom_call_target="tpu_custom_call" | custom-call | tf_op jit(solution)/shard_map/convolve_finish/pallas_call | solution.py:455
  (19 shorter events, 0.1 us)
Async XLA Ops:
  0.6 16.1 %copy-start.2 = (bf16[256,1024]{1,0:T(8,128)(2,1)S(1)}, bf16[256,1024]{1,0:T(8,128)(2,1)}, u32[]{:S(2)}) copy-start(bf16[256,1024]{1,0:T(8,128)(2,1)} %w0_ref) | copy-start | bytes 1572868
  0.6 32.3 %copy-start.4 = (s32[8,16,1]{1,2,0:T(1,128)S(1)}, s32[8,16,1]{1,2,0:T(1,128)}, u32[]{:S(2)}) copy-start(s32[8,16,1]{1,2,0:T(1,128)} %param.20) | copy-start | bytes 1540
  0.7 32.3 %copy-start.6 = (s32[8,16]{1,0:T(8,128)S(1)}, s32[8,16]{1,0:T(8,128)}, u32[]{:S(2)}) copy-start(s32[8,16]{1,0:T(8,128)} %tok_ref.1) | copy-start | bytes 1540
  3.1 17.0 %collective-permute-start = (bf16[272,1024]{1,0:T(8,128)(2,1)S(1)}, bf16[272,1024]{1,0:T(8,128)(2,1)S(1)}, u32[]{:S(2)}, u32[]{:S(2)}) collective-permute-start(bf16[272,1024]{1,0:T(8,128)(2,1)S(1)} %get-tuple-element.45), channel_id=1, source_target_pairs={{0,4},{4,8},{8,12},{12,16},{16,20},{20,24},{24,28},{28,32},{32,36}... | collective-permute-start | bytes 1671176 | tf_op jit(solution)/shard_map/ppermute | solution.py:469
  5.0 15.0 %collective-permute-start.1 = (bf16[272,1024]{1,0:T(8,128)(2,1)S(1)}, bf16[272,1024]{1,0:T(8,128)(2,1)S(1)}, u32[]{:S(2)}, u32[]{:S(2)}) collective-permute-start(bf16[272,1024]{1,0:T(8,128)(2,1)S(1)} %get-tuple-element.46), channel_id=1, source_target_pairs={{4,0},{8,4},{12,8},{16,12},{20,16},{24,20},{28,24},{32,28},{36,32}... | collective-permute-start | bytes 1671176 | tf_op jit(solution)/shard_map/ppermute | solution.py:469
  11.4 0.7 copy-start.5
  12.1 53.5 %copy-start = (bf16[512,1024]{1,0:T(8,128)(2,1)S(1)}, bf16[512,1024]{1,0:T(8,128)(2,1)}, u32[]{:S(2)}) copy-start(bf16[512,1024]{1,0:T(8,128)(2,1)} %x_ref.3) | copy-start | bytes 3145732
  12.1 53.5 %copy-start.1 = (bf16[1024,512]{1,0:T(8,128)(2,1)S(1)}, bf16[1024,512]{1,0:T(8,128)(2,1)}, u32[]{:S(2)}) copy-start(bf16[1024,512]{1,0:T(8,128)(2,1)} %w_bound_ref.1) | copy-start | bytes 3145732
  16.7 12.8 %collective-permute-start.2 = (bf16[256,1024]{1,0:T(8,128)(2,1)S(1)}, bf16[256,1024]{1,0:T(8,128)(2,1)S(1)}, u32[]{:S(2)}, u32[]{:S(2)}) collective-permute-start(bf16[256,1024]{1,0:T(8,128)(2,1)S(1)} %copy-done.2), channel_id=1, source_target_pairs={{0,1},{1,2},{2,3},{3,0},{4,5},{5,6},{6,7},{7,4},{8,9},{9,10},{10,1... | collective-permute-start | bytes 1572872 | tf_op jit(solution)/shard_map/ppermute | solution.py:501
  18.4 11.2 %collective-permute-start.3 = (bf16[256,1024]{1,0:T(8,128)(2,1)S(1)}, bf16[256,1024]{1,0:T(8,128)(2,1)S(1)}, u32[]{:S(2)}, u32[]{:S(2)}) collective-permute-start(bf16[256,1024]{1,0:T(8,128)(2,1)S(1)} %copy-done.2), channel_id=1, source_target_pairs={{1,0},{2,1},{3,2},{0,3},{5,4},{6,5},{7,6},{4,7},{9,8},{10,9},{11,1... | collective-permute-start | bytes 1572872 | tf_op jit(solution)/shard_map/ppermute | solution.py:501
  29.6 12.8 %collective-permute-start.4 = (bf16[128,1024]{1,0:T(8,128)(2,1)S(1)}, bf16[128,1024]{1,0:T(8,128)(2,1)S(1)}, u32[]{:S(2)}, u32[]{:S(2)}) collective-permute-start(bf16[128,1024]{1,0:T(8,128)(2,1)S(1)} %slice.6), channel_id=1, source_target_pairs={{0,1},{1,2},{2,3},{3,0},{4,5},{5,6},{6,7},{7,4},{8,9},{9,10},{10,1... | collective-permute-start | bytes 786440 | tf_op jit(solution)/shard_map/ppermute | solution.py:507
  31.3 11.1 %collective-permute-start.5 = (bf16[128,1024]{1,0:T(8,128)(2,1)S(1)}, bf16[128,1024]{1,0:T(8,128)(2,1)S(1)}, u32[]{:S(2)}, u32[]{:S(2)}) collective-permute-start(bf16[128,1024]{1,0:T(8,128)(2,1)S(1)} %slice.7), channel_id=1, source_target_pairs={{1,0},{2,1},{3,2},{0,3},{5,4},{6,5},{7,6},{4,7},{9,8},{10,9},{11,1... | collective-permute-start | bytes 786440 | tf_op jit(solution)/shard_map/ppermute | solution.py:507
  42.4 23.2 %collective-permute-start.6 = (bf16[384,256]{1,0:T(8,128)(2,1)S(1)}, bf16[384,256]{1,0:T(8,128)(2,1)S(1)}, u32[]{:S(2)}, u32[]{:S(2)}) collective-permute-start(bf16[384,256]{1,0:T(8,128)(2,1)S(1)} %get-tuple-element.63), channel_id=1, source_target_pairs={{0,1},{1,2},{2,3},{3,0},{4,5},{5,6},{6,7},{7,4},{8,9},{9,10},{10,1... | collective-permute-start | bytes 589832 | tf_op jit(solution)/shard_map/ppermute | solution.py:511
  42.8 22.7 %collective-permute-start.7 = (bf16[384,256]{1,0:T(8,128)(2,1)S(1)}, bf16[384,256]{1,0:T(8,128)(2,1)S(1)}, u32[]{:S(2)}, u32[]{:S(2)}) collective-permute-start(bf16[384,256]{1,0:T(8,128)(2,1)S(1)} %get-tuple-element.64), channel_id=1, source_target_pairs={{0,2},{1,3},{2,0},{3,1},{4,6},{5,7},{6,4},{7,5},{8,10},{9,11},{10,... | collective-permute-start | bytes 589832 | tf_op jit(solution)/shard_map/ppermute | solution.py:511
  45.8 19.8 %collective-permute-start.8 = (bf16[384,256]{1,0:T(8,128)(2,1)S(1)}, bf16[384,256]{1,0:T(8,128)(2,1)S(1)}, u32[]{:S(2)}, u32[]{:S(2)}) collective-permute-start(bf16[384,256]{1,0:T(8,128)(2,1)S(1)} %get-tuple-element.65), channel_id=1, source_target_pairs={{0,3},{1,0},{2,1},{3,2},{4,7},{5,4},{6,5},{7,6},{8,11},{9,8},{10,9... | collective-permute-start | bytes 589832 | tf_op jit(solution)/shard_map/ppermute | solution.py:511
  69.3 30.7 %copy-start.3 = (bf16[8,16,512]{2,1,0:T(8,128)(2,1)S(1)}, bf16[8,16,512]{2,1,0:T(8,128)(2,1)}, u32[]{:S(2)}) copy-start(bf16[8,16,512]{2,1,0:T(8,128)(2,1)} %reg_ref.1) | copy-start | bytes 393220
  69.4 30.7 %all-to-all-start.1 = ((bf16[64,16,384]{2,1,0:T(8,128)(2,1)}), bf16[64,16,384]{2,1,0:T(8,128)(2,1)}, u32[]{:S(2)}, u32[]{:S(2)}) async-start(bf16[64,16,384]{2,1,0:T(8,128)(2,1)} %get-tuple-element.72), calls=%async_computation.1 | async-start | bytes 1572864 | tf_op jit(solution)/shard_map/all_to_all | solution.py:521
  102.2 12.6 %collective-permute-start.9 = (bf16[48,512]{1,0:T(8,128)(2,1)S(1)}, bf16[48,512]{1,0:T(8,128)(2,1)S(1)}, u32[]{:S(2)}, u32[]{:S(2)}) collective-permute-start(bf16[48,512]{1,0:T(8,128)(2,1)S(1)} %get-tuple-element.75), channel_id=1, source_target_pairs={{0,1},{1,2},{2,3},{3,4},{4,5},{5,6},{6,7},{7,8},{8,9},{9,10},{10,1... | collective-permute-start | bytes 147464 | tf_op jit(solution)/shard_map/ppermute | solution.py:469
  105.1 9.7 %collective-permute-start.10 = (bf16[48,512]{1,0:T(8,128)(2,1)S(1)}, bf16[48,512]{1,0:T(8,128)(2,1)S(1)}, u32[]{:S(2)}, u32[]{:S(2)}) collective-permute-start(bf16[48,512]{1,0:T(8,128)(2,1)S(1)} %get-tuple-element.76), channel_id=1, source_target_pairs={{1,0},{2,1},{3,2},{4,3},{5,4},{6,5},{7,6},{8,7},{9,8},{10,9},{11,1... | collective-permute-start | bytes 147464 | tf_op jit(solution)/shard_map/ppermute | solution.py:469

commit v5 on v4

--- a/solution.py
+++ b/solution.py
@@ -295,19 +295,22 @@
     return (iota((rows, 4 * cells), 1) == target).astype(jnp.float32).astype(jnp.bfloat16)
 
 
-def combine_kernel(code_ref, att0_ref, att1_ref, att2_ref, att3_ref, w0_ref, w1_ref, w3_ref, top_ref, low_ref, x_ref, w_bound_ref, asked_ref, out_ref, send_ref):
+def combine_kernel(code_ref, att0_ref, att1_ref, att2_ref, att3_ref, w0_ref, w1_ref, w3_ref, top_ref, low_ref, x_ref, w_bound_ref, out_ref, table_ref, own_ref, sem):
     cols = att0_ref.shape[1]
     features = x_ref.shape[1]
     quarter = out_ref.shape[1]
     rank = lax.axis_index("tp")
-    x = x_ref[pl.ds(pl.multiple_of(rank * quarter, quarter), quarter), :].astype(jnp.float32)
+    rows = pl.ds(pl.multiple_of(rank * quarter, quarter), quarter)
+    copy = pltpu.make_async_copy(x_ref.at[rows], own_ref, sem)
+    copy.start()
     code = jnp.full((1, 1), code_ref[0], jnp.int32)
     p = wiggle(code, rank * quarter, quarter, features)
-    pick = pick_rows(asked_ref[...], send_ref.shape[0] * 16, quarter)
     total = dot(att0_ref[...], w0_ref[...]) + dot(att1_ref[...], w1_ref[...])
     total = total + dot(att3_ref[...], w3_ref[...])
     total = total + dot(att2_ref[:, : cols // 2], top_ref[...])
     total = total + dot(att2_ref[:, cols // 2 :], low_ref[...])
+    copy.wait()
+    x = own_ref[...].astype(jnp.float32)
     made = []
     for s, sign in enumerate(SIGNS):
         part = x if sign == 0.0 else (x + p if sign > 0 else x - p)
@@ -315,31 +318,49 @@
         out_ref[s] = part
         made.append(part)
     forced = dot(jnp.concatenate(made, 0), w_bound_ref[...]).astype(jnp.bfloat16)
-    rows = [forced[s * quarter : (s + 1) * quarter] for s in range(3)]
-    parts = forced.shape[1] // 128
-    table = jnp.concatenate(
-        [
-            jnp.concatenate([f[:, c * 128 : (c + 1) * 128] for f in rows], 1)
-            for c in range(parts)
+    for part in range(forced.shape[1] // 128):
+        for s in range(3):
+            table_ref[part * quarter : (part + 1) * quarter, s * 128 : (s + 1) * 128] = forced[
+                s * quarter : (s + 1) * quarter, part * 128 : (part + 1) * 128
+            ]
+
+
+def combine(code, att, w_outs, x, w_bound):
+    quarter = att[0].shape[0] // 3
+    shape = (3, quarter, x.shape[1])
+    table = (quarter * w_bound.shape[1] // 128, 384)
+    operands = [*att, *(in_hbm(a) for a in (*w_outs, x, w_bound))]
+    specs = [pl.BlockSpec(a.shape, lambda: (0, 0)) for a in operands]
+    specs[-2] = pl.BlockSpec(memory_space=pltpu.HBM)
+    return pl.pallas_call(
+        combine_kernel,
+        out_shape=[jax.ShapeDtypeStruct(s, jnp.bfloat16) for s in (shape, table)],
+        in_specs=[SCALARS] + specs,
+        out_specs=[pl.BlockSpec(shape, lambda: (0, 0, 0)), ON_CHIP],
+        scratch_shapes=[
+            pltpu.VMEM((quarter, x.shape[1]), jnp.bfloat16),
+            pltpu.SemaphoreType.DMA(()),
         ],
-        0,
-    )
-    picked = dot(pick, table).astype(jnp.bfloat16)
-    send_ref[...] = picked.reshape(send_ref.shape)
-
-
-def combine(code, att, w_outs, x, w_bound, asked):
-    shapes = [(3, att[0].shape[0] // 3, x.shape[1]), (asked.shape[0], 16, 384)]
-    operands = [*att, *w_outs, x, w_bound, asked]
-    whole = lambda: (0, 0, 0)
-    return pl.pallas_call(
-        combine_kernel,
-        out_shape=[jax.ShapeDtypeStruct(s, jnp.bfloat16) for s in shapes],
-        in_specs=[SCALARS] + [ON_CHIP] * len(operands),
-        out_specs=[pl.BlockSpec(s, whole) for s in shapes],
         compiler_params=pltpu.CompilerParams(vmem_limit_bytes=16 * MIB),
         name="combine",
     )(code, *operands)
+
+
+def serve_kernel(asked_ref, table_ref, send_ref):
+    pick = pick_rows(asked_ref[...], send_ref.shape[0] * 16, table_ref.shape[0] // 4)
+    send_ref[...] = dot(pick, table_ref[...]).astype(jnp.bfloat16).reshape(send_ref.shape)
+
+
+def serve(asked, table):
+    shape = (asked.shape[0], 16, table.shape[1])
+    return pl.pallas_call(
+        serve_kernel,
+        out_shape=jax.ShapeDtypeStruct(shape, jnp.bfloat16),
+        in_specs=[ON_CHIP] * 2,
+        out_specs=pl.BlockSpec(shape, lambda: (0, 0, 0)),
+        compiler_params=pltpu.CompilerParams(vmem_limit_bytes=8 * MIB),
+        name="serve",
+    )(asked, table)
 
 
 def inputs_kernel(arrived_ref, band_ref, reg_ref, out_ref, first_ref, last_ref):
@@ -487,7 +508,7 @@
     bands = lax.axis_size(BANDS)
     tokens, features = global_state.shape
     half = tokens // 2
-    gain = norm_gain
+    gain = in_hbm(norm_gain)
     cell_band = src_band.reshape(src_tok.shape)
 
     up = [(i, (i + 1) % ranks) for i in range(ranks)]
@@ -496,15 +517,14 @@
         band_codes, in_hbm(global_state), [in_hbm(w) for w in (w_query, w_key, w_value)]
     )
     before, after = neighbours(last, first, BANDS)
+    w1, w3 = lax.ppermute(w_out, "tp", up), lax.ppermute(w_out, "tp", down)
     q, k, v = project(band_codes, [in_hbm(global_state)], gain, weights, False)
-    q, w_out = lax.optimization_barrier((q, w_out))
-    w1, w3 = lax.ppermute(w_out, "tp", up), lax.ppermute(w_out, "tp", down)
     asked = ask(cell_band, src_tok, bands)
+    q, w1, w3 = lax.optimization_barrier((q, w1, w3))
+    middle = w_out.shape[0] // 2
+    top, low = lax.ppermute(w1[:middle], "tp", up), lax.ppermute(w3[middle:], "tp", down)
     q, before, after = lax.optimization_barrier((q, before, after))
     k_halo, v_halo = project(band_codes, [before, after], gain, weights[1:], True)
-    k_halo, w1, w3 = lax.optimization_barrier((k_halo, w1, w3))
-    middle = w_out.shape[0] // 2
-    top, low = lax.ppermute(w1[:middle], "tp", up), lax.ppermute(w3[middle:], "tp", down)
     attended = attend(q, k, v, k_halo, v_halo, ranks, bands)
     attended, asked, top, low = lax.optimization_barrier((attended, asked, top, low))
     attended = [attended[0]] + [
@@ -512,9 +532,8 @@
         for d in range(1, ranks)
     ]
     asked = lax.all_to_all(asked[:, None, :], BANDS, 0, 0, tiled=True)[:, 0, :]
-    global_out, send = combine(
-        band_codes, attended, [w_out, w1, w3, top, low], global_state, w_bound, asked
-    )
+    global_out, table = combine(band_codes, attended, [w_out, w1, w3, top, low], global_state, w_bound)
+    send = serve(asked, table)
     conv_w, send = lax.optimization_barrier((conv_w, send))
     conv_w = in_hbm(conv_w)
     outer = fetch_outer(conv_w)

time: 117 us -> 112 us (0.957)
  blocking collectives: 18.8 us -> 0 us
  starting transfers between devices: 37.2 us -> 51.2 us
  Pallas kernels: 30.3 us -> 34.5 us
  waiting for transfers between devices: 27.8 us -> 23.7 us
    all_to_all x1 -> x0, blocking collectives: 18.8 us -> none  [per_device(): asked = lax.all_to_all(asked[:, None, :], BANDS, 0, 0, tiled=True)[:, 0, :]]
    all_to_all x0 -> x1, starting transfers between devices: none -> 13.8 us  [per_device(): asked = lax.all_to_all(asked[:, None, :], BANDS, 0, 0, tiled=True)[:, 0, :]]
    ppermute x2, waiting for transfers between devices: 6.54 us -> 0.01 us  [per_device(): w1, w3 = (lax.ppermute(w_out, 'tp', up), lax.ppermute(w_out, 'tp', down))]
    all_to_all x0 -> x1, waiting for transfers between devices: none -> 2.41 us  [per_device(): asked = lax.all_to_all(asked[:, None, :], BANDS, 0, 0, tiled=True)[:, 0, :]]
    pallas_call x0 -> x1, Pallas kernels: none -> 1.83 us  [serve(): pl.pallas_call(serve_kernel, out_shape=jax.ShapeDtypeStruct(shape, jnp.bf...]
    pallas_call x1, Pallas kernels: 3.76 us -> 5.22 us  [combine(): pl.pallas_call(combine_kernel, out_shape=[jax.ShapeDtypeStruct(s, jnp.bfl...]
    ppermute x1, starting transfers between devices: 1.74 us -> 2.95 us  [per_device(): lax.ppermute(w3[middle:], 'tp', down)]
    ppermute x1, starting transfers between devices: 1.65 us -> 0.44 us  [per_device(): lax.ppermute(w1[:middle], 'tp', up)]
  transfers between devices with their start and end apart: 12 -> 13, of which waited for: 2 -> 2; matrix products, arithmetic and copies ran while one was open for 0% -> 0% of each run, Pallas kernels for 18% -> 26%
where the time goes in v5:
time: 112 us; the launch traced here: 111 us
  starting transfers between devices  51.2 us (46%)
  Pallas kernels  34.5 us (31%)
  waiting for transfers between devices  23.7 us (21%)
  between operations  1.57 us (1%)
    all_to_all x1, waiting for transfers between devices, per_device(): arrived = lax.all_to_all(send, BANDS, 0, 0, tiled=True)  21.2 us
    ppermute x4, starting transfers between devices, neighbours(): return (lax.ppermute(last, axis, up), lax.ppermute(first, axis, down))  18.6 us
    all_to_all x1, starting transfers between devices, per_device(): asked = lax.all_to_all(asked[:, None, :], BANDS, 0, 0, tiled=True)[:, 0, :]  13.8 us
    pallas_call x1, Pallas kernels, attend(): pl.pallas_call(functools.partial(attend_kernel, bands=bands), out_shape=[...  9.01 us
    all_to_all x1, starting transfers between devices, per_device(): arrived = lax.all_to_all(send, BANDS, 0, 0, tiled=True)  8.27 us
    pallas_call x2, Pallas kernels, project(): pl.pallas_call(functools.partial(project_kernel, halo=halo), out_shape=[j...  8.01 us
    pallas_call x1, Pallas kernels, combine(): pl.pallas_call(combine_kernel, out_shape=[jax.ShapeDtypeStruct(s, jnp.bfl...  5.22 us
    ppermute x3, starting transfers between devices, per_device(): lax.ppermute(attended[d], 'tp', [(i, (i + d) % ranks) for i in range(rank...  3.78 us
  transfers between devices with their start and end apart: 13, of which 2 were waited for; matrix products, arithmetic and copies ran while one was open for 0% of the time, Pallas kernels for 26%

profile of v5, /device:TPU:4, one launch (start us, length us, event | category | flops | bytes accessed | tf_op | source)
XLA Modules:
  0.0 111.1 jit_solution(9181172423166847145)
XLA Ops:
  0.7 1.7 %collective-permute-start = (bf16[256,1024]{1,0:T(8,128)(2,1)}, bf16[256,1024]{1,0:T(8,128)(2,1)S(1)}, u32[]{:S(2)}, u32[]{:S(2)}) collective-permute-start(bf16[256,1024]{1,0:T(8,128)(2,1)} %w0_ref.1), channel_id=1, source_target_pairs={{0,1},{1,2},{2,3},{3,0},{4,5},{5,6},{6,7},{7,4},{8,9},{9,10},{10,1... | collective-permute-start | bytes 1572872 | tf_op jit(solution)/shard_map/ppermute | solution.py:520
  2.3 1.7 %collective-permute-start.1 = (bf16[256,1024]{1,0:T(8,128)(2,1)}, bf16[256,1024]{1,0:T(8,128)(2,1)S(1)}, u32[]{:S(2)}, u32[]{:S(2)}) collective-permute-start(bf16[256,1024]{1,0:T(8,128)(2,1)} %w0_ref.1), channel_id=1, source_target_pairs={{1,0},{2,1},{3,2},{0,3},{5,4},{6,5},{7,6},{4,7},{9,8},{10,9},{11,1... | collective-permute-start | bytes 1572872 | tf_op jit(solution)/shard_map/ppermute | solution.py:520
  4.6 1.7 %edges.1 = (bf16[272,1024]{1,0:T(8,128)(2,1)S(1)}, bf16[272,1024]{1,0:T(8,128)(2,1)S(1)}, bf16[1024,256]{1,0:T(8,128)(2,1)S(1)}, bf16[1024,256]{1,0:T(8,128)(2,1)S(1)}, bf16[1024,256]{1,0:T(8,128)(2,1)S(1)}) custom-call(s32[1]{0:T(128)S(6)} %copy.15.code_ref, bf16[512,1024]{1,0:T(8,128)(2,1)} %x_ref.3, bf16[1024,256]{1,0:T(8,128)(2,1)} %refs_0_.2, ...), custom_call_target="tpu_custom_call" | custom-call | tf_op jit(solution)/shard_map/edges/pallas_call | solution.py:78
  6.3 1.9 %collective-permute-start.2 = (bf16[272,1024]{1,0:T(8,128)(2,1)S(1)}, bf16[272,1024]{1,0:T(8,128)(2,1)S(1)}, u32[]{:S(2)}, u32[]{:S(2)}) collective-permute-start(bf16[272,1024]{1,0:T(8,128)(2,1)S(1)} %get-tuple-element.43), channel_id=1, source_target_pairs={{0,4},{4,8},{8,12},{12,16},{16,20},{20,24},{24,28},{28,32},{32,36}... | collective-permute-start | bytes 1671176 | tf_op jit(solution)/shard_map/ppermute | solution.py:490
  8.3 6.3 %collective-permute-start.3 = (bf16[272,1024]{1,0:T(8,128)(2,1)S(1)}, bf16[272,1024]{1,0:T(8,128)(2,1)S(1)}, u32[]{:S(2)}, u32[]{:S(2)}) collective-permute-start(bf16[272,1024]{1,0:T(8,128)(2,1)S(1)} %get-tuple-element.44), channel_id=1, source_target_pairs={{4,0},{8,4},{12,8},{16,12},{20,16},{24,20},{28,24},{32,28},{36,32}... | collective-permute-start | bytes 1671176 | tf_op jit(solution)/shard_map/ppermute | solution.py:490
  14.6 4.5 %project_own.1 = (bf16[3,512,256]{2,1,0:T(8,128)(2,1)S(1)}, bf16[3,512,256]{2,1,0:T(8,128)(2,1)S(1)}, bf16[3,512,256]{2,1,0:T(8,128)(2,1)S(1)}) custom-call(s32[1]{0:T(128)S(6)} %copy.15.code_ref, bf16[512,1024]{1,0:T(8,128)(2,1)} %x_ref.3, bf16[1024]{0:T(1024)(128)(2,1)} %refs_2_.3, bf16[1024,256]{1,0:T(8,128)(2,1)S(1)} %get-tuple-element.38.refs_2_, ...), custom_call_target="tpu_custom_call" | custom-call | tf_op jit(solution)/shard_map/project_own/pallas_call | solution.py:147
  19.1 0.0 collective-permute-done.w1_ref
  19.2 0.4 collective-permute-start.4
  19.6 2.9 %collective-permute-start.5 = (bf16[128,1024]{1,0:T(8,128)(2,1)S(1)}, bf16[128,1024]{1,0:T(8,128)(2,1)S(1)}, u32[]{:S(2)}, u32[]{:S(2)}) collective-permute-start(bf16[128,1024]{1,0:T(8,128)(2,1)S(1)} %slice.7), channel_id=1, source_target_pairs={{1,0},{2,1},{3,2},{0,3},{5,4},{6,5},{7,6},{4,7},{9,8},{10,9},{11,1... | collective-permute-start | bytes 786440 | tf_op jit(solution)/shard_map/ppermute | solution.py:525
  22.6 1.0 ask.1
  23.5 0.0 collective-permute-done.2.refs_0_
  23.5 0.0 collective-permute-done.3.refs_1_
  23.6 3.5 %project_halo.1 = (bf16[3,512,256]{2,1,0:T(8,128)(2,1)S(1)}, bf16[3,512,256]{2,1,0:T(8,128)(2,1)S(1)}) custom-call(s32[1]{0:T(128)S(6)} %copy.15.code_ref, bf16[272,1024]{1,0:T(8,128)(2,1)S(1)} %collective-permute-done.2.refs_0_, bf16[272,1024]{1,0:T(8,128)(2,1)S(1)} %collective-permute-done.3.refs_1_, bf16[1024]{0:T(1024)(128)(2,1)} %refs_2_.3, ...), custom_call_target="tpu_custom_call" | custom-call | tf_op jit(solution)/shard_map/project_halo/pallas_call | solution.py:147
  27.1 9.0 %attend.1 = (bf16[384,256]{1,0:T(8,128)(2,1)S(1)}, bf16[384,256]{1,0:T(8,128)(2,1)S(1)}, bf16[384,256]{1,0:T(8,128)(2,1)S(1)}, bf16[384,256]{1,0:T(8,128)(2,1)S(1)}) custom-call(bf16[3,512,256]{2,1,0:T(8,128)(2,1)S(1)} %get-tuple-element.45.q_ref, bf16[3,512,256]{2,1,0:T(8,128)(2,1)S(1)} %get-tuple-element.46.k_ref, ...), custom_call_target="tpu_custom_call" | custom-call | tf_op jit(solution)/shard_map/attend/pallas_call | solution.py:213
  36.1 0.0 collective-permute-done.4.top_ref
  36.1 0.0 copy-start.5
  36.2 0.1 collective-permute-start.6
  36.3 2.4 %collective-permute-start.7 = (bf16[384,256]{1,0:T(8,128)(2,1)S(1)}, bf16[384,256]{1,0:T(8,128)(2,1)S(1)}, u32[]{:S(2)}, u32[]{:S(2)}) collective-permute-start(bf16[384,256]{1,0:T(8,128)(2,1)S(1)} %get-tuple-element.60), channel_id=1, source_target_pairs={{0,2},{1,3},{2,0},{3,1},{4,6},{5,7},{6,4},{7,5},{8,10},{9,11},{10,... | collective-permute-start | bytes 589832 | tf_op jit(solution)/shard_map/ppermute | solution.py:531
  38.6 1.3 %collective-permute-start.8 = (bf16[384,256]{1,0:T(8,128)(2,1)S(1)}, bf16[384,256]{1,0:T(8,128)(2,1)S(1)}, u32[]{:S(2)}, u32[]{:S(2)}) collective-permute-start(bf16[384,256]{1,0:T(8,128)(2,1)S(1)} %get-tuple-element.61), channel_id=1, source_target_pairs={{0,3},{1,0},{2,1},{3,2},{4,7},{5,4},{6,5},{7,6},{8,11},{9,8},{10,9... | collective-permute-start | bytes 589832 | tf_op jit(solution)/shard_map/ppermute | solution.py:531
  39.9 13.8 %all-to-all-start = ((s32[64,1,4]{2,1,0:T(1,128)}), s32[64,1,4]{2,1,0:T(1,128)S(1)}, u32[]{:S(2)}, u32[]{:S(2)}) async-start(s32[64,1,4]{2,1,0:T(1,128)} %bitcast.2), calls=%async_computation | async-start | bytes 65536 | tf_op jit(solution)/shard_map/all_to_all | solution.py:534
  53.8 0.0 collective-permute-done.6.att1_ref
  53.9 5.2 %combine.1 = (bf16[3,128,1024]{2,1,0:T(8,128)(2,1)}, bf16[512,384]{1,0:T(8,128)(2,1)S(1)}) custom-call(s32[1]{0:T(128)S(6)} %copy.15.code_ref, bf16[384,256]{1,0:T(8,128)(2,1)S(1)} %get-tuple-element.58.att0_ref, bf16[384,256]{1,0:T(8,128)(2,1)S(1)} %collective-permute-done.6.att1_ref, bf16[384,256]{1,0:T(8,128)(2,1)S(1)} %collective-permute-done.7.att2_ref, ...), custom_call_target="tpu_custom_call" | custom-call | tf_op jit(solution)/shard_map/combine/pallas_call | solution.py:335
  59.1 2.4 %all-to-all-done = s32[64,1,4]{2,1,0:T(1,128)S(1)} async-done(((s32[64,1,4]{2,1,0:T(1,128)}), s32[64,1,4]{2,1,0:T(1,128)S(1)}, u32[]{:S(2)}, u32[]{:S(2)}) %all-to-all-start) | async-done | bytes 1056 | tf_op jit(solution)/shard_map/all_to_all | solution.py:534
  61.5 1.8 %serve.1 = bf16[64,16,384]{2,1,0:T(8,128)(2,1)} custom-call(s32[64,4]{1,0:T(8,128)S(1)} %bitcast.5, bf16[512,384]{1,0:T(8,128)(2,1)S(1)} %get-tuple-element.66.table_ref), custom_call_target="tpu_custom_call" | custom-call | tf_op jit(solution)/shard_map/serve/pallas_call | solution.py:356
  63.3 8.3 %all-to-all-start.1 = ((bf16[64,16,384]{2,1,0:T(8,128)(2,1)}), bf16[64,16,384]{2,1,0:T(8,128)(2,1)}, u32[]{:S(2)}, u32[]{:S(2)}) async-start(bf16[64,16,384]{2,1,0:T(8,128)(2,1)} %serve.1), calls=%async_computation.1 | async-start | bytes 1572864 | tf_op jit(solution)/shard_map/all_to_all | solution.py:540
  71.6 1.9 %fetch.1.outer_ref = bf16[6,512,512]{2,1,0:T(8,128)(2,1)S(1)} custom-call(bf16[9,512,512]{2,1,0:T(8,128)(2,1)} %conv_hbm_ref.1), custom_call_target="tpu_custom_call" | custom-call | tf_op jit(solution)/shard_map/fetch/pallas_call | solution.py:276
  73.5 21.2 %all-to-all-done.1.arrived_ref = bf16[64,16,384]{2,1,0:T(8,128)(2,1)} async-done(((bf16[64,16,384]{2,1,0:T(8,128)(2,1)}), bf16[64,16,384]{2,1,0:T(8,128)(2,1)}, u32[]{:S(2)}, u32[]{:S(2)}) %all-to-all-start.1) | async-done | bytes 786464 | tf_op jit(solution)/shard_map/all_to_all | solution.py:540
  94.8 2.1 %inputs.1 = (bf16[8,48,512]{2,1,0:T(8,128)(2,1)S(1)}, bf16[48,512]{1,0:T(8,128)(2,1)S(1)}, bf16[48,512]{1,0:T(8,128)(2,1)S(1)}) custom-call(bf16[64,16,384]{2,1,0:T(8,128)(2,1)} %all-to-all-done.1.arrived_ref, s32[8,16]{1,0:T(8,128)S(1)} %bitcast.7, bf16[8,16,512]{2,1,0:T(8,128)(2,1)S(1)} %copy-done), custom_call_target="tpu_custom_call" | custom-call | tf_op jit(solution)/shard_map/inputs/pallas_call | solution.py:394
  96.9 2.6 %collective-permute-start.9 = (bf16[48,512]{1,0:T(8,128)(2,1)S(1)}, bf16[48,512]{1,0:T(8,128)(2,1)S(1)}, u32[]{:S(2)}, u32[]{:S(2)}) collective-permute-start(bf16[48,512]{1,0:T(8,128)(2,1)S(1)} %get-tuple-element.71), channel_id=1, source_target_pairs={{0,1},{1,2},{2,3},{3,4},{4,5},{5,6},{6,7},{7,8},{8,9},{9,10},{10,1... | collective-permute-start | bytes 147464 | tf_op jit(solution)/shard_map/ppermute | solution.py:490
  99.5 7.8 %collective-permute-start.10 = (bf16[48,512]{1,0:T(8,128)(2,1)S(1)}, bf16[48,512]{1,0:T(8,128)(2,1)S(1)}, u32[]{:S(2)}, u32[]{:S(2)}) collective-permute-start(bf16[48,512]{1,0:T(8,128)(2,1)S(1)} %get-tuple-element.72), channel_id=1, source_target_pairs={{1,0},{2,1},{3,2},{4,3},{5,4},{6,5},{7,6},{8,7},{9,8},{10,9},{11,1... | collective-permute-start | bytes 147464 | tf_op jit(solution)/shard_map/ppermute | solution.py:490
  107.3 2.2 %convolve_inner.1.sum_ref = f32[384,512]{1,0:T(8,128)S(1)} custom-call(bf16[8,48,512]{2,1,0:T(8,128)(2,1)S(1)} %get-tuple-element.70.x_ref, bf16[6,512,512]{2,1,0:T(8,128)(2,1)S(1)} %fetch.1.outer_ref, bf16[9,512,512]{2,1,0:T(8,128)(2,1)} %conv_hbm_ref.1), custom_call_target="tpu_custom_call" | custom-call | tf_op jit(solution)/shard_map/convolve_inner/pallas_call | solution.py:437
  109.5 1.6 %convolve_finish.1 = bf16[3,8,16,512]{3,2,1,0:T(8,128)(2,1)} custom-call(bf16[8,48,512]{2,1,0:T(8,128)(2,1)S(1)} %get-tuple-element.70.x_ref, bf16[48,512]{1,0:T(8,128)(2,1)S(1)} %collective-permute-done.9.before_ref, bf16[48,512]{1,0:T(8,128)(2,1)S(1)} %collective-permute-done.10.after_ref, bf16[6,512,512]{2,1,0:T(8,128)(2,1)S(1)} %fetch.1.outer_ref, ...), custom_call_target="tpu_custom_call" | custom-call | tf_op jit(solution)/shard_map/convolve_finish/pallas_call | solution.py:476
  (21 shorter events, 0.1 us)
Async XLA Ops:
  0.6 22.0 %copy-start.1 = (s32[8,16,1]{1,2,0:T(1,128)S(1)}, s32[8,16,1]{1,2,0:T(1,128)}, u32[]{:S(2)}) copy-start(s32[8,16,1]{1,2,0:T(1,128)} %param.20) | copy-start | bytes 1540
  0.6 21.9 %copy-start.2 = (s32[8,16]{1,0:T(8,128)S(1)}, s32[8,16]{1,0:T(8,128)}, u32[]{:S(2)}) copy-start(s32[8,16]{1,0:T(8,128)} %tok_ref.1) | copy-start | bytes 1540
  0.7 18.5 %collective-permute-start = (bf16[256,1024]{1,0:T(8,128)(2,1)}, bf16[256,1024]{1,0:T(8,128)(2,1)S(1)}, u32[]{:S(2)}, u32[]{:S(2)}) collective-permute-start(bf16[256,1024]{1,0:T(8,128)(2,1)} %w0_ref.1), channel_id=1, source_target_pairs={{0,1},{1,2},{2,3},{3,0},{4,5},{5,6},{6,7},{7,4},{8,9},{9,10},{10,1... | collective-permute-start | bytes 1572872 | tf_op jit(solution)/shard_map/ppermute | solution.py:520
  2.3 16.8 %collective-permute-start.1 = (bf16[256,1024]{1,0:T(8,128)(2,1)}, bf16[256,1024]{1,0:T(8,128)(2,1)S(1)}, u32[]{:S(2)}, u32[]{:S(2)}) collective-permute-start(bf16[256,1024]{1,0:T(8,128)(2,1)} %w0_ref.1), channel_id=1, source_target_pairs={{1,0},{2,1},{3,2},{0,3},{5,4},{6,5},{7,6},{4,7},{9,8},{10,9},{11,1... | collective-permute-start | bytes 1572872 | tf_op jit(solution)/shard_map/ppermute | solution.py:520
  6.3 17.2 %collective-permute-start.2 = (bf16[272,1024]{1,0:T(8,128)(2,1)S(1)}, bf16[272,1024]{1,0:T(8,128)(2,1)S(1)}, u32[]{:S(2)}, u32[]{:S(2)}) collective-permute-start(bf16[272,1024]{1,0:T(8,128)(2,1)S(1)} %get-tuple-element.43), channel_id=1, source_target_pairs={{0,4},{4,8},{8,12},{12,16},{16,20},{20,24},{24,28},{28,32},{32,36}... | collective-permute-start | bytes 1671176 | tf_op jit(solution)/shard_map/ppermute | solution.py:490
  8.3 15.3 %collective-permute-start.3 = (bf16[272,1024]{1,0:T(8,128)(2,1)S(1)}, bf16[272,1024]{1,0:T(8,128)(2,1)S(1)}, u32[]{:S(2)}, u32[]{:S(2)}) collective-permute-start(bf16[272,1024]{1,0:T(8,128)(2,1)S(1)} %get-tuple-element.44), channel_id=1, source_target_pairs={{4,0},{8,4},{12,8},{16,12},{20,16},{24,20},{28,24},{32,28},{36,32}... | collective-permute-start | bytes 1671176 | tf_op jit(solution)/shard_map/ppermute | solution.py:490
  19.1 34.7 %copy-start.3 = (bf16[256,1024]{1,0:T(8,128)(2,1)}, bf16[256,1024]{1,0:T(8,128)(2,1)S(1)}, u32[]{:S(2)}) copy-start(bf16[256,1024]{1,0:T(8,128)(2,1)S(1)} %collective-permute-done.w1_ref) | copy-start | bytes 1572868
  19.1 34.7 %copy-start.4 = (bf16[256,1024]{1,0:T(8,128)(2,1)}, bf16[256,1024]{1,0:T(8,128)(2,1)S(1)}, u32[]{:S(2)}) copy-start(bf16[256,1024]{1,0:T(8,128)(2,1)S(1)} %collective-permute-done.1.w3_ref) | copy-start | bytes 1572868
  19.2 16.9 %collective-permute-start.4 = (bf16[128,1024]{1,0:T(8,128)(2,1)S(1)}, bf16[128,1024]{1,0:T(8,128)(2,1)S(1)}, u32[]{:S(2)}, u32[]{:S(2)}) collective-permute-start(bf16[128,1024]{1,0:T(8,128)(2,1)S(1)} %slice.6), channel_id=1, source_target_pairs={{0,1},{1,2},{2,3},{3,0},{4,5},{5,6},{6,7},{7,4},{8,9},{9,10},{10,1... | collective-permute-start | bytes 786440 | tf_op jit(solution)/shard_map/ppermute | solution.py:525
  19.6 16.5 %collective-permute-start.5 = (bf16[128,1024]{1,0:T(8,128)(2,1)S(1)}, bf16[128,1024]{1,0:T(8,128)(2,1)S(1)}, u32[]{:S(2)}, u32[]{:S(2)}) collective-permute-start(bf16[128,1024]{1,0:T(8,128)(2,1)S(1)} %slice.7), channel_id=1, source_target_pairs={{1,0},{2,1},{3,2},{0,3},{5,4},{6,5},{7,6},{4,7},{9,8},{10,9},{11,1... | collective-permute-start | bytes 786440 | tf_op jit(solution)/shard_map/ppermute | solution.py:525
  36.1 17.7 %copy-start.5 = (bf16[128,1024]{1,0:T(8,128)(2,1)}, bf16[128,1024]{1,0:T(8,128)(2,1)S(1)}, u32[]{:S(2)}) copy-start(bf16[128,1024]{1,0:T(8,128)(2,1)S(1)} %collective-permute-done.4.top_ref) | copy-start | bytes 786436
  36.1 17.7 %copy-start.6 = (bf16[128,1024]{1,0:T(8,128)(2,1)}, bf16[128,1024]{1,0:T(8,128)(2,1)S(1)}, u32[]{:S(2)}) copy-start(bf16[128,1024]{1,0:T(8,128)(2,1)S(1)} %collective-permute-done.5.low_ref) | copy-start | bytes 786436
  36.2 17.6 %collective-permute-start.6 = (bf16[384,256]{1,0:T(8,128)(2,1)S(1)}, bf16[384,256]{1,0:T(8,128)(2,1)S(1)}, u32[]{:S(2)}, u32[]{:S(2)}) collective-permute-start(bf16[384,256]{1,0:T(8,128)(2,1)S(1)} %get-tuple-element.59), channel_id=1, source_target_pairs={{0,1},{1,2},{2,3},{3,0},{4,5},{5,6},{6,7},{7,4},{8,9},{9,10},{10,1... | collective-permute-start | bytes 589832 | tf_op jit(solution)/shard_map/ppermute | solution.py:531
  36.3 17.5 %collective-permute-start.7 = (bf16[384,256]{1,0:T(8,128)(2,1)S(1)}, bf16[384,256]{1,0:T(8,128)(2,1)S(1)}, u32[]{:S(2)}, u32[]{:S(2)}) collective-permute-start(bf16[384,256]{1,0:T(8,128)(2,1)S(1)} %get-tuple-element.60), channel_id=1, source_target_pairs={{0,2},{1,3},{2,0},{3,1},{4,6},{5,7},{6,4},{7,5},{8,10},{9,11},{10,... | collective-permute-start | bytes 589832 | tf_op jit(solution)/shard_map/ppermute | solution.py:531
  38.6 15.2 %collective-permute-start.8 = (bf16[384,256]{1,0:T(8,128)(2,1)S(1)}, bf16[384,256]{1,0:T(8,128)(2,1)S(1)}, u32[]{:S(2)}, u32[]{:S(2)}) collective-permute-start(bf16[384,256]{1,0:T(8,128)(2,1)S(1)} %get-tuple-element.61), channel_id=1, source_target_pairs={{0,3},{1,0},{2,1},{3,2},{4,7},{5,4},{6,5},{7,6},{8,11},{9,8},{10,9... | collective-permute-start | bytes 589832 | tf_op jit(solution)/shard_map/ppermute | solution.py:531
  39.9 21.5 %all-to-all-start = ((s32[64,1,4]{2,1,0:T(1,128)}), s32[64,1,4]{2,1,0:T(1,128)S(1)}, u32[]{:S(2)}, u32[]{:S(2)}) async-start(s32[64,1,4]{2,1,0:T(1,128)} %bitcast.2), calls=%async_computation | async-start | bytes 65536 | tf_op jit(solution)/shard_map/all_to_all | solution.py:534
  63.3 31.4 %copy-start = (bf16[8,16,512]{2,1,0:T(8,128)(2,1)S(1)}, bf16[8,16,512]{2,1,0:T(8,128)(2,1)}, u32[]{:S(2)}) copy-start(bf16[8,16,512]{2,1,0:T(8,128)(2,1)} %reg_ref.1) | copy-start | bytes 393220
  63.3 31.4 %all-to-all-start.1 = ((bf16[64,16,384]{2,1,0:T(8,128)(2,1)}), bf16[64,16,384]{2,1,0:T(8,128)(2,1)}, u32[]{:S(2)}, u32[]{:S(2)}) async-start(bf16[64,16,384]{2,1,0:T(8,128)(2,1)} %serve.1), calls=%async_computation.1 | async-start | bytes 1572864 | tf_op jit(solution)/shard_map/all_to_all | solution.py:540
  96.9 12.6 %collective-permute-start.9 = (bf16[48,512]{1,0:T(8,128)(2,1)S(1)}, bf16[48,512]{1,0:T(8,128)(2,1)S(1)}, u32[]{:S(2)}, u32[]{:S(2)}) collective-permute-start(bf16[48,512]{1,0:T(8,128)(2,1)S(1)} %get-tuple-element.71), channel_id=1, source_target_pairs={{0,1},{1,2},{2,3},{3,4},{4,5},{5,6},{6,7},{7,8},{8,9},{9,10},{10,1... | collective-permute-start | bytes 147464 | tf_op jit(solution)/shard_map/ppermute | solution.py:490
  99.5 10.0 %collective-permute-start.10 = (bf16[48,512]{1,0:T(8,128)(2,1)S(1)}, bf16[48,512]{1,0:T(8,128)(2,1)S(1)}, u32[]{:S(2)}, u32[]{:S(2)}) collective-permute-start(bf16[48,512]{1,0:T(8,128)(2,1)S(1)} %get-tuple-element.72), channel_id=1, source_target_pairs={{1,0},{2,1},{3,2},{4,3},{5,4},{6,5},{7,6},{8,7},{9,8},{10,9},{11,1... | collective-permute-start | bytes 147464 | tf_op jit(solution)/shard_map/ppermute | solution.py:490

commit v6 on v5

--- a/solution.py
+++ b/solution.py
@@ -86,23 +86,20 @@
     )(code, x, *weights)
 
 
-def project_kernel(code_ref, *refs, halo):
+def project_kernel(code_ref, early_ref, late_ref, gain_ref, *refs, halo):
+    *refs, both_ref, inv_ref = refs
     step = pl.program_id(0)
-    both_ref, inv_ref = refs[-2:]
+    rows = early_ref.shape[0] - 16
     if halo:
-        before_ref, after_ref, gain_ref, *refs = refs[:-2]
-        rows = before_ref.shape[0] - 16
         first = (1 - step) * rows
         digits = jnp.where(
-            step == 0, before_ref[rows : rows + 16, 0:128], after_ref[rows : rows + 16, 0:128]
+            step == 0, early_ref[rows : rows + 16, 0:128], late_ref[rows : rows + 16, 0:128]
         ).astype(jnp.float32)[0:1]
         lane = iota((1, 128), 1)
         place = jnp.where(lane == 0, 65536.0, jnp.where(lane == 1, 256.0, 1.0))
         code = jnp.sum(jnp.where(lane < 3, digits * place, 0.0), -1, keepdims=True)
         code = code.astype(jnp.int32)
     else:
-        x_ref, gain_ref, *refs = refs[:-2]
-        rows = x_ref.shape[0]
         first = step * rows
         code = jnp.full((1, 1), code_ref[0], jnp.int32)
     weights, outs = refs[: len(refs) // 2], refs[len(refs) // 2 :]
@@ -111,10 +108,7 @@
     chunk, block = 16, 128
     for at in range(0, rows, block):
         for r in range(at, at + block, chunk):
-            if halo:
-                x = jnp.where(step == 0, before_ref[r : r + chunk], after_ref[r : r + chunk])
-            else:
-                x = x_ref[r : r + chunk]
+            x = jnp.where(step == 0, early_ref[r : r + chunk], late_ref[r : r + chunk])
             x = x.astype(jnp.float32)
             p = wiggle(code, first + r, chunk, features)
             place = 2 * at + (r - at)
@@ -137,12 +131,8 @@
 def project(code, arrays, gain, weights, halo):
     features = gain.shape[0]
     cols = weights[0].shape[1]
-    if halo:
-        tokens = 2 * (arrays[0].shape[0] - 16)
-        specs = [ON_CHIP for a in arrays]
-    else:
-        tokens = arrays[0].shape[0]
-        specs = [pl.BlockSpec((tokens // 2, features), lambda i: (i, 0))]
+    tokens = 2 * (arrays[0].shape[0] - 16)
+    specs = [ON_CHIP for a in arrays]
     rows = tokens // 2
     return pl.pallas_call(
         functools.partial(project_kernel, halo=halo),
@@ -259,26 +249,19 @@
     )(band, tok)
 
 
-def fetch_kernel(conv_hbm_ref, outer_ref, sems):
-    copies = [
-        pltpu.make_async_copy(
-            conv_hbm_ref.at[pl.ds(6 * i, 3)], outer_ref.at[pl.ds(3 * i, 3)], sems.at[i]
-        )
-        for i in range(2)
-    ]
-    for copy in copies:
-        copy.start()
-    for copy in copies:
-        copy.wait()
-
-
-def fetch_outer(conv_w):
+def fetch_kernel(conv_hbm_ref, taps_ref, sem):
+    copy = pltpu.make_async_copy(conv_hbm_ref.at[pl.ds(0, 3)], taps_ref, sem)
+    copy.start()
+    copy.wait()
+
+
+def fetch_taps(conv_w):
     return pl.pallas_call(
         fetch_kernel,
-        out_shape=jax.ShapeDtypeStruct((6, *conv_w.shape[1:]), conv_w.dtype),
+        out_shape=jax.ShapeDtypeStruct((3, *conv_w.shape[1:]), conv_w.dtype),
         in_specs=[pl.BlockSpec(memory_space=pltpu.HBM)],
         out_specs=ON_CHIP,
-        scratch_shapes=[pltpu.SemaphoreType.DMA((2,))],
+        scratch_shapes=[pltpu.SemaphoreType.DMA(())],
         compiler_params=pltpu.CompilerParams(vmem_limit_bytes=2 * MIB),
         name="fetch",
     )(conv_w)
@@ -295,21 +278,37 @@
     return (iota((rows, 4 * cells), 1) == target).astype(jnp.float32).astype(jnp.bfloat16)
 
 
-def combine_kernel(code_ref, att0_ref, att1_ref, att2_ref, att3_ref, w0_ref, w1_ref, w3_ref, top_ref, low_ref, x_ref, w_bound_ref, out_ref, table_ref, own_ref, sem):
+def combine_kernel(code_ref, att0_ref, att1_ref, att2_ref, att3_ref, w0_ref, w1_ref, w3_ref, top_ref, low_ref, x_ref, w_bound_ref, out_ref, table_ref, own_ref, held_ref, bound_ref, sems):
     cols = att0_ref.shape[1]
+    half = cols // 2
     features = x_ref.shape[1]
     quarter = out_ref.shape[1]
     rank = lax.axis_index("tp")
     rows = pl.ds(pl.multiple_of(rank * quarter, quarter), quarter)
-    copy = pltpu.make_async_copy(x_ref.at[rows], own_ref, sem)
-    copy.start()
+    pairs = [
+        (w0_ref, held_ref.at[pl.ds(0, cols)]),
+        (w1_ref, held_ref.at[pl.ds(cols, cols)]),
+        (w3_ref, held_ref.at[pl.ds(2 * cols, cols)]),
+        (top_ref, held_ref.at[pl.ds(3 * cols, half)]),
+        (low_ref, held_ref.at[pl.ds(3 * cols + half, half)]),
+        (x_ref.at[rows], own_ref),
+        (w_bound_ref, bound_ref),
+    ]
+    copies = [pltpu.make_async_copy(a, b, sems.at[i]) for i, (a, b) in enumerate(pairs)]
+    for copy in copies:
+        copy.start()
     code = jnp.full((1, 1), code_ref[0], jnp.int32)
     p = wiggle(code, rank * quarter, quarter, features)
-    total = dot(att0_ref[...], w0_ref[...]) + dot(att1_ref[...], w1_ref[...])
-    total = total + dot(att3_ref[...], w3_ref[...])
-    total = total + dot(att2_ref[:, : cols // 2], top_ref[...])
-    total = total + dot(att2_ref[:, cols // 2 :], low_ref[...])
-    copy.wait()
+    copies[0].wait()
+    total = dot(att0_ref[...], held_ref[:cols])
+    copies[1].wait()
+    total = total + dot(att1_ref[...], held_ref[cols : 2 * cols])
+    copies[2].wait()
+    total = total + dot(att3_ref[...], held_ref[2 * cols : 3 * cols])
+    copies[3].wait()
+    copies[4].wait()
+    total = total + dot(att2_ref[...], held_ref[3 * cols :])
+    copies[5].wait()
     x = own_ref[...].astype(jnp.float32)
     made = []
     for s, sign in enumerate(SIGNS):
@@ -317,7 +316,8 @@
         part = (part + total[s * quarter : (s + 1) * quarter]).astype(jnp.bfloat16)
         out_ref[s] = part
         made.append(part)
-    forced = dot(jnp.concatenate(made, 0), w_bound_ref[...]).astype(jnp.bfloat16)
+    copies[6].wait()
+    forced = dot(jnp.concatenate(made, 0), bound_ref[...]).astype(jnp.bfloat16)
     for part in range(forced.shape[1] // 128):
         for s in range(3):
             table_ref[part * quarter : (part + 1) * quarter, s * 128 : (s + 1) * 128] = forced[
@@ -329,21 +329,23 @@
     quarter = att[0].shape[0] // 3
     shape = (3, quarter, x.shape[1])
     table = (quarter * w_bound.shape[1] // 128, 384)
-    operands = [*att, *(in_hbm(a) for a in (*w_outs, x, w_bound))]
-    specs = [pl.BlockSpec(a.shape, lambda: (0, 0)) for a in operands]
-    specs[-2] = pl.BlockSpec(memory_space=pltpu.HBM)
+    far = [in_hbm(a) for a in (*w_outs, x, w_bound)]
     return pl.pallas_call(
         combine_kernel,
         out_shape=[jax.ShapeDtypeStruct(s, jnp.bfloat16) for s in (shape, table)],
-        in_specs=[SCALARS] + specs,
+        in_specs=[SCALARS]
+        + [pl.BlockSpec(a.shape, lambda: (0, 0)) for a in att]
+        + [pl.BlockSpec(memory_space=pltpu.HBM)] * len(far),
         out_specs=[pl.BlockSpec(shape, lambda: (0, 0, 0)), ON_CHIP],
         scratch_shapes=[
             pltpu.VMEM((quarter, x.shape[1]), jnp.bfloat16),
-            pltpu.SemaphoreType.DMA(()),
+            pltpu.VMEM((len(att) * att[0].shape[1], x.shape[1]), jnp.bfloat16),
+            pltpu.VMEM(w_bound.shape, jnp.bfloat16),
+            pltpu.SemaphoreType.DMA((len(far),)),
         ],
         compiler_params=pltpu.CompilerParams(vmem_limit_bytes=16 * MIB),
         name="combine",
-    )(code, *operands)
+    )(code, *att, *far)
 
 
 def serve_kernel(asked_ref, table_ref, send_ref):
@@ -410,52 +412,61 @@
     return low, x, high
 
 
-def inner_kernel(x_ref, outer_ref, conv_hbm_ref, sum_ref, held_ref, sem):
-    copy = pltpu.make_async_copy(conv_hbm_ref.at[pl.ds(3, 3)], held_ref, sem)
-    copy.start()
+def inner_kernel(x_ref, before_ref, conv_hbm_ref, sum_ref, after_ref, held_ref, sems):
+    copies = [
+        pltpu.make_async_copy(conv_hbm_ref.at[pl.ds(3, 3)], held_ref, sems.at[0]),
+        pltpu.make_async_copy(conv_hbm_ref.at[pl.ds(6, 3)], after_ref, sems.at[1]),
+    ]
+    for copy in copies:
+        copy.start()
     cols, slab, channels = x_ref.shape
     cells = cols * slab
     shifts = row_shifts(x_ref[...].reshape(cells, channels), slab // 3)
-    before = after = None
-    for b, x in enumerate(shifts):
-        one = dot(x[: cells - slab], outer_ref[b])
-        two = dot(x[slab:], outer_ref[3 + b])
-        before = one if before is None else before + one
-        after = two if after is None else after + two
-    copy.wait()
-    middle = None
-    for b, x in enumerate(shifts):
-        one = dot(x, held_ref[b])
-        middle = one if middle is None else middle + one
+
+    def product(first, last, w_ref):
+        total = None
+        for b, x in enumerate(shifts):
+            one = dot(x[first:last], w_ref[b])
+            total = one if total is None else total + one
+        return total
+
+    before = product(0, cells - slab, before_ref)
+    copies[0].wait()
+    middle = product(0, cells, held_ref)
+    copies[1].wait()
+    after = product(slab, cells, after_ref)
     sum_ref[:slab] = middle[:slab] + after[:slab]
     sum_ref[slab : cells - slab] = middle[slab : cells - slab] + before[: cells - 2 * slab] + after[slab:]
     sum_ref[cells - slab :] = middle[cells - slab :] + before[cells - 2 * slab :]
 
 
-def convolve_inner(x, outer, conv_w):
+def convolve_inner(x, taps, conv_w):
     cols, slab, channels = x.shape
     return pl.pallas_call(
         inner_kernel,
-        out_shape=jax.ShapeDtypeStruct((cols * slab, channels), jnp.float32),
+        out_shape=[
+            jax.ShapeDtypeStruct((cols * slab, channels), jnp.float32),
+            jax.ShapeDtypeStruct(taps.shape, taps.dtype),
+        ],
         in_specs=[ON_CHIP] * 2 + [pl.BlockSpec(memory_space=pltpu.HBM)],
-        out_specs=ON_CHIP,
+        out_specs=[ON_CHIP] * 2,
         scratch_shapes=[
             pltpu.VMEM((3, channels, channels), jnp.bfloat16),
-            pltpu.SemaphoreType.DMA(()),
+            pltpu.SemaphoreType.DMA((2,)),
         ],
         compiler_params=pltpu.CompilerParams(vmem_limit_bytes=16 * MIB),
         name="convolve_inner",
-    )(x, outer, conv_w)
-
-
-def finish_kernel(x_ref, before_ref, after_ref, outer_ref, sum_ref, out_ref):
+    )(x, taps, conv_w)
+
+
+def finish_kernel(x_ref, before_ref, after_ref, w_before_ref, w_after_ref, sum_ref, out_ref):
     cols, slab, channels = x_ref.shape
     rows = slab // 3
     sides = []
-    for side, ref in enumerate((before_ref, after_ref)):
+    for ref, w_ref in ((before_ref, w_before_ref), (after_ref, w_after_ref)):
         total = None
         for b, x in enumerate(row_shifts(ref[...], rows)):
-            one = dot(x, outer_ref[3 * side + b])
+            one = dot(x, w_ref[b])
             total = one if total is None else total + one
         sides.append(total)
     for col in range(cols):
@@ -470,17 +481,17 @@
             out_ref[s, col] = result[s * rows : (s + 1) * rows]
 
 
-def convolve_finish(x, before, after, outer, total):
+def convolve_finish(x, before, after, w_before, w_after, total):
     cols, slab, channels = x.shape
     shape = (3, cols, slab // 3, channels)
     return pl.pallas_call(
         finish_kernel,
         out_shape=jax.ShapeDtypeStruct(shape, jnp.bfloat16),
-        in_specs=[ON_CHIP] * 5,
+        in_specs=[ON_CHIP] * 6,
         out_specs=pl.BlockSpec(shape, lambda: (0, 0, 0, 0)),
         compiler_params=pltpu.CompilerParams(vmem_limit_bytes=8 * MIB),
         name="convolve_finish",
-    )(x, before, after, outer, total)
+    )(x, before, after, w_before, w_after, total)
 
 
 def neighbours(last, first, axis):
@@ -518,7 +529,7 @@
     )
     before, after = neighbours(last, first, BANDS)
     w1, w3 = lax.ppermute(w_out, "tp", up), lax.ppermute(w_out, "tp", down)
-    q, k, v = project(band_codes, [in_hbm(global_state)], gain, weights, False)
+    q, k, v = project(band_codes, [first, last], gain, weights, False)
     asked = ask(cell_band, src_tok, bands)
     q, w1, w3 = lax.optimization_barrier((q, w1, w3))
     middle = w_out.shape[0] // 2
@@ -536,13 +547,13 @@
     send = serve(asked, table)
     conv_w, send = lax.optimization_barrier((conv_w, send))
     conv_w = in_hbm(conv_w)
-    outer = fetch_outer(conv_w)
+    taps = fetch_taps(conv_w)
     arrived = lax.all_to_all(send, BANDS, 0, 0, tiled=True)
-    outer, arrived = lax.optimization_barrier((outer, arrived))
+    taps, arrived = lax.optimization_barrier((taps, arrived))
     inputs, first, last = make_inputs(arrived, cell_band, reg_state)
     before, after = neighbours(last, first, CELLS)
-    total = convolve_inner(inputs, outer, conv_w)
-    return global_out, convolve_finish(inputs, before, after, outer, total)
+    total, late = convolve_inner(inputs, taps, conv_w)
+    return global_out, convolve_finish(inputs, before, after, taps, late, total)
 
 
 def solution(mesh):

time: 112 us -> 110 us (0.982)
  Pallas kernels: 34.5 us -> 32 us
  waiting for transfers between devices: 23.7 us -> 26 us
  starting transfers between devices: 51.2 us -> 49.8 us
    all_to_all x1, waiting for transfers between devices: 2.41 us -> 4.19 us  [per_device(): asked = lax.all_to_all(asked[:, None, :], BANDS, 0, 0, tiled=True)[:, 0, :]]
    pallas_call x1, Pallas kernels: 5.22 us -> 3.45 us  [combine(): pl.pallas_call(combine_kernel, out_shape=[jax.ShapeDtypeStruct(s, jnp.bfl...]
    all_to_all x1, starting transfers between devices: 8.27 us -> 6.6 us  [per_device(): arrived = lax.all_to_all(send, BANDS, 0, 0, tiled=True)]
    pallas_call x1, Pallas kernels: 2.12 us -> 0.98 us  [make_inputs(): pl.pallas_call(inputs_kernel, out_shape=[jax.ShapeDtypeStruct(s, jnp.bflo...]
  transfers between devices with their start and end apart: 13 -> 13, of which waited for: 2 -> 2; matrix products, arithmetic and copies ran while one was open for 0% -> 0% of each run, Pallas kernels for 26% -> 25%
where the time goes in v6:
time: 110 us
  starting transfers between devices  49.8 us (45%)
  Pallas kernels  32 us (29%)
  waiting for transfers between devices  26 us (24%)
  between operations  1.57 us (1%)
    all_to_all x1, waiting for transfers between devices, per_device(): arrived = lax.all_to_all(send, BANDS, 0, 0, tiled=True)  21.8 us
    ppermute x4, starting transfers between devices, neighbours(): return (lax.ppermute(last, axis, up), lax.ppermute(first, axis, down))  18.6 us
    all_to_all x1, starting transfers between devices, per_device(): asked = lax.all_to_all(asked[:, None, :], BANDS, 0, 0, tiled=True)[:, 0, :]  13.8 us
    pallas_call x1, Pallas kernels, attend(): pl.pallas_call(functools.partial(attend_kernel, bands=bands), out_shape=[...  9.01 us
    pallas_call x2, Pallas kernels, project(): pl.pallas_call(functools.partial(project_kernel, halo=halo), out_shape=[j...  7.68 us
    all_to_all x1, starting transfers between devices, per_device(): arrived = lax.all_to_all(send, BANDS, 0, 0, tiled=True)  6.6 us
    all_to_all x1, waiting for transfers between devices, per_device(): asked = lax.all_to_all(asked[:, None, :], BANDS, 0, 0, tiled=True)[:, 0, :]  4.19 us
    ppermute x3, starting transfers between devices, per_device(): lax.ppermute(attended[d], 'tp', [(i, (i + d) % ranks) for i in range(rank...  4.07 us
  transfers between devices with their start and end apart: 13, of which 2 were waited for; matrix products, arithmetic and copies ran while one was open for 0% of the time, Pallas kernels for 25%

profile of v6, /device:TPU:4, one launch (start us, length us, event | category | flops | bytes accessed | tf_op | source)
XLA Modules:
  0.0 109.5 jit_solution(16381444625012359506)
XLA Ops:
  0.6 1.7 %collective-permute-start = (bf16[256,1024]{1,0:T(8,128)(2,1)}, bf16[256,1024]{1,0:T(8,128)(2,1)S(1)}, u32[]{:S(2)}, u32[]{:S(2)}) collective-permute-start(bf16[256,1024]{1,0:T(8,128)(2,1)} %w0_ref.1), channel_id=1, source_target_pairs={{0,1},{1,2},{2,3},{3,0},{4,5},{5,6},{6,7},{7,4},{8,9},{9,10},{10,1... | collective-permute-start | bytes 1572872 | tf_op jit(solution)/shard_map/ppermute | solution.py:531
  2.3 1.7 %collective-permute-start.1 = (bf16[256,1024]{1,0:T(8,128)(2,1)}, bf16[256,1024]{1,0:T(8,128)(2,1)S(1)}, u32[]{:S(2)}, u32[]{:S(2)}) collective-permute-start(bf16[256,1024]{1,0:T(8,128)(2,1)} %w0_ref.1), channel_id=1, source_target_pairs={{1,0},{2,1},{3,2},{0,3},{5,4},{6,5},{7,6},{4,7},{9,8},{10,9},{11,1... | collective-permute-start | bytes 1572872 | tf_op jit(solution)/shard_map/ppermute | solution.py:531
  4.6 1.7 %edges.1 = (bf16[272,1024]{1,0:T(8,128)(2,1)S(1)}, bf16[272,1024]{1,0:T(8,128)(2,1)S(1)}, bf16[1024,256]{1,0:T(8,128)(2,1)S(1)}, bf16[1024,256]{1,0:T(8,128)(2,1)S(1)}, bf16[1024,256]{1,0:T(8,128)(2,1)S(1)}) custom-call(s32[1]{0:T(128)S(6)} %copy.15.code_ref, bf16[512,1024]{1,0:T(8,128)(2,1)} %x_ref.3, bf16[1024,256]{1,0:T(8,128)(2,1)} %refs_0_.1, ...), custom_call_target="tpu_custom_call" | custom-call | tf_op jit(solution)/shard_map/edges/pallas_call | solution.py:78
  6.3 1.9 %collective-permute-start.2 = (bf16[272,1024]{1,0:T(8,128)(2,1)S(1)}, bf16[272,1024]{1,0:T(8,128)(2,1)S(1)}, u32[]{:S(2)}, u32[]{:S(2)}) collective-permute-start(bf16[272,1024]{1,0:T(8,128)(2,1)S(1)} %get-tuple-element.41.late_ref), channel_id=1, source_target_pairs={{0,4},{4,8},{8,12},{12,16},{16,20},{20,24},{24,28},{28,32},{32,36}... | collective-permute-start | bytes 1671176 | tf_op jit(solution)/shard_map/ppermute | solution.py:501
  8.3 6.3 %collective-permute-start.3 = (bf16[272,1024]{1,0:T(8,128)(2,1)S(1)}, bf16[272,1024]{1,0:T(8,128)(2,1)S(1)}, u32[]{:S(2)}, u32[]{:S(2)}) collective-permute-start(bf16[272,1024]{1,0:T(8,128)(2,1)S(1)} %get-tuple-element.40.early_ref), channel_id=1, source_target_pairs={{4,0},{8,4},{12,8},{16,12},{20,16},{24,20},{28,24},{32,28},{36,32}... | collective-permute-start | bytes 1671176 | tf_op jit(solution)/shard_map/ppermute | solution.py:501
  14.6 0.0 copy-start.1
  14.6 0.0 copy-start.2
  14.6 4.1 %project_own.1 = (bf16[3,512,256]{2,1,0:T(8,128)(2,1)S(1)}, bf16[3,512,256]{2,1,0:T(8,128)(2,1)S(1)}, bf16[3,512,256]{2,1,0:T(8,128)(2,1)S(1)}) custom-call(s32[1]{0:T(128)S(6)} %copy.15.code_ref, bf16[272,1024]{1,0:T(8,128)(2,1)S(1)} %get-tuple-element.40.early_ref, bf16[272,1024]{1,0:T(8,128)(2,1)S(1)} %get-tuple-element.41.late_ref, ...), custom_call_target="tpu_custom_call" | custom-call | tf_op jit(solution)/shard_map/project_own/pallas_call | solution.py:137
  18.8 0.0 collective-permute-done.w1_ref
  18.8 0.0 collective-permute-done.1.w3_ref
  18.8 0.4 collective-permute-start.4
  19.3 2.9 %collective-permute-start.5 = (bf16[128,1024]{1,0:T(8,128)(2,1)S(1)}, bf16[128,1024]{1,0:T(8,128)(2,1)S(1)}, u32[]{:S(2)}, u32[]{:S(2)}) collective-permute-start(bf16[128,1024]{1,0:T(8,128)(2,1)S(1)} %slice.7), channel_id=1, source_target_pairs={{1,0},{2,1},{3,2},{0,3},{5,4},{6,5},{7,6},{4,7},{9,8},{10,9},{11,1... | collective-permute-start | bytes 786440 | tf_op jit(solution)/shard_map/ppermute | solution.py:536
  22.3 1.0 ask.1
  23.2 3.5 %project_halo.1 = (bf16[3,512,256]{2,1,0:T(8,128)(2,1)S(1)}, bf16[3,512,256]{2,1,0:T(8,128)(2,1)S(1)}) custom-call(s32[1]{0:T(128)S(6)} %copy.15.code_ref, bf16[272,1024]{1,0:T(8,128)(2,1)S(1)} %collective-permute-done.2.early_ref, bf16[272,1024]{1,0:T(8,128)(2,1)S(1)} %collective-permute-done.3.late_ref, bf16[1024]{0:T(1024)(128)(2,1)} %gain_ref.3, ...), custom_call_target="tpu_custom_call" | custom-call | tf_op jit(solution)/shard_map/project_halo/pallas_call | solution.py:137
  26.8 9.0 %attend.1 = (bf16[384,256]{1,0:T(8,128)(2,1)S(1)}, bf16[384,256]{1,0:T(8,128)(2,1)S(1)}, bf16[384,256]{1,0:T(8,128)(2,1)S(1)}, bf16[384,256]{1,0:T(8,128)(2,1)S(1)}) custom-call(bf16[3,512,256]{2,1,0:T(8,128)(2,1)S(1)} %get-tuple-element.47.q_ref, bf16[3,512,256]{2,1,0:T(8,128)(2,1)S(1)} %get-tuple-element.48.k_ref, ...), custom_call_target="tpu_custom_call" | custom-call | tf_op jit(solution)/shard_map/attend/pallas_call | solution.py:203
  35.8 0.0 copy-start.5
  35.9 0.1 collective-permute-start.6
  36.0 2.7 %collective-permute-start.7 = (bf16[384,256]{1,0:T(8,128)(2,1)S(1)}, bf16[384,256]{1,0:T(8,128)(2,1)S(1)}, u32[]{:S(2)}, u32[]{:S(2)}) collective-permute-start(bf16[384,256]{1,0:T(8,128)(2,1)S(1)} %get-tuple-element.62), channel_id=1, source_target_pairs={{0,2},{1,3},{2,0},{3,1},{4,6},{5,7},{6,4},{7,5},{8,10},{9,11},{10,... | collective-permute-start | bytes 589832 | tf_op jit(solution)/shard_map/ppermute | solution.py:542
  38.6 1.3 %collective-permute-start.8 = (bf16[384,256]{1,0:T(8,128)(2,1)S(1)}, bf16[384,256]{1,0:T(8,128)(2,1)S(1)}, u32[]{:S(2)}, u32[]{:S(2)}) collective-permute-start(bf16[384,256]{1,0:T(8,128)(2,1)S(1)} %get-tuple-element.63), channel_id=1, source_target_pairs={{0,3},{1,0},{2,1},{3,2},{4,7},{5,4},{6,5},{7,6},{8,11},{9,8},{10,9... | collective-permute-start | bytes 589832 | tf_op jit(solution)/shard_map/ppermute | solution.py:542
  40.0 13.8 %all-to-all-start = ((s32[64,1,4]{2,1,0:T(1,128)}), s32[64,1,4]{2,1,0:T(1,128)S(1)}, u32[]{:S(2)}, u32[]{:S(2)}) async-start(s32[64,1,4]{2,1,0:T(1,128)} %bitcast.2), calls=%async_computation | async-start | bytes 65536 | tf_op jit(solution)/shard_map/all_to_all | solution.py:545
  53.8 3.4 %combine.1 = (bf16[3,128,1024]{2,1,0:T(8,128)(2,1)}, bf16[512,384]{1,0:T(8,128)(2,1)S(1)}) custom-call(s32[1]{0:T(128)S(6)} %copy.15.code_ref, bf16[384,256]{1,0:T(8,128)(2,1)S(1)} %get-tuple-element.60.att0_ref, bf16[384,256]{1,0:T(8,128)(2,1)S(1)} %collective-permute-done.6.att1_ref, bf16[384,256]{1,0:T(8,128)(2,1)S(1)} %collective-permute-done.7.att2_ref, ...), custom_call_target="tpu_custom_call" | custom-call | tf_op jit(solution)/shard_map/combine/pallas_call | solution.py:333
  57.3 4.2 %all-to-all-done = s32[64,1,4]{2,1,0:T(1,128)S(1)} async-done(((s32[64,1,4]{2,1,0:T(1,128)}), s32[64,1,4]{2,1,0:T(1,128)S(1)}, u32[]{:S(2)}, u32[]{:S(2)}) %all-to-all-start) | async-done | bytes 1056 | tf_op jit(solution)/shard_map/all_to_all | solution.py:545
  61.5 1.8 %serve.1 = bf16[64,16,384]{2,1,0:T(8,128)(2,1)} custom-call(s32[64,4]{1,0:T(8,128)S(1)} %bitcast.5, bf16[512,384]{1,0:T(8,128)(2,1)S(1)} %get-tuple-element.68.table_ref), custom_call_target="tpu_custom_call" | custom-call | tf_op jit(solution)/shard_map/serve/pallas_call | solution.py:358
  63.3 6.6 %all-to-all-start.1 = ((bf16[64,16,384]{2,1,0:T(8,128)(2,1)}), bf16[64,16,384]{2,1,0:T(8,128)(2,1)S(1)}, u32[]{:S(2)}, u32[]{:S(2)}) async-start(bf16[64,16,384]{2,1,0:T(8,128)(2,1)} %serve.1), calls=%async_computation.1 | async-start | bytes 1572864 | tf_op jit(solution)/shard_map/all_to_all | solution.py:551
  69.9 0.0 copy-start
  69.9 1.5 %fetch.1.before_ref.w_before_ref = bf16[3,512,512]{2,1,0:T(8,128)(2,1)S(1)} custom-call(bf16[9,512,512]{2,1,0:T(8,128)(2,1)} %conv_hbm_ref.1), custom_call_target="tpu_custom_call" | custom-call | tf_op jit(solution)/shard_map/fetch/pallas_call | solution.py:259
  71.4 21.8 %all-to-all-done.1.arrived_ref = bf16[64,16,384]{2,1,0:T(8,128)(2,1)S(1)} async-done(((bf16[64,16,384]{2,1,0:T(8,128)(2,1)}), bf16[64,16,384]{2,1,0:T(8,128)(2,1)S(1)}, u32[]{:S(2)}, u32[]{:S(2)}) %all-to-all-start.1) | async-done | bytes 786464 | tf_op jit(solution)/shard_map/all_to_all | solution.py:551
  93.1 1.0 inputs.1
  94.1 2.6 %collective-permute-start.9 = (bf16[48,512]{1,0:T(8,128)(2,1)S(1)}, bf16[48,512]{1,0:T(8,128)(2,1)S(1)}, u32[]{:S(2)}, u32[]{:S(2)}) collective-permute-start(bf16[48,512]{1,0:T(8,128)(2,1)S(1)} %get-tuple-element.73), channel_id=1, source_target_pairs={{0,1},{1,2},{2,3},{3,4},{4,5},{5,6},{6,7},{7,8},{8,9},{9,10},{10,1... | collective-permute-start | bytes 147464 | tf_op jit(solution)/shard_map/ppermute | solution.py:501
  96.7 7.8 %collective-permute-start.10 = (bf16[48,512]{1,0:T(8,128)(2,1)S(1)}, bf16[48,512]{1,0:T(8,128)(2,1)S(1)}, u32[]{:S(2)}, u32[]{:S(2)}) collective-permute-start(bf16[48,512]{1,0:T(8,128)(2,1)S(1)} %get-tuple-element.74), channel_id=1, source_target_pairs={{1,0},{2,1},{3,2},{4,3},{5,4},{6,5},{7,6},{8,7},{9,8},{10,9},{11,1... | collective-permute-start | bytes 147464 | tf_op jit(solution)/shard_map/ppermute | solution.py:501
  104.5 3.4 %convolve_inner.1 = (f32[384,512]{1,0:T(8,128)S(1)}, bf16[3,512,512]{2,1,0:T(8,128)(2,1)S(1)}) custom-call(bf16[8,48,512]{2,1,0:T(8,128)(2,1)S(1)} %get-tuple-element.72.x_ref, bf16[3,512,512]{2,1,0:T(8,128)(2,1)S(1)} %fetch.1.before_ref.w_before_ref, bf16[9,512,512]{2,1,0:T(8,128)(2,1)} %conv_hbm_ref.1), custom_call_target="tpu_custom_call" | custom-call | tf_op jit(solution)/shard_map/convolve_inner/pallas_call | solution.py:445
  107.9 1.6 %convolve_finish.1 = bf16[3,8,16,512]{3,2,1,0:T(8,128)(2,1)} custom-call(bf16[8,48,512]{2,1,0:T(8,128)(2,1)S(1)} %get-tuple-element.72.x_ref, bf16[48,512]{1,0:T(8,128)(2,1)S(1)} %collective-permute-done.9.before_ref, bf16[48,512]{1,0:T(8,128)(2,1)S(1)} %collective-permute-done.10.after_ref, bf16[3,512,512]{2,1,0:T(8,128)(2,1)S(1)} %fetch.1.before_ref.w_before_ref, ...), custom_call_target="tpu_custom_call" | custom-call | tf_op jit(solution)/shard_map/convolve_finish/pallas_call | solution.py:487
  (21 shorter events, 0.1 us)
Async XLA Ops:
  0.6 18.2 %collective-permute-start = (bf16[256,1024]{1,0:T(8,128)(2,1)}, bf16[256,1024]{1,0:T(8,128)(2,1)S(1)}, u32[]{:S(2)}, u32[]{:S(2)}) collective-permute-start(bf16[256,1024]{1,0:T(8,128)(2,1)} %w0_ref.1), channel_id=1, source_target_pairs={{0,1},{1,2},{2,3},{3,0},{4,5},{5,6},{6,7},{7,4},{8,9},{9,10},{10,1... | collective-permute-start | bytes 1572872 | tf_op jit(solution)/shard_map/ppermute | solution.py:531
  2.3 16.5 %collective-permute-start.1 = (bf16[256,1024]{1,0:T(8,128)(2,1)}, bf16[256,1024]{1,0:T(8,128)(2,1)S(1)}, u32[]{:S(2)}, u32[]{:S(2)}) collective-permute-start(bf16[256,1024]{1,0:T(8,128)(2,1)} %w0_ref.1), channel_id=1, source_target_pairs={{1,0},{2,1},{3,2},{0,3},{5,4},{6,5},{7,6},{4,7},{9,8},{10,9},{11,1... | collective-permute-start | bytes 1572872 | tf_op jit(solution)/shard_map/ppermute | solution.py:531
  6.3 16.9 %collective-permute-start.2 = (bf16[272,1024]{1,0:T(8,128)(2,1)S(1)}, bf16[272,1024]{1,0:T(8,128)(2,1)S(1)}, u32[]{:S(2)}, u32[]{:S(2)}) collective-permute-start(bf16[272,1024]{1,0:T(8,128)(2,1)S(1)} %get-tuple-element.41.late_ref), channel_id=1, source_target_pairs={{0,4},{4,8},{8,12},{12,16},{16,20},{20,24},{24,28},{28,32},{32,36}... | collective-permute-start | bytes 1671176 | tf_op jit(solution)/shard_map/ppermute | solution.py:501
  8.3 15.0 %collective-permute-start.3 = (bf16[272,1024]{1,0:T(8,128)(2,1)S(1)}, bf16[272,1024]{1,0:T(8,128)(2,1)S(1)}, u32[]{:S(2)}, u32[]{:S(2)}) collective-permute-start(bf16[272,1024]{1,0:T(8,128)(2,1)S(1)} %get-tuple-element.40.early_ref), channel_id=1, source_target_pairs={{4,0},{8,4},{12,8},{16,12},{20,16},{24,20},{28,24},{32,28},{36,32}... | collective-permute-start | bytes 1671176 | tf_op jit(solution)/shard_map/ppermute | solution.py:501
  14.6 7.7 %copy-start.1 = (s32[8,16,1]{1,2,0:T(1,128)S(1)}, s32[8,16,1]{1,2,0:T(1,128)}, u32[]{:S(2)}) copy-start(s32[8,16,1]{1,2,0:T(1,128)} %param.20) | copy-start | bytes 1540
  14.6 7.7 %copy-start.2 = (s32[8,16]{1,0:T(8,128)S(1)}, s32[8,16]{1,0:T(8,128)}, u32[]{:S(2)}) copy-start(s32[8,16]{1,0:T(8,128)} %tok_ref.1) | copy-start | bytes 1540
  18.8 8.0 %copy-start.3 = (bf16[256,1024]{1,0:T(8,128)(2,1)}, bf16[256,1024]{1,0:T(8,128)(2,1)S(1)}, u32[]{:S(2)}) copy-start(bf16[256,1024]{1,0:T(8,128)(2,1)S(1)} %collective-permute-done.w1_ref) | copy-start | bytes 1572868
  18.8 8.0 %copy-start.4 = (bf16[256,1024]{1,0:T(8,128)(2,1)}, bf16[256,1024]{1,0:T(8,128)(2,1)S(1)}, u32[]{:S(2)}) copy-start(bf16[256,1024]{1,0:T(8,128)(2,1)S(1)} %collective-permute-done.1.w3_ref) | copy-start | bytes 1572868
  18.8 17.0 %collective-permute-start.4 = (bf16[128,1024]{1,0:T(8,128)(2,1)S(1)}, bf16[128,1024]{1,0:T(8,128)(2,1)S(1)}, u32[]{:S(2)}, u32[]{:S(2)}) collective-permute-start(bf16[128,1024]{1,0:T(8,128)(2,1)S(1)} %slice.6), channel_id=1, source_target_pairs={{0,1},{1,2},{2,3},{3,0},{4,5},{5,6},{6,7},{7,4},{8,9},{9,10},{10,1... | collective-permute-start | bytes 786440 | tf_op jit(solution)/shard_map/ppermute | solution.py:536
  19.3 16.5 %collective-permute-start.5 = (bf16[128,1024]{1,0:T(8,128)(2,1)S(1)}, bf16[128,1024]{1,0:T(8,128)(2,1)S(1)}, u32[]{:S(2)}, u32[]{:S(2)}) collective-permute-start(bf16[128,1024]{1,0:T(8,128)(2,1)S(1)} %slice.7), channel_id=1, source_target_pairs={{1,0},{2,1},{3,2},{0,3},{5,4},{6,5},{7,6},{4,7},{9,8},{10,9},{11,1... | collective-permute-start | bytes 786440 | tf_op jit(solution)/shard_map/ppermute | solution.py:536
  35.8 18.0 %copy-start.5 = (bf16[128,1024]{1,0:T(8,128)(2,1)}, bf16[128,1024]{1,0:T(8,128)(2,1)S(1)}, u32[]{:S(2)}) copy-start(bf16[128,1024]{1,0:T(8,128)(2,1)S(1)} %collective-permute-done.4.top_ref) | copy-start | bytes 786436
  35.9 18.0 %copy-start.6 = (bf16[128,1024]{1,0:T(8,128)(2,1)}, bf16[128,1024]{1,0:T(8,128)(2,1)S(1)}, u32[]{:S(2)}) copy-start(bf16[128,1024]{1,0:T(8,128)(2,1)S(1)} %collective-permute-done.5.low_ref) | copy-start | bytes 786436
  35.9 17.9 %collective-permute-start.6 = (bf16[384,256]{1,0:T(8,128)(2,1)S(1)}, bf16[384,256]{1,0:T(8,128)(2,1)S(1)}, u32[]{:S(2)}, u32[]{:S(2)}) collective-permute-start(bf16[384,256]{1,0:T(8,128)(2,1)S(1)} %get-tuple-element.61), channel_id=1, source_target_pairs={{0,1},{1,2},{2,3},{3,0},{4,5},{5,6},{6,7},{7,4},{8,9},{9,10},{10,1... | collective-permute-start | bytes 589832 | tf_op jit(solution)/shard_map/ppermute | solution.py:542
  36.0 17.8 %collective-permute-start.7 = (bf16[384,256]{1,0:T(8,128)(2,1)S(1)}, bf16[384,256]{1,0:T(8,128)(2,1)S(1)}, u32[]{:S(2)}, u32[]{:S(2)}) collective-permute-start(bf16[384,256]{1,0:T(8,128)(2,1)S(1)} %get-tuple-element.62), channel_id=1, source_target_pairs={{0,2},{1,3},{2,0},{3,1},{4,6},{5,7},{6,4},{7,5},{8,10},{9,11},{10,... | collective-permute-start | bytes 589832 | tf_op jit(solution)/shard_map/ppermute | solution.py:542
  38.6 15.2 %collective-permute-start.8 = (bf16[384,256]{1,0:T(8,128)(2,1)S(1)}, bf16[384,256]{1,0:T(8,128)(2,1)S(1)}, u32[]{:S(2)}, u32[]{:S(2)}) collective-permute-start(bf16[384,256]{1,0:T(8,128)(2,1)S(1)} %get-tuple-element.63), channel_id=1, source_target_pairs={{0,3},{1,0},{2,1},{3,2},{4,7},{5,4},{6,5},{7,6},{8,11},{9,8},{10,9... | collective-permute-start | bytes 589832 | tf_op jit(solution)/shard_map/ppermute | solution.py:542
  40.0 21.5 %all-to-all-start = ((s32[64,1,4]{2,1,0:T(1,128)}), s32[64,1,4]{2,1,0:T(1,128)S(1)}, u32[]{:S(2)}, u32[]{:S(2)}) async-start(s32[64,1,4]{2,1,0:T(1,128)} %bitcast.2), calls=%async_computation | async-start | bytes 65536 | tf_op jit(solution)/shard_map/all_to_all | solution.py:545
  63.3 29.8 %all-to-all-start.1 = ((bf16[64,16,384]{2,1,0:T(8,128)(2,1)}), bf16[64,16,384]{2,1,0:T(8,128)(2,1)S(1)}, u32[]{:S(2)}, u32[]{:S(2)}) async-start(bf16[64,16,384]{2,1,0:T(8,128)(2,1)} %serve.1), calls=%async_computation.1 | async-start | bytes 1572864 | tf_op jit(solution)/shard_map/all_to_all | solution.py:551
  69.9 23.2 %copy-start = (bf16[8,16,512]{2,1,0:T(8,128)(2,1)S(1)}, bf16[8,16,512]{2,1,0:T(8,128)(2,1)}, u32[]{:S(2)}) copy-start(bf16[8,16,512]{2,1,0:T(8,128)(2,1)} %reg_ref.1) | copy-start | bytes 393220
  94.1 13.8 %collective-permute-start.9 = (bf16[48,512]{1,0:T(8,128)(2,1)S(1)}, bf16[48,512]{1,0:T(8,128)(2,1)S(1)}, u32[]{:S(2)}, u32[]{:S(2)}) collective-permute-start(bf16[48,512]{1,0:T(8,128)(2,1)S(1)} %get-tuple-element.73), channel_id=1, source_target_pairs={{0,1},{1,2},{2,3},{3,4},{4,5},{5,6},{6,7},{7,8},{8,9},{9,10},{10,1... | collective-permute-start | bytes 147464 | tf_op jit(solution)/shard_map/ppermute | solution.py:501
  96.7 11.2 %collective-permute-start.10 = (bf16[48,512]{1,0:T(8,128)(2,1)S(1)}, bf16[48,512]{1,0:T(8,128)(2,1)S(1)}, u32[]{:S(2)}, u32[]{:S(2)}) collective-permute-start(bf16[48,512]{1,0:T(8,128)(2,1)S(1)} %get-tuple-element.74), channel_id=1, source_target_pairs={{1,0},{2,1},{3,2},{4,3},{5,4},{6,5},{7,6},{8,7},{9,8},{10,9},{11,1... | collective-permute-start | bytes 147464 | tf_op jit(solution)/shard_map/ppermute | solution.py:501

commit v7 on v6

--- a/solution.py
+++ b/solution.py
@@ -221,12 +221,36 @@
     return jnp.sum(jnp.where(mine, wide, 0.0), 0, keepdims=True)
 
 
-def ask_kernel(band_ref, tok_ref, ask_ref):
-    bands = ask_ref.shape[0]
-    named = cells_row(band_ref[...])
-    token = cells_row(tok_ref[...])
-    cells = named.shape[1]
-    match = (named.astype(jnp.int32) == iota((bands, cells), 0)).astype(jnp.float32)
+def names_kernel(band_ref, tok_ref, out_ref):
+    names = cells_row(band_ref[...]) * 128.0 + cells_row(tok_ref[...])
+    out_ref[...] = names.astype(jnp.int32)
+
+
+def make_names(band, tok):
+    return pl.pallas_call(
+        names_kernel,
+        out_shape=jax.ShapeDtypeStruct((1, band.size), jnp.int32),
+        in_specs=[ON_CHIP] * 2,
+        out_specs=ON_CHIP,
+        compiler_params=pltpu.CompilerParams(vmem_limit_bytes=2 * MIB),
+        name="names",
+    )(band, tok)
+
+
+def pass_on(rows, distance):
+    count = lax.axis_size(BANDS)
+    came = lax.ppermute(rows, BANDS, [(i, (i + distance) % count) for i in range(count)])
+    return jnp.concatenate([rows, came])
+
+
+def pick_kernel(names_ref, pick_ref):
+    bands, cells = names_ref.shape
+    rows, wide = pick_ref.shape
+    me = lax.axis_index(BANDS)
+    names = names_ref[...]
+    match = lax.shift_right_arithmetic(names, jnp.full_like(names, 7)) == me
+    match = match.astype(jnp.float32)
+    token = lax.bitwise_and(names, 127).astype(jnp.float32)
     before = (iota((cells, cells), 0) < iota((cells, cells), 1)).astype(jnp.float32)
     slot = dot(match.astype(jnp.bfloat16), before.astype(jnp.bfloat16))
     lanes = iota((bands, cells), 1)
@@ -235,18 +259,26 @@
         hit = jnp.where(slot == s, match, 0.0)
         token_s = jnp.sum(hit * (token + 1.0), -1, keepdims=True) - 1.0
         asked = jnp.where(lanes == s, token_s, asked)
-    ask_ref[...] = asked[:, :4].astype(jnp.int32)
-
-
-def ask(band, tok, bands):
-    return pl.pallas_call(
-        ask_kernel,
-        out_shape=jax.ShapeDtypeStruct((bands, 4), jnp.int32),
-        in_specs=[ON_CHIP] * 2,
+    r = iota((rows, 1), 0)
+    row_of = lax.rem(me + bands - r // 16, bands)
+    spread = (iota((rows, bands), 1) == row_of).astype(jnp.float32).astype(jnp.bfloat16)
+    per_row = dot(spread, asked.astype(jnp.bfloat16))
+    mine = iota((rows, cells), 1) == (r // 4) % 4
+    token_r = jnp.sum(jnp.where(mine, per_row, 0.0), -1, keepdims=True).astype(jnp.int32)
+    target = jnp.where(token_r >= 0, (r % 4) * cells + token_r, -1)
+    pick_ref[...] = (iota((rows, wide), 1) == target).astype(jnp.float32).astype(jnp.bfloat16)
+
+
+def make_pick(names):
+    bands, cells = names.shape
+    return pl.pallas_call(
+        pick_kernel,
+        out_shape=jax.ShapeDtypeStruct((bands * 16, 4 * cells), jnp.bfloat16),
+        in_specs=[ON_CHIP],
         out_specs=ON_CHIP,
-        compiler_params=pltpu.CompilerParams(vmem_limit_bytes=4 * MIB),
-        name="ask",
-    )(band, tok)
+        compiler_params=pltpu.CompilerParams(vmem_limit_bytes=6 * MIB),
+        name="pick",
+    )(names)
 
 
 def fetch_kernel(conv_hbm_ref, taps_ref, sem):
@@ -267,18 +299,7 @@
     )(conv_w)
 
 
-def pick_rows(asked, rows, cells):
-    bands = asked.shape[0]
-    spread = (iota((rows, bands), 0) // 16 == iota((rows, bands), 1)).astype(jnp.float32)
-    per_row = dot(spread.astype(jnp.bfloat16), asked.astype(jnp.float32).astype(jnp.bfloat16))
-    r = iota((rows, 1), 0)
-    mine = iota((rows, 4), 1) == (r // 4) % 4
-    token_r = jnp.sum(jnp.where(mine, per_row, 0.0), -1, keepdims=True).astype(jnp.int32)
-    target = jnp.where(token_r >= 0, (r % 4) * cells + token_r, -1)
-    return (iota((rows, 4 * cells), 1) == target).astype(jnp.float32).astype(jnp.bfloat16)
-
-
-def combine_kernel(code_ref, att0_ref, att1_ref, att2_ref, att3_ref, w0_ref, w1_ref, w3_ref, top_ref, low_ref, x_ref, w_bound_ref, out_ref, table_ref, own_ref, held_ref, bound_ref, sems):
+def combine_kernel(code_ref, att0_ref, att1_ref, att2_ref, att3_ref, w0_ref, w1_ref, w3_ref, top_ref, low_ref, x_ref, w_bound_ref, pick_ref, out_ref, send_ref, table_ref, own_ref, held_ref, bound_ref, sems):
     cols = att0_ref.shape[1]
     half = cols // 2
     features = x_ref.shape[1]
@@ -323,21 +344,26 @@
             table_ref[part * quarter : (part + 1) * quarter, s * 128 : (s + 1) * 128] = forced[
                 s * quarter : (s + 1) * quarter, part * 128 : (part + 1) * 128
             ]
-
-
-def combine(code, att, w_outs, x, w_bound):
+    picked = dot(pick_ref[...], table_ref[...])
+    send_ref[...] = picked.astype(jnp.bfloat16).reshape(send_ref.shape)
+
+
+def combine(code, att, w_outs, x, w_bound, pick):
     quarter = att[0].shape[0] // 3
     shape = (3, quarter, x.shape[1])
     table = (quarter * w_bound.shape[1] // 128, 384)
+    sent = (pick.shape[0] // 16, 16, 384)
     far = [in_hbm(a) for a in (*w_outs, x, w_bound)]
     return pl.pallas_call(
         combine_kernel,
-        out_shape=[jax.ShapeDtypeStruct(s, jnp.bfloat16) for s in (shape, table)],
+        out_shape=[jax.ShapeDtypeStruct(s, jnp.bfloat16) for s in (shape, sent)],
         in_specs=[SCALARS]
         + [pl.BlockSpec(a.shape, lambda: (0, 0)) for a in att]
-        + [pl.BlockSpec(memory_space=pltpu.HBM)] * len(far),
-        out_specs=[pl.BlockSpec(shape, lambda: (0, 0, 0)), ON_CHIP],
+        + [pl.BlockSpec(memory_space=pltpu.HBM)] * len(far)
+        + [ON_CHIP],
+        out_specs=[pl.BlockSpec(s, lambda: (0, 0, 0)) for s in (shape, sent)],
         scratch_shapes=[
+            pltpu.VMEM(table, jnp.bfloat16),
             pltpu.VMEM((quarter, x.shape[1]), jnp.bfloat16),
             pltpu.VMEM((len(att) * att[0].shape[1], x.shape[1]), jnp.bfloat16),
             pltpu.VMEM(w_bound.shape, jnp.bfloat16),
@@ -345,24 +371,7 @@
         ],
         compiler_params=pltpu.CompilerParams(vmem_limit_bytes=16 * MIB),
         name="combine",
-    )(code, *att, *far)
-
-
-def serve_kernel(asked_ref, table_ref, send_ref):
-    pick = pick_rows(asked_ref[...], send_ref.shape[0] * 16, table_ref.shape[0] // 4)
-    send_ref[...] = dot(pick, table_ref[...]).astype(jnp.bfloat16).reshape(send_ref.shape)
-
-
-def serve(asked, table):
-    shape = (asked.shape[0], 16, table.shape[1])
-    return pl.pallas_call(
-        serve_kernel,
-        out_shape=jax.ShapeDtypeStruct(shape, jnp.bfloat16),
-        in_specs=[ON_CHIP] * 2,
-        out_specs=pl.BlockSpec(shape, lambda: (0, 0, 0)),
-        compiler_params=pltpu.CompilerParams(vmem_limit_bytes=8 * MIB),
-        name="serve",
-    )(asked, table)
+    )(code, *att, *far, pick)
 
 
 def inputs_kernel(arrived_ref, band_ref, reg_ref, out_ref, first_ref, last_ref):
@@ -530,21 +539,27 @@
     before, after = neighbours(last, first, BANDS)
     w1, w3 = lax.ppermute(w_out, "tp", up), lax.ppermute(w_out, "tp", down)
     q, k, v = project(band_codes, [first, last], gain, weights, False)
-    asked = ask(cell_band, src_tok, bands)
+    names = pass_on(make_names(cell_band, src_tok), 1)
+    q, names = lax.optimization_barrier((q, names))
+    names = pass_on(pass_on(names, 2), 4)
     q, w1, w3 = lax.optimization_barrier((q, w1, w3))
     middle = w_out.shape[0] // 2
     top, low = lax.ppermute(w1[:middle], "tp", up), lax.ppermute(w3[middle:], "tp", down)
-    q, before, after = lax.optimization_barrier((q, before, after))
+    q, before, after, names = lax.optimization_barrier((q, before, after, names))
     k_halo, v_halo = project(band_codes, [before, after], gain, weights[1:], True)
+    k_halo, names = lax.optimization_barrier((k_halo, names))
+    names = pass_on(names, 8)
     attended = attend(q, k, v, k_halo, v_halo, ranks, bands)
-    attended, asked, top, low = lax.optimization_barrier((attended, asked, top, low))
+    attended, names, top, low = lax.optimization_barrier((attended, names, top, low))
     attended = [attended[0]] + [
         lax.ppermute(attended[d], "tp", [(i, (i + d) % ranks) for i in range(ranks)])
         for d in range(1, ranks)
     ]
-    asked = lax.all_to_all(asked[:, None, :], BANDS, 0, 0, tiled=True)[:, 0, :]
-    global_out, table = combine(band_codes, attended, [w_out, w1, w3, top, low], global_state, w_bound)
-    send = serve(asked, table)
+    for distance in (16, 32):
+        names = pass_on(names, distance)
+    global_out, send = combine(
+        band_codes, attended, [w_out, w1, w3, top, low], global_state, w_bound, make_pick(names)
+    )
     conv_w, send = lax.optimization_barrier((conv_w, send))
     conv_w = in_hbm(conv_w)
     taps = fetch_taps(conv_w)

time: 110 us -> 124 us (1.13)
  waiting for transfers between devices: 26 us -> 39.2 us
  starting transfers between devices: 49.8 us -> 51.5 us
    ppermute x0 -> x6, waiting for transfers between devices: none -> 17.4 us  [pass_on(): lax.ppermute(rows, BANDS, [(i, (i + distance) % count) for i in range(cou...]
    all_to_all x1 -> x0, starting transfers between devices: 13.8 us -> none  [per_device(): asked = lax.all_to_all(asked[:, None, :], BANDS, 0, 0, tiled=True)[:, 0, :]]
    ppermute x0 -> x6, starting transfers between devices: none -> 12.9 us  [pass_on(): lax.ppermute(rows, BANDS, [(i, (i + distance) % count) for i in range(cou...]
    all_to_all x1 -> x0, waiting for transfers between devices: 4.19 us -> none  [per_device(): asked = lax.all_to_all(asked[:, None, :], BANDS, 0, 0, tiled=True)[:, 0, :]]
    all_to_all x1, starting transfers between devices: 6.6 us -> 8.69 us  [per_device(): arrived = lax.all_to_all(send, BANDS, 0, 0, tiled=True)]
    pallas_call x2, Pallas kernels: 2.77 us -> 0.98 us  [the longest x1 0.85 us: make_pick(): pl.pallas_call(pick_kernel, out_shape=jax.ShapeDtypeStruct((bands * 16, 4...]
    pallas_call x1, Pallas kernels: 3.45 us -> 4.84 us  [combine(): pl.pallas_call(combine_kernel, out_shape=[jax.ShapeDtypeStruct(s, jnp.bfl...]
  transfers between devices with their start and end apart: 13 -> 18, of which waited for: 2 -> 5; matrix products, arithmetic and copies ran while one was open for 0% -> 0% of each run, Pallas kernels for 25% -> 20%
where the time goes in v7:
time: 124 us
  starting transfers between devices  51.5 us (42%)
  waiting for transfers between devices  39.2 us (32%)
  Pallas kernels  31.6 us (25%)
  between operations  1.62 us (1%)
    all_to_all x1, waiting for transfers between devices, per_device(): arrived = lax.all_to_all(send, BANDS, 0, 0, tiled=True)  21.7 us
    ppermute x4, starting transfers between devices, neighbours(): return (lax.ppermute(last, axis, up), lax.ppermute(first, axis, down))  18.6 us
    ppermute x6, waiting for transfers between devices, pass_on(): lax.ppermute(rows, BANDS, [(i, (i + distance) % count) for i in range(cou...  17.4 us
    ppermute x6, starting transfers between devices, pass_on(): lax.ppermute(rows, BANDS, [(i, (i + distance) % count) for i in range(cou...  12.9 us
    pallas_call x1, Pallas kernels, attend(): pl.pallas_call(functools.partial(attend_kernel, bands=bands), out_shape=[...  8.99 us
    all_to_all x1, starting transfers between devices, per_device(): arrived = lax.all_to_all(send, BANDS, 0, 0, tiled=True)  8.69 us
    pallas_call x2, Pallas kernels, project(): pl.pallas_call(functools.partial(project_kernel, halo=halo), out_shape=[j...  7.7 us
    pallas_call x1, Pallas kernels, combine(): pl.pallas_call(combine_kernel, out_shape=[jax.ShapeDtypeStruct(s, jnp.bfl...  4.84 us
  transfers between devices with their start and end apart: 18, of which 5 were waited for; matrix products, arithmetic and copies ran while one was open for 0% of the time, Pallas kernels for 20%

profile of v7, /device:TPU:4, one launch (start us, length us, event | category | flops | bytes accessed | tf_op | source)
XLA Modules:
  0.0 124.1 jit_solution(1939788210455167690)
XLA Ops:
  0.7 1.7 %collective-permute-start.1 = (bf16[256,1024]{1,0:T(8,128)(2,1)}, bf16[256,1024]{1,0:T(8,128)(2,1)S(1)}, u32[]{:S(2)}, u32[]{:S(2)}) collective-permute-start(bf16[256,1024]{1,0:T(8,128)(2,1)} %w0_ref.1), channel_id=1, source_target_pairs={{0,1},{1,2},{2,3},{3,0},{4,5},{5,6},{6,7},{7,4},{8,9},{9,10},{10,1... | collective-permute-start | bytes 1572872 | tf_op jit(solution)/shard_map/ppermute | solution.py:540
  2.3 1.7 %collective-permute-start.2 = (bf16[256,1024]{1,0:T(8,128)(2,1)}, bf16[256,1024]{1,0:T(8,128)(2,1)S(1)}, u32[]{:S(2)}, u32[]{:S(2)}) collective-permute-start(bf16[256,1024]{1,0:T(8,128)(2,1)} %w0_ref.1), channel_id=1, source_target_pairs={{1,0},{2,1},{3,2},{0,3},{5,4},{6,5},{7,6},{4,7},{9,8},{10,9},{11,1... | collective-permute-start | bytes 1572872 | tf_op jit(solution)/shard_map/ppermute | solution.py:540
  4.6 1.7 %edges.1 = (bf16[272,1024]{1,0:T(8,128)(2,1)S(1)}, bf16[272,1024]{1,0:T(8,128)(2,1)S(1)}, bf16[1024,256]{1,0:T(8,128)(2,1)S(1)}, bf16[1024,256]{1,0:T(8,128)(2,1)S(1)}, bf16[1024,256]{1,0:T(8,128)(2,1)S(1)}) custom-call(s32[1]{0:T(128)S(6)} %copy.14.code_ref, bf16[512,1024]{1,0:T(8,128)(2,1)} %x_ref.3, bf16[1024,256]{1,0:T(8,128)(2,1)} %refs_0_.1, ...), custom_call_target="tpu_custom_call" | custom-call | tf_op jit(solution)/shard_map/edges/pallas_call | solution.py:78
  6.3 1.9 %collective-permute-start.3 = (bf16[272,1024]{1,0:T(8,128)(2,1)S(1)}, bf16[272,1024]{1,0:T(8,128)(2,1)S(1)}, u32[]{:S(2)}, u32[]{:S(2)}) collective-permute-start(bf16[272,1024]{1,0:T(8,128)(2,1)S(1)} %get-tuple-element.46.late_ref), channel_id=1, source_target_pairs={{0,4},{4,8},{8,12},{12,16},{16,20},{20,24},{24,28},{28,32},{32,36}... | collective-permute-start | bytes 1671176 | tf_op jit(solution)/shard_map/ppermute | solution.py:510
  8.3 6.3 %collective-permute-start.4 = (bf16[272,1024]{1,0:T(8,128)(2,1)S(1)}, bf16[272,1024]{1,0:T(8,128)(2,1)S(1)}, u32[]{:S(2)}, u32[]{:S(2)}) collective-permute-start(bf16[272,1024]{1,0:T(8,128)(2,1)S(1)} %get-tuple-element.45.early_ref), channel_id=1, source_target_pairs={{4,0},{8,4},{12,8},{16,12},{20,16},{24,20},{28,24},{32,28},{36,32}... | collective-permute-start | bytes 1671176 | tf_op jit(solution)/shard_map/ppermute | solution.py:510
  14.6 0.1 names.1
  14.8 4.1 %project_own.1 = (bf16[3,512,256]{2,1,0:T(8,128)(2,1)S(1)}, bf16[3,512,256]{2,1,0:T(8,128)(2,1)S(1)}, bf16[3,512,256]{2,1,0:T(8,128)(2,1)S(1)}) custom-call(s32[1]{0:T(128)S(6)} %copy.14.code_ref, bf16[272,1024]{1,0:T(8,128)(2,1)S(1)} %get-tuple-element.45.early_ref, bf16[272,1024]{1,0:T(8,128)(2,1)S(1)} %get-tuple-element.46.late_ref, ...), custom_call_target="tpu_custom_call" | custom-call | tf_op jit(solution)/shard_map/project_own/pallas_call | solution.py:137
  18.9 2.8 %collective-permute-done = s32[1,128]{1,0:T(1,128)S(1)} collective-permute-done((s32[1,128]{1,0:T(1,128)S(1)}, s32[1,128]{1,0:T(1,128)S(1)}, u32[]{:S(2)}, u32[]{:S(2)}) %collective-permute-start) | collective-permute-done | bytes 544 | tf_op jit(solution)/shard_map/ppermute | solution.py:242
  21.8 0.4 collective-permute-start.8
  22.3 2.9 %collective-permute-start.9 = (bf16[128,1024]{1,0:T(8,128)(2,1)S(1)}, bf16[128,1024]{1,0:T(8,128)(2,1)S(1)}, u32[]{:S(2)}, u32[]{:S(2)}) collective-permute-start(bf16[128,1024]{1,0:T(8,128)(2,1)S(1)} %slice.7), channel_id=1, source_target_pairs={{1,0},{2,1},{3,2},{0,3},{5,4},{6,5},{7,6},{4,7},{9,8},{10,9},{11,1... | collective-permute-start | bytes 786440 | tf_op jit(solution)/shard_map/ppermute | solution.py:547
  25.2 4.1 %collective-permute-done.5 = s32[2,128]{1,0:T(2,128)S(1)} collective-permute-done((s32[2,128]{1,0:T(2,128)S(1)}, s32[2,128]{1,0:T(2,128)S(1)}, u32[]{:S(2)}, u32[]{:S(2)}) %collective-permute-start.5) | collective-permute-done | bytes 1056 | tf_op jit(solution)/shard_map/ppermute | solution.py:242
  29.4 2.6 %collective-permute-start.6 = (s32[4,128]{1,0:T(4,128)S(1)}, s32[4,128]{1,0:T(4,128)S(1)}, u32[]{:S(2)}, u32[]{:S(2)}) collective-permute-start(s32[4,128]{1,0:T(4,128)S(1)} %pad_add_fusion.4), channel_id=1, source_target_pairs={{0,16},{4,20},{8,24},{12,28},{16,32},{20,36},{24,40},{28,44},{32,4... | collective-permute-start | bytes 6152 | tf_op jit(solution)/shard_map/ppermute | solution.py:242
  32.0 2.8 %collective-permute-done.6 = s32[4,128]{1,0:T(4,128)S(1)} collective-permute-done((s32[4,128]{1,0:T(4,128)S(1)}, s32[4,128]{1,0:T(4,128)S(1)}, u32[]{:S(2)}, u32[]{:S(2)}) %collective-permute-start.6) | collective-permute-done | bytes 2080 | tf_op jit(solution)/shard_map/ppermute | solution.py:242
  34.8 3.6 %project_halo.1 = (bf16[3,512,256]{2,1,0:T(8,128)(2,1)S(1)}, bf16[3,512,256]{2,1,0:T(8,128)(2,1)S(1)}) custom-call(s32[1]{0:T(128)S(6)} %copy.14.code_ref, bf16[272,1024]{1,0:T(8,128)(2,1)S(1)} %collective-permute-done.3.early_ref, bf16[272,1024]{1,0:T(8,128)(2,1)S(1)} %collective-permute-done.4.late_ref, bf16[1024]{0:T(1024)(128)(2,1)} %gain_ref.3, ...), custom_call_target="tpu_custom_call" | custom-call | tf_op jit(solution)/shard_map/project_halo/pallas_call | solution.py:137
  38.4 1.7 %collective-permute-start.7 = (s32[8,128]{1,0:T(8,128)S(1)}, s32[8,128]{1,0:T(8,128)S(1)}, u32[]{:S(2)}, u32[]{:S(2)}) collective-permute-start(s32[8,128]{1,0:T(8,128)S(1)} %pad_add_fusion.3), channel_id=1, source_target_pairs={{0,32},{4,36},{8,40},{12,44},{16,48},{20,52},{24,56},{28,60},{32,6... | collective-permute-start | bytes 12296 | tf_op jit(solution)/shard_map/ppermute | solution.py:242
  40.1 9.0 %attend.1 = (bf16[384,256]{1,0:T(8,128)(2,1)S(1)}, bf16[384,256]{1,0:T(8,128)(2,1)S(1)}, bf16[384,256]{1,0:T(8,128)(2,1)S(1)}, bf16[384,256]{1,0:T(8,128)(2,1)S(1)}) custom-call(bf16[3,512,256]{2,1,0:T(8,128)(2,1)S(1)} %get-tuple-element.54.q_ref, bf16[3,512,256]{2,1,0:T(8,128)(2,1)S(1)} %get-tuple-element.55.k_ref, ...), custom_call_target="tpu_custom_call" | custom-call | tf_op jit(solution)/shard_map/attend/pallas_call | solution.py:203
  49.2 0.0 copy-start.5
  49.2 8.6 %collective-permute-start.13 = (s32[16,128]{1,0:T(8,128)S(1)}, s32[16,128]{1,0:T(8,128)S(1)}, u32[]{:S(2)}, u32[]{:S(2)}) collective-permute-start(s32[16,128]{1,0:T(8,128)S(1)} %pad_add_fusion.2), channel_id=1, source_target_pairs={{0,64},{4,68},{8,72},{12,76},{16,80},{20,84},{24,88},{28,92},{32,9... | collective-permute-start | bytes 24584 | tf_op jit(solution)/shard_map/ppermute | solution.py:242
  57.8 0.4 collective-permute-start.10
  58.1 2.9 %collective-permute-start.11 = (bf16[384,256]{1,0:T(8,128)(2,1)S(1)}, bf16[384,256]{1,0:T(8,128)(2,1)S(1)}, u32[]{:S(2)}, u32[]{:S(2)}) collective-permute-start(bf16[384,256]{1,0:T(8,128)(2,1)S(1)} %get-tuple-element.72), channel_id=1, source_target_pairs={{0,2},{1,3},{2,0},{3,1},{4,6},{5,7},{6,4},{7,5},{8,10},{9,11},{10,... | collective-permute-start | bytes 589832 | tf_op jit(solution)/shard_map/ppermute | solution.py:555
  61.0 1.3 %collective-permute-start.12 = (bf16[384,256]{1,0:T(8,128)(2,1)S(1)}, bf16[384,256]{1,0:T(8,128)(2,1)S(1)}, u32[]{:S(2)}, u32[]{:S(2)}) collective-permute-start(bf16[384,256]{1,0:T(8,128)(2,1)S(1)} %get-tuple-element.73), channel_id=1, source_target_pairs={{0,3},{1,0},{2,1},{3,2},{4,7},{5,4},{6,5},{7,6},{8,11},{9,8},{10,9... | collective-permute-start | bytes 589832 | tf_op jit(solution)/shard_map/ppermute | solution.py:555
  62.4 7.6 %collective-permute-done.14 = s32[32,128]{1,0:T(8,128)S(1)} collective-permute-done((s32[32,128]{1,0:T(8,128)S(1)}, s32[32,128]{1,0:T(8,128)S(1)}, u32[]{:S(2)}, u32[]{:S(2)}) %collective-permute-start.14) | collective-permute-done | bytes 16416 | tf_op jit(solution)/shard_map/ppermute | solution.py:242
  70.0 0.8 pick.1.pick_ref
  70.9 4.8 %combine.1 = (bf16[3,128,1024]{2,1,0:T(8,128)(2,1)}, bf16[64,16,384]{2,1,0:T(8,128)(2,1)}) custom-call(s32[1]{0:T(128)S(6)} %copy.14.code_ref, bf16[384,256]{1,0:T(8,128)(2,1)S(1)} %get-tuple-element.70.att0_ref, bf16[384,256]{1,0:T(8,128)(2,1)S(1)} %collective-permute-done.10.att1_ref, bf16[384,256]{1,0:T(8,128)(2,1)S(1)} %collective-permute-done.11.att2_ref, ...), custom_call_target="tpu_custom_call" | custom-call | tf_op jit(solution)/shard_map/combine/pallas_call | solution.py:357
  75.8 8.7 %all-to-all-start = ((bf16[64,16,384]{2,1,0:T(8,128)(2,1)}), bf16[64,16,384]{2,1,0:T(8,128)(2,1)S(1)}, u32[]{:S(2)}, u32[]{:S(2)}) async-start(bf16[64,16,384]{2,1,0:T(8,128)(2,1)} %get-tuple-element.80), calls=%async_computation | async-start | bytes 1572864 | tf_op jit(solution)/shard_map/all_to_all | solution.py:566
  84.5 1.5 %fetch.1.before_ref.w_before_ref = bf16[3,512,512]{2,1,0:T(8,128)(2,1)S(1)} custom-call(bf16[9,512,512]{2,1,0:T(8,128)(2,1)} %conv_hbm_ref.1), custom_call_target="tpu_custom_call" | custom-call | tf_op jit(solution)/shard_map/fetch/pallas_call | solution.py:291
  86.0 21.7 %all-to-all-done.arrived_ref = bf16[64,16,384]{2,1,0:T(8,128)(2,1)S(1)} async-done(((bf16[64,16,384]{2,1,0:T(8,128)(2,1)}), bf16[64,16,384]{2,1,0:T(8,128)(2,1)S(1)}, u32[]{:S(2)}, u32[]{:S(2)}) %all-to-all-start) | async-done | bytes 786464 | tf_op jit(solution)/shard_map/all_to_all | solution.py:566
  107.7 1.0 inputs.1
  108.7 2.3 %collective-permute-start.15 = (bf16[48,512]{1,0:T(8,128)(2,1)S(1)}, bf16[48,512]{1,0:T(8,128)(2,1)S(1)}, u32[]{:S(2)}, u32[]{:S(2)}) collective-permute-start(bf16[48,512]{1,0:T(8,128)(2,1)S(1)} %get-tuple-element.83), channel_id=1, source_target_pairs={{0,1},{1,2},{2,3},{3,4},{4,5},{5,6},{6,7},{7,8},{8,9},{9,10},{10,1... | collective-permute-start | bytes 147464 | tf_op jit(solution)/shard_map/ppermute | solution.py:510
  111.0 8.1 %collective-permute-start.16 = (bf16[48,512]{1,0:T(8,128)(2,1)S(1)}, bf16[48,512]{1,0:T(8,128)(2,1)S(1)}, u32[]{:S(2)}, u32[]{:S(2)}) collective-permute-start(bf16[48,512]{1,0:T(8,128)(2,1)S(1)} %get-tuple-element.84), channel_id=1, source_target_pairs={{1,0},{2,1},{3,2},{4,3},{5,4},{6,5},{7,6},{8,7},{9,8},{10,9},{11,1... | collective-permute-start | bytes 147464 | tf_op jit(solution)/shard_map/ppermute | solution.py:510
  119.1 3.4 %convolve_inner.1 = (f32[384,512]{1,0:T(8,128)S(1)}, bf16[3,512,512]{2,1,0:T(8,128)(2,1)S(1)}) custom-call(bf16[8,48,512]{2,1,0:T(8,128)(2,1)S(1)} %get-tuple-element.82.x_ref, bf16[3,512,512]{2,1,0:T(8,128)(2,1)S(1)} %fetch.1.before_ref.w_before_ref, bf16[9,512,512]{2,1,0:T(8,128)(2,1)} %conv_hbm_ref.1), custom_call_target="tpu_custom_call" | custom-call | tf_op jit(solution)/shard_map/convolve_inner/pallas_call | solution.py:454
  122.5 1.6 %convolve_finish.1 = bf16[3,8,16,512]{3,2,1,0:T(8,128)(2,1)} custom-call(bf16[8,48,512]{2,1,0:T(8,128)(2,1)S(1)} %get-tuple-element.82.x_ref, bf16[48,512]{1,0:T(8,128)(2,1)S(1)} %collective-permute-done.15.before_ref, bf16[48,512]{1,0:T(8,128)(2,1)S(1)} %collective-permute-done.16.after_ref, bf16[3,512,512]{2,1,0:T(8,128)(2,1)S(1)} %fetch.1.before_ref.w_before_ref, ...), custom_call_target="tpu_custom_call" | custom-call | tf_op jit(solution)/shard_map/convolve_finish/pallas_call | solution.py:496
  (37 shorter events, 0.1 us)
Async XLA Ops:
  0.6 14.0 %copy-start.1 = (s32[8,16,1]{1,2,0:T(1,128)S(1)}, s32[8,16,1]{1,2,0:T(1,128)}, u32[]{:S(2)}) copy-start(s32[8,16,1]{1,2,0:T(1,128)} %param.20) | copy-start | bytes 1540
  0.6 14.0 %copy-start.2 = (s32[8,16]{1,0:T(8,128)S(1)}, s32[8,16]{1,0:T(8,128)}, u32[]{:S(2)}) copy-start(s32[8,16]{1,0:T(8,128)} %tok_ref.1) | copy-start | bytes 1540
  0.7 21.1 %collective-permute-start.1 = (bf16[256,1024]{1,0:T(8,128)(2,1)}, bf16[256,1024]{1,0:T(8,128)(2,1)S(1)}, u32[]{:S(2)}, u32[]{:S(2)}) collective-permute-start(bf16[256,1024]{1,0:T(8,128)(2,1)} %w0_ref.1), channel_id=1, source_target_pairs={{0,1},{1,2},{2,3},{3,0},{4,5},{5,6},{6,7},{7,4},{8,9},{9,10},{10,1... | collective-permute-start | bytes 1572872 | tf_op jit(solution)/shard_map/ppermute | solution.py:540
  2.3 19.5 %collective-permute-start.2 = (bf16[256,1024]{1,0:T(8,128)(2,1)}, bf16[256,1024]{1,0:T(8,128)(2,1)S(1)}, u32[]{:S(2)}, u32[]{:S(2)}) collective-permute-start(bf16[256,1024]{1,0:T(8,128)(2,1)} %w0_ref.1), channel_id=1, source_target_pairs={{1,0},{2,1},{3,2},{0,3},{5,4},{6,5},{7,6},{4,7},{9,8},{10,9},{11,1... | collective-permute-start | bytes 1572872 | tf_op jit(solution)/shard_map/ppermute | solution.py:540
  6.3 28.4 %collective-permute-start.3 = (bf16[272,1024]{1,0:T(8,128)(2,1)S(1)}, bf16[272,1024]{1,0:T(8,128)(2,1)S(1)}, u32[]{:S(2)}, u32[]{:S(2)}) collective-permute-start(bf16[272,1024]{1,0:T(8,128)(2,1)S(1)} %get-tuple-element.46.late_ref), channel_id=1, source_target_pairs={{0,4},{4,8},{8,12},{12,16},{16,20},{20,24},{24,28},{28,32},{32,36}... | collective-permute-start | bytes 1671176 | tf_op jit(solution)/shard_map/ppermute | solution.py:510
  8.3 26.5 %collective-permute-start.4 = (bf16[272,1024]{1,0:T(8,128)(2,1)S(1)}, bf16[272,1024]{1,0:T(8,128)(2,1)S(1)}, u32[]{:S(2)}, u32[]{:S(2)}) collective-permute-start(bf16[272,1024]{1,0:T(8,128)(2,1)S(1)} %get-tuple-element.45.early_ref), channel_id=1, source_target_pairs={{4,0},{8,4},{12,8},{16,12},{20,16},{24,20},{28,24},{32,28},{36,32}... | collective-permute-start | bytes 1671176 | tf_op jit(solution)/shard_map/ppermute | solution.py:510
  14.8 7.0 %collective-permute-start = (s32[1,128]{1,0:T(1,128)S(1)}, s32[1,128]{1,0:T(1,128)S(1)}, u32[]{:S(2)}, u32[]{:S(2)}) collective-permute-start(s32[1,128]{1,0:T(1,128)S(1)} %names.1), channel_id=1, source_target_pairs={{0,4},{4,8},{8,12},{12,16},{16,20},{20,24},{24,28},{28,32},{32,36}... | collective-permute-start | bytes 1544 | tf_op jit(solution)/shard_map/ppermute | solution.py:242
  21.8 7.6 %collective-permute-start.5 = (s32[2,128]{1,0:T(2,128)S(1)}, s32[2,128]{1,0:T(2,128)S(1)}, u32[]{:S(2)}, u32[]{:S(2)}) collective-permute-start(s32[2,128]{1,0:T(2,128)S(1)} %pad_add_fusion.5), channel_id=1, source_target_pairs={{0,8},{4,12},{8,16},{12,20},{16,24},{20,28},{24,32},{28,36},{32,40... | collective-permute-start | bytes 3080 | tf_op jit(solution)/shard_map/ppermute | solution.py:242
  21.8 16.6 %copy-start.3 = (bf16[256,1024]{1,0:T(8,128)(2,1)}, bf16[256,1024]{1,0:T(8,128)(2,1)S(1)}, u32[]{:S(2)}) copy-start(bf16[256,1024]{1,0:T(8,128)(2,1)S(1)} %collective-permute-done.1.w1_ref) | copy-start | bytes 1572868
  21.8 16.6 %copy-start.4 = (bf16[256,1024]{1,0:T(8,128)(2,1)}, bf16[256,1024]{1,0:T(8,128)(2,1)S(1)}, u32[]{:S(2)}) copy-start(bf16[256,1024]{1,0:T(8,128)(2,1)S(1)} %collective-permute-done.2.w3_ref) | copy-start | bytes 1572868
  21.8 27.3 %collective-permute-start.8 = (bf16[128,1024]{1,0:T(8,128)(2,1)S(1)}, bf16[128,1024]{1,0:T(8,128)(2,1)S(1)}, u32[]{:S(2)}, u32[]{:S(2)}) collective-permute-start(bf16[128,1024]{1,0:T(8,128)(2,1)S(1)} %slice.6), channel_id=1, source_target_pairs={{0,1},{1,2},{2,3},{3,0},{4,5},{5,6},{6,7},{7,4},{8,9},{9,10},{10,1... | collective-permute-start | bytes 786440 | tf_op jit(solution)/shard_map/ppermute | solution.py:547
  22.3 26.9 %collective-permute-start.9 = (bf16[128,1024]{1,0:T(8,128)(2,1)S(1)}, bf16[128,1024]{1,0:T(8,128)(2,1)S(1)}, u32[]{:S(2)}, u32[]{:S(2)}) collective-permute-start(bf16[128,1024]{1,0:T(8,128)(2,1)S(1)} %slice.7), channel_id=1, source_target_pairs={{1,0},{2,1},{3,2},{0,3},{5,4},{6,5},{7,6},{4,7},{9,8},{10,9},{11,1... | collective-permute-start | bytes 786440 | tf_op jit(solution)/shard_map/ppermute | solution.py:547
  29.4 5.4 %collective-permute-start.6 = (s32[4,128]{1,0:T(4,128)S(1)}, s32[4,128]{1,0:T(4,128)S(1)}, u32[]{:S(2)}, u32[]{:S(2)}) collective-permute-start(s32[4,128]{1,0:T(4,128)S(1)} %pad_add_fusion.4), channel_id=1, source_target_pairs={{0,16},{4,20},{8,24},{12,28},{16,32},{20,36},{24,40},{28,44},{32,4... | collective-permute-start | bytes 6152 | tf_op jit(solution)/shard_map/ppermute | solution.py:242
  38.4 10.8 %collective-permute-start.7 = (s32[8,128]{1,0:T(8,128)S(1)}, s32[8,128]{1,0:T(8,128)S(1)}, u32[]{:S(2)}, u32[]{:S(2)}) collective-permute-start(s32[8,128]{1,0:T(8,128)S(1)} %pad_add_fusion.3), channel_id=1, source_target_pairs={{0,32},{4,36},{8,40},{12,44},{16,48},{20,52},{24,56},{28,60},{32,6... | collective-permute-start | bytes 12296 | tf_op jit(solution)/shard_map/ppermute | solution.py:242
  49.2 21.8 %copy-start.5 = (bf16[128,1024]{1,0:T(8,128)(2,1)}, bf16[128,1024]{1,0:T(8,128)(2,1)S(1)}, u32[]{:S(2)}) copy-start(bf16[128,1024]{1,0:T(8,128)(2,1)S(1)} %collective-permute-done.8.top_ref) | copy-start | bytes 786436
  49.2 21.7 %copy-start.6 = (bf16[128,1024]{1,0:T(8,128)(2,1)}, bf16[128,1024]{1,0:T(8,128)(2,1)S(1)}, u32[]{:S(2)}) copy-start(bf16[128,1024]{1,0:T(8,128)(2,1)S(1)} %collective-permute-done.9.low_ref) | copy-start | bytes 786436
  49.2 13.2 %collective-permute-start.13 = (s32[16,128]{1,0:T(8,128)S(1)}, s32[16,128]{1,0:T(8,128)S(1)}, u32[]{:S(2)}, u32[]{:S(2)}) collective-permute-start(s32[16,128]{1,0:T(8,128)S(1)} %pad_add_fusion.2), channel_id=1, source_target_pairs={{0,64},{4,68},{8,72},{12,76},{16,80},{20,84},{24,88},{28,92},{32,9... | collective-permute-start | bytes 24584 | tf_op jit(solution)/shard_map/ppermute | solution.py:242
  57.8 13.1 %collective-permute-start.10 = (bf16[384,256]{1,0:T(8,128)(2,1)S(1)}, bf16[384,256]{1,0:T(8,128)(2,1)S(1)}, u32[]{:S(2)}, u32[]{:S(2)}) collective-permute-start(bf16[384,256]{1,0:T(8,128)(2,1)S(1)} %get-tuple-element.71), channel_id=1, source_target_pairs={{0,1},{1,2},{2,3},{3,0},{4,5},{5,6},{6,7},{7,4},{8,9},{9,10},{10,1... | collective-permute-start | bytes 589832 | tf_op jit(solution)/shard_map/ppermute | solution.py:555
  58.1 12.8 %collective-permute-start.11 = (bf16[384,256]{1,0:T(8,128)(2,1)S(1)}, bf16[384,256]{1,0:T(8,128)(2,1)S(1)}, u32[]{:S(2)}, u32[]{:S(2)}) collective-permute-start(bf16[384,256]{1,0:T(8,128)(2,1)S(1)} %get-tuple-element.72), channel_id=1, source_target_pairs={{0,2},{1,3},{2,0},{3,1},{4,6},{5,7},{6,4},{7,5},{8,10},{9,11},{10,... | collective-permute-start | bytes 589832 | tf_op jit(solution)/shard_map/ppermute | solution.py:555
  61.0 9.9 %collective-permute-start.12 = (bf16[384,256]{1,0:T(8,128)(2,1)S(1)}, bf16[384,256]{1,0:T(8,128)(2,1)S(1)}, u32[]{:S(2)}, u32[]{:S(2)}) collective-permute-start(bf16[384,256]{1,0:T(8,128)(2,1)S(1)} %get-tuple-element.73), channel_id=1, source_target_pairs={{0,3},{1,0},{2,1},{3,2},{4,7},{5,4},{6,5},{7,6},{8,11},{9,8},{10,9... | collective-permute-start | bytes 589832 | tf_op jit(solution)/shard_map/ppermute | solution.py:555
  62.4 7.6 %collective-permute-start.14 = (s32[32,128]{1,0:T(8,128)S(1)}, s32[32,128]{1,0:T(8,128)S(1)}, u32[]{:S(2)}, u32[]{:S(2)}) collective-permute-start(s32[32,128]{1,0:T(8,128)S(1)} %pad_add_fusion.1), channel_id=1, source_target_pairs={{0,128},{4,132},{8,136},{12,140},{16,144},{20,148},{24,152},{28,15... | collective-permute-start | bytes 49160 | tf_op jit(solution)/shard_map/ppermute | solution.py:242
  75.8 31.9 %all-to-all-start = ((bf16[64,16,384]{2,1,0:T(8,128)(2,1)}), bf16[64,16,384]{2,1,0:T(8,128)(2,1)S(1)}, u32[]{:S(2)}, u32[]{:S(2)}) async-start(bf16[64,16,384]{2,1,0:T(8,128)(2,1)} %get-tuple-element.80), calls=%async_computation | async-start | bytes 1572864 | tf_op jit(solution)/shard_map/all_to_all | solution.py:566
  84.5 23.2 %copy-start = (bf16[8,16,512]{2,1,0:T(8,128)(2,1)S(1)}, bf16[8,16,512]{2,1,0:T(8,128)(2,1)}, u32[]{:S(2)}) copy-start(bf16[8,16,512]{2,1,0:T(8,128)(2,1)} %reg_ref.1) | copy-start | bytes 393220
  108.7 13.8 %collective-permute-start.15 = (bf16[48,512]{1,0:T(8,128)(2,1)S(1)}, bf16[48,512]{1,0:T(8,128)(2,1)S(1)}, u32[]{:S(2)}, u32[]{:S(2)}) collective-permute-start(bf16[48,512]{1,0:T(8,128)(2,1)S(1)} %get-tuple-element.83), channel_id=1, source_target_pairs={{0,1},{1,2},{2,3},{3,4},{4,5},{5,6},{6,7},{7,8},{8,9},{9,10},{10,1... | collective-permute-start | bytes 147464 | tf_op jit(solution)/shard_map/ppermute | solution.py:510
  111.0 11.5 %collective-permute-start.16 = (bf16[48,512]{1,0:T(8,128)(2,1)S(1)}, bf16[48,512]{1,0:T(8,128)(2,1)S(1)}, u32[]{:S(2)}, u32[]{:S(2)}) collective-permute-start(bf16[48,512]{1,0:T(8,128)(2,1)S(1)} %get-tuple-element.84), channel_id=1, source_target_pairs={{1,0},{2,1},{3,2},{4,3},{5,4},{6,5},{7,6},{8,7},{9,8},{10,9},{11,1... | collective-permute-start | bytes 147464 | tf_op jit(solution)/shard_map/ppermute | solution.py:510

commit v8 on v6

--- a/solution.py
+++ b/solution.py
@@ -12,6 +12,7 @@
 BANDS = ("sec", "tile")
 CELLS = ("sec", "tile", "tp")
 LOG2E = 1.4426950408889634
+FETCHED = 5
 MIB = 1024 * 1024
 ON_CHIP = pl.BlockSpec(memory_space=pltpu.VMEM)
 SCALARS = pl.BlockSpec(memory_space=pltpu.SMEM)
@@ -159,35 +160,44 @@
     band = lax.axis_index(BANDS)
     left = band > 0
     right = band < bands - 1
-    head_of = iota((1, cols), 1) // HD
     k = k_ref[0]
     v = v_ref[0]
     row = iota((tokens, 1), 0)
     there = jnp.where(row < half, left.astype(jnp.int32), right.astype(jnp.int32)) > 0
     k_halo = jnp.where(there, k_halo_ref[0], k)
-    v_halo = v_halo_ref[0]
     one = there.astype(jnp.bfloat16)
-    v_halo = v_halo * one
-    block = half
-    for part in range(tokens // block):
-        q = q_ref[0, part * block : (part + 1) * block, :]
-        gathered = jnp.zeros((block, cols), jnp.float32)
-        for head in range(cols // HD):
-            mine = head_of == head
-            q_head = jnp.where(mine, q, jnp.zeros_like(q))
-            own = dot_t(q_head, k)
-            far = dot_t(q_head, k_halo)
-            top = jnp.maximum(
-                jnp.max(own, -1, keepdims=True), jnp.max(far, -1, keepdims=True)
-            )
-            own = jnp.exp2(own - top).astype(jnp.bfloat16)
-            far = jnp.exp2(far - top).astype(jnp.bfloat16)
-            v_own = jnp.where(mine, v, jnp.ones_like(v))
-            v_far = jnp.where(mine, v_halo, jnp.broadcast_to(one, v.shape))
-            acc = dot(own, v_own) + dot(far, v_far)
-            total = pltpu.roll(acc, cols // 2, 1)
-            gathered = jnp.where(mine, acc / total, gathered)
-        held_ref[part * block : (part + 1) * block] = gathered.astype(jnp.bfloat16)
+    v_halo = v_halo_ref[0] * one
+    block, pair = half, 2 * HD
+    which = iota((1, pair), 1) // HD
+    work = [(head, part) for head in range(cols // HD) for part in range(tokens // block)]
+
+    def lanes(head):
+        return slice(head // 2 * pair, (head // 2 + 1) * pair)
+
+    def scores(head, part):
+        q = q_ref[0, part * block : (part + 1) * block, lanes(head)]
+        q = jnp.where(which == head % 2, q, jnp.zeros_like(q))
+        return dot_t(q, k[:, lanes(head)]), dot_t(q, k_halo[:, lanes(head)])
+
+    first = {}
+    own, far = scores(*work[0])
+    for index, (head, part) in enumerate(work):
+        later = scores(*work[index + 1]) if index + 1 < len(work) else (None, None)
+        mine = which == head % 2
+        top = jnp.maximum(jnp.max(own, -1, keepdims=True), jnp.max(far, -1, keepdims=True))
+        own = jnp.exp2(own - top).astype(jnp.bfloat16)
+        far = jnp.exp2(far - top).astype(jnp.bfloat16)
+        v_own, v_far = v[:, lanes(head)], v_halo[:, lanes(head)]
+        v_own = jnp.where(mine, v_own, jnp.ones_like(v_own))
+        v_far = jnp.where(mine, v_far, jnp.broadcast_to(one, v_far.shape))
+        acc = dot(own, v_own) + dot(far, v_far)
+        made = acc / pltpu.roll(acc, HD, 1)
+        if head % 2 == 0:
+            first[part] = made
+        else:
+            both = jnp.where(mine, made, first[part]).astype(jnp.bfloat16)
+            held_ref[part * block : (part + 1) * block, lanes(head)] = both
+        own, far = later
     ranks = len(out_refs)
     quarter = tokens // ranks
     rank = lax.axis_index("tp")
@@ -250,7 +260,7 @@
 
 
 def fetch_kernel(conv_hbm_ref, taps_ref, sem):
-    copy = pltpu.make_async_copy(conv_hbm_ref.at[pl.ds(0, 3)], taps_ref, sem)
+    copy = pltpu.make_async_copy(conv_hbm_ref.at[pl.ds(0, FETCHED)], taps_ref, sem)
     copy.start()
     copy.wait()
 
@@ -258,7 +268,7 @@
 def fetch_taps(conv_w):
     return pl.pallas_call(
         fetch_kernel,
-        out_shape=jax.ShapeDtypeStruct((3, *conv_w.shape[1:]), conv_w.dtype),
+        out_shape=jax.ShapeDtypeStruct((FETCHED, *conv_w.shape[1:]), conv_w.dtype),
         in_specs=[pl.BlockSpec(memory_space=pltpu.HBM)],
         out_specs=ON_CHIP,
         scratch_shapes=[pltpu.SemaphoreType.DMA(())],
@@ -412,9 +422,11 @@
     return low, x, high
 
 
-def inner_kernel(x_ref, before_ref, conv_hbm_ref, sum_ref, after_ref, held_ref, sems):
+def inner_kernel(x_ref, taps_ref, conv_hbm_ref, sum_ref, after_ref, held_ref, sems):
     copies = [
-        pltpu.make_async_copy(conv_hbm_ref.at[pl.ds(3, 3)], held_ref, sems.at[0]),
+        pltpu.make_async_copy(
+            conv_hbm_ref.at[pl.ds(FETCHED, 6 - FETCHED)], held_ref, sems.at[0]
+        ),
         pltpu.make_async_copy(conv_hbm_ref.at[pl.ds(6, 3)], after_ref, sems.at[1]),
     ]
     for copy in copies:
@@ -422,19 +434,23 @@
     cols, slab, channels = x_ref.shape
     cells = cols * slab
     shifts = row_shifts(x_ref[...].reshape(cells, channels), slab // 3)
-
-    def product(first, last, w_ref):
-        total = None
-        for b, x in enumerate(shifts):
-            one = dot(x[first:last], w_ref[b])
-            total = one if total is None else total + one
-        return total
-
-    before = product(0, cells - slab, before_ref)
-    copies[0].wait()
-    middle = product(0, cells, held_ref)
-    copies[1].wait()
-    after = product(slab, cells, after_ref)
+    sums = [None] * 3
+    for tap in range(9):
+        if tap == FETCHED:
+            copies[0].wait()
+        if tap == 6:
+            copies[1].wait()
+        if tap < FETCHED:
+            w = taps_ref[tap]
+        elif tap < 6:
+            w = held_ref[tap - FETCHED]
+        else:
+            w = after_ref[tap - 6]
+        x = shifts[tap % 3]
+        x = (x[: cells - slab], x, x[slab:])[tap // 3]
+        one = dot(x, w)
+        sums[tap // 3] = one if sums[tap // 3] is None else sums[tap // 3] + one
+    before, middle, after = sums
     sum_ref[:slab] = middle[:slab] + after[:slab]
     sum_ref[slab : cells - slab] = middle[slab : cells - slab] + before[: cells - 2 * slab] + after[slab:]
     sum_ref[cells - slab :] = middle[cells - slab :] + before[cells - 2 * slab :]
@@ -446,12 +462,12 @@
         inner_kernel,
         out_shape=[
             jax.ShapeDtypeStruct((cols * slab, channels), jnp.float32),
-            jax.ShapeDtypeStruct(taps.shape, taps.dtype),
+            jax.ShapeDtypeStruct((3, channels, channels), taps.dtype),
         ],
         in_specs=[ON_CHIP] * 2 + [pl.BlockSpec(memory_space=pltpu.HBM)],
         out_specs=[ON_CHIP] * 2,
         scratch_shapes=[
-            pltpu.VMEM((3, channels, channels), jnp.bfloat16),
+            pltpu.VMEM((6 - FETCHED, channels, channels), jnp.bfloat16),
             pltpu.SemaphoreType.DMA((2,)),
         ],
         compiler_params=pltpu.CompilerParams(vmem_limit_bytes=16 * MIB),

time: 110 us -> 108 us (0.982)
  Pallas kernels: 32 us -> 30.6 us
  transfers between devices with their start and end apart: 13 -> 13, of which waited for: 2 -> 2; matrix products, arithmetic and copies ran while one was open for 0% -> 0% of each run, Pallas kernels for 25% -> 24%
where the time goes in v8:
time: 108 us
  starting transfers between devices  49.9 us (46%)
  Pallas kernels  30.6 us (28%)
  waiting for transfers between devices  25.6 us (24%)
  between operations  1.58 us (1%)
    all_to_all x1, waiting for transfers between devices, per_device(): arrived = lax.all_to_all(send, BANDS, 0, 0, tiled=True)  21.4 us
    ppermute x4, starting transfers between devices, neighbours(): return (lax.ppermute(last, axis, up), lax.ppermute(first, axis, down))  18.6 us
    all_to_all x1, starting transfers between devices, per_device(): asked = lax.all_to_all(asked[:, None, :], BANDS, 0, 0, tiled=True)[:, 0, :]  13.8 us
    pallas_call x1, Pallas kernels, attend(): pl.pallas_call(functools.partial(attend_kernel, bands=bands), out_shape=[...  8.31 us
    pallas_call x2, Pallas kernels, project(): pl.pallas_call(functools.partial(project_kernel, halo=halo), out_shape=[j...  7.68 us
    all_to_all x1, starting transfers between devices, per_device(): arrived = lax.all_to_all(send, BANDS, 0, 0, tiled=True)  6.6 us
    all_to_all x1, waiting for transfers between devices, per_device(): asked = lax.all_to_all(asked[:, None, :], BANDS, 0, 0, tiled=True)[:, 0, :]  4.19 us
    ppermute x3, starting transfers between devices, per_device(): lax.ppermute(attended[d], 'tp', [(i, (i + d) % ranks) for i in range(rank...  4.1 us
  transfers between devices with their start and end apart: 13, of which 2 were waited for; matrix products, arithmetic and copies ran while one was open for 0% of the time, Pallas kernels for 24%

profile of v8, /device:TPU:4, one launch (start us, length us, event | category | flops | bytes accessed | tf_op | source)
XLA Modules:
  0.0 107.7 jit_solution(742020460012094522)
XLA Ops:
  0.6 1.7 %collective-permute-start = (bf16[256,1024]{1,0:T(8,128)(2,1)}, bf16[256,1024]{1,0:T(8,128)(2,1)S(1)}, u32[]{:S(2)}, u32[]{:S(2)}) collective-permute-start(bf16[256,1024]{1,0:T(8,128)(2,1)} %w0_ref.1), channel_id=1, source_target_pairs={{0,1},{1,2},{2,3},{3,0},{4,5},{5,6},{6,7},{7,4},{8,9},{9,10},{10,1... | collective-permute-start | bytes 1572872 | tf_op jit(solution)/shard_map/ppermute | solution.py:547
  2.3 1.7 %collective-permute-start.1 = (bf16[256,1024]{1,0:T(8,128)(2,1)}, bf16[256,1024]{1,0:T(8,128)(2,1)S(1)}, u32[]{:S(2)}, u32[]{:S(2)}) collective-permute-start(bf16[256,1024]{1,0:T(8,128)(2,1)} %w0_ref.1), channel_id=1, source_target_pairs={{1,0},{2,1},{3,2},{0,3},{5,4},{6,5},{7,6},{4,7},{9,8},{10,9},{11,1... | collective-permute-start | bytes 1572872 | tf_op jit(solution)/shard_map/ppermute | solution.py:547
  4.6 1.7 %edges.1 = (bf16[272,1024]{1,0:T(8,128)(2,1)S(1)}, bf16[272,1024]{1,0:T(8,128)(2,1)S(1)}, bf16[1024,256]{1,0:T(8,128)(2,1)S(1)}, bf16[1024,256]{1,0:T(8,128)(2,1)S(1)}, bf16[1024,256]{1,0:T(8,128)(2,1)S(1)}) custom-call(s32[1]{0:T(128)S(6)} %copy.15.code_ref, bf16[512,1024]{1,0:T(8,128)(2,1)} %x_ref.3, bf16[1024,256]{1,0:T(8,128)(2,1)} %refs_0_.1, ...), custom_call_target="tpu_custom_call" | custom-call | tf_op jit(solution)/shard_map/edges/pallas_call | solution.py:79
  6.4 1.9 %collective-permute-start.2 = (bf16[272,1024]{1,0:T(8,128)(2,1)S(1)}, bf16[272,1024]{1,0:T(8,128)(2,1)S(1)}, u32[]{:S(2)}, u32[]{:S(2)}) collective-permute-start(bf16[272,1024]{1,0:T(8,128)(2,1)S(1)} %get-tuple-element.41.late_ref), channel_id=1, source_target_pairs={{0,4},{4,8},{8,12},{12,16},{16,20},{20,24},{24,28},{28,32},{32,36}... | collective-permute-start | bytes 1671176 | tf_op jit(solution)/shard_map/ppermute | solution.py:517
  8.3 6.3 %collective-permute-start.3 = (bf16[272,1024]{1,0:T(8,128)(2,1)S(1)}, bf16[272,1024]{1,0:T(8,128)(2,1)S(1)}, u32[]{:S(2)}, u32[]{:S(2)}) collective-permute-start(bf16[272,1024]{1,0:T(8,128)(2,1)S(1)} %get-tuple-element.40.early_ref), channel_id=1, source_target_pairs={{4,0},{8,4},{12,8},{16,12},{20,16},{24,20},{28,24},{32,28},{36,32}... | collective-permute-start | bytes 1671176 | tf_op jit(solution)/shard_map/ppermute | solution.py:517
  14.6 4.1 %project_own.1 = (bf16[3,512,256]{2,1,0:T(8,128)(2,1)S(1)}, bf16[3,512,256]{2,1,0:T(8,128)(2,1)S(1)}, bf16[3,512,256]{2,1,0:T(8,128)(2,1)S(1)}) custom-call(s32[1]{0:T(128)S(6)} %copy.15.code_ref, bf16[272,1024]{1,0:T(8,128)(2,1)S(1)} %get-tuple-element.40.early_ref, bf16[272,1024]{1,0:T(8,128)(2,1)S(1)} %get-tuple-element.41.late_ref, ...), custom_call_target="tpu_custom_call" | custom-call | tf_op jit(solution)/shard_map/project_own/pallas_call | solution.py:138
  18.8 0.0 collective-permute-done.1.w3_ref
  18.8 0.4 collective-permute-start.4
  19.3 2.9 %collective-permute-start.5 = (bf16[128,1024]{1,0:T(8,128)(2,1)S(1)}, bf16[128,1024]{1,0:T(8,128)(2,1)S(1)}, u32[]{:S(2)}, u32[]{:S(2)}) collective-permute-start(bf16[128,1024]{1,0:T(8,128)(2,1)S(1)} %slice.7), channel_id=1, source_target_pairs={{1,0},{2,1},{3,2},{0,3},{5,4},{6,5},{7,6},{4,7},{9,8},{10,9},{11,1... | collective-permute-start | bytes 786440 | tf_op jit(solution)/shard_map/ppermute | solution.py:552
  22.3 1.0 ask.1
  23.2 0.0 collective-permute-done.3.late_ref
  23.2 3.5 %project_halo.1 = (bf16[3,512,256]{2,1,0:T(8,128)(2,1)S(1)}, bf16[3,512,256]{2,1,0:T(8,128)(2,1)S(1)}) custom-call(s32[1]{0:T(128)S(6)} %copy.15.code_ref, bf16[272,1024]{1,0:T(8,128)(2,1)S(1)} %collective-permute-done.2.early_ref, bf16[272,1024]{1,0:T(8,128)(2,1)S(1)} %collective-permute-done.3.late_ref, bf16[1024]{0:T(1024)(128)(2,1)} %gain_ref.3, ...), custom_call_target="tpu_custom_call" | custom-call | tf_op jit(solution)/shard_map/project_halo/pallas_call | solution.py:138
  26.8 8.3 %attend.1 = (bf16[384,256]{1,0:T(8,128)(2,1)S(1)}, bf16[384,256]{1,0:T(8,128)(2,1)S(1)}, bf16[384,256]{1,0:T(8,128)(2,1)S(1)}, bf16[384,256]{1,0:T(8,128)(2,1)S(1)}) custom-call(bf16[3,512,256]{2,1,0:T(8,128)(2,1)S(1)} %get-tuple-element.47.q_ref, bf16[3,512,256]{2,1,0:T(8,128)(2,1)S(1)} %get-tuple-element.48.k_ref, ...), custom_call_target="tpu_custom_call" | custom-call | tf_op jit(solution)/shard_map/attend/pallas_call | solution.py:213
  35.1 0.0 copy-start.5
  35.1 0.0 collective-permute-done.5.low_ref
  35.2 0.1 collective-permute-start.6
  35.3 2.7 %collective-permute-start.7 = (bf16[384,256]{1,0:T(8,128)(2,1)S(1)}, bf16[384,256]{1,0:T(8,128)(2,1)S(1)}, u32[]{:S(2)}, u32[]{:S(2)}) collective-permute-start(bf16[384,256]{1,0:T(8,128)(2,1)S(1)} %get-tuple-element.62), channel_id=1, source_target_pairs={{0,2},{1,3},{2,0},{3,1},{4,6},{5,7},{6,4},{7,5},{8,10},{9,11},{10,... | collective-permute-start | bytes 589832 | tf_op jit(solution)/shard_map/ppermute | solution.py:558
  37.9 1.3 %collective-permute-start.8 = (bf16[384,256]{1,0:T(8,128)(2,1)S(1)}, bf16[384,256]{1,0:T(8,128)(2,1)S(1)}, u32[]{:S(2)}, u32[]{:S(2)}) collective-permute-start(bf16[384,256]{1,0:T(8,128)(2,1)S(1)} %get-tuple-element.63), channel_id=1, source_target_pairs={{0,3},{1,0},{2,1},{3,2},{4,7},{5,4},{6,5},{7,6},{8,11},{9,8},{10,9... | collective-permute-start | bytes 589832 | tf_op jit(solution)/shard_map/ppermute | solution.py:558
  39.3 13.8 %all-to-all-start = ((s32[64,1,4]{2,1,0:T(1,128)}), s32[64,1,4]{2,1,0:T(1,128)S(1)}, u32[]{:S(2)}, u32[]{:S(2)}) async-start(s32[64,1,4]{2,1,0:T(1,128)} %bitcast.2), calls=%async_computation | async-start | bytes 65536 | tf_op jit(solution)/shard_map/all_to_all | solution.py:561
  53.1 0.0 collective-permute-done.6.att1_ref
  53.2 3.4 %combine.1 = (bf16[3,128,1024]{2,1,0:T(8,128)(2,1)}, bf16[512,384]{1,0:T(8,128)(2,1)S(1)}) custom-call(s32[1]{0:T(128)S(6)} %copy.15.code_ref, bf16[384,256]{1,0:T(8,128)(2,1)S(1)} %get-tuple-element.60.att0_ref, bf16[384,256]{1,0:T(8,128)(2,1)S(1)} %collective-permute-done.6.att1_ref, bf16[384,256]{1,0:T(8,128)(2,1)S(1)} %collective-permute-done.7.att2_ref, ...), custom_call_target="tpu_custom_call" | custom-call | tf_op jit(solution)/shard_map/combine/pallas_call | solution.py:343
  56.6 4.2 %all-to-all-done = s32[64,1,4]{2,1,0:T(1,128)S(1)} async-done(((s32[64,1,4]{2,1,0:T(1,128)}), s32[64,1,4]{2,1,0:T(1,128)S(1)}, u32[]{:S(2)}, u32[]{:S(2)}) %all-to-all-start) | async-done | bytes 1056 | tf_op jit(solution)/shard_map/all_to_all | solution.py:561
  60.8 1.8 %serve.1 = bf16[64,16,384]{2,1,0:T(8,128)(2,1)} custom-call(s32[64,4]{1,0:T(8,128)S(1)} %bitcast.5, bf16[512,384]{1,0:T(8,128)(2,1)S(1)} %get-tuple-element.68.table_ref), custom_call_target="tpu_custom_call" | custom-call | tf_op jit(solution)/shard_map/serve/pallas_call | solution.py:368
  62.6 6.6 %all-to-all-start.1 = ((bf16[64,16,384]{2,1,0:T(8,128)(2,1)}), bf16[64,16,384]{2,1,0:T(8,128)(2,1)S(1)}, u32[]{:S(2)}, u32[]{:S(2)}) async-start(bf16[64,16,384]{2,1,0:T(8,128)(2,1)} %serve.1), calls=%async_computation.1 | async-start | bytes 1572864 | tf_op jit(solution)/shard_map/all_to_all | solution.py:567
  69.2 0.0 copy-start
  69.2 1.8 %fetch.1.taps_ref.w_before_ref = bf16[5,512,512]{2,1,0:T(8,128)(2,1)S(1)} custom-call(bf16[9,512,512]{2,1,0:T(8,128)(2,1)} %conv_hbm_ref.1), custom_call_target="tpu_custom_call" | custom-call | tf_op jit(solution)/shard_map/fetch/pallas_call | solution.py:269
  71.0 21.4 %all-to-all-done.1.arrived_ref = bf16[64,16,384]{2,1,0:T(8,128)(2,1)S(1)} async-done(((bf16[64,16,384]{2,1,0:T(8,128)(2,1)}), bf16[64,16,384]{2,1,0:T(8,128)(2,1)S(1)}, u32[]{:S(2)}, u32[]{:S(2)}) %all-to-all-start.1) | async-done | bytes 786464 | tf_op jit(solution)/shard_map/all_to_all | solution.py:567
  92.4 1.0 inputs.1
  93.4 2.6 %collective-permute-start.9 = (bf16[48,512]{1,0:T(8,128)(2,1)S(1)}, bf16[48,512]{1,0:T(8,128)(2,1)S(1)}, u32[]{:S(2)}, u32[]{:S(2)}) collective-permute-start(bf16[48,512]{1,0:T(8,128)(2,1)S(1)} %get-tuple-element.73), channel_id=1, source_target_pairs={{0,1},{1,2},{2,3},{3,4},{4,5},{5,6},{6,7},{7,8},{8,9},{9,10},{10,1... | collective-permute-start | bytes 147464 | tf_op jit(solution)/shard_map/ppermute | solution.py:517
  96.0 7.8 %collective-permute-start.10 = (bf16[48,512]{1,0:T(8,128)(2,1)S(1)}, bf16[48,512]{1,0:T(8,128)(2,1)S(1)}, u32[]{:S(2)}, u32[]{:S(2)}) collective-permute-start(bf16[48,512]{1,0:T(8,128)(2,1)S(1)} %get-tuple-element.74), channel_id=1, source_target_pairs={{1,0},{2,1},{3,2},{4,3},{5,4},{6,5},{7,6},{8,7},{9,8},{10,9},{11,1... | collective-permute-start | bytes 147464 | tf_op jit(solution)/shard_map/ppermute | solution.py:517
  103.8 2.3 %convolve_inner.1 = (f32[384,512]{1,0:T(8,128)S(1)}, bf16[3,512,512]{2,1,0:T(8,128)(2,1)S(1)}) custom-call(bf16[8,48,512]{2,1,0:T(8,128)(2,1)S(1)} %get-tuple-element.72.x_ref, bf16[5,512,512]{2,1,0:T(8,128)(2,1)S(1)} %fetch.1.taps_ref.w_before_ref, bf16[9,512,512]{2,1,0:T(8,128)(2,1)} %conv_hbm_ref.1), custom_call_target="tpu_custom_call" | custom-call | tf_op jit(solution)/shard_map/convolve_inner/pallas_call | solution.py:461
  106.2 1.6 %convolve_finish.1 = bf16[3,8,16,512]{3,2,1,0:T(8,128)(2,1)} custom-call(bf16[8,48,512]{2,1,0:T(8,128)(2,1)S(1)} %get-tuple-element.72.x_ref, bf16[48,512]{1,0:T(8,128)(2,1)S(1)} %collective-permute-done.9.before_ref, bf16[48,512]{1,0:T(8,128)(2,1)S(1)} %collective-permute-done.10.after_ref, bf16[5,512,512]{2,1,0:T(8,128)(2,1)S(1)} %fetch.1.taps_ref.w_before_ref, ...), custom_call_target="tpu_custom_call" | custom-call | tf_op jit(solution)/shard_map/convolve_finish/pallas_call | solution.py:503
  (21 shorter events, 0.1 us)
Async XLA Ops:
  0.6 18.2 %collective-permute-start = (bf16[256,1024]{1,0:T(8,128)(2,1)}, bf16[256,1024]{1,0:T(8,128)(2,1)S(1)}, u32[]{:S(2)}, u32[]{:S(2)}) collective-permute-start(bf16[256,1024]{1,0:T(8,128)(2,1)} %w0_ref.1), channel_id=1, source_target_pairs={{0,1},{1,2},{2,3},{3,0},{4,5},{5,6},{6,7},{7,4},{8,9},{9,10},{10,1... | collective-permute-start | bytes 1572872 | tf_op jit(solution)/shard_map/ppermute | solution.py:547
  2.3 16.5 %collective-permute-start.1 = (bf16[256,1024]{1,0:T(8,128)(2,1)}, bf16[256,1024]{1,0:T(8,128)(2,1)S(1)}, u32[]{:S(2)}, u32[]{:S(2)}) collective-permute-start(bf16[256,1024]{1,0:T(8,128)(2,1)} %w0_ref.1), channel_id=1, source_target_pairs={{1,0},{2,1},{3,2},{0,3},{5,4},{6,5},{7,6},{4,7},{9,8},{10,9},{11,1... | collective-permute-start | bytes 1572872 | tf_op jit(solution)/shard_map/ppermute | solution.py:547
  4.6 17.7 %copy-start.1 = (s32[8,16,1]{1,2,0:T(1,128)S(1)}, s32[8,16,1]{1,2,0:T(1,128)}, u32[]{:S(2)}) copy-start(s32[8,16,1]{1,2,0:T(1,128)} %param.20) | copy-start | bytes 1540
  4.6 17.7 %copy-start.2 = (s32[8,16]{1,0:T(8,128)S(1)}, s32[8,16]{1,0:T(8,128)}, u32[]{:S(2)}) copy-start(s32[8,16]{1,0:T(8,128)} %tok_ref.1) | copy-start | bytes 1540
  6.4 16.9 %collective-permute-start.2 = (bf16[272,1024]{1,0:T(8,128)(2,1)S(1)}, bf16[272,1024]{1,0:T(8,128)(2,1)S(1)}, u32[]{:S(2)}, u32[]{:S(2)}) collective-permute-start(bf16[272,1024]{1,0:T(8,128)(2,1)S(1)} %get-tuple-element.41.late_ref), channel_id=1, source_target_pairs={{0,4},{4,8},{8,12},{12,16},{16,20},{20,24},{24,28},{28,32},{32,36}... | collective-permute-start | bytes 1671176 | tf_op jit(solution)/shard_map/ppermute | solution.py:517
  8.3 15.0 %collective-permute-start.3 = (bf16[272,1024]{1,0:T(8,128)(2,1)S(1)}, bf16[272,1024]{1,0:T(8,128)(2,1)S(1)}, u32[]{:S(2)}, u32[]{:S(2)}) collective-permute-start(bf16[272,1024]{1,0:T(8,128)(2,1)S(1)} %get-tuple-element.40.early_ref), channel_id=1, source_target_pairs={{4,0},{8,4},{12,8},{16,12},{20,16},{24,20},{28,24},{32,28},{36,32}... | collective-permute-start | bytes 1671176 | tf_op jit(solution)/shard_map/ppermute | solution.py:517
  18.8 16.3 %copy-start.3 = (bf16[256,1024]{1,0:T(8,128)(2,1)}, bf16[256,1024]{1,0:T(8,128)(2,1)S(1)}, u32[]{:S(2)}) copy-start(bf16[256,1024]{1,0:T(8,128)(2,1)S(1)} %collective-permute-done.w1_ref) | copy-start | bytes 1572868
  18.8 16.3 %copy-start.4 = (bf16[256,1024]{1,0:T(8,128)(2,1)}, bf16[256,1024]{1,0:T(8,128)(2,1)S(1)}, u32[]{:S(2)}) copy-start(bf16[256,1024]{1,0:T(8,128)(2,1)S(1)} %collective-permute-done.1.w3_ref) | copy-start | bytes 1572868
  18.8 16.3 %collective-permute-start.4 = (bf16[128,1024]{1,0:T(8,128)(2,1)S(1)}, bf16[128,1024]{1,0:T(8,128)(2,1)S(1)}, u32[]{:S(2)}, u32[]{:S(2)}) collective-permute-start(bf16[128,1024]{1,0:T(8,128)(2,1)S(1)} %slice.6), channel_id=1, source_target_pairs={{0,1},{1,2},{2,3},{3,0},{4,5},{5,6},{6,7},{7,4},{8,9},{9,10},{10,1... | collective-permute-start | bytes 786440 | tf_op jit(solution)/shard_map/ppermute | solution.py:552
  19.3 15.8 %collective-permute-start.5 = (bf16[128,1024]{1,0:T(8,128)(2,1)S(1)}, bf16[128,1024]{1,0:T(8,128)(2,1)S(1)}, u32[]{:S(2)}, u32[]{:S(2)}) collective-permute-start(bf16[128,1024]{1,0:T(8,128)(2,1)S(1)} %slice.7), channel_id=1, source_target_pairs={{1,0},{2,1},{3,2},{0,3},{5,4},{6,5},{7,6},{4,7},{9,8},{10,9},{11,1... | collective-permute-start | bytes 786440 | tf_op jit(solution)/shard_map/ppermute | solution.py:552
  35.1 18.0 %copy-start.5 = (bf16[128,1024]{1,0:T(8,128)(2,1)}, bf16[128,1024]{1,0:T(8,128)(2,1)S(1)}, u32[]{:S(2)}) copy-start(bf16[128,1024]{1,0:T(8,128)(2,1)S(1)} %collective-permute-done.4.top_ref) | copy-start | bytes 786436
  35.2 18.0 %copy-start.6 = (bf16[128,1024]{1,0:T(8,128)(2,1)}, bf16[128,1024]{1,0:T(8,128)(2,1)S(1)}, u32[]{:S(2)}) copy-start(bf16[128,1024]{1,0:T(8,128)(2,1)S(1)} %collective-permute-done.5.low_ref) | copy-start | bytes 786436
  35.2 17.9 %collective-permute-start.6 = (bf16[384,256]{1,0:T(8,128)(2,1)S(1)}, bf16[384,256]{1,0:T(8,128)(2,1)S(1)}, u32[]{:S(2)}, u32[]{:S(2)}) collective-permute-start(bf16[384,256]{1,0:T(8,128)(2,1)S(1)} %get-tuple-element.61), channel_id=1, source_target_pairs={{0,1},{1,2},{2,3},{3,0},{4,5},{5,6},{6,7},{7,4},{8,9},{9,10},{10,1... | collective-permute-start | bytes 589832 | tf_op jit(solution)/shard_map/ppermute | solution.py:558
  35.3 17.9 %collective-permute-start.7 = (bf16[384,256]{1,0:T(8,128)(2,1)S(1)}, bf16[384,256]{1,0:T(8,128)(2,1)S(1)}, u32[]{:S(2)}, u32[]{:S(2)}) collective-permute-start(bf16[384,256]{1,0:T(8,128)(2,1)S(1)} %get-tuple-element.62), channel_id=1, source_target_pairs={{0,2},{1,3},{2,0},{3,1},{4,6},{5,7},{6,4},{7,5},{8,10},{9,11},{10,... | collective-permute-start | bytes 589832 | tf_op jit(solution)/shard_map/ppermute | solution.py:558
  37.9 15.2 %collective-permute-start.8 = (bf16[384,256]{1,0:T(8,128)(2,1)S(1)}, bf16[384,256]{1,0:T(8,128)(2,1)S(1)}, u32[]{:S(2)}, u32[]{:S(2)}) collective-permute-start(bf16[384,256]{1,0:T(8,128)(2,1)S(1)} %get-tuple-element.63), channel_id=1, source_target_pairs={{0,3},{1,0},{2,1},{3,2},{4,7},{5,4},{6,5},{7,6},{8,11},{9,8},{10,9... | collective-permute-start | bytes 589832 | tf_op jit(solution)/shard_map/ppermute | solution.py:558
  39.3 21.5 %all-to-all-start = ((s32[64,1,4]{2,1,0:T(1,128)}), s32[64,1,4]{2,1,0:T(1,128)S(1)}, u32[]{:S(2)}, u32[]{:S(2)}) async-start(s32[64,1,4]{2,1,0:T(1,128)} %bitcast.2), calls=%async_computation | async-start | bytes 65536 | tf_op jit(solution)/shard_map/all_to_all | solution.py:561
  62.6 29.8 %all-to-all-start.1 = ((bf16[64,16,384]{2,1,0:T(8,128)(2,1)}), bf16[64,16,384]{2,1,0:T(8,128)(2,1)S(1)}, u32[]{:S(2)}, u32[]{:S(2)}) async-start(bf16[64,16,384]{2,1,0:T(8,128)(2,1)} %serve.1), calls=%async_computation.1 | async-start | bytes 1572864 | tf_op jit(solution)/shard_map/all_to_all | solution.py:567
  69.2 23.2 %copy-start = (bf16[8,16,512]{2,1,0:T(8,128)(2,1)S(1)}, bf16[8,16,512]{2,1,0:T(8,128)(2,1)}, u32[]{:S(2)}) copy-start(bf16[8,16,512]{2,1,0:T(8,128)(2,1)} %reg_ref.1) | copy-start | bytes 393220
  93.4 12.7 %collective-permute-start.9 = (bf16[48,512]{1,0:T(8,128)(2,1)S(1)}, bf16[48,512]{1,0:T(8,128)(2,1)S(1)}, u32[]{:S(2)}, u32[]{:S(2)}) collective-permute-start(bf16[48,512]{1,0:T(8,128)(2,1)S(1)} %get-tuple-element.73), channel_id=1, source_target_pairs={{0,1},{1,2},{2,3},{3,4},{4,5},{5,6},{6,7},{7,8},{8,9},{9,10},{10,1... | collective-permute-start | bytes 147464 | tf_op jit(solution)/shard_map/ppermute | solution.py:517
  96.0 10.1 %collective-permute-start.10 = (bf16[48,512]{1,0:T(8,128)(2,1)S(1)}, bf16[48,512]{1,0:T(8,128)(2,1)S(1)}, u32[]{:S(2)}, u32[]{:S(2)}) collective-permute-start(bf16[48,512]{1,0:T(8,128)(2,1)S(1)} %get-tuple-element.74), channel_id=1, source_target_pairs={{1,0},{2,1},{3,2},{4,3},{5,4},{6,5},{7,6},{8,7},{9,8},{10,9},{11,1... | collective-permute-start | bytes 147464 | tf_op jit(solution)/shard_map/ppermute | solution.py:517

commit v9 on v8

--- a/solution.py
+++ b/solution.py
@@ -50,7 +50,8 @@
 
 
 def edges_kernel(code_ref, x_ref, *refs):
-    *refs, sems = refs
+    *refs, flat_ref, sems = refs
+    gain_ref, *refs, row_ref = refs
     count = (len(refs) - 2) // 2
     weights, (last_ref, first_ref, *held) = refs[:count], refs[count:]
     half = x_ref.shape[0] // 2
@@ -58,6 +59,7 @@
         (x_ref.at[pl.ds(half, half)], last_ref.at[pl.ds(0, half)]),
         (x_ref.at[pl.ds(0, half)], first_ref.at[pl.ds(0, half)]),
         *zip(weights, held),
+        (gain_ref, flat_ref),
     ]
     copies = [pltpu.make_async_copy(a, b, sems.at[i]) for i, (a, b) in enumerate(pairs)]
     for copy in copies:
@@ -71,20 +73,26 @@
     first_ref[half:] = digit
     for copy in copies:
         copy.wait()
-
-
-def make_edges(code, x, weights):
+    row_ref[...] = flat_ref[...].astype(jnp.float32).reshape(row_ref.shape)
+
+
+def make_edges(code, x, gain, weights):
     tokens, features = x.shape
     shapes = [(tokens // 2 + 16, features)] * 2 + [w.shape for w in weights]
+    shapes = [jax.ShapeDtypeStruct(s, jnp.bfloat16) for s in shapes]
+    shapes.append(jax.ShapeDtypeStruct((1, features), jnp.float32))
     return pl.pallas_call(
         edges_kernel,
-        out_shape=[jax.ShapeDtypeStruct(s, jnp.bfloat16) for s in shapes],
-        in_specs=[SCALARS] + [pl.BlockSpec(memory_space=pltpu.HBM)] * (1 + len(weights)),
+        out_shape=shapes,
+        in_specs=[SCALARS] + [pl.BlockSpec(memory_space=pltpu.HBM)] * (2 + len(weights)),
         out_specs=[ON_CHIP] * len(shapes),
-        scratch_shapes=[pltpu.SemaphoreType.DMA((2 + len(weights),))],
+        scratch_shapes=[
+            pltpu.VMEM(gain.shape, gain.dtype),
+            pltpu.SemaphoreType.DMA((3 + len(weights),)),
+        ],
         compiler_params=pltpu.CompilerParams(vmem_limit_bytes=2 * MIB),
         name="edges",
-    )(code, x, *weights)
+    )(code, x, gain, *weights)
 
 
 def project_kernel(code_ref, early_ref, late_ref, gain_ref, *refs, halo):
@@ -105,7 +113,7 @@
         code = jnp.full((1, 1), code_ref[0], jnp.int32)
     weights, outs = refs[: len(refs) // 2], refs[len(refs) // 2 :]
     features = both_ref.shape[1]
-    gain = gain_ref[...].astype(jnp.float32).reshape(1, features)
+    gain = gain_ref[...]
     chunk, block = 16, 128
     for at in range(0, rows, block):
         for r in range(at, at + block, chunk):
@@ -120,17 +128,18 @@
                 mean = jnp.sum(state * state, -1, keepdims=True) * (1.0 / features)
                 inv_ref[s, r : r + chunk] = lax.rsqrt(mean + 1e-06)
         here = slice(at, at + block)
+        there = pl.ds(pl.multiple_of(step * rows + at, block), block)
         for index, (w_ref, out_ref) in enumerate(zip(weights, outs)):
             scale = HD**-0.5 * LOG2E if (index == 0 and not halo) else 1.0
             made = dot(both_ref[2 * at : 2 * at + 2 * block], w_ref[...])
             base, diff = made[:block], made[block:]
             for s, sign in enumerate(SIGNS):
                 full = base if sign == 0.0 else (base + diff if sign > 0 else base - diff)
-                out_ref[s, here] = (full * (inv_ref[s, here] * scale)).astype(jnp.bfloat16)
+                out_ref[s, there] = (full * (inv_ref[s, here] * scale)).astype(jnp.bfloat16)
 
 
 def project(code, arrays, gain, weights, halo):
-    features = gain.shape[0]
+    features = gain.shape[1]
     cols = weights[0].shape[1]
     tokens = 2 * (arrays[0].shape[0] - 16)
     specs = [ON_CHIP for a in arrays]
@@ -141,9 +150,9 @@
         grid=(2,),
         in_specs=[SCALARS]
         + specs
-        + [pl.BlockSpec(gain.shape, lambda i: (0,))]
+        + [ON_CHIP]
         + [ON_CHIP for w in weights],
-        out_specs=[pl.BlockSpec((3, rows, cols), lambda i: (0, i, 0)) for _ in weights],
+        out_specs=[ON_CHIP for _ in weights],
         scratch_shapes=[
             pltpu.VMEM((2 * rows, features), jnp.bfloat16),
             pltpu.VMEM((3, rows, 1), jnp.float32),
@@ -156,17 +165,18 @@
 def attend_kernel(q_ref, k_ref, v_ref, k_halo_ref, v_halo_ref, *refs, bands):
     *out_refs, held_ref = refs
     tokens, cols = q_ref.shape[1:]
+    step = pl.program_id(0)
     half = tokens // 2
     band = lax.axis_index(BANDS)
     left = band > 0
     right = band < bands - 1
-    k = k_ref[0]
-    v = v_ref[0]
+    k = k_ref[step]
+    v = v_ref[step]
     row = iota((tokens, 1), 0)
     there = jnp.where(row < half, left.astype(jnp.int32), right.astype(jnp.int32)) > 0
-    k_halo = jnp.where(there, k_halo_ref[0], k)
+    k_halo = jnp.where(there, k_halo_ref[step], k)
     one = there.astype(jnp.bfloat16)
-    v_halo = v_halo_ref[0] * one
+    v_halo = v_halo_ref[step] * one
     block, pair = half, 2 * HD
     which = iota((1, pair), 1) // HD
     work = [(head, part) for head in range(cols // HD) for part in range(tokens // block)]
@@ -175,7 +185,7 @@
         return slice(head // 2 * pair, (head // 2 + 1) * pair)
 
     def scores(head, part):
-        q = q_ref[0, part * block : (part + 1) * block, lanes(head)]
+        q = q_ref[step, part * block : (part + 1) * block, lanes(head)]
         q = jnp.where(which == head % 2, q, jnp.zeros_like(q))
         return dot_t(q, k[:, lanes(head)]), dot_t(q, k_halo[:, lanes(head)])
 
@@ -203,19 +213,19 @@
     rank = lax.axis_index("tp")
     for distance, out_ref in enumerate(out_refs):
         first = pl.multiple_of(lax.rem(rank + distance, ranks) * quarter, quarter)
-        out_ref[...] = held_ref[pl.ds(first, quarter), :]
+        mine = pl.ds(pl.multiple_of(step * quarter, quarter), quarter)
+        out_ref[mine, :] = held_ref[pl.ds(first, quarter), :]
 
 
 def attend(q, k, v, k_halo, v_halo, ranks, bands):
     forwards, tokens, cols = q.shape
-    spec = pl.BlockSpec((1, tokens, cols), lambda i: (i, 0, 0))
     quarter = tokens // ranks
     return pl.pallas_call(
         functools.partial(attend_kernel, bands=bands),
         out_shape=[jax.ShapeDtypeStruct((forwards * quarter, cols), jnp.bfloat16)] * ranks,
         grid=(forwards,),
-        in_specs=[spec] * 5,
-        out_specs=[pl.BlockSpec((quarter, cols), lambda i: (i, 0))] * ranks,
+        in_specs=[ON_CHIP] * 5,
+        out_specs=[ON_CHIP] * ranks,
         scratch_shapes=[pltpu.VMEM((tokens, cols), jnp.bfloat16)],
         compiler_params=pltpu.CompilerParams(vmem_limit_bytes=14 * MIB),
         name="attend",
@@ -344,7 +354,7 @@
         combine_kernel,
         out_shape=[jax.ShapeDtypeStruct(s, jnp.bfloat16) for s in (shape, table)],
         in_specs=[SCALARS]
-        + [pl.BlockSpec(a.shape, lambda: (0, 0)) for a in att]
+        + [ON_CHIP for a in att]
         + [pl.BlockSpec(memory_space=pltpu.HBM)] * len(far),
         out_specs=[pl.BlockSpec(shape, lambda: (0, 0, 0)), ON_CHIP],
         scratch_shapes=[
@@ -535,13 +545,12 @@
     bands = lax.axis_size(BANDS)
     tokens, features = global_state.shape
     half = tokens // 2
-    gain = in_hbm(norm_gain)
     cell_band = src_band.reshape(src_tok.shape)
 
     up = [(i, (i + 1) % ranks) for i in range(ranks)]
     down = [(j, i) for i, j in up]
-    last, first, *weights = make_edges(
-        band_codes, in_hbm(global_state), [in_hbm(w) for w in (w_query, w_key, w_value)]
+    last, first, *weights, gain = make_edges(
+        band_codes, in_hbm(global_state), in_hbm(norm_gain), [in_hbm(w) for w in (w_query, w_key, w_value)]
     )
     before, after = neighbours(last, first, BANDS)
     w1, w3 = lax.ppermute(w_out, "tp", up), lax.ppermute(w_out, "tp", down)

time: 108 us -> 108 us (level)
  Pallas kernels: 30.6 us -> 29.3 us
    pallas_call x2, Pallas kernels: 7.68 us -> 6.35 us  [project(): pl.pallas_call(functools.partial(project_kernel, halo=halo), out_shape=[j...]
  transfers between devices with their start and end apart: 13 -> 13, of which waited for: 2 -> 3; matrix products, arithmetic and copies ran while one was open for 0% -> 0% of each run, Pallas kernels for 24% -> 23%
where the time goes in v9:
time: 108 us; the launch traced here: 107 us
  starting transfers between devices  50.5 us (47%)
  Pallas kernels  29.3 us (27%)
  waiting for transfers between devices  25.7 us (24%)
  between operations  1.57 us (1%)
    all_to_all x1, waiting for transfers between devices, per_device(): arrived = lax.all_to_all(send, BANDS, 0, 0, tiled=True)  21.4 us
    ppermute x4, starting transfers between devices, neighbours(): return (lax.ppermute(last, axis, up), lax.ppermute(first, axis, down))  18.6 us
    all_to_all x1, starting transfers between devices, per_device(): asked = lax.all_to_all(asked[:, None, :], BANDS, 0, 0, tiled=True)[:, 0, :]  13.8 us
    pallas_call x1, Pallas kernels, attend(): pl.pallas_call(functools.partial(attend_kernel, bands=bands), out_shape=[...  8.3 us
    all_to_all x1, starting transfers between devices, per_device(): arrived = lax.all_to_all(send, BANDS, 0, 0, tiled=True)  6.6 us
    pallas_call x2, Pallas kernels, project(): pl.pallas_call(functools.partial(project_kernel, halo=halo), out_shape=[j...  6.35 us
    ppermute x3, starting transfers between devices, per_device(): lax.ppermute(attended[d], 'tp', [(i, (i + d) % ranks) for i in range(rank...  4.69 us
    all_to_all x1, waiting for transfers between devices, per_device(): asked = lax.all_to_all(asked[:, None, :], BANDS, 0, 0, tiled=True)[:, 0, :]  4.19 us
  transfers between devices with their start and end apart: 13, of which 3 were waited for; matrix products, arithmetic and copies ran while one was open for 0% of the time, Pallas kernels for 23%

profile of v9, /device:TPU:4, one launch (start us, length us, event | category | flops | bytes accessed | tf_op | source)
XLA Modules:
  0.0 107.1 jit_solution(1352482520979555690)
XLA Ops:
  0.6 1.7 %collective-permute-start = (bf16[256,1024]{1,0:T(8,128)(2,1)}, bf16[256,1024]{1,0:T(8,128)(2,1)S(1)}, u32[]{:S(2)}, u32[]{:S(2)}) collective-permute-start(bf16[256,1024]{1,0:T(8,128)(2,1)} %w0_ref.1), channel_id=1, source_target_pairs={{0,1},{1,2},{2,3},{3,0},{4,5},{5,6},{6,7},{7,4},{8,9},{9,10},{10,1... | collective-permute-start | bytes 1572872 | tf_op jit(solution)/shard_map/ppermute | solution.py:556
  2.3 1.7 %collective-permute-start.1 = (bf16[256,1024]{1,0:T(8,128)(2,1)}, bf16[256,1024]{1,0:T(8,128)(2,1)S(1)}, u32[]{:S(2)}, u32[]{:S(2)}) collective-permute-start(bf16[256,1024]{1,0:T(8,128)(2,1)} %w0_ref.1), channel_id=1, source_target_pairs={{1,0},{2,1},{3,2},{0,3},{5,4},{6,5},{7,6},{4,7},{9,8},{10,9},{11,1... | collective-permute-start | bytes 1572872 | tf_op jit(solution)/shard_map/ppermute | solution.py:556
  4.6 1.7 %edges.1 = (bf16[272,1024]{1,0:T(8,128)(2,1)S(1)}, bf16[272,1024]{1,0:T(8,128)(2,1)S(1)}, bf16[1024,256]{1,0:T(8,128)(2,1)S(1)}, bf16[1024,256]{1,0:T(8,128)(2,1...) custom-call(s32[1]{0:T(128)S(6)} %copy.15.code_ref, bf16[512,1024]{1,0:T(8,128)(2,1)} %x_ref.3, ...), custom_call_target="tpu_custom_call" | custom-call | tf_op jit(solution)/shard_map/edges/pallas_call | solution.py:84
  6.4 1.9 %collective-permute-start.2 = (bf16[272,1024]{1,0:T(8,128)(2,1)S(1)}, bf16[272,1024]{1,0:T(8,128)(2,1)S(1)}, u32[]{:S(2)}, u32[]{:S(2)}) collective-permute-start(bf16[272,1024]{1,0:T(8,128)(2,1)S(1)} %get-tuple-element.42.late_ref), channel_id=1, source_target_pairs={{0,4},{4,8},{8,12},{12,16},{16,20},{20,24},{24,28},{28,32},{32,36}... | collective-permute-start | bytes 1671176 | tf_op jit(solution)/shard_map/ppermute | solution.py:527
  8.3 6.3 %collective-permute-start.3 = (bf16[272,1024]{1,0:T(8,128)(2,1)S(1)}, bf16[272,1024]{1,0:T(8,128)(2,1)S(1)}, u32[]{:S(2)}, u32[]{:S(2)}) collective-permute-start(bf16[272,1024]{1,0:T(8,128)(2,1)S(1)} %get-tuple-element.41.early_ref), channel_id=1, source_target_pairs={{4,0},{8,4},{12,8},{16,12},{20,16},{24,20},{28,24},{32,28},{36,32}... | collective-permute-start | bytes 1671176 | tf_op jit(solution)/shard_map/ppermute | solution.py:527
  14.7 3.5 %project_own.1 = (bf16[3,512,256]{2,1,0:T(8,128)(2,1)S(1)}, bf16[3,512,256]{2,1,0:T(8,128)(2,1)S(1)}, bf16[3,512,256]{2,1,0:T(8,128)(2,1)S(1)}) custom-call(s32[1]{0:T(128)S(6)} %copy.15.code_ref, bf16[272,1024]{1,0:T(8,128)(2,1)S(1)} %get-tuple-element.41.early_ref, bf16[272,1024]{1,0:T(8,128)(2,1)S(1)} %get-tuple-element.42.late_ref, ...), custom_call_target="tpu_custom_call" | custom-call | tf_op jit(solution)/shard_map/project_own/pallas_call | solution.py:147
  18.2 0.0 collective-permute-done.w1_ref
  18.2 0.0 collective-permute-done.1.w3_ref
  18.2 0.4 collective-permute-start.4
  18.7 3.0 %collective-permute-start.5 = (bf16[128,1024]{1,0:T(8,128)(2,1)S(1)}, bf16[128,1024]{1,0:T(8,128)(2,1)S(1)}, u32[]{:S(2)}, u32[]{:S(2)}) collective-permute-start(bf16[128,1024]{1,0:T(8,128)(2,1)S(1)} %slice.7), channel_id=1, source_target_pairs={{1,0},{2,1},{3,2},{0,3},{5,4},{6,5},{7,6},{4,7},{9,8},{10,9},{11,1... | collective-permute-start | bytes 786440 | tf_op jit(solution)/shard_map/ppermute | solution.py:561
  21.6 1.0 ask.1
  22.6 0.1 collective-permute-done.3.late_ref
  22.7 2.9 %project_halo.1 = (bf16[3,512,256]{2,1,0:T(8,128)(2,1)S(1)}, bf16[3,512,256]{2,1,0:T(8,128)(2,1)S(1)}) custom-call(s32[1]{0:T(128)S(6)} %copy.15.code_ref, bf16[272,1024]{1,0:T(8,128)(2,1)S(1)} %collective-permute-done.2.early_ref, bf16[272,1024]{1,0:T(8,128)(2,1)S(1)} %collective-permute-done.3.late_ref, f32[1,1024]{1,0:T(1,128)S(1)} %get-tuple-element.43.gain_ref, ...), custom_call_target="tpu_custom_call" | custom-call | tf_op jit(solution)/shard_map/project_halo/pallas_call | solution.py:147
  25.5 8.3 %attend.1 = (bf16[384,256]{1,0:T(8,128)(2,1)S(1)}, bf16[384,256]{1,0:T(8,128)(2,1)S(1)}, bf16[384,256]{1,0:T(8,128)(2,1)S(1)}, bf16[384,256]{1,0:T(8,128)(2,1)S(1)}) custom-call(bf16[3,512,256]{2,1,0:T(8,128)(2,1)S(1)} %get-tuple-element.49.q_ref, bf16[3,512,256]{2,1,0:T(8,128)(2,1)S(1)} %get-tuple-element.50.k_ref, ...), custom_call_target="tpu_custom_call" | custom-call | tf_op jit(solution)/shard_map/attend/pallas_call | solution.py:223
  33.9 0.0 collective-permute-done.4.top_ref
  33.9 0.0 copy-start.5
  33.9 0.4 collective-permute-start.6
  34.4 2.9 %collective-permute-start.7 = (bf16[384,256]{1,0:T(8,128)(2,1)S(1)}, bf16[384,256]{1,0:T(8,128)(2,1)S(1)}, u32[]{:S(2)}, u32[]{:S(2)}) collective-permute-start(bf16[384,256]{1,0:T(8,128)(2,1)S(1)} %get-tuple-element.64), channel_id=1, source_target_pairs={{0,2},{1,3},{2,0},{3,1},{4,6},{5,7},{6,4},{7,5},{8,10},{9,11},{10,... | collective-permute-start | bytes 589832 | tf_op jit(solution)/shard_map/ppermute | solution.py:567
  37.3 1.3 %collective-permute-start.8 = (bf16[384,256]{1,0:T(8,128)(2,1)S(1)}, bf16[384,256]{1,0:T(8,128)(2,1)S(1)}, u32[]{:S(2)}, u32[]{:S(2)}) collective-permute-start(bf16[384,256]{1,0:T(8,128)(2,1)S(1)} %get-tuple-element.65), channel_id=1, source_target_pairs={{0,3},{1,0},{2,1},{3,2},{4,7},{5,4},{6,5},{7,6},{8,11},{9,8},{10,9... | collective-permute-start | bytes 589832 | tf_op jit(solution)/shard_map/ppermute | solution.py:567
  38.6 13.8 %all-to-all-start = ((s32[64,1,4]{2,1,0:T(1,128)}), s32[64,1,4]{2,1,0:T(1,128)S(1)}, u32[]{:S(2)}, u32[]{:S(2)}) async-start(s32[64,1,4]{2,1,0:T(1,128)} %bitcast.2), calls=%async_computation | async-start | bytes 65536 | tf_op jit(solution)/shard_map/all_to_all | solution.py:570
  52.5 3.4 %combine.1 = (bf16[3,128,1024]{2,1,0:T(8,128)(2,1)}, bf16[512,384]{1,0:T(8,128)(2,1)S(1)}) custom-call(s32[1]{0:T(128)S(6)} %copy.15.code_ref, bf16[384,256]{1,0:T(8,128)(2,1)S(1)} %get-tuple-element.62.att0_ref, bf16[384,256]{1,0:T(8,128)(2,1)S(1)} %collective-permute-done.6.att1_ref, bf16[384,256]{1,0:T(8,128)(2,1)S(1)} %collective-permute-done.7.att2_ref, ...), custom_call_target="tpu_custom_call" | custom-call | tf_op jit(solution)/shard_map/combine/pallas_call | solution.py:353
  55.9 4.2 %all-to-all-done = s32[64,1,4]{2,1,0:T(1,128)S(1)} async-done(((s32[64,1,4]{2,1,0:T(1,128)}), s32[64,1,4]{2,1,0:T(1,128)S(1)}, u32[]{:S(2)}, u32[]{:S(2)}) %all-to-all-start) | async-done | bytes 1056 | tf_op jit(solution)/shard_map/all_to_all | solution.py:570
  60.1 1.8 %serve.1 = bf16[64,16,384]{2,1,0:T(8,128)(2,1)} custom-call(s32[64,4]{1,0:T(8,128)S(1)} %bitcast.5, bf16[512,384]{1,0:T(8,128)(2,1)S(1)} %get-tuple-element.70.table_ref), custom_call_target="tpu_custom_call" | custom-call | tf_op jit(solution)/shard_map/serve/pallas_call | solution.py:378
  61.9 6.6 %all-to-all-start.1 = ((bf16[64,16,384]{2,1,0:T(8,128)(2,1)}), bf16[64,16,384]{2,1,0:T(8,128)(2,1)S(1)}, u32[]{:S(2)}, u32[]{:S(2)}) async-start(bf16[64,16,384]{2,1,0:T(8,128)(2,1)} %serve.1), calls=%async_computation.1 | async-start | bytes 1572864 | tf_op jit(solution)/shard_map/all_to_all | solution.py:576
  68.5 0.0 copy-start
  68.6 1.8 %fetch.1.taps_ref.w_before_ref = bf16[5,512,512]{2,1,0:T(8,128)(2,1)S(1)} custom-call(bf16[9,512,512]{2,1,0:T(8,128)(2,1)} %conv_hbm_ref.1), custom_call_target="tpu_custom_call" | custom-call | tf_op jit(solution)/shard_map/fetch/pallas_call | solution.py:279
  70.4 21.4 %all-to-all-done.1.arrived_ref = bf16[64,16,384]{2,1,0:T(8,128)(2,1)S(1)} async-done(((bf16[64,16,384]{2,1,0:T(8,128)(2,1)}), bf16[64,16,384]{2,1,0:T(8,128)(2,1)S(1)}, u32[]{:S(2)}, u32[]{:S(2)}) %all-to-all-start.1) | async-done | bytes 786464 | tf_op jit(solution)/shard_map/all_to_all | solution.py:576
  91.8 1.0 inputs.1
  92.8 2.6 %collective-permute-start.9 = (bf16[48,512]{1,0:T(8,128)(2,1)S(1)}, bf16[48,512]{1,0:T(8,128)(2,1)S(1)}, u32[]{:S(2)}, u32[]{:S(2)}) collective-permute-start(bf16[48,512]{1,0:T(8,128)(2,1)S(1)} %get-tuple-element.75), channel_id=1, source_target_pairs={{0,1},{1,2},{2,3},{3,4},{4,5},{5,6},{6,7},{7,8},{8,9},{9,10},{10,1... | collective-permute-start | bytes 147464 | tf_op jit(solution)/shard_map/ppermute | solution.py:527
  95.4 7.8 %collective-permute-start.10 = (bf16[48,512]{1,0:T(8,128)(2,1)S(1)}, bf16[48,512]{1,0:T(8,128)(2,1)S(1)}, u32[]{:S(2)}, u32[]{:S(2)}) collective-permute-start(bf16[48,512]{1,0:T(8,128)(2,1)S(1)} %get-tuple-element.76), channel_id=1, source_target_pairs={{1,0},{2,1},{3,2},{4,3},{5,4},{6,5},{7,6},{8,7},{9,8},{10,9},{11,1... | collective-permute-start | bytes 147464 | tf_op jit(solution)/shard_map/ppermute | solution.py:527
  103.2 2.3 %convolve_inner.1 = (f32[384,512]{1,0:T(8,128)S(1)}, bf16[3,512,512]{2,1,0:T(8,128)(2,1)S(1)}) custom-call(bf16[8,48,512]{2,1,0:T(8,128)(2,1)S(1)} %get-tuple-element.74.x_ref, bf16[5,512,512]{2,1,0:T(8,128)(2,1)S(1)} %fetch.1.taps_ref.w_before_ref, bf16[9,512,512]{2,1,0:T(8,128)(2,1)} %conv_hbm_ref.1), custom_call_target="tpu_custom_call" | custom-call | tf_op jit(solution)/shard_map/convolve_inner/pallas_call | solution.py:471
  105.5 1.6 %convolve_finish.1 = bf16[3,8,16,512]{3,2,1,0:T(8,128)(2,1)} custom-call(bf16[8,48,512]{2,1,0:T(8,128)(2,1)S(1)} %get-tuple-element.74.x_ref, bf16[48,512]{1,0:T(8,128)(2,1)S(1)} %collective-permute-done.9.before_ref, bf16[48,512]{1,0:T(8,128)(2,1)S(1)} %collective-permute-done.10.after_ref, bf16[5,512,512]{2,1,0:T(8,128)(2,1)S(1)} %fetch.1.taps_ref.w_before_ref, ...), custom_call_target="tpu_custom_call" | custom-call | tf_op jit(solution)/shard_map/convolve_finish/pallas_call | solution.py:513
  (21 shorter events, 0.1 us)
Async XLA Ops:
  0.6 17.5 %collective-permute-start = (bf16[256,1024]{1,0:T(8,128)(2,1)}, bf16[256,1024]{1,0:T(8,128)(2,1)S(1)}, u32[]{:S(2)}, u32[]{:S(2)}) collective-permute-start(bf16[256,1024]{1,0:T(8,128)(2,1)} %w0_ref.1), channel_id=1, source_target_pairs={{0,1},{1,2},{2,3},{3,0},{4,5},{5,6},{6,7},{7,4},{8,9},{9,10},{10,1... | collective-permute-start | bytes 1572872 | tf_op jit(solution)/shard_map/ppermute | solution.py:556
  2.3 15.9 %collective-permute-start.1 = (bf16[256,1024]{1,0:T(8,128)(2,1)}, bf16[256,1024]{1,0:T(8,128)(2,1)S(1)}, u32[]{:S(2)}, u32[]{:S(2)}) collective-permute-start(bf16[256,1024]{1,0:T(8,128)(2,1)} %w0_ref.1), channel_id=1, source_target_pairs={{1,0},{2,1},{3,2},{0,3},{5,4},{6,5},{7,6},{4,7},{9,8},{10,9},{11,1... | collective-permute-start | bytes 1572872 | tf_op jit(solution)/shard_map/ppermute | solution.py:556
  4.6 17.0 %copy-start.1 = (s32[8,16,1]{1,2,0:T(1,128)S(1)}, s32[8,16,1]{1,2,0:T(1,128)}, u32[]{:S(2)}) copy-start(s32[8,16,1]{1,2,0:T(1,128)} %param.20) | copy-start | bytes 1540
  4.6 17.0 %copy-start.2 = (s32[8,16]{1,0:T(8,128)S(1)}, s32[8,16]{1,0:T(8,128)}, u32[]{:S(2)}) copy-start(s32[8,16]{1,0:T(8,128)} %tok_ref.1) | copy-start | bytes 1540
  6.4 16.2 %collective-permute-start.2 = (bf16[272,1024]{1,0:T(8,128)(2,1)S(1)}, bf16[272,1024]{1,0:T(8,128)(2,1)S(1)}, u32[]{:S(2)}, u32[]{:S(2)}) collective-permute-start(bf16[272,1024]{1,0:T(8,128)(2,1)S(1)} %get-tuple-element.42.late_ref), channel_id=1, source_target_pairs={{0,4},{4,8},{8,12},{12,16},{16,20},{20,24},{24,28},{28,32},{32,36}... | collective-permute-start | bytes 1671176 | tf_op jit(solution)/shard_map/ppermute | solution.py:527
  8.3 14.4 %collective-permute-start.3 = (bf16[272,1024]{1,0:T(8,128)(2,1)S(1)}, bf16[272,1024]{1,0:T(8,128)(2,1)S(1)}, u32[]{:S(2)}, u32[]{:S(2)}) collective-permute-start(bf16[272,1024]{1,0:T(8,128)(2,1)S(1)} %get-tuple-element.41.early_ref), channel_id=1, source_target_pairs={{4,0},{8,4},{12,8},{16,12},{20,16},{24,20},{28,24},{32,28},{36,32}... | collective-permute-start | bytes 1671176 | tf_op jit(solution)/shard_map/ppermute | solution.py:527
  18.2 15.7 %copy-start.3 = (bf16[256,1024]{1,0:T(8,128)(2,1)}, bf16[256,1024]{1,0:T(8,128)(2,1)S(1)}, u32[]{:S(2)}) copy-start(bf16[256,1024]{1,0:T(8,128)(2,1)S(1)} %collective-permute-done.w1_ref) | copy-start | bytes 1572868
  18.2 15.7 %copy-start.4 = (bf16[256,1024]{1,0:T(8,128)(2,1)}, bf16[256,1024]{1,0:T(8,128)(2,1)S(1)}, u32[]{:S(2)}) copy-start(bf16[256,1024]{1,0:T(8,128)(2,1)S(1)} %collective-permute-done.1.w3_ref) | copy-start | bytes 1572868
  18.2 15.7 %collective-permute-start.4 = (bf16[128,1024]{1,0:T(8,128)(2,1)S(1)}, bf16[128,1024]{1,0:T(8,128)(2,1)S(1)}, u32[]{:S(2)}, u32[]{:S(2)}) collective-permute-start(bf16[128,1024]{1,0:T(8,128)(2,1)S(1)} %slice.6), channel_id=1, source_target_pairs={{0,1},{1,2},{2,3},{3,0},{4,5},{5,6},{6,7},{7,4},{8,9},{9,10},{10,1... | collective-permute-start | bytes 786440 | tf_op jit(solution)/shard_map/ppermute | solution.py:561
  18.7 15.2 %collective-permute-start.5 = (bf16[128,1024]{1,0:T(8,128)(2,1)S(1)}, bf16[128,1024]{1,0:T(8,128)(2,1)S(1)}, u32[]{:S(2)}, u32[]{:S(2)}) collective-permute-start(bf16[128,1024]{1,0:T(8,128)(2,1)S(1)} %slice.7), channel_id=1, source_target_pairs={{1,0},{2,1},{3,2},{0,3},{5,4},{6,5},{7,6},{4,7},{9,8},{10,9},{11,1... | collective-permute-start | bytes 786440 | tf_op jit(solution)/shard_map/ppermute | solution.py:561
  33.9 18.6 %copy-start.5 = (bf16[128,1024]{1,0:T(8,128)(2,1)}, bf16[128,1024]{1,0:T(8,128)(2,1)S(1)}, u32[]{:S(2)}) copy-start(bf16[128,1024]{1,0:T(8,128)(2,1)S(1)} %collective-permute-done.4.top_ref) | copy-start | bytes 786436
  33.9 18.6 %copy-start.6 = (bf16[128,1024]{1,0:T(8,128)(2,1)}, bf16[128,1024]{1,0:T(8,128)(2,1)S(1)}, u32[]{:S(2)}) copy-start(bf16[128,1024]{1,0:T(8,128)(2,1)S(1)} %collective-permute-done.5.low_ref) | copy-start | bytes 786436
  33.9 18.5 %collective-permute-start.6 = (bf16[384,256]{1,0:T(8,128)(2,1)S(1)}, bf16[384,256]{1,0:T(8,128)(2,1)S(1)}, u32[]{:S(2)}, u32[]{:S(2)}) collective-permute-start(bf16[384,256]{1,0:T(8,128)(2,1)S(1)} %get-tuple-element.63), channel_id=1, source_target_pairs={{0,1},{1,2},{2,3},{3,0},{4,5},{5,6},{6,7},{7,4},{8,9},{9,10},{10,1... | collective-permute-start | bytes 589832 | tf_op jit(solution)/shard_map/ppermute | solution.py:567
  34.4 18.1 %collective-permute-start.7 = (bf16[384,256]{1,0:T(8,128)(2,1)S(1)}, bf16[384,256]{1,0:T(8,128)(2,1)S(1)}, u32[]{:S(2)}, u32[]{:S(2)}) collective-permute-start(bf16[384,256]{1,0:T(8,128)(2,1)S(1)} %get-tuple-element.64), channel_id=1, source_target_pairs={{0,2},{1,3},{2,0},{3,1},{4,6},{5,7},{6,4},{7,5},{8,10},{9,11},{10,... | collective-permute-start | bytes 589832 | tf_op jit(solution)/shard_map/ppermute | solution.py:567
  37.3 15.2 %collective-permute-start.8 = (bf16[384,256]{1,0:T(8,128)(2,1)S(1)}, bf16[384,256]{1,0:T(8,128)(2,1)S(1)}, u32[]{:S(2)}, u32[]{:S(2)}) collective-permute-start(bf16[384,256]{1,0:T(8,128)(2,1)S(1)} %get-tuple-element.65), channel_id=1, source_target_pairs={{0,3},{1,0},{2,1},{3,2},{4,7},{5,4},{6,5},{7,6},{8,11},{9,8},{10,9... | collective-permute-start | bytes 589832 | tf_op jit(solution)/shard_map/ppermute | solution.py:567
  38.6 21.5 %all-to-all-start = ((s32[64,1,4]{2,1,0:T(1,128)}), s32[64,1,4]{2,1,0:T(1,128)S(1)}, u32[]{:S(2)}, u32[]{:S(2)}) async-start(s32[64,1,4]{2,1,0:T(1,128)} %bitcast.2), calls=%async_computation | async-start | bytes 65536 | tf_op jit(solution)/shard_map/all_to_all | solution.py:570
  61.9 29.8 %all-to-all-start.1 = ((bf16[64,16,384]{2,1,0:T(8,128)(2,1)}), bf16[64,16,384]{2,1,0:T(8,128)(2,1)S(1)}, u32[]{:S(2)}, u32[]{:S(2)}) async-start(bf16[64,16,384]{2,1,0:T(8,128)(2,1)} %serve.1), calls=%async_computation.1 | async-start | bytes 1572864 | tf_op jit(solution)/shard_map/all_to_all | solution.py:576
  68.5 23.2 %copy-start = (bf16[8,16,512]{2,1,0:T(8,128)(2,1)S(1)}, bf16[8,16,512]{2,1,0:T(8,128)(2,1)}, u32[]{:S(2)}) copy-start(bf16[8,16,512]{2,1,0:T(8,128)(2,1)} %reg_ref.1) | copy-start | bytes 393220
  92.8 12.7 %collective-permute-start.9 = (bf16[48,512]{1,0:T(8,128)(2,1)S(1)}, bf16[48,512]{1,0:T(8,128)(2,1)S(1)}, u32[]{:S(2)}, u32[]{:S(2)}) collective-permute-start(bf16[48,512]{1,0:T(8,128)(2,1)S(1)} %get-tuple-element.75), channel_id=1, source_target_pairs={{0,1},{1,2},{2,3},{3,4},{4,5},{5,6},{6,7},{7,8},{8,9},{9,10},{10,1... | collective-permute-start | bytes 147464 | tf_op jit(solution)/shard_map/ppermute | solution.py:527
  95.4 10.1 %collective-permute-start.10 = (bf16[48,512]{1,0:T(8,128)(2,1)S(1)}, bf16[48,512]{1,0:T(8,128)(2,1)S(1)}, u32[]{:S(2)}, u32[]{:S(2)}) collective-permute-start(bf16[48,512]{1,0:T(8,128)(2,1)S(1)} %get-tuple-element.76), channel_id=1, source_target_pairs={{1,0},{2,1},{3,2},{4,3},{5,4},{6,5},{7,6},{8,7},{9,8},{10,9},{11,1... | collective-permute-start | bytes 147464 | tf_op jit(solution)/shard_map/ppermute | solution.py:527

commit v10 on v9

--- a/solution.py
+++ b/solution.py
@@ -49,19 +49,12 @@
     return (level - 511.5) * (0.5 / 295.6)
 
 
-def edges_kernel(code_ref, x_ref, *refs):
-    *refs, flat_ref, sems = refs
-    gain_ref, *refs, row_ref = refs
-    count = (len(refs) - 2) // 2
-    weights, (last_ref, first_ref, *held) = refs[:count], refs[count:]
+def edges_kernel(code_ref, x_ref, last_ref, first_ref, sems):
     half = x_ref.shape[0] // 2
-    pairs = [
-        (x_ref.at[pl.ds(half, half)], last_ref.at[pl.ds(0, half)]),
-        (x_ref.at[pl.ds(0, half)], first_ref.at[pl.ds(0, half)]),
-        *zip(weights, held),
-        (gain_ref, flat_ref),
+    copies = [
+        pltpu.make_async_copy(x_ref.at[pl.ds(half, half)], last_ref.at[pl.ds(0, half)], sems.at[0]),
+        pltpu.make_async_copy(x_ref.at[pl.ds(0, half)], first_ref.at[pl.ds(0, half)], sems.at[1]),
     ]
-    copies = [pltpu.make_async_copy(a, b, sems.at[i]) for i, (a, b) in enumerate(pairs)]
     for copy in copies:
         copy.start()
     code = jnp.full((16, x_ref.shape[1]), code_ref[0], jnp.int32)
@@ -73,26 +66,47 @@
     first_ref[half:] = digit
     for copy in copies:
         copy.wait()
-    row_ref[...] = flat_ref[...].astype(jnp.float32).reshape(row_ref.shape)
-
-
-def make_edges(code, x, gain, weights):
+
+
+def make_edges(code, x):
     tokens, features = x.shape
-    shapes = [(tokens // 2 + 16, features)] * 2 + [w.shape for w in weights]
-    shapes = [jax.ShapeDtypeStruct(s, jnp.bfloat16) for s in shapes]
-    shapes.append(jax.ShapeDtypeStruct((1, features), jnp.float32))
+    shape = jax.ShapeDtypeStruct((tokens // 2 + 16, features), jnp.bfloat16)
     return pl.pallas_call(
         edges_kernel,
-        out_shape=shapes,
-        in_specs=[SCALARS] + [pl.BlockSpec(memory_space=pltpu.HBM)] * (2 + len(weights)),
-        out_specs=[ON_CHIP] * len(shapes),
-        scratch_shapes=[
-            pltpu.VMEM(gain.shape, gain.dtype),
-            pltpu.SemaphoreType.DMA((3 + len(weights),)),
-        ],
+        out_shape=[shape, shape],
+        in_specs=[SCALARS, pl.BlockSpec(memory_space=pltpu.HBM)],
+        out_specs=[ON_CHIP] * 2,
+        scratch_shapes=[pltpu.SemaphoreType.DMA((2,))],
         compiler_params=pltpu.CompilerParams(vmem_limit_bytes=2 * MIB),
         name="edges",
-    )(code, x, gain, *weights)
+    )(code, x)
+
+
+def load_kernel(gain_ref, *refs):
+    *refs, row_ref, flat_ref, sems = refs
+    count = len(refs) // 2
+    pairs = [*zip(refs[:count], refs[count:]), (gain_ref, flat_ref)]
+    copies = [pltpu.make_async_copy(a, b, sems.at[i]) for i, (a, b) in enumerate(pairs)]
+    for copy in copies:
+        copy.start()
+    for copy in copies:
+        copy.wait()
+    row_ref[...] = flat_ref[...].astype(jnp.float32).reshape(row_ref.shape)
+
+
+def load(gain, weights):
+    shapes = [jax.ShapeDtypeStruct(w.shape, w.dtype) for w in weights]
+    shapes.append(jax.ShapeDtypeStruct((1, gain.shape[0]), jnp.float32))
+    count = len(weights) + 1
+    return pl.pallas_call(
+        load_kernel,
+        out_shape=shapes,
+        in_specs=[pl.BlockSpec(memory_space=pltpu.HBM)] * count,
+        out_specs=[ON_CHIP] * count,
+        scratch_shapes=[pltpu.VMEM(gain.shape, gain.dtype), pltpu.SemaphoreType.DMA((count,))],
+        compiler_params=pltpu.CompilerParams(vmem_limit_bytes=2 * MIB),
+        name="load",
+    )(gain, *weights)
 
 
 def project_kernel(code_ref, early_ref, late_ref, gain_ref, *refs, halo):
@@ -549,10 +563,10 @@
 
     up = [(i, (i + 1) % ranks) for i in range(ranks)]
     down = [(j, i) for i, j in up]
-    last, first, *weights, gain = make_edges(
-        band_codes, in_hbm(global_state), in_hbm(norm_gain), [in_hbm(w) for w in (w_query, w_key, w_value)]
-    )
+    last, first = make_edges(band_codes, in_hbm(global_state))
     before, after = neighbours(last, first, BANDS)
+    last, w_query, w_key, w_value = lax.optimization_barrier((last, w_query, w_key, w_value))
+    *weights, gain = load(in_hbm(norm_gain), [in_hbm(w) for w in (w_query, w_key, w_value)])
     w1, w3 = lax.ppermute(w_out, "tp", up), lax.ppermute(w_out, "tp", down)
     q, k, v = project(band_codes, [first, last], gain, weights, False)
     asked = ask(cell_band, src_tok, bands)

time: 108 us -> 107 us (level)
  starting transfers between devices: 50.5 us -> 49.1 us
    ppermute x3, starting transfers between devices: 4.69 us -> 3.47 us  [per_device(): lax.ppermute(attended[d], 'tp', [(i, (i + d) % ranks) for i in range(rank...]
    pallas_call x1 -> x2, Pallas kernels: 1.75 us -> 2.63 us  [the longest x1 1.41 us: load(): pl.pallas_call(load_kernel, out_shape=shapes, in_specs=[pl.BlockSpec(memo...]
  transfers between devices with their start and end apart: 13 -> 13, of which waited for: 3 -> 2; matrix products, arithmetic and copies ran while one was open for 0% -> 0% of each run, Pallas kernels for 23% -> 24%
where the time goes in v10:
time: 107 us
  starting transfers between devices  49.1 us (46%)
  Pallas kernels  30.1 us (28%)
  waiting for transfers between devices  25.6 us (24%)
  between operations  1.58 us (1%)
    all_to_all x1, waiting for transfers between devices, per_device(): arrived = lax.all_to_all(send, BANDS, 0, 0, tiled=True)  21.4 us
    ppermute x4, starting transfers between devices, neighbours(): return (lax.ppermute(last, axis, up), lax.ppermute(first, axis, down))  18.6 us
    all_to_all x1, starting transfers between devices, per_device(): asked = lax.all_to_all(asked[:, None, :], BANDS, 0, 0, tiled=True)[:, 0, :]  13.7 us
    pallas_call x1, Pallas kernels, attend(): pl.pallas_call(functools.partial(attend_kernel, bands=bands), out_shape=[...  8.3 us
    all_to_all x1, starting transfers between devices, per_device(): arrived = lax.all_to_all(send, BANDS, 0, 0, tiled=True)  6.61 us
    pallas_call x2, Pallas kernels, project(): pl.pallas_call(functools.partial(project_kernel, halo=halo), out_shape=[j...  6.36 us
    all_to_all x1, waiting for transfers between devices, per_device(): asked = lax.all_to_all(asked[:, None, :], BANDS, 0, 0, tiled=True)[:, 0, :]  4.18 us
    ppermute x3, starting transfers between devices, per_device(): lax.ppermute(attended[d], 'tp', [(i, (i + d) % ranks) for i in range(rank...  3.47 us
  transfers between devices with their start and end apart: 13, of which 2 were waited for; matrix products, arithmetic and copies ran while one was open for 0% of the time, Pallas kernels for 24%

profile of v10, /device:TPU:4, one launch (start us, length us, event | category | flops | bytes accessed | tf_op | source)
XLA Modules:
  0.0 106.5 jit_solution(7451388793312427953)
XLA Ops:
  0.6 1.7 %collective-permute-start = (bf16[256,1024]{1,0:T(8,128)(2,1)}, bf16[256,1024]{1,0:T(8,128)(2,1)S(1)}, u32[]{:S(2)}, u32[]{:S(2)}) collective-permute-start(bf16[256,1024]{1,0:T(8,128)(2,1)} %w0_ref.1), channel_id=1, source_target_pairs={{0,1},{1,2},{2,3},{3,0},{4,5},{5,6},{6,7},{7,4},{8,9},{9,10},{10,1... | collective-permute-start | bytes 1572872 | tf_op jit(solution)/shard_map/ppermute | solution.py:570
  2.3 1.7 %collective-permute-start.1 = (bf16[256,1024]{1,0:T(8,128)(2,1)}, bf16[256,1024]{1,0:T(8,128)(2,1)S(1)}, u32[]{:S(2)}, u32[]{:S(2)}) collective-permute-start(bf16[256,1024]{1,0:T(8,128)(2,1)} %w0_ref.1), channel_id=1, source_target_pairs={{1,0},{2,1},{3,2},{0,3},{5,4},{6,5},{7,6},{4,7},{9,8},{10,9},{11,1... | collective-permute-start | bytes 1572872 | tf_op jit(solution)/shard_map/ppermute | solution.py:570
  4.6 1.2 %edges.1 = (bf16[272,1024]{1,0:T(8,128)(2,1)S(1)}, bf16[272,1024]{1,0:T(8,128)(2,1)S(1)}) custom-call(s32[1]{0:T(128)S(6)} %copy.15.code_ref, bf16[512,1024]{1,0:T(8,128)(2,1)} %x_ref.3), custom_call_target="tpu_custom_call" | custom-call | tf_op jit(solution)/shard_map/edges/pallas_call | solution.py:74
  5.8 1.9 %collective-permute-start.2 = (bf16[272,1024]{1,0:T(8,128)(2,1)S(1)}, bf16[272,1024]{1,0:T(8,128)(2,1)S(1)}, u32[]{:S(2)}, u32[]{:S(2)}) collective-permute-start(bf16[272,1024]{1,0:T(8,128)(2,1)S(1)} %get-tuple-element.47.late_ref), channel_id=1, source_target_pairs={{0,4},{4,8},{8,12},{12,16},{16,20},{20,24},{24,28},{28,32},{32,36}... | collective-permute-start | bytes 1671176 | tf_op jit(solution)/shard_map/ppermute | solution.py:541
  7.8 0.0 copy-start.1
  7.8 0.0 copy-start.2
  7.8 6.3 %collective-permute-start.3 = (bf16[272,1024]{1,0:T(8,128)(2,1)S(1)}, bf16[272,1024]{1,0:T(8,128)(2,1)S(1)}, u32[]{:S(2)}, u32[]{:S(2)}) collective-permute-start(bf16[272,1024]{1,0:T(8,128)(2,1)S(1)} %get-tuple-element.45.early_ref), channel_id=1, source_target_pairs={{4,0},{8,4},{12,8},{16,12},{20,16},{24,20},{28,24},{32,28},{36,32}... | collective-permute-start | bytes 1671176 | tf_op jit(solution)/shard_map/ppermute | solution.py:541
  14.1 1.4 %load.1 = (bf16[1024,256]{1,0:T(8,128)(2,1)S(1)}, bf16[1024,256]{1,0:T(8,128)(2,1)S(1)}, bf16[1024,256]{1,0:T(8,128)(2,1)S(1)}, f32[1,1024]{1,0:T(1,128)S(1)}) custom-call(bf16[1024]{0:T(1024)(128)(2,1)} %gain_ref.1, bf16[1024,256]{1,0:T(8,128)(2,1)} %refs_0_, bf16[1024,256]{1,0:T(8,128)(2,1)} %refs_1_, bf16[1024,256]{1,0:T(8,128)(2,1)} %refs_2_), custom_call_target="tpu_custom_call" | custom-call | tf_op jit(solution)/shard_map/load/pallas_call | solution.py:101
  15.5 3.5 %project_own.1 = (bf16[3,512,256]{2,1,0:T(8,128)(2,1)S(1)}, bf16[3,512,256]{2,1,0:T(8,128)(2,1)S(1)}, bf16[3,512,256]{2,1,0:T(8,128)(2,1)S(1)}) custom-call(s32[1]{0:T(128)S(6)} %copy.15.code_ref, bf16[272,1024]{1,0:T(8,128)(2,1)S(1)} %get-tuple-element.45.early_ref, bf16[272,1024]{1,0:T(8,128)(2,1)S(1)} %get-tuple-element.47.late_ref, ...), custom_call_target="tpu_custom_call" | custom-call | tf_op jit(solution)/shard_map/project_own/pallas_call | solution.py:161
  19.0 0.0 collective-permute-done.w1_ref
  19.1 0.4 collective-permute-start.4
  19.6 2.9 %collective-permute-start.5 = (bf16[128,1024]{1,0:T(8,128)(2,1)S(1)}, bf16[128,1024]{1,0:T(8,128)(2,1)S(1)}, u32[]{:S(2)}, u32[]{:S(2)}) collective-permute-start(bf16[128,1024]{1,0:T(8,128)(2,1)S(1)} %slice.7), channel_id=1, source_target_pairs={{1,0},{2,1},{3,2},{0,3},{5,4},{6,5},{7,6},{4,7},{9,8},{10,9},{11,1... | collective-permute-start | bytes 786440 | tf_op jit(solution)/shard_map/ppermute | solution.py:575
  22.5 1.0 ask.1
  23.5 2.9 %project_halo.1 = (bf16[3,512,256]{2,1,0:T(8,128)(2,1)S(1)}, bf16[3,512,256]{2,1,0:T(8,128)(2,1)S(1)}) custom-call(s32[1]{0:T(128)S(6)} %copy.15.code_ref, bf16[272,1024]{1,0:T(8,128)(2,1)S(1)} %collective-permute-done.2.early_ref, bf16[272,1024]{1,0:T(8,128)(2,1)S(1)} %collective-permute-done.3.late_ref, f32[1,1024]{1,0:T(1,128)S(1)} %get-tuple-element.51.gain_ref, ...), custom_call_target="tpu_custom_call" | custom-call | tf_op jit(solution)/shard_map/project_halo/pallas_call | solution.py:161
  26.4 8.3 %attend.1 = (bf16[384,256]{1,0:T(8,128)(2,1)S(1)}, bf16[384,256]{1,0:T(8,128)(2,1)S(1)}, bf16[384,256]{1,0:T(8,128)(2,1)S(1)}, bf16[384,256]{1,0:T(8,128)(2,1)S(1)}) custom-call(bf16[3,512,256]{2,1,0:T(8,128)(2,1)S(1)} %get-tuple-element.57.q_ref, bf16[3,512,256]{2,1,0:T(8,128)(2,1)S(1)} %get-tuple-element.58.k_ref, ...), custom_call_target="tpu_custom_call" | custom-call | tf_op jit(solution)/shard_map/attend/pallas_call | solution.py:237
  34.7 0.0 copy-start.5
  34.7 0.1 collective-permute-start.6
  34.8 2.1 %collective-permute-start.7 = (bf16[384,256]{1,0:T(8,128)(2,1)S(1)}, bf16[384,256]{1,0:T(8,128)(2,1)S(1)}, u32[]{:S(2)}, u32[]{:S(2)}) collective-permute-start(bf16[384,256]{1,0:T(8,128)(2,1)S(1)} %get-tuple-element.72), channel_id=1, source_target_pairs={{0,2},{1,3},{2,0},{3,1},{4,6},{5,7},{6,4},{7,5},{8,10},{9,11},{10,... | collective-permute-start | bytes 589832 | tf_op jit(solution)/shard_map/ppermute | solution.py:581
  36.9 1.3 %collective-permute-start.8 = (bf16[384,256]{1,0:T(8,128)(2,1)S(1)}, bf16[384,256]{1,0:T(8,128)(2,1)S(1)}, u32[]{:S(2)}, u32[]{:S(2)}) collective-permute-start(bf16[384,256]{1,0:T(8,128)(2,1)S(1)} %get-tuple-element.73), channel_id=1, source_target_pairs={{0,3},{1,0},{2,1},{3,2},{4,7},{5,4},{6,5},{7,6},{8,11},{9,8},{10,9... | collective-permute-start | bytes 589832 | tf_op jit(solution)/shard_map/ppermute | solution.py:581
  38.2 13.7 %all-to-all-start = ((s32[64,1,4]{2,1,0:T(1,128)}), s32[64,1,4]{2,1,0:T(1,128)S(1)}, u32[]{:S(2)}, u32[]{:S(2)}) async-start(s32[64,1,4]{2,1,0:T(1,128)} %bitcast.2), calls=%async_computation | async-start | bytes 65536 | tf_op jit(solution)/shard_map/all_to_all | solution.py:584
  51.9 3.4 %combine.1 = (bf16[3,128,1024]{2,1,0:T(8,128)(2,1)}, bf16[512,384]{1,0:T(8,128)(2,1)S(1)}) custom-call(s32[1]{0:T(128)S(6)} %copy.15.code_ref, bf16[384,256]{1,0:T(8,128)(2,1)S(1)} %get-tuple-element.70.att0_ref, bf16[384,256]{1,0:T(8,128)(2,1)S(1)} %collective-permute-done.6.att1_ref, bf16[384,256]{1,0:T(8,128)(2,1)S(1)} %collective-permute-done.7.att2_ref, ...), custom_call_target="tpu_custom_call" | custom-call | tf_op jit(solution)/shard_map/combine/pallas_call | solution.py:367
  55.4 4.2 %all-to-all-done = s32[64,1,4]{2,1,0:T(1,128)S(1)} async-done(((s32[64,1,4]{2,1,0:T(1,128)}), s32[64,1,4]{2,1,0:T(1,128)S(1)}, u32[]{:S(2)}, u32[]{:S(2)}) %all-to-all-start) | async-done | bytes 1056 | tf_op jit(solution)/shard_map/all_to_all | solution.py:584
  59.6 1.8 %serve.1 = bf16[64,16,384]{2,1,0:T(8,128)(2,1)} custom-call(s32[64,4]{1,0:T(8,128)S(1)} %bitcast.5, bf16[512,384]{1,0:T(8,128)(2,1)S(1)} %get-tuple-element.78.table_ref), custom_call_target="tpu_custom_call" | custom-call | tf_op jit(solution)/shard_map/serve/pallas_call | solution.py:392
  61.4 6.6 %all-to-all-start.1 = ((bf16[64,16,384]{2,1,0:T(8,128)(2,1)}), bf16[64,16,384]{2,1,0:T(8,128)(2,1)S(1)}, u32[]{:S(2)}, u32[]{:S(2)}) async-start(bf16[64,16,384]{2,1,0:T(8,128)(2,1)} %serve.1), calls=%async_computation.1 | async-start | bytes 1572864 | tf_op jit(solution)/shard_map/all_to_all | solution.py:590
  68.0 0.0 copy-start
  68.0 1.8 %fetch.1.taps_ref.w_before_ref = bf16[5,512,512]{2,1,0:T(8,128)(2,1)S(1)} custom-call(bf16[9,512,512]{2,1,0:T(8,128)(2,1)} %conv_hbm_ref.1), custom_call_target="tpu_custom_call" | custom-call | tf_op jit(solution)/shard_map/fetch/pallas_call | solution.py:293
  69.8 21.4 %all-to-all-done.1.arrived_ref = bf16[64,16,384]{2,1,0:T(8,128)(2,1)S(1)} async-done(((bf16[64,16,384]{2,1,0:T(8,128)(2,1)}), bf16[64,16,384]{2,1,0:T(8,128)(2,1)S(1)}, u32[]{:S(2)}, u32[]{:S(2)}) %all-to-all-start.1) | async-done | bytes 786464 | tf_op jit(solution)/shard_map/all_to_all | solution.py:590
  91.2 1.0 inputs.1
  92.2 2.6 %collective-permute-start.9 = (bf16[48,512]{1,0:T(8,128)(2,1)S(1)}, bf16[48,512]{1,0:T(8,128)(2,1)S(1)}, u32[]{:S(2)}, u32[]{:S(2)}) collective-permute-start(bf16[48,512]{1,0:T(8,128)(2,1)S(1)} %get-tuple-element.83), channel_id=1, source_target_pairs={{0,1},{1,2},{2,3},{3,4},{4,5},{5,6},{6,7},{7,8},{8,9},{9,10},{10,1... | collective-permute-start | bytes 147464 | tf_op jit(solution)/shard_map/ppermute | solution.py:541
  94.8 7.8 %collective-permute-start.10 = (bf16[48,512]{1,0:T(8,128)(2,1)S(1)}, bf16[48,512]{1,0:T(8,128)(2,1)S(1)}, u32[]{:S(2)}, u32[]{:S(2)}) collective-permute-start(bf16[48,512]{1,0:T(8,128)(2,1)S(1)} %get-tuple-element.84), channel_id=1, source_target_pairs={{1,0},{2,1},{3,2},{4,3},{5,4},{6,5},{7,6},{8,7},{9,8},{10,9},{11,1... | collective-permute-start | bytes 147464 | tf_op jit(solution)/shard_map/ppermute | solution.py:541
  102.6 2.3 %convolve_inner.1 = (f32[384,512]{1,0:T(8,128)S(1)}, bf16[3,512,512]{2,1,0:T(8,128)(2,1)S(1)}) custom-call(bf16[8,48,512]{2,1,0:T(8,128)(2,1)S(1)} %get-tuple-element.82.x_ref, bf16[5,512,512]{2,1,0:T(8,128)(2,1)S(1)} %fetch.1.taps_ref.w_before_ref, bf16[9,512,512]{2,1,0:T(8,128)(2,1)} %conv_hbm_ref.1), custom_call_target="tpu_custom_call" | custom-call | tf_op jit(solution)/shard_map/convolve_inner/pallas_call | solution.py:485
  104.9 1.6 %convolve_finish.1 = bf16[3,8,16,512]{3,2,1,0:T(8,128)(2,1)} custom-call(bf16[8,48,512]{2,1,0:T(8,128)(2,1)S(1)} %get-tuple-element.82.x_ref, bf16[48,512]{1,0:T(8,128)(2,1)S(1)} %collective-permute-done.9.before_ref, bf16[48,512]{1,0:T(8,128)(2,1)S(1)} %collective-permute-done.10.after_ref, bf16[5,512,512]{2,1,0:T(8,128)(2,1)S(1)} %fetch.1.taps_ref.w_before_ref, ...), custom_call_target="tpu_custom_call" | custom-call | tf_op jit(solution)/shard_map/convolve_finish/pallas_call | solution.py:527
  (22 shorter events, 0.1 us)
Async XLA Ops:
  0.6 18.4 %collective-permute-start = (bf16[256,1024]{1,0:T(8,128)(2,1)}, bf16[256,1024]{1,0:T(8,128)(2,1)S(1)}, u32[]{:S(2)}, u32[]{:S(2)}) collective-permute-start(bf16[256,1024]{1,0:T(8,128)(2,1)} %w0_ref.1), channel_id=1, source_target_pairs={{0,1},{1,2},{2,3},{3,0},{4,5},{5,6},{6,7},{7,4},{8,9},{9,10},{10,1... | collective-permute-start | bytes 1572872 | tf_op jit(solution)/shard_map/ppermute | solution.py:570
  2.3 16.8 %collective-permute-start.1 = (bf16[256,1024]{1,0:T(8,128)(2,1)}, bf16[256,1024]{1,0:T(8,128)(2,1)S(1)}, u32[]{:S(2)}, u32[]{:S(2)}) collective-permute-start(bf16[256,1024]{1,0:T(8,128)(2,1)} %w0_ref.1), channel_id=1, source_target_pairs={{1,0},{2,1},{3,2},{0,3},{5,4},{6,5},{7,6},{4,7},{9,8},{10,9},{11,1... | collective-permute-start | bytes 1572872 | tf_op jit(solution)/shard_map/ppermute | solution.py:570
  5.8 17.7 %collective-permute-start.2 = (bf16[272,1024]{1,0:T(8,128)(2,1)S(1)}, bf16[272,1024]{1,0:T(8,128)(2,1)S(1)}, u32[]{:S(2)}, u32[]{:S(2)}) collective-permute-start(bf16[272,1024]{1,0:T(8,128)(2,1)S(1)} %get-tuple-element.47.late_ref), channel_id=1, source_target_pairs={{0,4},{4,8},{8,12},{12,16},{16,20},{20,24},{24,28},{28,32},{32,36}... | collective-permute-start | bytes 1671176 | tf_op jit(solution)/shard_map/ppermute | solution.py:541
  7.8 14.8 %copy-start.1 = (s32[8,16,1]{1,2,0:T(1,128)S(1)}, s32[8,16,1]{1,2,0:T(1,128)}, u32[]{:S(2)}) copy-start(s32[8,16,1]{1,2,0:T(1,128)} %param.20) | copy-start | bytes 1540
  7.8 14.8 %copy-start.2 = (s32[8,16]{1,0:T(8,128)S(1)}, s32[8,16]{1,0:T(8,128)}, u32[]{:S(2)}) copy-start(s32[8,16]{1,0:T(8,128)} %tok_ref.1) | copy-start | bytes 1540
  7.8 15.7 %collective-permute-start.3 = (bf16[272,1024]{1,0:T(8,128)(2,1)S(1)}, bf16[272,1024]{1,0:T(8,128)(2,1)S(1)}, u32[]{:S(2)}, u32[]{:S(2)}) collective-permute-start(bf16[272,1024]{1,0:T(8,128)(2,1)S(1)} %get-tuple-element.45.early_ref), channel_id=1, source_target_pairs={{4,0},{8,4},{12,8},{16,12},{20,16},{24,20},{28,24},{32,28},{36,32}... | collective-permute-start | bytes 1671176 | tf_op jit(solution)/shard_map/ppermute | solution.py:541
  19.1 15.6 %copy-start.3 = (bf16[256,1024]{1,0:T(8,128)(2,1)}, bf16[256,1024]{1,0:T(8,128)(2,1)S(1)}, u32[]{:S(2)}) copy-start(bf16[256,1024]{1,0:T(8,128)(2,1)S(1)} %collective-permute-done.w1_ref) | copy-start | bytes 1572868
  19.1 15.6 %copy-start.4 = (bf16[256,1024]{1,0:T(8,128)(2,1)}, bf16[256,1024]{1,0:T(8,128)(2,1)S(1)}, u32[]{:S(2)}) copy-start(bf16[256,1024]{1,0:T(8,128)(2,1)S(1)} %collective-permute-done.1.w3_ref) | copy-start | bytes 1572868
  19.1 15.6 %collective-permute-start.4 = (bf16[128,1024]{1,0:T(8,128)(2,1)S(1)}, bf16[128,1024]{1,0:T(8,128)(2,1)S(1)}, u32[]{:S(2)}, u32[]{:S(2)}) collective-permute-start(bf16[128,1024]{1,0:T(8,128)(2,1)S(1)} %slice.6), channel_id=1, source_target_pairs={{0,1},{1,2},{2,3},{3,0},{4,5},{5,6},{6,7},{7,4},{8,9},{9,10},{10,1... | collective-permute-start | bytes 786440 | tf_op jit(solution)/shard_map/ppermute | solution.py:575
  19.6 15.1 %collective-permute-start.5 = (bf16[128,1024]{1,0:T(8,128)(2,1)S(1)}, bf16[128,1024]{1,0:T(8,128)(2,1)S(1)}, u32[]{:S(2)}, u32[]{:S(2)}) collective-permute-start(bf16[128,1024]{1,0:T(8,128)(2,1)S(1)} %slice.7), channel_id=1, source_target_pairs={{1,0},{2,1},{3,2},{0,3},{5,4},{6,5},{7,6},{4,7},{9,8},{10,9},{11,1... | collective-permute-start | bytes 786440 | tf_op jit(solution)/shard_map/ppermute | solution.py:575
  34.7 17.2 %copy-start.5 = (bf16[128,1024]{1,0:T(8,128)(2,1)}, bf16[128,1024]{1,0:T(8,128)(2,1)S(1)}, u32[]{:S(2)}) copy-start(bf16[128,1024]{1,0:T(8,128)(2,1)S(1)} %collective-permute-done.4.top_ref) | copy-start | bytes 786436
  34.7 17.2 %copy-start.6 = (bf16[128,1024]{1,0:T(8,128)(2,1)}, bf16[128,1024]{1,0:T(8,128)(2,1)S(1)}, u32[]{:S(2)}) copy-start(bf16[128,1024]{1,0:T(8,128)(2,1)S(1)} %collective-permute-done.5.low_ref) | copy-start | bytes 786436
  34.7 17.2 %collective-permute-start.6 = (bf16[384,256]{1,0:T(8,128)(2,1)S(1)}, bf16[384,256]{1,0:T(8,128)(2,1)S(1)}, u32[]{:S(2)}, u32[]{:S(2)}) collective-permute-start(bf16[384,256]{1,0:T(8,128)(2,1)S(1)} %get-tuple-element.71), channel_id=1, source_target_pairs={{0,1},{1,2},{2,3},{3,0},{4,5},{5,6},{6,7},{7,4},{8,9},{9,10},{10,1... | collective-permute-start | bytes 589832 | tf_op jit(solution)/shard_map/ppermute | solution.py:581
  34.8 17.1 %collective-permute-start.7 = (bf16[384,256]{1,0:T(8,128)(2,1)S(1)}, bf16[384,256]{1,0:T(8,128)(2,1)S(1)}, u32[]{:S(2)}, u32[]{:S(2)}) collective-permute-start(bf16[384,256]{1,0:T(8,128)(2,1)S(1)} %get-tuple-element.72), channel_id=1, source_target_pairs={{0,2},{1,3},{2,0},{3,1},{4,6},{5,7},{6,4},{7,5},{8,10},{9,11},{10,... | collective-permute-start | bytes 589832 | tf_op jit(solution)/shard_map/ppermute | solution.py:581
  36.9 15.0 %collective-permute-start.8 = (bf16[384,256]{1,0:T(8,128)(2,1)S(1)}, bf16[384,256]{1,0:T(8,128)(2,1)S(1)}, u32[]{:S(2)}, u32[]{:S(2)}) collective-permute-start(bf16[384,256]{1,0:T(8,128)(2,1)S(1)} %get-tuple-element.73), channel_id=1, source_target_pairs={{0,3},{1,0},{2,1},{3,2},{4,7},{5,4},{6,5},{7,6},{8,11},{9,8},{10,9... | collective-permute-start | bytes 589832 | tf_op jit(solution)/shard_map/ppermute | solution.py:581
  38.2 21.4 %all-to-all-start = ((s32[64,1,4]{2,1,0:T(1,128)}), s32[64,1,4]{2,1,0:T(1,128)S(1)}, u32[]{:S(2)}, u32[]{:S(2)}) async-start(s32[64,1,4]{2,1,0:T(1,128)} %bitcast.2), calls=%async_computation | async-start | bytes 65536 | tf_op jit(solution)/shard_map/all_to_all | solution.py:584
  61.4 29.9 %all-to-all-start.1 = ((bf16[64,16,384]{2,1,0:T(8,128)(2,1)}), bf16[64,16,384]{2,1,0:T(8,128)(2,1)S(1)}, u32[]{:S(2)}, u32[]{:S(2)}) async-start(bf16[64,16,384]{2,1,0:T(8,128)(2,1)} %serve.1), calls=%async_computation.1 | async-start | bytes 1572864 | tf_op jit(solution)/shard_map/all_to_all | solution.py:590
  68.0 23.2 %copy-start = (bf16[8,16,512]{2,1,0:T(8,128)(2,1)S(1)}, bf16[8,16,512]{2,1,0:T(8,128)(2,1)}, u32[]{:S(2)}) copy-start(bf16[8,16,512]{2,1,0:T(8,128)(2,1)} %reg_ref.1) | copy-start | bytes 393220
  92.2 12.7 %collective-permute-start.9 = (bf16[48,512]{1,0:T(8,128)(2,1)S(1)}, bf16[48,512]{1,0:T(8,128)(2,1)S(1)}, u32[]{:S(2)}, u32[]{:S(2)}) collective-permute-start(bf16[48,512]{1,0:T(8,128)(2,1)S(1)} %get-tuple-element.83), channel_id=1, source_target_pairs={{0,1},{1,2},{2,3},{3,4},{4,5},{5,6},{6,7},{7,8},{8,9},{9,10},{10,1... | collective-permute-start | bytes 147464 | tf_op jit(solution)/shard_map/ppermute | solution.py:541
  94.8 10.1 %collective-permute-start.10 = (bf16[48,512]{1,0:T(8,128)(2,1)S(1)}, bf16[48,512]{1,0:T(8,128)(2,1)S(1)}, u32[]{:S(2)}, u32[]{:S(2)}) collective-permute-start(bf16[48,512]{1,0:T(8,128)(2,1)S(1)} %get-tuple-element.84), channel_id=1, source_target_pairs={{1,0},{2,1},{3,2},{4,3},{5,4},{6,5},{7,6},{8,7},{9,8},{10,9},{11,1... | collective-permute-start | bytes 147464 | tf_op jit(solution)/shard_map/ppermute | solution.py:541

commit v11 on v10

--- a/solution.py
+++ b/solution.py
@@ -567,14 +567,15 @@
     before, after = neighbours(last, first, BANDS)
     last, w_query, w_key, w_value = lax.optimization_barrier((last, w_query, w_key, w_value))
     *weights, gain = load(in_hbm(norm_gain), [in_hbm(w) for w in (w_query, w_key, w_value)])
+    gain, w_out = lax.optimization_barrier((gain, w_out))
     w1, w3 = lax.ppermute(w_out, "tp", up), lax.ppermute(w_out, "tp", down)
     q, k, v = project(band_codes, [first, last], gain, weights, False)
     asked = ask(cell_band, src_tok, bands)
-    q, w1, w3 = lax.optimization_barrier((q, w1, w3))
+    q, before, after, asked = lax.optimization_barrier((q, before, after, asked))
+    k_halo, v_halo = project(band_codes, [before, after], gain, weights[1:], True)
+    k_halo, w1, w3 = lax.optimization_barrier((k_halo, w1, w3))
     middle = w_out.shape[0] // 2
     top, low = lax.ppermute(w1[:middle], "tp", up), lax.ppermute(w3[middle:], "tp", down)
-    q, before, after = lax.optimization_barrier((q, before, after))
-    k_halo, v_halo = project(band_codes, [before, after], gain, weights[1:], True)
     attended = attend(q, k, v, k_halo, v_halo, ranks, bands)
     attended, asked, top, low = lax.optimization_barrier((attended, asked, top, low))
     attended = [attended[0]] + [

time: 107 us -> 108 us (level)
  waiting for transfers between devices: 25.6 us -> 27.7 us
  starting transfers between devices: 49.1 us -> 47.6 us
    all_to_all x1, starting transfers between devices: 13.7 us -> 11.3 us  [per_device(): asked = lax.all_to_all(asked[:, None, :], BANDS, 0, 0, tiled=True)[:, 0, :]]
    ppermute x2, waiting for transfers between devices: 0.01 us -> 2.13 us  [per_device(): w1, w3 = (lax.ppermute(w_out, 'tp', up), lax.ppermute(w_out, 'tp', down))]
    ppermute x1, starting transfers between devices: 0.44 us -> 1.65 us  [per_device(): lax.ppermute(w1[:middle], 'tp', up)]
    ppermute x1, starting transfers between devices: 2.95 us -> 1.74 us  [per_device(): lax.ppermute(w3[middle:], 'tp', down)]
  transfers between devices with their start and end apart: 13 -> 13, of which waited for: 2 -> 3; matrix products, arithmetic and copies ran while one was open for 0% -> 0% of each run, Pallas kernels for 24% -> 23%
where the time goes in v11:
time: 108 us; the launch traced here: 107 us
  starting transfers between devices  47.6 us (44%)
  Pallas kernels  30.1 us (28%)
  waiting for transfers between devices  27.7 us (26%)
  between operations  1.62 us (2%)
    all_to_all x1, waiting for transfers between devices, per_device(): arrived = lax.all_to_all(send, BANDS, 0, 0, tiled=True)  21.4 us
    ppermute x4, starting transfers between devices, neighbours(): return (lax.ppermute(last, axis, up), lax.ppermute(first, axis, down))  18.6 us
    all_to_all x1, starting transfers between devices, per_device(): asked = lax.all_to_all(asked[:, None, :], BANDS, 0, 0, tiled=True)[:, 0, :]  11.3 us
    pallas_call x1, Pallas kernels, attend(): pl.pallas_call(functools.partial(attend_kernel, bands=bands), out_shape=[...  8.28 us
    all_to_all x1, starting transfers between devices, per_device(): arrived = lax.all_to_all(send, BANDS, 0, 0, tiled=True)  6.61 us
    pallas_call x2, Pallas kernels, project(): pl.pallas_call(functools.partial(project_kernel, halo=halo), out_shape=[j...  6.35 us
    ppermute x3, starting transfers between devices, per_device(): lax.ppermute(attended[d], 'tp', [(i, (i + d) % ranks) for i in range(rank...  4.4 us
    all_to_all x1, waiting for transfers between devices, per_device(): asked = lax.all_to_all(asked[:, None, :], BANDS, 0, 0, tiled=True)[:, 0, :]  4.17 us
  transfers between devices with their start and end apart: 13, of which 3 were waited for; matrix products, arithmetic and copies ran while one was open for 0% of the time, Pallas kernels for 23%

profile of v11, /device:TPU:4, one launch (start us, length us, event | category | flops | bytes accessed | tf_op | source)
XLA Modules:
  0.0 107.2 jit_solution(3704106541189397921)
XLA Ops:
  0.6 0.0 copy-start.5
  1.4 1.2 %edges.1 = (bf16[272,1024]{1,0:T(8,128)(2,1)S(1)}, bf16[272,1024]{1,0:T(8,128)(2,1)S(1)}) custom-call(s32[1]{0:T(128)S(6)} %copy.15.code_ref, bf16[512,1024]{1,0:T(8,128)(2,1)} %x_ref.3), custom_call_target="tpu_custom_call" | custom-call | tf_op jit(solution)/shard_map/edges/pallas_call | solution.py:74
  2.6 1.9 %collective-permute-start = (bf16[272,1024]{1,0:T(8,128)(2,1)S(1)}, bf16[272,1024]{1,0:T(8,128)(2,1)S(1)}, u32[]{:S(2)}, u32[]{:S(2)}) collective-permute-start(bf16[272,1024]{1,0:T(8,128)(2,1)S(1)} %get-tuple-element.50.late_ref), channel_id=1, source_target_pairs={{0,4},{4,8},{8,12},{12,16},{16,20},{20,24},{24,28},{28,32},{32,36}... | collective-permute-start | bytes 1671176 | tf_op jit(solution)/shard_map/ppermute | solution.py:541
  4.5 6.3 %collective-permute-start.1 = (bf16[272,1024]{1,0:T(8,128)(2,1)S(1)}, bf16[272,1024]{1,0:T(8,128)(2,1)S(1)}, u32[]{:S(2)}, u32[]{:S(2)}) collective-permute-start(bf16[272,1024]{1,0:T(8,128)(2,1)S(1)} %get-tuple-element.48.early_ref), channel_id=1, source_target_pairs={{4,0},{8,4},{12,8},{16,12},{20,16},{24,20},{28,24},{32,28},{36,32}... | collective-permute-start | bytes 1671176 | tf_op jit(solution)/shard_map/ppermute | solution.py:541
  10.9 1.4 %load.1 = (bf16[1024,256]{1,0:T(8,128)(2,1)S(1)}, bf16[1024,256]{1,0:T(8,128)(2,1)S(1)}, bf16[1024,256]{1,0:T(8,128)(2,1)S(1)}, f32[1,1024]{1,0:T(1,128)S(1)}) custom-call(bf16[1024]{0:T(1024)(128)(2,1)} %gain_ref.1, bf16[1024,256]{1,0:T(8,128)(2,1)} %refs_0_, bf16[1024,256]{1,0:T(8,128)(2,1)} %refs_1_, bf16[1024,256]{1,0:T(8,128)(2,1)} %refs_2_), custom_call_target="tpu_custom_call" | custom-call | tf_op jit(solution)/shard_map/load/pallas_call | solution.py:101
  12.3 1.7 %collective-permute-start.2 = (bf16[256,1024]{1,0:T(8,128)(2,1)S(1)}, bf16[256,1024]{1,0:T(8,128)(2,1)S(1)}, u32[]{:S(2)}, u32[]{:S(2)}) collective-permute-start(bf16[256,1024]{1,0:T(8,128)(2,1)S(1)} %copy-done.5), channel_id=1, source_target_pairs={{0,1},{1,2},{2,3},{3,0},{4,5},{5,6},{6,7},{7,4},{8,9},{9,10},{10,1... | collective-permute-start | bytes 1572872 | tf_op jit(solution)/shard_map/ppermute | solution.py:571
  13.9 1.7 %collective-permute-start.3 = (bf16[256,1024]{1,0:T(8,128)(2,1)S(1)}, bf16[256,1024]{1,0:T(8,128)(2,1)S(1)}, u32[]{:S(2)}, u32[]{:S(2)}) collective-permute-start(bf16[256,1024]{1,0:T(8,128)(2,1)S(1)} %copy-done.5), channel_id=1, source_target_pairs={{1,0},{2,1},{3,2},{0,3},{5,4},{6,5},{7,6},{4,7},{9,8},{10,9},{11,1... | collective-permute-start | bytes 1572872 | tf_op jit(solution)/shard_map/ppermute | solution.py:571
  15.6 1.0 ask.1
  16.6 3.5 %project_own.1 = (bf16[3,512,256]{2,1,0:T(8,128)(2,1)S(1)}, bf16[3,512,256]{2,1,0:T(8,128)(2,1)S(1)}, bf16[3,512,256]{2,1,0:T(8,128)(2,1)S(1)}) custom-call(s32[1]{0:T(128)S(6)} %copy.15.code_ref, bf16[272,1024]{1,0:T(8,128)(2,1)S(1)} %get-tuple-element.48.early_ref, bf16[272,1024]{1,0:T(8,128)(2,1)S(1)} %get-tuple-element.50.late_ref, ...), custom_call_target="tpu_custom_call" | custom-call | tf_op jit(solution)/shard_map/project_own/pallas_call | solution.py:161
  20.1 2.9 %project_halo.1 = (bf16[3,512,256]{2,1,0:T(8,128)(2,1)S(1)}, bf16[3,512,256]{2,1,0:T(8,128)(2,1)S(1)}) custom-call(s32[1]{0:T(128)S(6)} %copy.15.code_ref, bf16[272,1024]{1,0:T(8,128)(2,1)S(1)} %collective-permute-done.early_ref, bf16[272,1024]{1,0:T(8,128)(2,1)S(1)} %collective-permute-done.1.late_ref, f32[1,1024]{1,0:T(1,128)S(1)} %get-tuple-element.55.gain_ref, ...), custom_call_target="tpu_custom_call" | custom-call | tf_op jit(solution)/shard_map/project_halo/pallas_call | solution.py:161
  23.0 2.1 %collective-permute-done.2.w1_ref = bf16[256,1024]{1,0:T(8,128)(2,1)S(1)} collective-permute-done((bf16[256,1024]{1,0:T(8,128)(2,1)S(1)}, bf16[256,1024]{1,0:T(8,128)(2,1)S(1)}, u32[]{:S(2)}, u32[]{:S(2)}) %collective-permute-start.2) | collective-permute-done | bytes 524320 | tf_op jit(solution)/shard_map/ppermute | solution.py:571
  25.1 0.0 collective-permute-done.3.w3_ref
  25.1 1.7 %collective-permute-start.4 = (bf16[128,1024]{1,0:T(8,128)(2,1)S(1)}, bf16[128,1024]{1,0:T(8,128)(2,1)S(1)}, u32[]{:S(2)}, u32[]{:S(2)}) collective-permute-start(bf16[128,1024]{1,0:T(8,128)(2,1)S(1)} %slice.6), channel_id=1, source_target_pairs={{0,1},{1,2},{2,3},{3,0},{4,5},{5,6},{6,7},{7,4},{8,9},{9,10},{10,1... | collective-permute-start | bytes 786440 | tf_op jit(solution)/shard_map/ppermute | solution.py:578
  26.8 1.7 %collective-permute-start.5 = (bf16[128,1024]{1,0:T(8,128)(2,1)S(1)}, bf16[128,1024]{1,0:T(8,128)(2,1)S(1)}, u32[]{:S(2)}, u32[]{:S(2)}) collective-permute-start(bf16[128,1024]{1,0:T(8,128)(2,1)S(1)} %slice.7), channel_id=1, source_target_pairs={{1,0},{2,1},{3,2},{0,3},{5,4},{6,5},{7,6},{4,7},{9,8},{10,9},{11,1... | collective-permute-start | bytes 786440 | tf_op jit(solution)/shard_map/ppermute | solution.py:578
  28.5 8.3 %attend.1 = (bf16[384,256]{1,0:T(8,128)(2,1)S(1)}, bf16[384,256]{1,0:T(8,128)(2,1)S(1)}, bf16[384,256]{1,0:T(8,128)(2,1)S(1)}, bf16[384,256]{1,0:T(8,128)(2,1)S(1)}) custom-call(bf16[3,512,256]{2,1,0:T(8,128)(2,1)S(1)} %get-tuple-element.60.q_ref, bf16[3,512,256]{2,1,0:T(8,128)(2,1)S(1)} %get-tuple-element.61.k_ref, ...), custom_call_target="tpu_custom_call" | custom-call | tf_op jit(solution)/shard_map/attend/pallas_call | solution.py:237
  36.8 0.0 copy-start.6
  36.9 0.4 collective-permute-start.6
  37.3 2.9 %collective-permute-start.7 = (bf16[384,256]{1,0:T(8,128)(2,1)S(1)}, bf16[384,256]{1,0:T(8,128)(2,1)S(1)}, u32[]{:S(2)}, u32[]{:S(2)}) collective-permute-start(bf16[384,256]{1,0:T(8,128)(2,1)S(1)} %get-tuple-element.78), channel_id=1, source_target_pairs={{0,2},{1,3},{2,0},{3,1},{4,6},{5,7},{6,4},{7,5},{8,10},{9,11},{10,... | collective-permute-start | bytes 589832 | tf_op jit(solution)/shard_map/ppermute | solution.py:582
  40.2 1.0 collective-permute-start.8
  41.3 11.3 %all-to-all-start = ((s32[64,1,4]{2,1,0:T(1,128)}), s32[64,1,4]{2,1,0:T(1,128)S(1)}, u32[]{:S(2)}, u32[]{:S(2)}) async-start(s32[64,1,4]{2,1,0:T(1,128)} %bitcast.2), calls=%async_computation | async-start | bytes 65536 | tf_op jit(solution)/shard_map/all_to_all | solution.py:585
  52.6 3.4 %combine.1 = (bf16[3,128,1024]{2,1,0:T(8,128)(2,1)}, bf16[512,384]{1,0:T(8,128)(2,1)S(1)}) custom-call(s32[1]{0:T(128)S(6)} %copy.15.code_ref, bf16[384,256]{1,0:T(8,128)(2,1)S(1)} %get-tuple-element.76.att0_ref, bf16[384,256]{1,0:T(8,128)(2,1)S(1)} %collective-permute-done.6.att1_ref, bf16[384,256]{1,0:T(8,128)(2,1)S(1)} %collective-permute-done.7.att2_ref, ...), custom_call_target="tpu_custom_call" | custom-call | tf_op jit(solution)/shard_map/combine/pallas_call | solution.py:367
  56.1 4.2 %all-to-all-done = s32[64,1,4]{2,1,0:T(1,128)S(1)} async-done(((s32[64,1,4]{2,1,0:T(1,128)}), s32[64,1,4]{2,1,0:T(1,128)S(1)}, u32[]{:S(2)}, u32[]{:S(2)}) %all-to-all-start) | async-done | bytes 1056 | tf_op jit(solution)/shard_map/all_to_all | solution.py:585
  60.2 1.8 %serve.1 = bf16[64,16,384]{2,1,0:T(8,128)(2,1)} custom-call(s32[64,4]{1,0:T(8,128)S(1)} %bitcast.5, bf16[512,384]{1,0:T(8,128)(2,1)S(1)} %get-tuple-element.84.table_ref), custom_call_target="tpu_custom_call" | custom-call | tf_op jit(solution)/shard_map/serve/pallas_call | solution.py:392
  62.0 6.6 %all-to-all-start.1 = ((bf16[64,16,384]{2,1,0:T(8,128)(2,1)}), bf16[64,16,384]{2,1,0:T(8,128)(2,1)S(1)}, u32[]{:S(2)}, u32[]{:S(2)}) async-start(bf16[64,16,384]{2,1,0:T(8,128)(2,1)} %serve.1), calls=%async_computation.1 | async-start | bytes 1572864 | tf_op jit(solution)/shard_map/all_to_all | solution.py:591
  68.7 0.0 copy-start
  68.7 1.8 %fetch.1.taps_ref.w_before_ref = bf16[5,512,512]{2,1,0:T(8,128)(2,1)S(1)} custom-call(bf16[9,512,512]{2,1,0:T(8,128)(2,1)} %conv_hbm_ref.1), custom_call_target="tpu_custom_call" | custom-call | tf_op jit(solution)/shard_map/fetch/pallas_call | solution.py:293
  70.5 21.4 %all-to-all-done.1.arrived_ref = bf16[64,16,384]{2,1,0:T(8,128)(2,1)S(1)} async-done(((bf16[64,16,384]{2,1,0:T(8,128)(2,1)}), bf16[64,16,384]{2,1,0:T(8,128)(2,1)S(1)}, u32[]{:S(2)}, u32[]{:S(2)}) %all-to-all-start.1) | async-done | bytes 786464 | tf_op jit(solution)/shard_map/all_to_all | solution.py:591
  91.9 1.0 inputs.1
  92.9 2.9 %collective-permute-start.9 = (bf16[48,512]{1,0:T(8,128)(2,1)S(1)}, bf16[48,512]{1,0:T(8,128)(2,1)S(1)}, u32[]{:S(2)}, u32[]{:S(2)}) collective-permute-start(bf16[48,512]{1,0:T(8,128)(2,1)S(1)} %get-tuple-element.89), channel_id=1, source_target_pairs={{0,1},{1,2},{2,3},{3,4},{4,5},{5,6},{6,7},{7,8},{8,9},{9,10},{10,1... | collective-permute-start | bytes 147464 | tf_op jit(solution)/shard_map/ppermute | solution.py:541
  95.8 7.5 %collective-permute-start.10 = (bf16[48,512]{1,0:T(8,128)(2,1)S(1)}, bf16[48,512]{1,0:T(8,128)(2,1)S(1)}, u32[]{:S(2)}, u32[]{:S(2)}) collective-permute-start(bf16[48,512]{1,0:T(8,128)(2,1)S(1)} %get-tuple-element.90), channel_id=1, source_target_pairs={{1,0},{2,1},{3,2},{4,3},{5,4},{6,5},{7,6},{8,7},{9,8},{10,9},{11,1... | collective-permute-start | bytes 147464 | tf_op jit(solution)/shard_map/ppermute | solution.py:541
  103.3 2.3 %convolve_inner.1 = (f32[384,512]{1,0:T(8,128)S(1)}, bf16[3,512,512]{2,1,0:T(8,128)(2,1)S(1)}) custom-call(bf16[8,48,512]{2,1,0:T(8,128)(2,1)S(1)} %get-tuple-element.88.x_ref, bf16[5,512,512]{2,1,0:T(8,128)(2,1)S(1)} %fetch.1.taps_ref.w_before_ref, bf16[9,512,512]{2,1,0:T(8,128)(2,1)} %conv_hbm_ref.1), custom_call_target="tpu_custom_call" | custom-call | tf_op jit(solution)/shard_map/convolve_inner/pallas_call | solution.py:485
  105.6 1.6 %convolve_finish.1 = bf16[3,8,16,512]{3,2,1,0:T(8,128)(2,1)} custom-call(bf16[8,48,512]{2,1,0:T(8,128)(2,1)S(1)} %get-tuple-element.88.x_ref, bf16[48,512]{1,0:T(8,128)(2,1)S(1)} %collective-permute-done.9.before_ref, bf16[48,512]{1,0:T(8,128)(2,1)S(1)} %collective-permute-done.10.after_ref, bf16[5,512,512]{2,1,0:T(8,128)(2,1)S(1)} %fetch.1.taps_ref.w_before_ref, ...), custom_call_target="tpu_custom_call" | custom-call | tf_op jit(solution)/shard_map/convolve_finish/pallas_call | solution.py:527
  (24 shorter events, 0.1 us)
Async XLA Ops:
  0.6 11.7 %copy-start.5 = (bf16[256,1024]{1,0:T(8,128)(2,1)S(1)}, bf16[256,1024]{1,0:T(8,128)(2,1)}, u32[]{:S(2)}) copy-start(bf16[256,1024]{1,0:T(8,128)(2,1)} %w0_ref) | copy-start | bytes 1572868
  0.6 15.0 %copy-start.1 = (s32[8,16,1]{1,2,0:T(1,128)S(1)}, s32[8,16,1]{1,2,0:T(1,128)}, u32[]{:S(2)}) copy-start(s32[8,16,1]{1,2,0:T(1,128)} %param.20) | copy-start | bytes 1540
  0.7 15.0 %copy-start.2 = (s32[8,16]{1,0:T(8,128)S(1)}, s32[8,16]{1,0:T(8,128)}, u32[]{:S(2)}) copy-start(s32[8,16]{1,0:T(8,128)} %tok_ref.1) | copy-start | bytes 1540
  2.6 17.5 %collective-permute-start = (bf16[272,1024]{1,0:T(8,128)(2,1)S(1)}, bf16[272,1024]{1,0:T(8,128)(2,1)S(1)}, u32[]{:S(2)}, u32[]{:S(2)}) collective-permute-start(bf16[272,1024]{1,0:T(8,128)(2,1)S(1)} %get-tuple-element.50.late_ref), channel_id=1, source_target_pairs={{0,4},{4,8},{8,12},{12,16},{16,20},{20,24},{24,28},{28,32},{32,36}... | collective-permute-start | bytes 1671176 | tf_op jit(solution)/shard_map/ppermute | solution.py:541
  4.5 15.6 %collective-permute-start.1 = (bf16[272,1024]{1,0:T(8,128)(2,1)S(1)}, bf16[272,1024]{1,0:T(8,128)(2,1)S(1)}, u32[]{:S(2)}, u32[]{:S(2)}) collective-permute-start(bf16[272,1024]{1,0:T(8,128)(2,1)S(1)} %get-tuple-element.48.early_ref), channel_id=1, source_target_pairs={{4,0},{8,4},{12,8},{16,12},{20,16},{24,20},{28,24},{32,28},{36,32}... | collective-permute-start | bytes 1671176 | tf_op jit(solution)/shard_map/ppermute | solution.py:541
  12.3 12.8 %collective-permute-start.2 = (bf16[256,1024]{1,0:T(8,128)(2,1)S(1)}, bf16[256,1024]{1,0:T(8,128)(2,1)S(1)}, u32[]{:S(2)}, u32[]{:S(2)}) collective-permute-start(bf16[256,1024]{1,0:T(8,128)(2,1)S(1)} %copy-done.5), channel_id=1, source_target_pairs={{0,1},{1,2},{2,3},{3,0},{4,5},{5,6},{6,7},{7,4},{8,9},{9,10},{10,1... | collective-permute-start | bytes 1572872 | tf_op jit(solution)/shard_map/ppermute | solution.py:571
  13.9 11.2 %collective-permute-start.3 = (bf16[256,1024]{1,0:T(8,128)(2,1)S(1)}, bf16[256,1024]{1,0:T(8,128)(2,1)S(1)}, u32[]{:S(2)}, u32[]{:S(2)}) collective-permute-start(bf16[256,1024]{1,0:T(8,128)(2,1)S(1)} %copy-done.5), channel_id=1, source_target_pairs={{1,0},{2,1},{3,2},{0,3},{5,4},{6,5},{7,6},{4,7},{9,8},{10,9},{11,1... | collective-permute-start | bytes 1572872 | tf_op jit(solution)/shard_map/ppermute | solution.py:571
  25.1 27.5 %copy-start.3 = (bf16[256,1024]{1,0:T(8,128)(2,1)}, bf16[256,1024]{1,0:T(8,128)(2,1)S(1)}, u32[]{:S(2)}) copy-start(bf16[256,1024]{1,0:T(8,128)(2,1)S(1)} %collective-permute-done.2.w1_ref) | copy-start | bytes 1572868
  25.1 27.5 %copy-start.4 = (bf16[256,1024]{1,0:T(8,128)(2,1)}, bf16[256,1024]{1,0:T(8,128)(2,1)S(1)}, u32[]{:S(2)}) copy-start(bf16[256,1024]{1,0:T(8,128)(2,1)S(1)} %collective-permute-done.3.w3_ref) | copy-start | bytes 1572868
  25.1 11.7 %collective-permute-start.4 = (bf16[128,1024]{1,0:T(8,128)(2,1)S(1)}, bf16[128,1024]{1,0:T(8,128)(2,1)S(1)}, u32[]{:S(2)}, u32[]{:S(2)}) collective-permute-start(bf16[128,1024]{1,0:T(8,128)(2,1)S(1)} %slice.6), channel_id=1, source_target_pairs={{0,1},{1,2},{2,3},{3,0},{4,5},{5,6},{6,7},{7,4},{8,9},{9,10},{10,1... | collective-permute-start | bytes 786440 | tf_op jit(solution)/shard_map/ppermute | solution.py:578
  26.8 10.1 %collective-permute-start.5 = (bf16[128,1024]{1,0:T(8,128)(2,1)S(1)}, bf16[128,1024]{1,0:T(8,128)(2,1)S(1)}, u32[]{:S(2)}, u32[]{:S(2)}) collective-permute-start(bf16[128,1024]{1,0:T(8,128)(2,1)S(1)} %slice.7), channel_id=1, source_target_pairs={{1,0},{2,1},{3,2},{0,3},{5,4},{6,5},{7,6},{4,7},{9,8},{10,9},{11,1... | collective-permute-start | bytes 786440 | tf_op jit(solution)/shard_map/ppermute | solution.py:578
  36.8 15.8 %copy-start.6 = (bf16[128,1024]{1,0:T(8,128)(2,1)}, bf16[128,1024]{1,0:T(8,128)(2,1)S(1)}, u32[]{:S(2)}) copy-start(bf16[128,1024]{1,0:T(8,128)(2,1)S(1)} %collective-permute-done.4.top_ref) | copy-start | bytes 786436
  36.9 15.8 %copy-start.7 = (bf16[128,1024]{1,0:T(8,128)(2,1)}, bf16[128,1024]{1,0:T(8,128)(2,1)S(1)}, u32[]{:S(2)}) copy-start(bf16[128,1024]{1,0:T(8,128)(2,1)S(1)} %collective-permute-done.5.low_ref) | copy-start | bytes 786436
  36.9 15.7 %collective-permute-start.6 = (bf16[384,256]{1,0:T(8,128)(2,1)S(1)}, bf16[384,256]{1,0:T(8,128)(2,1)S(1)}, u32[]{:S(2)}, u32[]{:S(2)}) collective-permute-start(bf16[384,256]{1,0:T(8,128)(2,1)S(1)} %get-tuple-element.77), channel_id=1, source_target_pairs={{0,1},{1,2},{2,3},{3,0},{4,5},{5,6},{6,7},{7,4},{8,9},{9,10},{10,1... | collective-permute-start | bytes 589832 | tf_op jit(solution)/shard_map/ppermute | solution.py:582
  37.3 15.3 %collective-permute-start.7 = (bf16[384,256]{1,0:T(8,128)(2,1)S(1)}, bf16[384,256]{1,0:T(8,128)(2,1)S(1)}, u32[]{:S(2)}, u32[]{:S(2)}) collective-permute-start(bf16[384,256]{1,0:T(8,128)(2,1)S(1)} %get-tuple-element.78), channel_id=1, source_target_pairs={{0,2},{1,3},{2,0},{3,1},{4,6},{5,7},{6,4},{7,5},{8,10},{9,11},{10,... | collective-permute-start | bytes 589832 | tf_op jit(solution)/shard_map/ppermute | solution.py:582
  40.2 12.3 %collective-permute-start.8 = (bf16[384,256]{1,0:T(8,128)(2,1)S(1)}, bf16[384,256]{1,0:T(8,128)(2,1)S(1)}, u32[]{:S(2)}, u32[]{:S(2)}) collective-permute-start(bf16[384,256]{1,0:T(8,128)(2,1)S(1)} %get-tuple-element.79), channel_id=1, source_target_pairs={{0,3},{1,0},{2,1},{3,2},{4,7},{5,4},{6,5},{7,6},{8,11},{9,8},{10,9... | collective-permute-start | bytes 589832 | tf_op jit(solution)/shard_map/ppermute | solution.py:582
  41.3 19.0 %all-to-all-start = ((s32[64,1,4]{2,1,0:T(1,128)}), s32[64,1,4]{2,1,0:T(1,128)S(1)}, u32[]{:S(2)}, u32[]{:S(2)}) async-start(s32[64,1,4]{2,1,0:T(1,128)} %bitcast.2), calls=%async_computation | async-start | bytes 65536 | tf_op jit(solution)/shard_map/all_to_all | solution.py:585
  62.0 29.8 %all-to-all-start.1 = ((bf16[64,16,384]{2,1,0:T(8,128)(2,1)}), bf16[64,16,384]{2,1,0:T(8,128)(2,1)S(1)}, u32[]{:S(2)}, u32[]{:S(2)}) async-start(bf16[64,16,384]{2,1,0:T(8,128)(2,1)} %serve.1), calls=%async_computation.1 | async-start | bytes 1572864 | tf_op jit(solution)/shard_map/all_to_all | solution.py:591
  68.7 23.2 %copy-start = (bf16[8,16,512]{2,1,0:T(8,128)(2,1)S(1)}, bf16[8,16,512]{2,1,0:T(8,128)(2,1)}, u32[]{:S(2)}) copy-start(bf16[8,16,512]{2,1,0:T(8,128)(2,1)} %reg_ref.1) | copy-start | bytes 393220
  92.9 12.7 %collective-permute-start.9 = (bf16[48,512]{1,0:T(8,128)(2,1)S(1)}, bf16[48,512]{1,0:T(8,128)(2,1)S(1)}, u32[]{:S(2)}, u32[]{:S(2)}) collective-permute-start(bf16[48,512]{1,0:T(8,128)(2,1)S(1)} %get-tuple-element.89), channel_id=1, source_target_pairs={{0,1},{1,2},{2,3},{3,4},{4,5},{5,6},{6,7},{7,8},{8,9},{9,10},{10,1... | collective-permute-start | bytes 147464 | tf_op jit(solution)/shard_map/ppermute | solution.py:541
  95.8 9.8 %collective-permute-start.10 = (bf16[48,512]{1,0:T(8,128)(2,1)S(1)}, bf16[48,512]{1,0:T(8,128)(2,1)S(1)}, u32[]{:S(2)}, u32[]{:S(2)}) collective-permute-start(bf16[48,512]{1,0:T(8,128)(2,1)S(1)} %get-tuple-element.90), channel_id=1, source_target_pairs={{1,0},{2,1},{3,2},{4,3},{5,4},{6,5},{7,6},{8,7},{9,8},{10,9},{11,1... | collective-permute-start | bytes 147464 | tf_op jit(solution)/shard_map/ppermute | solution.py:541

commit v12 on v10

--- a/solution.py
+++ b/solution.py
@@ -577,10 +577,11 @@
     k_halo, v_halo = project(band_codes, [before, after], gain, weights[1:], True)
     attended = attend(q, k, v, k_halo, v_halo, ranks, bands)
     attended, asked, top, low = lax.optimization_barrier((attended, asked, top, low))
-    attended = [attended[0]] + [
+    att2, att1, att3 = (
         lax.ppermute(attended[d], "tp", [(i, (i + d) % ranks) for i in range(ranks)])
-        for d in range(1, ranks)
-    ]
+        for d in (2, 1, 3)
+    )
+    attended = [attended[0], att1, att2, att3]
     asked = lax.all_to_all(asked[:, None, :], BANDS, 0, 0, tiled=True)[:, 0, :]
     global_out, table = combine(band_codes, attended, [w_out, w1, w3, top, low], global_state, w_bound)
     send = serve(asked, table)

time: 107 us -> 107 us (level)
  no operation moved by 1% of the time
where the time goes in v12:
time: 107 us
  starting transfers between devices  49.1 us (46%)
  Pallas kernels  30.1 us (28%)
  waiting for transfers between devices  25.6 us (24%)
  between operations  1.58 us (1%)
    all_to_all x1, waiting for transfers between devices, per_device(): arrived = lax.all_to_all(send, BANDS, 0, 0, tiled=True)  21.4 us
    ppermute x4, starting transfers between devices, neighbours(): return (lax.ppermute(last, axis, up), lax.ppermute(first, axis, down))  18.6 us
    all_to_all x1, starting transfers between devices, per_device(): asked = lax.all_to_all(asked[:, None, :], BANDS, 0, 0, tiled=True)[:, 0, :]  13.7 us
    pallas_call x1, Pallas kernels, attend(): pl.pallas_call(functools.partial(attend_kernel, bands=bands), out_shape=[...  8.3 us
    all_to_all x1, starting transfers between devices, per_device(): arrived = lax.all_to_all(send, BANDS, 0, 0, tiled=True)  6.61 us
    pallas_call x2, Pallas kernels, project(): pl.pallas_call(functools.partial(project_kernel, halo=halo), out_shape=[j...  6.36 us
    all_to_all x1, waiting for transfers between devices, per_device(): asked = lax.all_to_all(asked[:, None, :], BANDS, 0, 0, tiled=True)[:, 0, :]  4.18 us
    ppermute x3, starting transfers between devices, per_device(): lax.ppermute(attended[d], 'tp', [(i, (i + d) % ranks) for i in range(rank...  3.47 us
  transfers between devices with their start and end apart: 13, of which 2 were waited for; matrix products, arithmetic and copies ran while one was open for 0% of the time, Pallas kernels for 24%

profile of v12, /device:TPU:4, one launch (start us, length us, event | category | flops | bytes accessed | tf_op | source)
XLA Modules:
  0.0 106.5 jit_solution(7451388793312427953)
XLA Ops:
  0.6 1.7 %collective-permute-start = (bf16[256,1024]{1,0:T(8,128)(2,1)}, bf16[256,1024]{1,0:T(8,128)(2,1)S(1)}, u32[]{:S(2)}, u32[]{:S(2)}) collective-permute-start(bf16[256,1024]{1,0:T(8,128)(2,1)} %w0_ref.1), channel_id=1, source_target_pairs={{0,1},{1,2},{2,3},{3,0},{4,5},{5,6},{6,7},{7,4},{8,9},{9,10},{10,1... | collective-permute-start | bytes 1572872 | tf_op jit(solution)/shard_map/ppermute | solution.py:570
  2.3 1.7 %collective-permute-start.1 = (bf16[256,1024]{1,0:T(8,128)(2,1)}, bf16[256,1024]{1,0:T(8,128)(2,1)S(1)}, u32[]{:S(2)}, u32[]{:S(2)}) collective-permute-start(bf16[256,1024]{1,0:T(8,128)(2,1)} %w0_ref.1), channel_id=1, source_target_pairs={{1,0},{2,1},{3,2},{0,3},{5,4},{6,5},{7,6},{4,7},{9,8},{10,9},{11,1... | collective-permute-start | bytes 1572872 | tf_op jit(solution)/shard_map/ppermute | solution.py:570
  4.6 1.2 %edges.1 = (bf16[272,1024]{1,0:T(8,128)(2,1)S(1)}, bf16[272,1024]{1,0:T(8,128)(2,1)S(1)}) custom-call(s32[1]{0:T(128)S(6)} %copy.15.code_ref, bf16[512,1024]{1,0:T(8,128)(2,1)} %x_ref.3), custom_call_target="tpu_custom_call" | custom-call | tf_op jit(solution)/shard_map/edges/pallas_call | solution.py:74
  5.8 1.9 %collective-permute-start.2 = (bf16[272,1024]{1,0:T(8,128)(2,1)S(1)}, bf16[272,1024]{1,0:T(8,128)(2,1)S(1)}, u32[]{:S(2)}, u32[]{:S(2)}) collective-permute-start(bf16[272,1024]{1,0:T(8,128)(2,1)S(1)} %get-tuple-element.47.late_ref), channel_id=1, source_target_pairs={{0,4},{4,8},{8,12},{12,16},{16,20},{20,24},{24,28},{28,32},{32,36}... | collective-permute-start | bytes 1671176 | tf_op jit(solution)/shard_map/ppermute | solution.py:541
  7.8 0.0 copy-start.1
  7.8 0.0 copy-start.2
  7.8 6.3 %collective-permute-start.3 = (bf16[272,1024]{1,0:T(8,128)(2,1)S(1)}, bf16[272,1024]{1,0:T(8,128)(2,1)S(1)}, u32[]{:S(2)}, u32[]{:S(2)}) collective-permute-start(bf16[272,1024]{1,0:T(8,128)(2,1)S(1)} %get-tuple-element.45.early_ref), channel_id=1, source_target_pairs={{4,0},{8,4},{12,8},{16,12},{20,16},{24,20},{28,24},{32,28},{36,32}... | collective-permute-start | bytes 1671176 | tf_op jit(solution)/shard_map/ppermute | solution.py:541
  14.1 1.4 %load.1 = (bf16[1024,256]{1,0:T(8,128)(2,1)S(1)}, bf16[1024,256]{1,0:T(8,128)(2,1)S(1)}, bf16[1024,256]{1,0:T(8,128)(2,1)S(1)}, f32[1,1024]{1,0:T(1,128)S(1)}) custom-call(bf16[1024]{0:T(1024)(128)(2,1)} %gain_ref.1, bf16[1024,256]{1,0:T(8,128)(2,1)} %refs_0_, bf16[1024,256]{1,0:T(8,128)(2,1)} %refs_1_, bf16[1024,256]{1,0:T(8,128)(2,1)} %refs_2_), custom_call_target="tpu_custom_call" | custom-call | tf_op jit(solution)/shard_map/load/pallas_call | solution.py:101
  15.5 3.5 %project_own.1 = (bf16[3,512,256]{2,1,0:T(8,128)(2,1)S(1)}, bf16[3,512,256]{2,1,0:T(8,128)(2,1)S(1)}, bf16[3,512,256]{2,1,0:T(8,128)(2,1)S(1)}) custom-call(s32[1]{0:T(128)S(6)} %copy.15.code_ref, bf16[272,1024]{1,0:T(8,128)(2,1)S(1)} %get-tuple-element.45.early_ref, bf16[272,1024]{1,0:T(8,128)(2,1)S(1)} %get-tuple-element.47.late_ref, ...), custom_call_target="tpu_custom_call" | custom-call | tf_op jit(solution)/shard_map/project_own/pallas_call | solution.py:161
  19.0 0.0 collective-permute-done.w1_ref
  19.1 0.4 collective-permute-start.4
  19.6 2.9 %collective-permute-start.5 = (bf16[128,1024]{1,0:T(8,128)(2,1)S(1)}, bf16[128,1024]{1,0:T(8,128)(2,1)S(1)}, u32[]{:S(2)}, u32[]{:S(2)}) collective-permute-start(bf16[128,1024]{1,0:T(8,128)(2,1)S(1)} %slice.7), channel_id=1, source_target_pairs={{1,0},{2,1},{3,2},{0,3},{5,4},{6,5},{7,6},{4,7},{9,8},{10,9},{11,1... | collective-permute-start | bytes 786440 | tf_op jit(solution)/shard_map/ppermute | solution.py:575
  22.5 1.0 ask.1
  23.5 2.9 %project_halo.1 = (bf16[3,512,256]{2,1,0:T(8,128)(2,1)S(1)}, bf16[3,512,256]{2,1,0:T(8,128)(2,1)S(1)}) custom-call(s32[1]{0:T(128)S(6)} %copy.15.code_ref, bf16[272,1024]{1,0:T(8,128)(2,1)S(1)} %collective-permute-done.2.early_ref, bf16[272,1024]{1,0:T(8,128)(2,1)S(1)} %collective-permute-done.3.late_ref, f32[1,1024]{1,0:T(1,128)S(1)} %get-tuple-element.51.gain_ref, ...), custom_call_target="tpu_custom_call" | custom-call | tf_op jit(solution)/shard_map/project_halo/pallas_call | solution.py:161
  26.4 8.3 %attend.1 = (bf16[384,256]{1,0:T(8,128)(2,1)S(1)}, bf16[384,256]{1,0:T(8,128)(2,1)S(1)}, bf16[384,256]{1,0:T(8,128)(2,1)S(1)}, bf16[384,256]{1,0:T(8,128)(2,1)S(1)}) custom-call(bf16[3,512,256]{2,1,0:T(8,128)(2,1)S(1)} %get-tuple-element.57.q_ref, bf16[3,512,256]{2,1,0:T(8,128)(2,1)S(1)} %get-tuple-element.58.k_ref, ...), custom_call_target="tpu_custom_call" | custom-call | tf_op jit(solution)/shard_map/attend/pallas_call | solution.py:237
  34.7 0.0 copy-start.5
  34.7 0.1 collective-permute-start.6
  34.8 2.1 %collective-permute-start.7 = (bf16[384,256]{1,0:T(8,128)(2,1)S(1)}, bf16[384,256]{1,0:T(8,128)(2,1)S(1)}, u32[]{:S(2)}, u32[]{:S(2)}) collective-permute-start(bf16[384,256]{1,0:T(8,128)(2,1)S(1)} %get-tuple-element.72), channel_id=1, source_target_pairs={{0,2},{1,3},{2,0},{3,1},{4,6},{5,7},{6,4},{7,5},{8,10},{9,11},{10,... | collective-permute-start | bytes 589832 | tf_op jit(solution)/shard_map/ppermute | solution.py:581
  36.9 1.3 %collective-permute-start.8 = (bf16[384,256]{1,0:T(8,128)(2,1)S(1)}, bf16[384,256]{1,0:T(8,128)(2,1)S(1)}, u32[]{:S(2)}, u32[]{:S(2)}) collective-permute-start(bf16[384,256]{1,0:T(8,128)(2,1)S(1)} %get-tuple-element.73), channel_id=1, source_target_pairs={{0,3},{1,0},{2,1},{3,2},{4,7},{5,4},{6,5},{7,6},{8,11},{9,8},{10,9... | collective-permute-start | bytes 589832 | tf_op jit(solution)/shard_map/ppermute | solution.py:581
  38.2 13.7 %all-to-all-start = ((s32[64,1,4]{2,1,0:T(1,128)}), s32[64,1,4]{2,1,0:T(1,128)S(1)}, u32[]{:S(2)}, u32[]{:S(2)}) async-start(s32[64,1,4]{2,1,0:T(1,128)} %bitcast.2), calls=%async_computation | async-start | bytes 65536 | tf_op jit(solution)/shard_map/all_to_all | solution.py:585
  51.9 3.4 %combine.1 = (bf16[3,128,1024]{2,1,0:T(8,128)(2,1)}, bf16[512,384]{1,0:T(8,128)(2,1)S(1)}) custom-call(s32[1]{0:T(128)S(6)} %copy.15.code_ref, bf16[384,256]{1,0:T(8,128)(2,1)S(1)} %get-tuple-element.70.att0_ref, bf16[384,256]{1,0:T(8,128)(2,1)S(1)} %collective-permute-done.6.att1_ref, bf16[384,256]{1,0:T(8,128)(2,1)S(1)} %collective-permute-done.7.att2_ref, ...), custom_call_target="tpu_custom_call" | custom-call | tf_op jit(solution)/shard_map/combine/pallas_call | solution.py:367
  55.4 4.2 %all-to-all-done = s32[64,1,4]{2,1,0:T(1,128)S(1)} async-done(((s32[64,1,4]{2,1,0:T(1,128)}), s32[64,1,4]{2,1,0:T(1,128)S(1)}, u32[]{:S(2)}, u32[]{:S(2)}) %all-to-all-start) | async-done | bytes 1056 | tf_op jit(solution)/shard_map/all_to_all | solution.py:585
  59.6 1.8 %serve.1 = bf16[64,16,384]{2,1,0:T(8,128)(2,1)} custom-call(s32[64,4]{1,0:T(8,128)S(1)} %bitcast.5, bf16[512,384]{1,0:T(8,128)(2,1)S(1)} %get-tuple-element.78.table_ref), custom_call_target="tpu_custom_call" | custom-call | tf_op jit(solution)/shard_map/serve/pallas_call | solution.py:392
  61.4 6.6 %all-to-all-start.1 = ((bf16[64,16,384]{2,1,0:T(8,128)(2,1)}), bf16[64,16,384]{2,1,0:T(8,128)(2,1)S(1)}, u32[]{:S(2)}, u32[]{:S(2)}) async-start(bf16[64,16,384]{2,1,0:T(8,128)(2,1)} %serve.1), calls=%async_computation.1 | async-start | bytes 1572864 | tf_op jit(solution)/shard_map/all_to_all | solution.py:591
  68.0 0.0 copy-start
  68.0 1.8 %fetch.1.taps_ref.w_before_ref = bf16[5,512,512]{2,1,0:T(8,128)(2,1)S(1)} custom-call(bf16[9,512,512]{2,1,0:T(8,128)(2,1)} %conv_hbm_ref.1), custom_call_target="tpu_custom_call" | custom-call | tf_op jit(solution)/shard_map/fetch/pallas_call | solution.py:293
  69.8 21.4 %all-to-all-done.1.arrived_ref = bf16[64,16,384]{2,1,0:T(8,128)(2,1)S(1)} async-done(((bf16[64,16,384]{2,1,0:T(8,128)(2,1)}), bf16[64,16,384]{2,1,0:T(8,128)(2,1)S(1)}, u32[]{:S(2)}, u32[]{:S(2)}) %all-to-all-start.1) | async-done | bytes 786464 | tf_op jit(solution)/shard_map/all_to_all | solution.py:591
  91.2 1.0 inputs.1
  92.2 2.6 %collective-permute-start.9 = (bf16[48,512]{1,0:T(8,128)(2,1)S(1)}, bf16[48,512]{1,0:T(8,128)(2,1)S(1)}, u32[]{:S(2)}, u32[]{:S(2)}) collective-permute-start(bf16[48,512]{1,0:T(8,128)(2,1)S(1)} %get-tuple-element.83), channel_id=1, source_target_pairs={{0,1},{1,2},{2,3},{3,4},{4,5},{5,6},{6,7},{7,8},{8,9},{9,10},{10,1... | collective-permute-start | bytes 147464 | tf_op jit(solution)/shard_map/ppermute | solution.py:541
  94.8 7.8 %collective-permute-start.10 = (bf16[48,512]{1,0:T(8,128)(2,1)S(1)}, bf16[48,512]{1,0:T(8,128)(2,1)S(1)}, u32[]{:S(2)}, u32[]{:S(2)}) collective-permute-start(bf16[48,512]{1,0:T(8,128)(2,1)S(1)} %get-tuple-element.84), channel_id=1, source_target_pairs={{1,0},{2,1},{3,2},{4,3},{5,4},{6,5},{7,6},{8,7},{9,8},{10,9},{11,1... | collective-permute-start | bytes 147464 | tf_op jit(solution)/shard_map/ppermute | solution.py:541
  102.6 2.3 %convolve_inner.1 = (f32[384,512]{1,0:T(8,128)S(1)}, bf16[3,512,512]{2,1,0:T(8,128)(2,1)S(1)}) custom-call(bf16[8,48,512]{2,1,0:T(8,128)(2,1)S(1)} %get-tuple-element.82.x_ref, bf16[5,512,512]{2,1,0:T(8,128)(2,1)S(1)} %fetch.1.taps_ref.w_before_ref, bf16[9,512,512]{2,1,0:T(8,128)(2,1)} %conv_hbm_ref.1), custom_call_target="tpu_custom_call" | custom-call | tf_op jit(solution)/shard_map/convolve_inner/pallas_call | solution.py:485
  104.9 1.6 %convolve_finish.1 = bf16[3,8,16,512]{3,2,1,0:T(8,128)(2,1)} custom-call(bf16[8,48,512]{2,1,0:T(8,128)(2,1)S(1)} %get-tuple-element.82.x_ref, bf16[48,512]{1,0:T(8,128)(2,1)S(1)} %collective-permute-done.9.before_ref, bf16[48,512]{1,0:T(8,128)(2,1)S(1)} %collective-permute-done.10.after_ref, bf16[5,512,512]{2,1,0:T(8,128)(2,1)S(1)} %fetch.1.taps_ref.w_before_ref, ...), custom_call_target="tpu_custom_call" | custom-call | tf_op jit(solution)/shard_map/convolve_finish/pallas_call | solution.py:527
  (22 shorter events, 0.1 us)
Async XLA Ops:
  0.6 18.4 %collective-permute-start = (bf16[256,1024]{1,0:T(8,128)(2,1)}, bf16[256,1024]{1,0:T(8,128)(2,1)S(1)}, u32[]{:S(2)}, u32[]{:S(2)}) collective-permute-start(bf16[256,1024]{1,0:T(8,128)(2,1)} %w0_ref.1), channel_id=1, source_target_pairs={{0,1},{1,2},{2,3},{3,0},{4,5},{5,6},{6,7},{7,4},{8,9},{9,10},{10,1... | collective-permute-start | bytes 1572872 | tf_op jit(solution)/shard_map/ppermute | solution.py:570
  2.3 16.8 %collective-permute-start.1 = (bf16[256,1024]{1,0:T(8,128)(2,1)}, bf16[256,1024]{1,0:T(8,128)(2,1)S(1)}, u32[]{:S(2)}, u32[]{:S(2)}) collective-permute-start(bf16[256,1024]{1,0:T(8,128)(2,1)} %w0_ref.1), channel_id=1, source_target_pairs={{1,0},{2,1},{3,2},{0,3},{5,4},{6,5},{7,6},{4,7},{9,8},{10,9},{11,1... | collective-permute-start | bytes 1572872 | tf_op jit(solution)/shard_map/ppermute | solution.py:570
  5.8 17.7 %collective-permute-start.2 = (bf16[272,1024]{1,0:T(8,128)(2,1)S(1)}, bf16[272,1024]{1,0:T(8,128)(2,1)S(1)}, u32[]{:S(2)}, u32[]{:S(2)}) collective-permute-start(bf16[272,1024]{1,0:T(8,128)(2,1)S(1)} %get-tuple-element.47.late_ref), channel_id=1, source_target_pairs={{0,4},{4,8},{8,12},{12,16},{16,20},{20,24},{24,28},{28,32},{32,36}... | collective-permute-start | bytes 1671176 | tf_op jit(solution)/shard_map/ppermute | solution.py:541
  7.8 14.8 %copy-start.1 = (s32[8,16,1]{1,2,0:T(1,128)S(1)}, s32[8,16,1]{1,2,0:T(1,128)}, u32[]{:S(2)}) copy-start(s32[8,16,1]{1,2,0:T(1,128)} %param.20) | copy-start | bytes 1540
  7.8 14.8 %copy-start.2 = (s32[8,16]{1,0:T(8,128)S(1)}, s32[8,16]{1,0:T(8,128)}, u32[]{:S(2)}) copy-start(s32[8,16]{1,0:T(8,128)} %tok_ref.1) | copy-start | bytes 1540
  7.8 15.7 %collective-permute-start.3 = (bf16[272,1024]{1,0:T(8,128)(2,1)S(1)}, bf16[272,1024]{1,0:T(8,128)(2,1)S(1)}, u32[]{:S(2)}, u32[]{:S(2)}) collective-permute-start(bf16[272,1024]{1,0:T(8,128)(2,1)S(1)} %get-tuple-element.45.early_ref), channel_id=1, source_target_pairs={{4,0},{8,4},{12,8},{16,12},{20,16},{24,20},{28,24},{32,28},{36,32}... | collective-permute-start | bytes 1671176 | tf_op jit(solution)/shard_map/ppermute | solution.py:541
  19.1 15.6 %copy-start.3 = (bf16[256,1024]{1,0:T(8,128)(2,1)}, bf16[256,1024]{1,0:T(8,128)(2,1)S(1)}, u32[]{:S(2)}) copy-start(bf16[256,1024]{1,0:T(8,128)(2,1)S(1)} %collective-permute-done.w1_ref) | copy-start | bytes 1572868
  19.1 15.6 %copy-start.4 = (bf16[256,1024]{1,0:T(8,128)(2,1)}, bf16[256,1024]{1,0:T(8,128)(2,1)S(1)}, u32[]{:S(2)}) copy-start(bf16[256,1024]{1,0:T(8,128)(2,1)S(1)} %collective-permute-done.1.w3_ref) | copy-start | bytes 1572868
  19.1 15.6 %collective-permute-start.4 = (bf16[128,1024]{1,0:T(8,128)(2,1)S(1)}, bf16[128,1024]{1,0:T(8,128)(2,1)S(1)}, u32[]{:S(2)}, u32[]{:S(2)}) collective-permute-start(bf16[128,1024]{1,0:T(8,128)(2,1)S(1)} %slice.6), channel_id=1, source_target_pairs={{0,1},{1,2},{2,3},{3,0},{4,5},{5,6},{6,7},{7,4},{8,9},{9,10},{10,1... | collective-permute-start | bytes 786440 | tf_op jit(solution)/shard_map/ppermute | solution.py:575
  19.6 15.1 %collective-permute-start.5 = (bf16[128,1024]{1,0:T(8,128)(2,1)S(1)}, bf16[128,1024]{1,0:T(8,128)(2,1)S(1)}, u32[]{:S(2)}, u32[]{:S(2)}) collective-permute-start(bf16[128,1024]{1,0:T(8,128)(2,1)S(1)} %slice.7), channel_id=1, source_target_pairs={{1,0},{2,1},{3,2},{0,3},{5,4},{6,5},{7,6},{4,7},{9,8},{10,9},{11,1... | collective-permute-start | bytes 786440 | tf_op jit(solution)/shard_map/ppermute | solution.py:575
  34.7 17.2 %copy-start.5 = (bf16[128,1024]{1,0:T(8,128)(2,1)}, bf16[128,1024]{1,0:T(8,128)(2,1)S(1)}, u32[]{:S(2)}) copy-start(bf16[128,1024]{1,0:T(8,128)(2,1)S(1)} %collective-permute-done.4.top_ref) | copy-start | bytes 786436
  34.7 17.2 %copy-start.6 = (bf16[128,1024]{1,0:T(8,128)(2,1)}, bf16[128,1024]{1,0:T(8,128)(2,1)S(1)}, u32[]{:S(2)}) copy-start(bf16[128,1024]{1,0:T(8,128)(2,1)S(1)} %collective-permute-done.5.low_ref) | copy-start | bytes 786436
  34.7 17.2 %collective-permute-start.6 = (bf16[384,256]{1,0:T(8,128)(2,1)S(1)}, bf16[384,256]{1,0:T(8,128)(2,1)S(1)}, u32[]{:S(2)}, u32[]{:S(2)}) collective-permute-start(bf16[384,256]{1,0:T(8,128)(2,1)S(1)} %get-tuple-element.71), channel_id=1, source_target_pairs={{0,1},{1,2},{2,3},{3,0},{4,5},{5,6},{6,7},{7,4},{8,9},{9,10},{10,1... | collective-permute-start | bytes 589832 | tf_op jit(solution)/shard_map/ppermute | solution.py:581
  34.8 17.1 %collective-permute-start.7 = (bf16[384,256]{1,0:T(8,128)(2,1)S(1)}, bf16[384,256]{1,0:T(8,128)(2,1)S(1)}, u32[]{:S(2)}, u32[]{:S(2)}) collective-permute-start(bf16[384,256]{1,0:T(8,128)(2,1)S(1)} %get-tuple-element.72), channel_id=1, source_target_pairs={{0,2},{1,3},{2,0},{3,1},{4,6},{5,7},{6,4},{7,5},{8,10},{9,11},{10,... | collective-permute-start | bytes 589832 | tf_op jit(solution)/shard_map/ppermute | solution.py:581
  36.9 15.0 %collective-permute-start.8 = (bf16[384,256]{1,0:T(8,128)(2,1)S(1)}, bf16[384,256]{1,0:T(8,128)(2,1)S(1)}, u32[]{:S(2)}, u32[]{:S(2)}) collective-permute-start(bf16[384,256]{1,0:T(8,128)(2,1)S(1)} %get-tuple-element.73), channel_id=1, source_target_pairs={{0,3},{1,0},{2,1},{3,2},{4,7},{5,4},{6,5},{7,6},{8,11},{9,8},{10,9... | collective-permute-start | bytes 589832 | tf_op jit(solution)/shard_map/ppermute | solution.py:581
  38.2 21.4 %all-to-all-start = ((s32[64,1,4]{2,1,0:T(1,128)}), s32[64,1,4]{2,1,0:T(1,128)S(1)}, u32[]{:S(2)}, u32[]{:S(2)}) async-start(s32[64,1,4]{2,1,0:T(1,128)} %bitcast.2), calls=%async_computation | async-start | bytes 65536 | tf_op jit(solution)/shard_map/all_to_all | solution.py:585
  61.4 29.9 %all-to-all-start.1 = ((bf16[64,16,384]{2,1,0:T(8,128)(2,1)}), bf16[64,16,384]{2,1,0:T(8,128)(2,1)S(1)}, u32[]{:S(2)}, u32[]{:S(2)}) async-start(bf16[64,16,384]{2,1,0:T(8,128)(2,1)} %serve.1), calls=%async_computation.1 | async-start | bytes 1572864 | tf_op jit(solution)/shard_map/all_to_all | solution.py:591
  68.0 23.2 %copy-start = (bf16[8,16,512]{2,1,0:T(8,128)(2,1)S(1)}, bf16[8,16,512]{2,1,0:T(8,128)(2,1)}, u32[]{:S(2)}) copy-start(bf16[8,16,512]{2,1,0:T(8,128)(2,1)} %reg_ref.1) | copy-start | bytes 393220
  92.2 12.7 %collective-permute-start.9 = (bf16[48,512]{1,0:T(8,128)(2,1)S(1)}, bf16[48,512]{1,0:T(8,128)(2,1)S(1)}, u32[]{:S(2)}, u32[]{:S(2)}) collective-permute-start(bf16[48,512]{1,0:T(8,128)(2,1)S(1)} %get-tuple-element.83), channel_id=1, source_target_pairs={{0,1},{1,2},{2,3},{3,4},{4,5},{5,6},{6,7},{7,8},{8,9},{9,10},{10,1... | collective-permute-start | bytes 147464 | tf_op jit(solution)/shard_map/ppermute | solution.py:541
  94.8 10.1 %collective-permute-start.10 = (bf16[48,512]{1,0:T(8,128)(2,1)S(1)}, bf16[48,512]{1,0:T(8,128)(2,1)S(1)}, u32[]{:S(2)}, u32[]{:S(2)}) collective-permute-start(bf16[48,512]{1,0:T(8,128)(2,1)S(1)} %get-tuple-element.84), channel_id=1, source_target_pairs={{1,0},{2,1},{3,2},{4,3},{5,4},{6,5},{7,6},{8,7},{9,8},{10,9},{11,1... | collective-permute-start | bytes 147464 | tf_op jit(solution)/shard_map/ppermute | solution.py:541
